TPU v7x, 32 devices: a whole 2x2x4 slice. The times are simulated.
32 devices in a mesh: dp: 8 (over y, x, core), tensor: 4 (over z).
Axes of the slice: x: 2, y: 2, z: 4, core: 2. Of those that a mesh axis runs over, the one named last changes fastest.
Arguments:
- tokens: bfloat16 [8192, 2048], P(('dp', 'tensor')), may hold values from -40 to 40
- cotangent: bfloat16 [8192, 2048], P(('dp', 'tensor')), may hold values from -6 to 6
- norm1_gain: bfloat16 [2048], replicated, may hold values from 0.5 to 1.5
- w_query: bfloat16 [2048, 2048], P(None, 'tensor'), may hold values from -0.125 to 0.125
- w_key: bfloat16 [2048, 512], P(None, 'tensor'), may hold values from -0.125 to 0.125
- w_value: bfloat16 [2048, 512], P(None, 'tensor'), may hold values from -0.125 to 0.125
- w_output: bfloat16 [2048, 2048], P('tensor'), may hold values from -1 to 1
- norm2_gain: bfloat16 [2048], replicated, may hold values from 0.5 to 1.5
- w_gate: bfloat16 [2048, 8192], P(None, 'tensor'), may hold values from -0.125 to 0.125
- w_up: bfloat16 [2048, 8192], P(None, 'tensor'), may hold values from -0.125 to 0.125
- w_down: bfloat16 [8192, 2048], P('tensor'), may hold values from -0.0625 to 0.0625
Outputs:
- output: bfloat16 [8192, 2048], P(('dp', 'tensor'))
- input_grad: bfloat16 [8192, 2048], P(('dp', 'tensor'))
- grad_norm1: float32 [2048], replicated
- grad_query: float32 [2048, 2048], P(None, 'tensor')
- grad_key: float32 [2048, 512], P(None, 'tensor')
- grad_value: float32 [2048, 512], P(None, 'tensor')
- grad_output: float32 [2048, 2048], P('tensor')
- grad_norm2: float32 [2048], replicated
- grad_gate: float32 [2048, 8192], P(None, 'tensor')
- grad_up: float32 [2048, 8192], P(None, 'tensor')
- grad_down: float32 [8192, 2048], P('tensor')
All inputs are finite; a program needn't handle non-finite values.
Results may differ from a plain program's by a relative error of at most 0.022.
Values may be sent and summed in bfloat16 or wider, within the bound.
No kernel may reach another device: no remote copies, remote signals or barrier semaphores. Data moves between devices by JAX's collectives and lax.ppermute only.
A program may use at most 384 MiB of HBM per device.

v0:
```python
import jax
import jax.numpy as jnp
from jax import lax
from jax.sharding import PartitionSpec as P

HQ = 32
KV = 8
HD = 64
SEQLEN = 512


EPS = 1e-05
ROPE_BASE = 500000.0
MASKED = -1e30


def rope_tables(length, columns):
    half_width = columns // 2
    frequency = ROPE_BASE ** (-(jnp.arange(half_width, dtype=jnp.float32) * 2.0 / columns))
    angles = jnp.arange(length, dtype=jnp.float32)[:, None] * frequency[None, :]
    return (jnp.cos(angles), jnp.sin(angles))


def rotate(values, cos_table, sin_table):
    half_width = values.shape[-1] // 2
    table_shape = (cos_table.shape[0],) + (1,) * (values.ndim - 3) + (half_width,)
    cos_table = cos_table.reshape(table_shape)
    sin_table = sin_table.reshape(table_shape)
    first_half = values[..., :half_width]
    second_half = values[..., half_width:]
    return jnp.concatenate(
        [
            first_half * cos_table - second_half * sin_table,
            second_half * cos_table + first_half * sin_table,
        ],
        axis=-1,
    )


def rms_norm(values, gain_vec):
    row_scale = lax.rsqrt(jnp.mean(values * values, axis=-1, keepdims=True) + EPS)
    return values * row_scale * gain_vec


def norm_backward(values, gain_vec, upstream):
    _, pull_back = jax.vjp(lambda inner_values: rms_norm(inner_values, gain_vec), values)
    return pull_back(upstream)[0]


def gain_gradient(values, upstream):
    row_scale = lax.rsqrt(jnp.mean(values * values, axis=-1, keepdims=True) + EPS)
    return jnp.sum(upstream * values * row_scale, axis=0)


def contract_rows(left_side, right_side):
    return lax.dot_general(
        left_side, right_side, (((0,), (0,)), ((), ())), preferred_element_type=jnp.float32
    )


def contract_cols(left_side, right_side):
    return lax.dot_general(
        left_side, right_side, (((1,), (1,)), ((), ())), preferred_element_type=jnp.float32
    )


def gated_unit(gate_in, up_in):
    return jax.nn.silu(gate_in) * up_in


def on_device(
    tokens,
    cotangent,
    norm1_gain,
    w_query,
    w_key,
    w_value,
    w_output,
    norm2_gain,
    w_gate,
    w_up,
    w_down,
):
    all_tokens, all_cot = (
        lax.all_gather(tokens, "tensor", axis=0, tiled=True),
        lax.all_gather(cotangent, "tensor", axis=0, tiled=True),
    )
    all_rows = all_tokens.shape[0]
    seq_count = all_rows // SEQLEN
    kv_heads = w_key.shape[1] // HD
    group_size = HQ // KV
    score_scale = HD ** (-0.5)
    gain_one = norm1_gain.astype(jnp.float32)
    gain_two = norm2_gain.astype(jnp.float32)
    token_values = all_tokens.astype(jnp.float32)
    own_tokens = tokens.astype(jnp.float32)
    normed1 = rms_norm(token_values, gain_one).astype(jnp.bfloat16)
    query_pre = jnp.dot(normed1, w_query, preferred_element_type=jnp.float32).reshape(
        seq_count, SEQLEN, kv_heads, group_size, HD
    )
    key_pre = jnp.dot(normed1, w_key, preferred_element_type=jnp.float32).reshape(
        seq_count, SEQLEN, kv_heads, HD
    )
    value_all = (
        jnp.dot(normed1, w_value, preferred_element_type=jnp.float32)
        .astype(jnp.bfloat16)
        .reshape(seq_count, SEQLEN, kv_heads, HD)
    )
    cos_table, sin_table = rope_tables(SEQLEN, HD)
    query_rot = rotate(query_pre, cos_table, sin_table).astype(jnp.bfloat16)
    key_rot = rotate(key_pre, cos_table, sin_table).astype(jnp.bfloat16)
    positions = jnp.arange(SEQLEN)
    causal = positions[:, None] >= positions[None, :]

    def masked_scores():
        raw_scores = (
            jnp.einsum("sqhgd,skhd->shgqk", query_rot, key_rot, preferred_element_type=jnp.float32)
            * score_scale
        )
        return jnp.where(causal, raw_scores, MASKED)

    scores = masked_scores()
    row_max = jnp.max(scores, axis=-1, keepdims=True)
    exp_scores = jnp.exp(scores - row_max)
    row_total = jnp.sum(exp_scores, axis=-1, keepdims=True)
    attn_probs = exp_scores / row_total
    log_total = row_max + jnp.log(row_total)
    mixed_heads = jnp.einsum(
        "shgqk,skhd->sqhgd",
        attn_probs.astype(jnp.bfloat16),
        value_all,
        preferred_element_type=jnp.float32,
    )
    heads_out = mixed_heads.astype(jnp.bfloat16).reshape(all_rows, kv_heads * group_size * HD)
    attn_part = jnp.dot(heads_out, w_output, preferred_element_type=jnp.float32)
    hidden_state = own_tokens + lax.psum_scatter(
        attn_part.astype(jnp.bfloat16), "tensor", scatter_dimension=0, tiled=True
    ).astype(jnp.float32)
    normed2 = lax.all_gather(
        rms_norm(hidden_state, gain_two).astype(jnp.bfloat16), "tensor", axis=0, tiled=True
    )
    gate_proj = jnp.dot(normed2, w_gate, preferred_element_type=jnp.float32)
    up_proj = jnp.dot(normed2, w_up, preferred_element_type=jnp.float32)
    activated = gated_unit(gate_proj, up_proj).astype(jnp.bfloat16)
    mlp_part = jnp.dot(activated, w_down, preferred_element_type=jnp.float32)
    output = (
        hidden_state
        + lax.psum_scatter(
            mlp_part.astype(jnp.bfloat16), "tensor", scatter_dimension=0, tiled=True
        ).astype(jnp.float32)
    ).astype(jnp.bfloat16)
    grad_down = contract_rows(activated, all_cot)
    d_activated = contract_cols(all_cot, w_down)
    _, pull_gated = jax.vjp(gated_unit, gate_proj, up_proj)
    d_gate, d_up = pull_gated(d_activated)
    d_gate = d_gate.astype(jnp.bfloat16)
    d_up = d_up.astype(jnp.bfloat16)
    grad_gate = contract_rows(normed2, d_gate)
    grad_up = contract_rows(normed2, d_up)
    dn2_part = contract_cols(d_gate, w_gate) + contract_cols(d_up, w_up)
    d_normed2 = lax.psum_scatter(
        dn2_part.astype(jnp.bfloat16), "tensor", scatter_dimension=0, tiled=True
    ).astype(jnp.float32)
    d_state = cotangent.astype(jnp.float32) + norm_backward(hidden_state, gain_two, d_normed2)
    d_state_low = lax.all_gather(d_state.astype(jnp.bfloat16), "tensor", axis=0, tiled=True)
    grad_gain2 = gain_gradient(hidden_state, d_normed2)
    grad_output = contract_rows(heads_out, d_state_low)
    d_heads = (
        contract_cols(d_state_low, w_output)
        .astype(jnp.bfloat16)
        .reshape(seq_count, SEQLEN, kv_heads, group_size, HD)
    )
    probs_again = jnp.exp(masked_scores() - log_total)
    probs_low = probs_again.astype(jnp.bfloat16)
    d_value = (
        jnp.einsum("shgqk,sqhgd->skhd", probs_low, d_heads, preferred_element_type=jnp.float32)
        .astype(jnp.bfloat16)
        .reshape(all_rows, kv_heads * HD)
    )
    d_probs = jnp.einsum(
        "sqhgd,skhd->shgqk", d_heads, value_all, preferred_element_type=jnp.float32
    )
    d_scores = (
        probs_again * (d_probs - jnp.sum(probs_again * d_probs, axis=-1, keepdims=True))
    ).astype(jnp.bfloat16)
    d_query = (
        jnp.einsum("shgqk,skhd->sqhgd", d_scores, key_rot, preferred_element_type=jnp.float32)
        * score_scale
    )
    d_key = (
        jnp.einsum("shgqk,sqhgd->skhd", d_scores, query_rot, preferred_element_type=jnp.float32)
        * score_scale
    )
    d_query = (
        rotate(d_query, cos_table, -sin_table)
        .astype(jnp.bfloat16)
        .reshape(all_rows, kv_heads * group_size * HD)
    )
    d_key = (
        rotate(d_key, cos_table, -sin_table).astype(jnp.bfloat16).reshape(all_rows, kv_heads * HD)
    )
    grad_query = contract_rows(normed1, d_query)
    grad_key = contract_rows(normed1, d_key)
    grad_value = contract_rows(normed1, d_value)
    dn1_part = (
        contract_cols(d_query, w_query)
        + contract_cols(d_key, w_key)
        + contract_cols(d_value, w_value)
    )
    d_normed1 = lax.psum_scatter(
        dn1_part.astype(jnp.bfloat16), "tensor", scatter_dimension=0, tiled=True
    ).astype(jnp.float32)
    input_grad = (d_state + norm_backward(own_tokens, gain_one, d_normed1)).astype(jnp.bfloat16)
    grad_gain1 = gain_gradient(own_tokens, d_normed1)
    gain_one_sum, gain_two_sum = lax.psum((grad_gain1, grad_gain2), ("dp", "tensor"))
    part_query, part_key, part_value, part_output, part_gate, part_up, part_down = (
        lax.psum_scatter(grad_query, "dp", scatter_dimension=0, tiled=True),
        lax.psum_scatter(grad_key, "dp", scatter_dimension=0, tiled=True),
        lax.psum_scatter(grad_value, "dp", scatter_dimension=0, tiled=True),
        lax.psum_scatter(grad_output, "dp", scatter_dimension=0, tiled=True),
        lax.psum_scatter(grad_gate, "dp", scatter_dimension=0, tiled=True),
        lax.psum_scatter(grad_up, "dp", scatter_dimension=0, tiled=True),
        lax.psum_scatter(grad_down, "dp", scatter_dimension=0, tiled=True),
    )
    full_query, full_key, full_value, full_output, full_gate, full_up, full_down = (
        lax.all_gather(part_query, "dp", axis=0, tiled=True),
        lax.all_gather(part_key, "dp", axis=0, tiled=True),
        lax.all_gather(part_value, "dp", axis=0, tiled=True),
        lax.all_gather(part_output, "dp", axis=0, tiled=True),
        lax.all_gather(part_gate, "dp", axis=0, tiled=True),
        lax.all_gather(part_up, "dp", axis=0, tiled=True),
        lax.all_gather(part_down, "dp", axis=0, tiled=True),
    )
    return (
        output,
        input_grad,
        gain_one_sum,
        full_query,
        full_key,
        full_value,
        full_output,
        gain_two_sum,
        full_gate,
        full_up,
        full_down,
    )


def solution(mesh):
    return jax.shard_map(
        on_device,
        mesh=mesh,
        in_specs=(
            P(("dp", "tensor"), None),
            P(("dp", "tensor"), None),
            P(),
            P(None, "tensor"),
            P(None, "tensor"),
            P(None, "tensor"),
            P("tensor", None),
            P(),
            P(None, "tensor"),
            P(None, "tensor"),
            P("tensor", None),
        ),
        out_specs=(
            P(("dp", "tensor"), None),
            P(("dp", "tensor"), None),
            P(),
            P(None, "tensor"),
            P(None, "tensor"),
            P(None, "tensor"),
            P("tensor", None),
            P(),
            P(None, "tensor"),
            P(None, "tensor"),
            P("tensor", None),
        ),
        check_vma=False,
    )
```

profile of v0, /device:TPU:0, one launch (start us, length us, event | category | flops | bytes accessed | tf_op | source)
XLA Modules:
  0.0 1798.0 jit_solution(11805181959332590701)
XLA Ops:
  10.4 82.7 %all-gather.12.cloned.1.call-done = bf16[1024,2048]{1,0:T(8,128)(2,1)} async-done(((bf16[256,2048]{1,0:T(8,128)(2,1)}), bf16[1024,2048]{1,0:T(8,128)(2,1)}) %all-gather.12.cloned.1.call-update) | async-done | bytes 4194320 | tf_op jit(solution)/shard_map/all_gather | solution.py:85
  154.7 74.8 %reduce-scatter.12.cloned.1.call-done = bf16[256,2048]{1,0:T(8,128)(2,1)} async-done(((bf16[1024,2048]{1,0:T(8,128)(2,1)}), bf16[256,2048]{1,0:T(8,128)(2,1)}) %reduce-scatter.12.cloned.1.call-update) | async-done | bytes 1048592 | tf_op jit(solution)/shard_map/reduce_scatter | solution.py:136
  234.3 80.8 %all-gather.14.cloned.1.call-done = bf16[1024,2048]{1,0:T(8,128)(2,1)} async-done(((bf16[256,2048]{1,0:T(8,128)(2,1)}), bf16[1024,2048]{1,0:T(8,128)(2,1)}) %all-gather.14.cloned.1.call-update) | async-done | bytes 4194320 | tf_op jit(solution)/shard_map/all_gather | solution.py:139
  315.1 15.9 fusion.59
  331.0 13.2 fusion.60
  344.2 51.6 %all-gather.16.cloned.1.call-done = bf16[1024,2048]{1,0:T(8,128)(2,1)} async-done(((bf16[256,2048]{1,0:T(8,128)(2,1)}), bf16[1024,2048]{1,0:T(8,128)(2,1)}) %all-gather.16.cloned.1.call-update) | async-done | bytes 4194320 | tf_op jit(solution)/shard_map/all_gather | solution.py:86
  395.8 21.8 %multiply_convert_fusion = (bf16[1024,2048]{1,0:T(8,128)(2,1)}, bf16[1024,2048]{1,0:T(8,128)(2,1)}, bf16[1024,2048]{1,0:T(8,128)(2,1)}) fusion(f32[1024,2048]{1,0:T(8,128)} %fusion.59, f32[1024,2048]{1,0:T(8,128)} %fusion.60, bf16[1024,2048]{1,0:T(8,128)(2,1)} %all-gather.16.cloned.1.call-done, bf16[2048,2048]{1,0:T(8,128)(2,1)} %param.21), kind=kOutput, calls=%fused_computation.24 | convolution fusion | flops 8623489024 | bytes 41943040 | tf_op jit(solution)/shard_map/dot_general | solution.py:62
  417.6 12.9 fusion.61
  430.5 12.8 add_convert_fusion.1
  443.4 75.4 %reduce-scatter.16.cloned.1.call-done = bf16[256,2048]{1,0:T(8,128)(2,1)} async-done(((bf16[1024,2048]{1,0:T(8,128)(2,1)}), bf16[256,2048]{1,0:T(8,128)(2,1)}) %reduce-scatter.16.cloned.1.call-update) | async-done | bytes 1048592 | tf_op jit(solution)/shard_map/reduce_scatter | solution.py:161
  525.8 81.3 %all-gather.18.cloned.1.call-done = bf16[1024,2048]{1,0:T(8,128)(2,1)} async-done(((bf16[256,2048]{1,0:T(8,128)(2,1)}), bf16[1024,2048]{1,0:T(8,128)(2,1)}) %all-gather.18.cloned.1.call-update) | async-done | bytes 4194320 | tf_op jit(solution)/shard_map/all_gather | solution.py:165
  639.6 12.9 fusion.2
  680.6 15.4 fusion.68
  696.3 15.6 fusion.69
  712.0 15.8 fusion.70
  736.9 14.5 convolution_convert_fusion
  751.5 16.9 reduce-scatter.20.cloned.1.call-done
  768.4 54.3 %reduce-scatter.26.cloned.1.call-done = f32[64,2048]{1,0:T(8,128)} async-done(((f32[512,2048]{1,0:T(8,128)}), f32[64,2048]{1,0:T(8,128)}) %reduce-scatter.26.cloned.1.call-update) | async-done | bytes 524304 | tf_op jit(solution)/shard_map/reduce_scatter | solution.py:220
  822.9 120.3 %reduce-scatter.28.cloned.1.call-done = f32[256,2048]{1,0:T(8,128)} async-done(((f32[2048,2048]{1,0:T(8,128)}), f32[256,2048]{1,0:T(8,128)}) %reduce-scatter.28.cloned.1.call-update) | async-done | bytes 2097168 | tf_op jit(solution)/shard_map/reduce_scatter | solution.py:221
  943.3 120.1 %reduce-scatter.30.cloned.1.call-done = f32[256,2048]{1,0:T(8,128)} async-done(((f32[2048,2048]{1,0:T(8,128)}), f32[256,2048]{1,0:T(8,128)}) %reduce-scatter.30.cloned.1.call-update) | async-done | bytes 2097168 | tf_op jit(solution)/shard_map/reduce_scatter | solution.py:222
  1063.4 120.3 %reduce-scatter.32.cloned.1.call-done = f32[256,2048]{1,0:T(8,128)} async-done(((f32[2048,2048]{1,0:T(8,128)}), f32[256,2048]{1,0:T(8,128)}) %reduce-scatter.32.cloned.1.call-update) | async-done | bytes 2097168 | tf_op jit(solution)/shard_map/reduce_scatter | solution.py:223
  1183.8 25.1 %all-gather.24.cloned.1.call-done = f32[2048,128]{1,0:T(8,128)} async-done(((f32[256,128]{1,0:T(8,128)}), f32[2048,128]{1,0:T(8,128)}) %all-gather.24.cloned.1.call-update) | async-done | bytes 1048592 | tf_op jit(solution)/shard_map/all_gather | solution.py:228
  1208.9 25.1 %all-gather.22.cloned.1.call-done = f32[2048,128]{1,0:T(8,128)} async-done(((f32[256,128]{1,0:T(8,128)}), f32[2048,128]{1,0:T(8,128)}) %all-gather.22.cloned.1.call-update) | async-done | bytes 1048592 | tf_op jit(solution)/shard_map/all_gather | solution.py:227
  1234.0 79.6 %reduce-scatter.18.cloned.1.call-done = bf16[256,2048]{1,0:T(8,128)(2,1)} async-done(((bf16[1024,2048]{1,0:T(8,128)(2,1)}), bf16[256,2048]{1,0:T(8,128)(2,1)}) %reduce-scatter.18.cloned.1.call-update) | async-done | bytes 1048592 | tf_op jit(solution)/shard_map/reduce_scatter | solution.py:210
  1315.4 43.6 %all-reduce = (f32[2048]{0:T(1024)}, f32[2048]{0:T(1024)}) all-reduce(f32[2048]{0:T(1024)S(1)} %get-tuple-element.13, f32[2048]{0:T(1024)S(1)} %copy-done.37), channel_id=1, replica_groups=mesh['dp'=8,'tensor'=4] {'dp','tensor'}, use_global_device_ids=true, to_apply=%region_13.14 | all-reduce | flops 4096 | bytes 32768 | tf_op jit(solution)/shard_map/psum | solution.py:215
  1359.1 35.5 %reduce-scatter.14.cloned.1.call-done = bf16[256,2048]{1,0:T(8,128)(2,1)} async-done(((bf16[1024,2048]{1,0:T(8,128)(2,1)}), bf16[256,2048]{1,0:T(8,128)(2,1)}) %reduce-scatter.14.cloned.1.call-update) | async-done | bytes 1048592 | tf_op jit(solution)/shard_map/reduce_scatter | solution.py:148
  1399.5 34.0 %all-gather.20.cloned.1.call-done = f32[2048,512]{1,0:T(8,128)} async-done(((f32[256,512]{1,0:T(8,128)}), f32[2048,512]{1,0:T(8,128)}) %all-gather.20.cloned.1.call-update) | async-done | bytes 4194320 | tf_op jit(solution)/shard_map/all_gather | solution.py:226
  1433.5 38.5 %all-gather.26.cloned.1.call-done = f32[512,2048]{1,0:T(8,128)} async-done(((f32[64,2048]{1,0:T(8,128)}), f32[512,2048]{1,0:T(8,128)}) %all-gather.26.cloned.1.call-update) | async-done | bytes 4194320 | tf_op jit(solution)/shard_map/all_gather | solution.py:229
  1472.0 91.5 %all-gather.28.cloned.1.call-done = f32[2048,2048]{1,0:T(8,128)} async-done(((f32[256,2048]{1,0:T(8,128)}), f32[2048,2048]{1,0:T(8,128)}) %all-gather.28.cloned.1.call-update) | async-done | bytes 16777232 | tf_op jit(solution)/shard_map/all_gather | solution.py:230
  1563.5 91.7 %all-gather.30.cloned.1.call-done = f32[2048,2048]{1,0:T(8,128)} async-done(((f32[256,2048]{1,0:T(8,128)}), f32[2048,2048]{1,0:T(8,128)}) %all-gather.30.cloned.1.call-update) | async-done | bytes 16777232 | tf_op jit(solution)/shard_map/all_gather | solution.py:231
  1655.1 91.6 %all-gather.32.cloned.1.call-done = f32[2048,2048]{1,0:T(8,128)} async-done(((f32[256,2048]{1,0:T(8,128)}), f32[2048,2048]{1,0:T(8,128)}) %all-gather.32.cloned.1.call-update) | async-done | bytes 16777232 | tf_op jit(solution)/shard_map/all_gather | solution.py:232
  1779.0 11.9 copy.106
  (215 shorter events, 185.4 us)
Async XLA Ops:
  7.2 85.9 %all-gather.12.cloned.1.call-start = ((), (), s32[]{:S(2)}) async-start(), calls=%async_computation.11 | async-start | bytes 5242880 | tf_op jit(solution)/shard_map/all_gather | solution.py:85
  7.9 221.5 %reduce-scatter.12.cloned.1.call-start = ((), (), s32[]{:S(2)}) async-start(), calls=%async_computation.12 | async-start | bytes 5242880 | tf_op jit(solution)/shard_map/reduce_scatter | solution.py:136
  154.0 161.1 %all-gather.14.cloned.1.call-start = ((), (), s32[]{:S(2)}) async-start(), calls=%async_computation.13 | async-start | bytes 5242880 | tf_op jit(solution)/shard_map/all_gather | solution.py:139
  154.7 367.2 %copy-start.33 = (f32[2048]{0:T(1024)}, f32[2048]{0:T(1024)S(1)}, u32[]{:S(2)}) copy-start(f32[2048]{0:T(1024)S(1)} %convert_element_type.112) | copy-start | bytes 24580
  233.7 162.1 %all-gather.16.cloned.1.call-start = ((), (), s32[]{:S(2)}) async-start(), calls=%async_computation.15 | async-start | bytes 5242880 | tf_op jit(solution)/shard_map/all_gather | solution.py:86
  234.3 284.5 %reduce-scatter.16.cloned.1.call-start = ((), (), s32[]{:S(2)}) async-start(), calls=%async_computation.16 | async-start | bytes 5242880 | tf_op jit(solution)/shard_map/reduce_scatter | solution.py:161
  443.3 163.8 %all-gather.18.cloned.1.call-start = ((), (), s32[]{:S(2)}) async-start(), calls=%async_computation.17 | async-start | bytes 5242880 | tf_op jit(solution)/shard_map/all_gather | solution.py:165
  525.7 202.1 %reduce-scatter.24.cloned.1.call-start = ((), (), s32[]{:S(2)}) async-start(), calls=%async_computation.23 | async-start | bytes 1179648 | tf_op jit(solution)/shard_map/reduce_scatter | solution.py:219
  639.5 88.9 %reduce-scatter.22.cloned.1.call-start = ((), (), s32[]{:S(2)}) async-start(), calls=%async_computation.21 | async-start | bytes 1179648 | tf_op jit(solution)/shard_map/reduce_scatter | solution.py:218
  660.1 108.3 %reduce-scatter.20.cloned.1.call-start = ((), (), s32[]{:S(2)}) async-start(), calls=%async_computation.19 | async-start | bytes 4718592 | tf_op jit(solution)/shard_map/reduce_scatter | solution.py:217
  672.8 150.0 %reduce-scatter.26.cloned.1.call-start = ((), (), s32[]{:S(2)}) async-start(), calls=%async_computation.25 | async-start | bytes 4718592 | tf_op jit(solution)/shard_map/reduce_scatter | solution.py:220
  680.6 262.6 %reduce-scatter.28.cloned.1.call-start = ((), (), s32[]{:S(2)}) async-start(), calls=%async_computation.27 | async-start | bytes 18874368 | tf_op jit(solution)/shard_map/reduce_scatter | solution.py:221
  696.1 367.3 %reduce-scatter.30.cloned.1.call-start = ((), (), s32[]{:S(2)}) async-start(), calls=%async_computation.29 | async-start | bytes 18874368 | tf_op jit(solution)/shard_map/reduce_scatter | solution.py:222
  711.9 471.8 %reduce-scatter.32.cloned.1.call-start = ((), (), s32[]{:S(2)}) async-start(), calls=%async_computation.31 | async-start | bytes 18874368 | tf_op jit(solution)/shard_map/reduce_scatter | solution.py:223
  727.8 481.1 %all-gather.24.cloned.1.call-start = ((), (), s32[]{:S(2)}) async-start(), calls=%async_computation.24 | async-start | bytes 1179648 | tf_op jit(solution)/shard_map/all_gather | solution.py:228
  728.4 505.6 %all-gather.22.cloned.1.call-start = ((), (), s32[]{:S(2)}) async-start(), calls=%async_computation.22 | async-start | bytes 1179648 | tf_op jit(solution)/shard_map/all_gather | solution.py:227
  729.0 584.6 %reduce-scatter.18.cloned.1.call-start = ((), (), s32[]{:S(2)}) async-start(), calls=%async_computation.18 | async-start | bytes 5242880 | tf_op jit(solution)/shard_map/reduce_scatter | solution.py:210
  736.9 657.8 %reduce-scatter.14.cloned.1.call-start = ((), (), s32[]{:S(2)}) async-start(), calls=%async_computation.14 | async-start | bytes 5242880 | tf_op jit(solution)/shard_map/reduce_scatter | solution.py:148
  751.4 432.3 %copy-start.40 = (f32[256]{0:T(256)S(1)}, f32[256]{0:T(256)}, u32[]{:S(2)}) copy-start(f32[256]{0:T(256)} %get-tuple-element.15) | copy-start | bytes 3076
  751.4 562.1 %copy-start.9 = (bf16[256,2048]{1,0:T(8,128)(2,1)S(1)}, bf16[256,2048]{1,0:T(8,128)(2,1)}, u32[]{:S(2)}) copy-start(bf16[256,2048]{1,0:T(8,128)(2,1)} %param.11) | copy-start | bytes 3145732
  751.4 562.1 %copy-start.36 = (f32[2048]{0:T(1024)S(1)}, f32[2048]{0:T(1024)}, u32[]{:S(2)}) copy-start(f32[2048]{0:T(1024)} %copy-done.35) | copy-start | bytes 24580
  751.5 682.0 %all-gather.20.cloned.1.call-start = ((), (), s32[]{:S(2)}) async-start(), calls=%async_computation.20 | async-start | bytes 4718592 | tf_op jit(solution)/shard_map/all_gather | solution.py:226
  768.4 703.6 %all-gather.26.cloned.1.call-start = ((), (), s32[]{:S(2)}) async-start(), calls=%async_computation.26 | async-start | bytes 4718592 | tf_op jit(solution)/shard_map/all_gather | solution.py:229
  822.8 740.6 %all-gather.28.cloned.1.call-start = ((), (), s32[]{:S(2)}) async-start(), calls=%async_computation.28 | async-start | bytes 18874368 | tf_op jit(solution)/shard_map/all_gather | solution.py:230
  943.2 372.3 %copy-start.37 = (f32[2048]{0:T(1024)S(1)}, f32[2048]{0:T(1024)}, u32[]{:S(2)}) copy-start(f32[2048]{0:T(1024)} %get-tuple-element.11) | copy-start | bytes 24580
  943.2 451.5 %copy-start.10 = (bf16[256,2048]{1,0:T(8,128)(2,1)S(1)}, bf16[256,2048]{1,0:T(8,128)(2,1)}, u32[]{:S(2)}) copy-start(bf16[256,2048]{1,0:T(8,128)(2,1)} %reduce-scatter.12.cloned.1.call-done) | copy-start | bytes 3145732
  943.2 451.5 %copy-start.13 = (bf16[256,2048]{1,0:T(8,128)(2,1)S(1)}, bf16[256,2048]{1,0:T(8,128)(2,1)}, u32[]{:S(2)}) copy-start(bf16[256,2048]{1,0:T(8,128)(2,1)} %reduce-scatter.16.cloned.1.call-done) | copy-start | bytes 3145732
  943.2 451.5 %copy-start.34 = (f32[2048]{0:T(1024)S(1)}, f32[2048]{0:T(1024)}, u32[]{:S(2)}) copy-start(f32[2048]{0:T(1024)} %copy-done.33) | copy-start | bytes 24580
  943.2 451.5 %copy-start.39 = (f32[256]{0:T(256)S(1)}, f32[256]{0:T(256)}, u32[]{:S(2)}) copy-start(f32[256]{0:T(256)} %copy-done.38) | copy-start | bytes 3076
  943.2 451.5 %copy-start.42 = (f32[256]{0:T(256)S(1)}, f32[256]{0:T(256)}, u32[]{:S(2)}) copy-start(f32[256]{0:T(256)} %copy-done.41) | copy-start | bytes 3076
  943.2 711.9 %all-gather.30.cloned.1.call-start = ((), (), s32[]{:S(2)}) async-start(), calls=%async_computation.30 | async-start | bytes 18874368 | tf_op jit(solution)/shard_map/all_gather | solution.py:231
  1063.4 683.4 %all-gather.32.cloned.1.call-start = ((), (), s32[]{:S(2)}) async-start(), calls=%async_computation.32 | async-start | bytes 18874368 | tf_op jit(solution)/shard_map/all_gather | solution.py:232
  (41 other events, 937.6 us)
Sparse Core Ops, SparseCore 0:
  9.6 83.4 all-gather.11
  154.1 75.2 reduce-scatter.11
  233.8 81.2 all-gather.13
  316.5 79.2 all-gather.15
  443.4 75.2 reduce-scatter.15
  525.8 81.2 all-gather.17
  639.6 34.4 reduce-scatter.23
  677.8 35.9 reduce-scatter.21
  717.2 51.1 reduce-scatter.19
  771.6 51.1 reduce-scatter.25
  826.9 116.1 reduce-scatter.27
  947.2 116.1 reduce-scatter.29
  1067.5 116.1 reduce-scatter.31
  1185.5 23.3 all-gather.23
  1210.6 23.3 all-gather.21
  1236.7 76.7 reduce-scatter.17
  1316.3 78.3 reduce-scatter.13
  1396.4 37.0 all-gather.19
  1435.3 36.5 all-gather.25
  1473.7 89.7 all-gather.27
  1565.3 89.7 all-gather.29
  1657.0 89.7 all-gather.31
where the time goes:
time: 1800 us
  waiting for transfers between devices  1390 us (77%)
  matrix products  222 us (12%)
  local copies, waits for them, and re-layouts  72.4 us (4%)
  other arithmetic  49 us (3%)
  blocking collectives  43.6 us (2%)
    reduce_scatter x1, waiting for transfers between devices, on_device(): lax.psum_scatter(grad_gate, 'dp', scatter_dimension=0, tiled=True)  120 us
    reduce_scatter x1, waiting for transfers between devices, on_device(): lax.psum_scatter(grad_down, 'dp', scatter_dimension=0, tiled=True)  120 us
    reduce_scatter x1, waiting for transfers between devices, on_device(): lax.psum_scatter(grad_up, 'dp', scatter_dimension=0, tiled=True)  120 us
    all_gather x1, waiting for transfers between devices, on_device(): lax.all_gather(part_up, 'dp', axis=0, tiled=True)  91.7 us
    all_gather x1, waiting for transfers between devices, on_device(): lax.all_gather(part_down, 'dp', axis=0, tiled=True)  91.6 us
    all_gather x1, waiting for transfers between devices, on_device(): lax.all_gather(part_gate, 'dp', axis=0, tiled=True)  91.5 us
    all_gather x1, waiting for transfers between devices, on_device(): lax.all_gather(tokens, 'tensor', axis=0, tiled=True)  82.7 us
    all_gather x1, waiting for transfers between devices, on_device(): lax.all_gather(d_state.astype(jnp.bfloat16), 'tensor', axis=0, tiled=True)  81.3 us
  transfers between devices with their start and end apart: 22, of which 20 were waited for; matrix products, arithmetic and copies ran while one was open for 8% of the time, Pallas kernels for 0%

commit v1 on v0

v1 whole, which is shorter than its diff:
```python
import jax
import jax.numpy as jnp
from jax import lax
from jax.experimental import pallas as pl
from jax.experimental.pallas import tpu as pltpu
from jax.experimental.layout import Layout, with_layout_constraint
from jax.sharding import PartitionSpec as P


HQ = 32
KV = 8
HD = 64
SEQLEN = 512


EPS = 1e-05
ROPE_BASE = 500000.0
MASKED = -1e30


def rope_tables(length, columns):
    half_width = columns // 2
    frequency = ROPE_BASE ** (-(jnp.arange(half_width, dtype=jnp.float32) * 2.0 / columns))
    angles = jnp.arange(length, dtype=jnp.float32)[:, None] * frequency[None, :]
    return (jnp.cos(angles), jnp.sin(angles))


def rotate(values, cos_table, sin_table):
    half_width = values.shape[-1] // 2
    table_shape = (cos_table.shape[0],) + (1,) * (values.ndim - 3) + (half_width,)
    cos_table = cos_table.reshape(table_shape)
    sin_table = sin_table.reshape(table_shape)
    first_half = values[..., :half_width]
    second_half = values[..., half_width:]
    return jnp.concatenate(
        [
            first_half * cos_table - second_half * sin_table,
            second_half * cos_table + first_half * sin_table,
        ],
        axis=-1,
    )


def rms_norm(values, gain_vec):
    row_scale = lax.rsqrt(jnp.mean(values * values, axis=-1, keepdims=True) + EPS)
    return values * row_scale * gain_vec


def norm_backward(values, gain_vec, upstream):
    _, pull_back = jax.vjp(lambda inner_values: rms_norm(inner_values, gain_vec), values)
    return pull_back(upstream)[0]


def gain_gradient(values, upstream):
    row_scale = lax.rsqrt(jnp.mean(values * values, axis=-1, keepdims=True) + EPS)
    return jnp.sum(upstream * values * row_scale, axis=0)


def contract_rows(left_side, right_side):
    return lax.dot_general(
        left_side, right_side, (((0,), (0,)), ((), ())), preferred_element_type=jnp.float32
    )


def contract_cols(left_side, right_side):
    return lax.dot_general(
        left_side, right_side, (((1,), (1,)), ((), ())), preferred_element_type=jnp.float32
    )


def gated_unit(gate_in, up_in):
    return jax.nn.silu(gate_in) * up_in


def gather_rows(block, axis):
    return lax.all_gather(block, axis, axis=0, tiled=True)


def scatter_sum(partial, axis):
    return lax.psum_scatter(partial, axis, scatter_dimension=0, tiled=True)


def exchange_sum(partial, axis):
    n = lax.axis_size(axis)
    me = lax.axis_index(axis)
    rows = partial.shape[0] // n

    def block(index):
        return lax.dynamic_slice_in_dim(partial, index * rows, rows, 0)

    total = block(me).astype(jnp.float32)
    for hop in range(1, n):
        moved = lax.ppermute(block((me + hop) % n), axis, [(i, (i + hop) % n) for i in range(n)])
        total += moved.astype(jnp.float32)
    return total


def cube_gather(block, axis):
    n = lax.axis_size(axis)
    bits = [1 << b for b in range(n.bit_length() - 1)]
    half = block.shape[0] // 2
    halves = []
    for part, order in ((block[:half], bits[1:] + bits[:1]), (block[half:], bits[:0:-1] + bits[:1])):
        held, offsets = part[None], [0]
        for bit in order:
            moved = lax.ppermute(held, axis, [(i, i ^ bit) for i in range(n)])
            held = jnp.concatenate([held, moved], axis=0)
            offsets = offsets + [o ^ bit for o in offsets]
        halves.append((held, tuple(offsets)))
    return halves


def cube_sum(vector, axes):
    for axis in axes:
        n = lax.axis_size(axis)
        bit = 1
        while bit < n:
            vector = vector + lax.ppermute(vector, axis, [(i, i ^ bit) for i in range(n)])
            bit *= 2
    return vector


def project_and_norm(all_heads, weights, all_tokens, gain_vec):
    groups, rows, group_columns = all_heads.shape
    (first, first_offsets), (second, second_offsets) = weights
    parts, _, part_columns = first.shape
    width = all_tokens.shape[1]
    tile = rows // groups
    places = jnp.stack([lax.axis_index("tensor"), lax.axis_index("dp")])

    def kernel(
        at_ref, heads_ref, first_ref, second_ref, tokens_ref, gain_ref, hidden_ref, normed_ref, acc_ref
    ):
        step = pl.program_id(0)
        acc_ref[...] = tokens_ref[...].astype(jnp.float32)
        for half, (weight_ref, offsets) in enumerate(
            ((first_ref, first_offsets), (second_ref, second_offsets))
        ):
            for part in range(parts):
                start = (at_ref[1] ^ offsets[part]) * part_columns
                columns = pl.ds(pl.multiple_of(start, part_columns), part_columns)
                for g in range(groups // 2):
                    acc_ref[:, columns] += jnp.dot(
                        heads_ref[half * (groups // 2) + g],
                        weight_ref[part, g * group_columns : (g + 1) * group_columns, :],
                        preferred_element_type=jnp.float32,
                    )
        hidden = acc_ref[...]
        row_scale = lax.rsqrt(jnp.mean(hidden * hidden, axis=-1, keepdims=True) + EPS)
        normed_ref[...] = (hidden * row_scale * gain_ref[...].astype(jnp.float32)).astype(
            jnp.bfloat16
        )

        @pl.when(step == at_ref[0])
        def _():
            hidden_ref[...] = hidden

    return pl.pallas_call(
        kernel,
        grid_spec=pltpu.PrefetchScalarGridSpec(
            num_scalar_prefetch=1,
            grid=(groups,),
            in_specs=[
                pl.BlockSpec((groups, tile, group_columns), lambda i, at_ref: (0, i, 0)),
                pl.BlockSpec(first.shape, lambda i, at_ref: (0, 0, 0)),
                pl.BlockSpec(second.shape, lambda i, at_ref: (0, 0, 0)),
                pl.BlockSpec((tile, width), lambda i, at_ref: (i, 0)),
                pl.BlockSpec((1, width), lambda i, at_ref: (0, 0)),
            ],
            out_specs=[
                pl.BlockSpec((tile, width), lambda i, at_ref: (0, 0)),
                pl.BlockSpec((tile, width), lambda i, at_ref: (i, 0)),
            ],
            scratch_shapes=[pltpu.VMEM((tile, width), jnp.float32)],
        ),
        out_shape=[
            jax.ShapeDtypeStruct((tile, width), jnp.float32),
            jax.ShapeDtypeStruct((rows, width), jnp.bfloat16),
        ],
        cost_estimate=pl.CostEstimate(
            flops=2 * rows * width * width, transcendentals=rows, bytes_accessed=20 << 20
        ),
        name="project_and_norm",
    )(places, all_heads, first, second, all_tokens, gain_vec.reshape(1, -1))


def row_major(array):
    return with_layout_constraint(array, Layout(major_to_minor=tuple(range(array.ndim))))


def split_columns(array, parts):
    columns = array.shape[1] // parts
    return jnp.concatenate(
        [array[:, p * columns : (p + 1) * columns] for p in range(parts)], axis=0
    )


def join_columns(array, parts):
    rows = array.shape[0] // parts
    return jnp.concatenate([array[p * rows : (p + 1) * rows] for p in range(parts)], axis=1)


def block(
    tokens,
    cotangent,
    norm1_gain,
    w_query,
    w_key,
    w_value,
    w_output,
    norm2_gain,
    w_gate,
    w_up,
    w_down,
):
    low = jnp.bfloat16
    n_dp = lax.axis_size("dp")
    nothing = scatter_sum(tokens[:, :128] * 0, "dp")[0, 0]
    all_tokens = gather_rows(tokens, "tensor")
    part_columns = w_output.shape[1] // n_dp
    own_part = lax.dynamic_slice_in_dim(
        w_output, lax.axis_index("dp") * part_columns, part_columns, 1
    )
    part_output = gather_rows(own_part, "tensor")
    all_output = cube_gather(part_output, "dp")
    all_rows = all_tokens.shape[0]
    seq_count = all_rows // SEQLEN
    kv_heads = w_key.shape[1] // HD
    group_size = HQ // KV
    score_scale = HD ** (-0.5)
    gain_one = norm1_gain.astype(jnp.float32)
    gain_two = norm2_gain.astype(jnp.float32)
    token_values = all_tokens.astype(jnp.float32)
    own_tokens = tokens.astype(jnp.float32)
    normed1 = rms_norm(token_values, gain_one).astype(low)
    query_pre = jnp.dot(normed1, w_query, preferred_element_type=jnp.float32).reshape(
        seq_count, SEQLEN, kv_heads, group_size, HD
    )
    key_pre = jnp.dot(normed1, w_key, preferred_element_type=jnp.float32).reshape(
        seq_count, SEQLEN, kv_heads, HD
    )
    value_all = (
        jnp.dot(normed1, w_value, preferred_element_type=jnp.float32)
        .astype(low)
        .reshape(seq_count, SEQLEN, kv_heads, HD)
    )
    cos_table, sin_table = rope_tables(SEQLEN, HD)
    query_rot = rotate(query_pre, cos_table, sin_table).astype(low)
    key_rot = rotate(key_pre, cos_table, sin_table).astype(low)
    positions = jnp.arange(SEQLEN)
    causal = positions[:, None] >= positions[None, :]

    def masked_scores():
        raw_scores = (
            jnp.einsum("sqhgd,skhd->shgqk", query_rot, key_rot, preferred_element_type=jnp.float32)
            * score_scale
        )
        return jnp.where(causal, raw_scores, MASKED)

    scores = masked_scores()
    row_max = jnp.max(scores, axis=-1, keepdims=True)
    exp_scores = jnp.exp(scores - row_max)
    row_total = jnp.sum(exp_scores, axis=-1, keepdims=True)
    attn_probs = exp_scores / row_total
    log_total = row_max + jnp.log(row_total)
    mixed_heads = jnp.einsum(
        "shgqk,skhd->sqhgd", attn_probs.astype(low), value_all, preferred_element_type=jnp.float32
    )
    heads_out = mixed_heads.astype(low).reshape(all_rows, kv_heads * group_size * HD)
    all_heads = lax.all_gather(heads_out, "tensor", axis=0)
    all_cot = gather_rows(cotangent, "tensor")
    hidden_state, normed2 = project_and_norm(
        all_heads, all_output, all_tokens, (gain_two + nothing.astype(jnp.float32))
    )
    gate_proj = jnp.dot(normed2, w_gate, preferred_element_type=jnp.float32)
    up_proj = jnp.dot(normed2, w_up, preferred_element_type=jnp.float32)
    activated = gated_unit(gate_proj, up_proj).astype(low)
    d_activated = contract_cols(all_cot, w_down)
    _, pull_gated = jax.vjp(gated_unit, gate_proj, up_proj)
    d_gate, d_up = pull_gated(d_activated)
    d_gate = d_gate.astype(low)
    d_up = d_up.astype(low)
    ff_columns = w_gate.shape[1]
    ff_folds = w_gate.shape[0] // w_down.shape[0]
    grad_down = row_major(split_columns(contract_rows(activated, all_cot).astype(low), ff_folds))
    part_down = scatter_sum(grad_down, "dp")
    dn2_part = (contract_cols(d_gate, w_gate) + contract_cols(d_up, w_up)).astype(low)
    d_normed2 = exchange_sum(dn2_part, "tensor")
    gate_up_grads = row_major(
        jnp.concatenate(
            [contract_rows(normed2, d_gate).astype(low), contract_rows(normed2, d_up).astype(low)],
            axis=1,
        )
    )
    part_gate_up = scatter_sum(gate_up_grads, "dp")
    mlp_part = jnp.dot(activated, w_down, preferred_element_type=jnp.float32).astype(low)
    mlp_sum = exchange_sum(mlp_part, "tensor")
    output = (hidden_state + mlp_sum).astype(low)
    d_state = cotangent.astype(jnp.float32) + norm_backward(hidden_state, gain_two, d_normed2)
    d_state_low = gather_rows(d_state.astype(low), "tensor")
    gain_two_sum = cube_sum(gain_gradient(hidden_state, d_normed2), ("dp", "tensor"))
    d_heads = contract_cols(d_state_low, w_output).astype(low)
    d_heads = d_heads.reshape(seq_count, SEQLEN, kv_heads, group_size, HD)
    probs_again = jnp.exp(masked_scores() - log_total)
    probs_low = probs_again.astype(low)
    d_value = (
        jnp.einsum("shgqk,sqhgd->skhd", probs_low, d_heads, preferred_element_type=jnp.float32)
        .astype(low)
        .reshape(all_rows, kv_heads * HD)
    )
    d_probs = jnp.einsum(
        "sqhgd,skhd->shgqk", d_heads, value_all, preferred_element_type=jnp.float32
    )
    d_scores = (
        probs_again * (d_probs - jnp.sum(probs_again * d_probs, axis=-1, keepdims=True))
    ).astype(low)
    d_query = (
        jnp.einsum("shgqk,skhd->sqhgd", d_scores, key_rot, preferred_element_type=jnp.float32)
        * score_scale
    )
    d_key = (
        jnp.einsum("shgqk,sqhgd->skhd", d_scores, query_rot, preferred_element_type=jnp.float32)
        * score_scale
    )
    d_query = (
        rotate(d_query, cos_table, -sin_table)
        .astype(low)
        .reshape(all_rows, kv_heads * group_size * HD)
    )
    d_key = rotate(d_key, cos_table, -sin_table).astype(low).reshape(all_rows, kv_heads * HD)
    dn1_part = (
        contract_cols(d_query, w_query)
        + contract_cols(d_key, w_key)
        + contract_cols(d_value, w_value)
    ).astype(low)
    d_normed1 = exchange_sum(dn1_part, "tensor")
    gain_one_sum = cube_sum(
        gain_gradient(token_values, dn1_part.astype(jnp.float32)), ("dp", "tensor")
    )
    q_columns, k_columns = w_query.shape[1], w_key.shape[1]
    folds = w_query.shape[0] // w_output.shape[0]
    low_attn = row_major(
        jnp.concatenate(
            [
                contract_rows(normed1, d_query).astype(low),
                contract_rows(normed1, d_key).astype(low),
                contract_rows(normed1, d_value).astype(low),
                split_columns(contract_rows(heads_out, d_state_low).astype(low), folds),
            ],
            axis=1,
        )
    )
    part_attn = scatter_sum(low_attn, "dp")
    shared_ff = row_major(
        gather_rows(row_major(jnp.concatenate([part_gate_up, part_down], axis=1)), "dp")
    )
    shared_attn = row_major(gather_rows(part_attn, "dp"))
    input_grad = (d_state + norm_backward(own_tokens, gain_one, d_normed1)).astype(low)
    full_gate = shared_ff[:, :ff_columns].astype(jnp.float32)
    full_up = shared_ff[:, ff_columns : 2 * ff_columns].astype(jnp.float32)
    full_down = join_columns(shared_ff[:, 2 * ff_columns :], ff_folds).astype(jnp.float32)
    ends = (q_columns, q_columns + k_columns, q_columns + 2 * k_columns)
    full_query = shared_attn[:, : ends[0]].astype(jnp.float32)
    full_key = shared_attn[:, ends[0] : ends[1]].astype(jnp.float32)
    full_value = shared_attn[:, ends[1] : ends[2]].astype(jnp.float32)
    full_output = join_columns(shared_attn[:, ends[2] :], folds).astype(jnp.float32)
    return (
        output,
        input_grad,
        gain_one_sum,
        full_query,
        full_key,
        full_value,
        full_output,
        gain_two_sum,
        full_gate,
        full_up,
        full_down,
    )


def solution(mesh):
    return jax.shard_map(
        block,
        mesh=mesh,
        in_specs=(
            P(("dp", "tensor"), None),
            P(("dp", "tensor"), None),
            P(),
            P(None, "tensor"),
            P(None, "tensor"),
            P(None, "tensor"),
            P("tensor", None),
            P(),
            P(None, "tensor"),
            P(None, "tensor"),
            P("tensor", None),
        ),
        out_specs=(
            P(("dp", "tensor"), None),
            P(("dp", "tensor"), None),
            P(),
            P(None, "tensor"),
            P(None, "tensor"),
            P(None, "tensor"),
            P("tensor", None),
            P(),
            P(None, "tensor"),
            P(None, "tensor"),
            P("tensor", None),
        ),
        check_vma=False,
    )
```

time: 1800 us -> 1150 us (0.64)
  waiting for transfers between devices: 1390 us -> 700 us
  other arithmetic: 49 us -> 124 us
  blocking collectives: 43.6 us -> 0 us
  starting transfers between devices: 1.67 us -> 29 us
  Pallas kernels: 0 us -> 18.8 us
  local copies, waits for them, and re-layouts: 72.4 us -> 54.2 us
    reduce_scatter x11 -> x4, waiting for transfers between devices: 697 us -> 206 us  [scatter_sum(): return lax.psum_scatter(partial, axis, scatter_dimension=0, tiled=True)]
    all_gather x11 -> x7, waiting for transfers between devices: 694 us -> 214 us  [the longest x6 184 us: gather_rows(): return lax.all_gather(block, axis, axis=0, tiled=True)]
    ppermute x0 -> x25, waiting for transfers between devices: none -> 278 us  [the longest x9 172 us: exchange_sum(): lax.ppermute(block((me + hop) % n), axis, [(i, (i + hop) % n) for i in ra...]
    concatenate x0 -> x9, other arithmetic: none -> 53 us  [the longest x1 29.3 us: block(): jnp.concatenate([contract_rows(normed1, d_query).astype(low), contract_ro...]
    psum x1 -> x0, blocking collectives: 43.6 us -> none  [on_device(): lax.psum((grad_gain1, grad_gain2), ('dp', 'tensor'))]
    unnamed x113 -> x124, local copies, waits for them, and re-layouts: 53.6 us -> 17 us
    ppermute x0 -> x25, starting transfers between devices: none -> 28.3 us  [the longest x9 12.4 us: exchange_sum(): lax.ppermute(block((me + hop) % n), axis, [(i, (i + hop) % n) for i in ra...]
    convert_element_type x7 -> x10, other arithmetic: 25.8 us -> 46.2 us  [the longest x1 23.5 us: block(): join_columns(shared_ff[:, 2 * ff_columns:], ff_folds).astype(jnp.float32)]
  transfers between devices with their start and end apart: 22 -> 36, of which waited for: 20 -> 18; matrix products, arithmetic and copies ran while one was open for 8% -> 16% of each run, Pallas kernels for 0% -> 0%
where the time goes in v1:
time: 1150 us
  waiting for transfers between devices  700 us (61%)
  matrix products  206 us (18%)
  other arithmetic  124 us (11%)
  local copies, waits for them, and re-layouts  54.2 us (5%)
  starting transfers between devices  29 us (3%)
  Pallas kernels  18.8 us (2%)
  between operations  17.1 us (1%)
    reduce_scatter x4, waiting for transfers between devices, scatter_sum(): return lax.psum_scatter(partial, axis, scatter_dimension=0, tiled=True)  206 us
    all_gather x6, waiting for transfers between devices, gather_rows(): return lax.all_gather(block, axis, axis=0, tiled=True)  184 us
    ppermute x9, waiting for transfers between devices, exchange_sum(): lax.ppermute(block((me + hop) % n), axis, [(i, (i + hop) % n) for i in ra...  172 us
    ppermute x10, waiting for transfers between devices, cube_sum(): lax.ppermute(vector, axis, [(i, i ^ bit) for i in range(n)])  75 us
    dot_general x7, matrix products, contract_cols(): lax.dot_general(left_side, right_side, (((1,), (1,)), ((), ())), preferre...  57.4 us
    dot_general x7, matrix products, contract_rows(): lax.dot_general(left_side, right_side, (((0,), (0,)), ((), ())), preferre...  44.1 us
    ppermute x6, waiting for transfers between devices, cube_gather(): moved = lax.ppermute(held, axis, [(i, i ^ bit) for i in range(n)])  31.2 us
    all_gather x1, waiting for transfers between devices, block(): all_heads = lax.all_gather(heads_out, 'tensor', axis=0)  30.2 us
  transfers between devices with their start and end apart: 36, of which 18 were waited for; matrix products, arithmetic and copies ran while one was open for 16% of the time, Pallas kernels for 0%

profile of v1, /device:TPU:0, one launch (start us, length us, event | category | flops | bytes accessed | tf_op | source)
XLA Modules:
  0.0 1148.6 jit_solution(7543600015502259426)
XLA Ops:
  15.4 26.3 %all-gather.12.cloned.1.call-done = bf16[2048,256]{1,0:T(8,128)(2,1)} async-done(((bf16[512,256]{1,0:T(8,128)(2,1)}), bf16[2048,256]{1,0:T(8,128)(2,1)}) %all-gather.12.cloned.1.call-update) | async-done | bytes 1048592 | tf_op jit(solution)/shard_map/all_gather | solution.py:76
  44.5 78.9 %all-gather.8.cloned.1.call-done.tokens_ref = bf16[1024,2048]{1,0:T(8,128)(2,1)} async-done(((bf16[256,2048]{1,0:T(8,128)(2,1)}), bf16[1024,2048]{1,0:T(8,128)(2,1)}) %all-gather.8.cloned.1.call-update) | async-done | bytes 4194320 | tf_op jit(solution)/shard_map/all_gather | solution.py:76
  162.1 8.2 fusion.3
  170.4 8.5 fusion.24
  191.5 11.6 %collective-permute-done.3 = bf16[1,1024,256]{2,1,0:T(8,128)(2,1)S(1)} collective-permute-done((bf16[1,1024,256]{2,1,0:T(8,128)(2,1)S(1)}, bf16[1,1024,256]{2,1,0:T(8,128)(2,1)S(1)}, u32[]{:S(2)}, u32[]{:S(2)}) %collective-permute-start.3) | collective-permute-done | bytes 524320 | tf_op jit(solution)/shard_map/ppermute | solution.py:106
  204.8 19.6 %collective-permute-done.1 = bf16[2,1024,256]{2,1,0:T(8,128)(2,1)S(1)} collective-permute-done((bf16[2,1024,256]{2,1,0:T(8,128)(2,1)S(1)}, bf16[2,1024,256]{2,1,0:T(8,128)(2,1)S(1)}, u32[]{:S(2)}, u32[]{:S(2)}) %collective-permute-start.1) | collective-permute-done | bytes 1048608 | tf_op jit(solution)/shard_map/ppermute | solution.py:106
  240.7 14.6 %fusion.56 = f32[1024,2048]{1,0:T(8,128)} fusion(bf16[1024,2048]{1,0:T(8,128)(2,1)} %all-gather.14.cloned.1.call-done, bf16[2048,2048]{1,0:T(8,128)(2,1)} %param.21), kind=kOutput, calls=%fused_computation.139 | convolution fusion | flops 8589934592 | bytes 20971520 | tf_op jit(solution)/shard_map/dot_general | solution.py:66
  255.3 30.2 %all-gather.10.cloned.1.call-done.heads_ref = bf16[4,1024,512]{2,1,0:T(8,128)(2,1)} async-done(((bf16[1,1024,512]{2,1,0:T(8,128)(2,1)}), bf16[4,1024,512]{2,1,0:T(8,128)(2,1)}) %all-gather.10.cloned.1.call-update) | async-done | bytes 4194320 | tf_op jit(solution)/shard_map/all_gather | solution.py:270
  285.5 18.8 %project_and_norm.1 = (f32[256,2048]{1,0:T(8,128)}, bf16[1024,2048]{1,0:T(8,128)(2,1)}) custom-call(s32[2]{0:T(128)} %pad_add_fusion.at_ref, bf16[4,1024,512]{2,1,0:T(8,128)(2,1)} %all-gather.10.cloned.1.call-done.heads_ref, bf16[8,1024,256]{2,1,0:T(8,128)(2,1)} %pad_maximum_fusion.1.first_ref, bf16[8,1024,256]{2,1,0:T(8,128)(2,1)} %pad_maximum_fusion.2.second_ref, ...), custom_call_target="tpu_custom_call" | custom-call | flops 8589934592 | bytes 20971520 | tf_op jit(solution)/shard_map/project_and_norm/pallas_call | solution.py:158
  304.3 14.6 %fusion.55 = f32[1024,2048]{1,0:T(8,128)} fusion(bf16[1024,2048]{1,0:T(8,128)(2,1)} %get-tuple-element.14, bf16[2048,2048]{1,0:T(8,128)(2,1)} %param.20), kind=kOutput, calls=%fused_computation.138 | convolution fusion | flops 8589934592 | bytes 20971520 | tf_op jit(solution)/shard_map/dot_general | solution.py:276
  318.9 20.1 %multiply_convert_fusion = (bf16[1024,2048]{1,0:T(8,128)(2,1)}, bf16[1024,2048]{1,0:T(8,128)(2,1)}, bf16[1024,2048]{1,0:T(8,128)(2,1)}) fusion(f32[1024,2048]{1,0:T(8,128)} %fusion.56, f32[1024,2048]{1,0:T(8,128)} %fusion.55, bf16[1024,2048]{1,0:T(8,128)(2,1)S(1)} %copy-done.52, bf16[2048,2048]{1,0:T(8,128)(2,1)} %param.19), kind=kOutput, calls=%fused_computation.31 | convolution fusion | flops 8623489024 | bytes 41943040 | tf_op jit(solution)/shard_map/dot_general | solution.py:275
  338.9 12.6 %fusion.57 = f32[1024,2048]{1,0:T(8,128)S(1)} fusion(bf16[1024,2048]{1,0:T(8,128)(2,1)} %get-tuple-element.24, bf16[2048,2048]{1,0:T(8,128)(2,1)} %param.19), kind=kOutput, calls=%fused_computation.140 | convolution fusion | flops 8589934592 | bytes 20971520 | tf_op jit(solution)/shard_map/dot_general | solution.py:66
  351.5 12.6 %add_convert_fusion.1 = bf16[1024,2048]{1,0:T(8,128)(2,1)S(1)} fusion(f32[1024,2048]{1,0:T(8,128)S(1)} %fusion.57, bf16[1024,2048]{1,0:T(8,128)(2,1)} %get-tuple-element.23, bf16[2048,2048]{1,0:T(8,128)(2,1)} %param.20), kind=kOutput, calls=%fused_computation.30 | convolution fusion | flops 8594128896 | bytes 25165824 | tf_op jit(solution)/shard_map/dot_general | solution.py:66
  372.9 20.9 %collective-permute-done.11 = bf16[256,2048]{1,0:T(8,128)(2,1)S(1)} collective-permute-done((bf16[256,2048]{1,0:T(8,128)(2,1)}, bf16[256,2048]{1,0:T(8,128)(2,1)S(1)}, u32[]{:S(2)}, u32[]{:S(2)}) %collective-permute-start.11) | collective-permute-done | bytes 1048608 | tf_op jit(solution)/shard_map/ppermute | solution.py:93
  393.8 65.7 %collective-permute-done.10 = bf16[256,2048]{1,0:T(8,128)(2,1)} collective-permute-done((bf16[256,2048]{1,0:T(8,128)(2,1)}, bf16[256,2048]{1,0:T(8,128)(2,1)}, u32[]{:S(2)}, u32[]{:S(2)}) %collective-permute-start.10) | collective-permute-done | bytes 1048608 | tf_op jit(solution)/shard_map/ppermute | solution.py:93
  468.5 79.0 %all-gather.16.cloned.1.call-done = bf16[1024,2048]{1,0:T(8,128)(2,1)} async-done(((bf16[256,2048]{1,0:T(8,128)(2,1)}), bf16[1024,2048]{1,0:T(8,128)(2,1)}) %all-gather.16.cloned.1.call-update) | async-done | bytes 4194320 | tf_op jit(solution)/shard_map/all_gather | solution.py:76
  558.6 9.3 fusion.33
  567.9 13.3 %fusion = (f32[2,2,4,512]{3,2,1,0:T(4,128)S(1)}, f32[2,2,512,512,4]{3,2,4,1,0:T(8,128)}) fusion(f32[2,2,4,512,512]{3,4,2,1,0:T(8,128)} %get-tuple-element.67, f32[2,2,4,512]{3,2,1,0:T(4,128)S(1)} %bitcast.141, bf16[2,512,2,4,64]{1,4,3,2,0:T(8,128)(2,1)} %copy-done.11, bf16[2,512,2,64,1]{1,0,3,2,4:T(2,128)(2,1)S(1)} %bitcast.132), kind=kOutput, calls=%fused_computation.3 | convolution fusion | flops 549445632 | bytes 34930688 | tf_op jit(solution)/shard_map/sqhgd,skhd->shgqk/dot_general | solution.py:311
  581.5 8.7 fusion.2
  614.4 29.3 %maximum_maximum_fusion = bf16[2048,1280]{1,0:T(8,128)(2,1)} fusion(bf16[512,512]{1,0:T(8,128)(2,1)S(1)} %get-tuple-element.46, bf16[512,512]{1,0:T(8,128)(2,1)S(1)} %get-tuple-element.47, bf16[512,512]{1,0:T(8,128)(2,1)S(1)} %get-tuple-element.48, bf16[512,512]{1,0:T(8,128)(2,1)S(1)} %get-tuple-element.45, ...), kind=kLoop, calls=%fused_computation.39 | loop fusion | flops 36700160 | bytes 10485760 | tf_op jit(solution)/shard_map/concatenate | solution.py:343
  643.8 14.2 %convolution_convert_fusion = bf16[2048,2048]{1,0:T(8,128)(2,1)} fusion(bf16[1024,2048]{1,0:T(8,128)(2,1)} %get-tuple-element.25, bf16[1024,2048]{1,0:T(8,128)(2,1)} %all-gather.14.cloned.1.call-done), kind=kOutput, calls=%fused_computation.36 | convolution fusion | flops 8594128896 | bytes 16777216 | tf_op jit(solution)/shard_map/dot_general | solution.py:60
  658.1 12.5 %convolution_convert_fusion.1 = bf16[2048,2048]{1,0:T(8,128)(2,1)S(1)} fusion(bf16[1024,2048]{1,0:T(8,128)(2,1)} %get-tuple-element.14, bf16[1024,2048]{1,0:T(8,128)(2,1)} %get-tuple-element.23), kind=kOutput, calls=%fused_computation.37 | convolution fusion | flops 8594128896 | bytes 16777216 | tf_op jit(solution)/shard_map/dot_general | solution.py:60
  670.7 9.8 convolution_convert_fusion.2
  687.4 11.3 reduce-scatter.7.cloned.1.call-done
  699.0 74.9 %reduce-scatter.11.cloned.1.call-done = bf16[256,2048]{1,0:T(8,128)(2,1)} async-done(((bf16[2048,2048]{1,0:T(8,128)(2,1)}), bf16[256,2048]{1,0:T(8,128)(2,1)}) %reduce-scatter.11.cloned.1.call-update) | async-done | bytes 1048592 | tf_op jit(solution)/shard_map/reduce_scatter | solution.py:80
  774.0 120.2 %reduce-scatter.9.cloned.1.call-done = bf16[256,4096]{1,0:T(8,128)(2,1)} async-done(((bf16[2048,4096]{1,0:T(8,128)(2,1)}), bf16[256,4096]{1,0:T(8,128)(2,1)}) %reduce-scatter.9.cloned.1.call-update) | async-done | bytes 2097168 | tf_op jit(solution)/shard_map/reduce_scatter | solution.py:80
  926.3 11.2 convolution_convert_fusion.3
  938.6 50.9 %collective-permute-done.18 = f32[2048]{0:T(1024)S(1)} collective-permute-done((f32[2048]{0:T(1024)S(1)}, f32[2048]{0:T(1024)S(1)}, u32[]{:S(2)}, u32[]{:S(2)}) %collective-permute-start.18) | collective-permute-done | bytes 8224 | tf_op jit(solution)/shard_map/ppermute | solution.py:118
  991.4 20.8 %collective-permute-done.24 = f32[2048]{0:T(1024)S(1)} collective-permute-done((f32[2048]{0:T(1024)S(1)}, f32[2048]{0:T(1024)S(1)}, u32[]{:S(2)}, u32[]{:S(2)}) %collective-permute-start.24) | collective-permute-done | bytes 8224 | tf_op jit(solution)/shard_map/ppermute | solution.py:118
  1019.2 20.3 %collective-permute-done.8 = bf16[256,2048]{1,0:T(8,128)(2,1)S(1)} collective-permute-done((bf16[256,2048]{1,0:T(8,128)(2,1)S(1)}, bf16[256,2048]{1,0:T(8,128)(2,1)S(1)}, u32[]{:S(2)}, u32[]{:S(2)}) %collective-permute-start.8) | collective-permute-done | bytes 1048608 | tf_op jit(solution)/shard_map/ppermute | solution.py:93
  1039.4 64.8 %collective-permute-done.7 = bf16[256,2048]{1,0:T(8,128)(2,1)S(1)} collective-permute-done((bf16[256,2048]{1,0:T(8,128)(2,1)S(1)}, bf16[256,2048]{1,0:T(8,128)(2,1)S(1)}, u32[]{:S(2)}, u32[]{:S(2)}) %collective-permute-start.7) | collective-permute-done | bytes 1048608 | tf_op jit(solution)/shard_map/ppermute | solution.py:93
  1117.9 23.5 %slice_convert_fusion = (f32[2048,2048]{1,0:T(8,128)}, f32[2048,2048]{1,0:T(8,128)}, f32[2048,2048]{1,0:T(8,128)}) fusion(bf16[2048,6144]{1,0:T(8,128)(2,1)} %all-gather.20.cloned.1.call-done), kind=kLoop, calls=%fused_computation.25 | loop fusion | flops 12582912 | bytes 75497472 | tf_op jit(solution)/shard_map/convert_element_type | solution.py:361
  (276 shorter events, 194.3 us)
Async XLA Ops:
  8.0 33.7 %all-gather.12.cloned.1.call-start = ((), (), s32[]{:S(2)}) async-start(), calls=%async_computation.6 | async-start | bytes 1310720 | tf_op jit(solution)/shard_map/all_gather | solution.py:76
  9.9 113.5 %all-gather.8.cloned.1.call-start = ((), (), s32[]{:S(2)}) async-start(), calls=%async_computation.4 | async-start | bytes 5242880 | tf_op jit(solution)/shard_map/all_gather | solution.py:76
  10.7 220.3 %reduce-scatter.5.cloned.1.call-start = ((), (), s32[]{:S(2)}) async-start(), calls=%async_computation.7 | async-start | bytes 73728 | tf_op jit(solution)/shard_map/reduce_scatter | solution.py:80
  12.2 228.4 %all-gather.14.cloned.1.call-start = ((), (), s32[]{:S(2)}) async-start(), calls=%async_computation.8 | async-start | bytes 5242880 | tf_op jit(solution)/shard_map/all_gather | solution.py:76
  12.9 272.6 %all-gather.10.cloned.1.call-start = ((), (), s32[]{:S(2)}) async-start(), calls=%async_computation.5 | async-start | bytes 5242880 | tf_op jit(solution)/shard_map/all_gather | solution.py:270
  43.0 146.8 %collective-permute-start = (bf16[1,1024,256]{2,1,0:T(8,128)(2,1)S(1)}, bf16[1,1024,256]{2,1,0:T(8,128)(2,1)}, u32[]{:S(2)}, u32[]{:S(2)}) collective-permute-start(bf16[1,1024,256]{2,1,0:T(8,128)(2,1)S(1)} %get-tuple-element.54), channel_id=1, source_target_pairs={{0,8},{4,12},{8,0},{12,4},{16,24},{20,28},{24,16},{28,20},{1,9},{5... | collective-permute-start | bytes 1572872 | tf_op jit(solution)/shard_map/ppermute | solution.py:106
  188.1 359.3 %all-gather.16.cloned.1.call-start = ((), (), s32[]{:S(2)}) async-start(), calls=%async_computation.9 | async-start | bytes 5242880 | tf_op jit(solution)/shard_map/all_gather | solution.py:76
  188.2 14.9 %collective-permute-start.3 = (bf16[1,1024,256]{2,1,0:T(8,128)(2,1)S(1)}, bf16[1,1024,256]{2,1,0:T(8,128)(2,1)S(1)}, u32[]{:S(2)}, u32[]{:S(2)}) collective-permute-start(bf16[1,1024,256]{2,1,0:T(8,128)(2,1)S(1)} %get-tuple-element.53), channel_id=1, source_target_pairs={{0,16},{4,20},{8,24},{12,28},{16,0},{20,4},{24,8},{28,12},{1,17},{... | collective-permute-start | bytes 1572872 | tf_op jit(solution)/shard_map/ppermute | solution.py:106
  190.9 33.4 %collective-permute-start.1 = (bf16[2,1024,256]{2,1,0:T(8,128)(2,1)S(1)}, bf16[2,1024,256]{2,1,0:T(8,128)(2,1)S(1)}, u32[]{:S(2)}, u32[]{:S(2)}) collective-permute-start(bf16[2,1024,256]{2,1,0:T(8,128)(2,1)S(1)} %pad_maximum_fusion.7), channel_id=1, source_target_pairs={{0,16},{4,20},{8,24},{12,28},{16,0},{20,4},{24,8},{28,12},{1,17},{... | collective-permute-start | bytes 3145736 | tf_op jit(solution)/shard_map/ppermute | solution.py:106
  203.2 24.1 %collective-permute-start.4 = (bf16[2,1024,256]{2,1,0:T(8,128)(2,1)S(1)}, bf16[2,1024,256]{2,1,0:T(8,128)(2,1)S(1)}, u32[]{:S(2)}, u32[]{:S(2)}) collective-permute-start(bf16[2,1024,256]{2,1,0:T(8,128)(2,1)S(1)} %pad_maximum_fusion.8), channel_id=1, source_target_pairs={{0,8},{4,12},{8,0},{12,4},{16,24},{20,28},{24,16},{28,20},{1,9},{5... | collective-permute-start | bytes 3145736 | tf_op jit(solution)/shard_map/ppermute | solution.py:106
  227.3 6.1 collective-permute-start.2
  229.8 7.4 collective-permute-start.5
  367.9 25.9 %collective-permute-start.11 = (bf16[256,2048]{1,0:T(8,128)(2,1)}, bf16[256,2048]{1,0:T(8,128)(2,1)S(1)}, u32[]{:S(2)}, u32[]{:S(2)}) collective-permute-start(bf16[256,2048]{1,0:T(8,128)(2,1)} %get-tuple-element.36), channel_id=1, source_target_pairs={{0,3},{1,0},{2,1},{3,2},{4,7},{5,4},{6,5},{7,6},{8,11},{9,8},{10,9... | collective-permute-start | bytes 3145736 | tf_op jit(solution)/shard_map/ppermute | solution.py:93
  368.5 91.0 %collective-permute-start.10 = (bf16[256,2048]{1,0:T(8,128)(2,1)}, bf16[256,2048]{1,0:T(8,128)(2,1)}, u32[]{:S(2)}, u32[]{:S(2)}) collective-permute-start(bf16[256,2048]{1,0:T(8,128)(2,1)} %get-tuple-element.37), channel_id=1, source_target_pairs={{0,2},{1,3},{2,0},{3,1},{4,6},{5,7},{6,4},{7,5},{8,10},{9,11},{10,... | collective-permute-start | bytes 3145736 | tf_op jit(solution)/shard_map/ppermute | solution.py:93
  368.8 90.7 %collective-permute-start.9 = (bf16[256,2048]{1,0:T(8,128)(2,1)}, bf16[256,2048]{1,0:T(8,128)(2,1)}, u32[]{:S(2)}, u32[]{:S(2)}) collective-permute-start(bf16[256,2048]{1,0:T(8,128)(2,1)} %get-tuple-element.35), channel_id=1, source_target_pairs={{0,1},{1,2},{2,3},{3,0},{4,5},{5,6},{6,7},{7,4},{8,9},{9,10},{10,1... | collective-permute-start | bytes 3145736 | tf_op jit(solution)/shard_map/ppermute | solution.py:93
  466.1 232.6 %reduce-scatter.7.cloned.1.call-start = ((), (), s32[]{:S(2)}) async-start(), calls=%async_computation.10 | async-start | bytes 5898240 | tf_op jit(solution)/shard_map/reduce_scatter | solution.py:80
  643.8 130.2 %reduce-scatter.11.cloned.1.call-start = ((), (), s32[]{:S(2)}) async-start(), calls=%async_computation.13 | async-start | bytes 9437184 | tf_op jit(solution)/shard_map/reduce_scatter | solution.py:80
  658.1 236.1 %reduce-scatter.9.cloned.1.call-start = ((), (), s32[]{:S(2)}) async-start(), calls=%async_computation.12 | async-start | bytes 18874368 | tf_op jit(solution)/shard_map/reduce_scatter | solution.py:80
  687.4 420.8 %all-gather.18.cloned.1.call-start = ((), (), s32[]{:S(2)}) async-start(), calls=%async_computation.11 | async-start | bytes 5898240 | tf_op jit(solution)/shard_map/all_gather | solution.py:76
  698.7 419.1 %all-gather.20.cloned.1.call-start = ((), (), s32[]{:S(2)}) async-start(), calls=%async_computation.14 | async-start | bytes 28311552 | tf_op jit(solution)/shard_map/all_gather | solution.py:76
  899.4 14.0 %collective-permute-start.21 = (f32[2048]{0:T(1024)S(1)}, f32[2048]{0:T(1024)S(1)}, u32[]{:S(2)}, u32[]{:S(2)}) collective-permute-start(f32[2048]{0:T(1024)S(1)} %add.241), channel_id=1, source_target_pairs={{0,8},{4,12},{8,0},{12,4},{16,24},{20,28},{24,16},{28,20},{1,9},{5... | collective-permute-start | bytes 24584 | tf_op jit(solution)/shard_map/ppermute | solution.py:118
  917.1 20.4 %collective-permute-start.23 = (f32[2048]{0:T(1024)S(1)}, f32[2048]{0:T(1024)S(1)}, u32[]{:S(2)}, u32[]{:S(2)}) collective-permute-start(f32[2048]{0:T(1024)S(1)} %add.243), channel_id=1, source_target_pairs={{0,1},{1,0},{2,3},{3,2},{4,5},{5,4},{6,7},{7,6},{8,9},{9,8},{10,11... | collective-permute-start | bytes 24584 | tf_op jit(solution)/shard_map/ppermute | solution.py:118
  918.6 5.3 collective-permute-start.17
  919.4 96.4 %collective-permute-start.14 = (bf16[256,2048]{1,0:T(8,128)(2,1)S(1)}, bf16[256,2048]{1,0:T(8,128)(2,1)S(1)}, u32[]{:S(2)}, u32[]{:S(2)}) collective-permute-start(bf16[256,2048]{1,0:T(8,128)(2,1)S(1)} %get-tuple-element.33), channel_id=1, source_target_pairs={{0,3},{1,0},{2,1},{3,2},{4,7},{5,4},{6,5},{7,6},{8,11},{9,8},{10,9... | collective-permute-start | bytes 3145736 | tf_op jit(solution)/shard_map/ppermute | solution.py:93
  922.8 95.4 %collective-permute-start.13 = (bf16[256,2048]{1,0:T(8,128)(2,1)S(1)}, bf16[256,2048]{1,0:T(8,128)(2,1)S(1)}, u32[]{:S(2)}, u32[]{:S(2)}) collective-permute-start(bf16[256,2048]{1,0:T(8,128)(2,1)S(1)} %get-tuple-element.34), channel_id=1, source_target_pairs={{0,2},{1,3},{2,0},{3,1},{4,6},{5,7},{6,4},{7,5},{8,10},{9,11},{10,... | collective-permute-start | bytes 3145736 | tf_op jit(solution)/shard_map/ppermute | solution.py:93
  922.8 95.4 %collective-permute-start.12 = (bf16[256,2048]{1,0:T(8,128)(2,1)S(1)}, bf16[256,2048]{1,0:T(8,128)(2,1)S(1)}, u32[]{:S(2)}, u32[]{:S(2)}) collective-permute-start(bf16[256,2048]{1,0:T(8,128)(2,1)S(1)} %get-tuple-element.32), channel_id=1, source_target_pairs={{0,1},{1,2},{2,3},{3,0},{4,5},{5,6},{6,7},{7,4},{8,9},{9,10},{10,1... | collective-permute-start | bytes 3145736 | tf_op jit(solution)/shard_map/ppermute | solution.py:93
  923.9 65.5 %collective-permute-start.18 = (f32[2048]{0:T(1024)S(1)}, f32[2048]{0:T(1024)S(1)}, u32[]{:S(2)}, u32[]{:S(2)}) collective-permute-start(f32[2048]{0:T(1024)S(1)} %add.238), channel_id=1, source_target_pairs={{0,1},{1,0},{2,3},{3,2},{4,5},{5,4},{6,7},{7,6},{8,9},{9,8},{10,11... | collective-permute-start | bytes 24584 | tf_op jit(solution)/shard_map/ppermute | solution.py:118
  937.5 74.6 %collective-permute-start.24 = (f32[2048]{0:T(1024)S(1)}, f32[2048]{0:T(1024)S(1)}, u32[]{:S(2)}, u32[]{:S(2)}) collective-permute-start(f32[2048]{0:T(1024)S(1)} %add.244), channel_id=1, source_target_pairs={{0,2},{1,3},{2,0},{3,1},{4,6},{5,7},{6,4},{7,5},{8,10},{9,11},{10,... | collective-permute-start | bytes 24584 | tf_op jit(solution)/shard_map/ppermute | solution.py:118
  989.4 26.4 %collective-permute-start.19 = (f32[2048]{0:T(1024)S(1)}, f32[2048]{0:T(1024)S(1)}, u32[]{:S(2)}, u32[]{:S(2)}) collective-permute-start(f32[2048]{0:T(1024)S(1)} %add.239), channel_id=1, source_target_pairs={{0,2},{1,3},{2,0},{3,1},{4,6},{5,7},{6,4},{7,5},{8,10},{9,11},{10,... | collective-permute-start | bytes 24584 | tf_op jit(solution)/shard_map/ppermute | solution.py:118
  1012.2 27.3 %collective-permute-start.8 = (bf16[256,2048]{1,0:T(8,128)(2,1)S(1)}, bf16[256,2048]{1,0:T(8,128)(2,1)S(1)}, u32[]{:S(2)}, u32[]{:S(2)}) collective-permute-start(bf16[256,2048]{1,0:T(8,128)(2,1)S(1)} %get-tuple-element.39), channel_id=1, source_target_pairs={{0,3},{1,0},{2,1},{3,2},{4,7},{5,4},{6,5},{7,6},{8,11},{9,8},{10,9... | collective-permute-start | bytes 3145736 | tf_op jit(solution)/shard_map/ppermute | solution.py:93
  1015.8 88.4 %collective-permute-start.7 = (bf16[256,2048]{1,0:T(8,128)(2,1)S(1)}, bf16[256,2048]{1,0:T(8,128)(2,1)S(1)}, u32[]{:S(2)}, u32[]{:S(2)}) collective-permute-start(bf16[256,2048]{1,0:T(8,128)(2,1)S(1)} %get-tuple-element.40), channel_id=1, source_target_pairs={{0,2},{1,3},{2,0},{3,1},{4,6},{5,7},{6,4},{7,5},{8,10},{9,11},{10,... | collective-permute-start | bytes 3145736 | tf_op jit(solution)/shard_map/ppermute | solution.py:93
  1015.8 88.4 %collective-permute-start.6 = (bf16[256,2048]{1,0:T(8,128)(2,1)S(1)}, bf16[256,2048]{1,0:T(8,128)(2,1)S(1)}, u32[]{:S(2)}, u32[]{:S(2)}) collective-permute-start(bf16[256,2048]{1,0:T(8,128)(2,1)S(1)} %get-tuple-element.38), channel_id=1, source_target_pairs={{0,1},{1,2},{2,3},{3,0},{4,5},{5,6},{6,7},{7,4},{8,9},{9,10},{10,1... | collective-permute-start | bytes 3145736 | tf_op jit(solution)/shard_map/ppermute | solution.py:93
  (64 other events, 2132.1 us)
Sparse Core Ops, SparseCore 0:
  11.0 30.6 all-gather.11
  43.3 80.1 all-gather.7
  125.0 79.2 all-gather.13
  206.3 79.2 all-gather.9
  466.2 81.1 all-gather.15
Sparse Core Ops, SparseCore 1:
  14.1 36.2 reduce-scatter.4
  643.8 54.8 reduce-scatter.6
  702.6 71.3 reduce-scatter.10
  778.1 116.0 reduce-scatter.8
  896.1 40.9 all-gather.17
  939.6 125.0 all-gather.19

commit v2 on v1

--- a/solution.py
+++ b/solution.py
@@ -1,3 +1,5 @@
+import functools
+
 import jax
 import jax.numpy as jnp
 from jax import lax
@@ -7,8 +9,6 @@
 from jax.sharding import PartitionSpec as P
 
 
-HQ = 32
-KV = 8
 HD = 64
 SEQLEN = 512
 
@@ -23,22 +23,6 @@
     frequency = ROPE_BASE ** (-(jnp.arange(half_width, dtype=jnp.float32) * 2.0 / columns))
     angles = jnp.arange(length, dtype=jnp.float32)[:, None] * frequency[None, :]
     return (jnp.cos(angles), jnp.sin(angles))
-
-
-def rotate(values, cos_table, sin_table):
-    half_width = values.shape[-1] // 2
-    table_shape = (cos_table.shape[0],) + (1,) * (values.ndim - 3) + (half_width,)
-    cos_table = cos_table.reshape(table_shape)
-    sin_table = sin_table.reshape(table_shape)
-    first_half = values[..., :half_width]
-    second_half = values[..., half_width:]
-    return jnp.concatenate(
-        [
-            first_half * cos_table - second_half * sin_table,
-            second_half * cos_table + first_half * sin_table,
-        ],
-        axis=-1,
-    )
 
 
 def rms_norm(values, gain_vec):
@@ -120,18 +104,254 @@
     return vector
 
 
+def rotate_rows(values, cos_rows, sin_rows):
+    half = HD // 2
+    heads = []
+    for h in range(values.shape[0] // HD):
+        upper = values[h * HD : h * HD + half]
+        lower = values[h * HD + half : (h + 1) * HD]
+        heads.append(upper * cos_rows - lower * sin_rows)
+        heads.append(lower * cos_rows + upper * sin_rows)
+    return jnp.concatenate(heads, axis=0)
+
+
+def dot_lanes(left_side, right_side):
+    return lax.dot_general(
+        left_side, right_side, (((1,), (1,)), ((), ())), preferred_element_type=jnp.float32
+    )
+
+
+def norm_project(all_tokens, gain_vec, weight_rows, cos_rows, sin_rows, rotated):
+    rows, width = all_tokens.shape
+    columns = weight_rows.shape[0]
+    tile = 256
+
+    def kernel(tokens_ref, gain_ref, weight_ref, cos_ref, sin_ref, normed_ref, out_ref):
+        values = tokens_ref[...].astype(jnp.float32)
+        row_scale = lax.rsqrt(jnp.mean(values * values, axis=-1, keepdims=True) + EPS)
+        normed = (values * row_scale * gain_ref[...].astype(jnp.float32)).astype(jnp.bfloat16)
+        normed_ref[...] = normed
+        projected = dot_lanes(weight_ref[...], normed)
+        out_ref[:rotated] = rotate_rows(projected[:rotated], cos_ref[...], sin_ref[...]).astype(
+            jnp.bfloat16
+        )
+        out_ref[rotated:] = projected[rotated:].astype(jnp.bfloat16)
+
+    half = HD // 2
+    return pl.pallas_call(
+        kernel,
+        grid=(rows // tile,),
+        in_specs=[
+            pl.BlockSpec((tile, width), lambda i: (i, 0)),
+            pl.BlockSpec((1, width), lambda i: (0, 0)),
+            pl.BlockSpec((columns, width), lambda i: (0, 0)),
+            pl.BlockSpec((half, tile), lambda i: (0, i % (SEQLEN // tile))),
+            pl.BlockSpec((half, tile), lambda i: (0, i % (SEQLEN // tile))),
+        ],
+        out_specs=[
+            pl.BlockSpec((tile, width), lambda i: (i, 0)),
+            pl.BlockSpec((columns, tile), lambda i: (0, i)),
+        ],
+        out_shape=[
+            jax.ShapeDtypeStruct((rows, width), jnp.bfloat16),
+            jax.ShapeDtypeStruct((columns, rows), jnp.bfloat16),
+        ],
+        cost_estimate=pl.CostEstimate(
+            flops=2 * rows * width * columns, transcendentals=rows, bytes_accessed=12 << 20
+        ),
+        name="norm_project",
+    )(all_tokens, gain_vec.reshape(1, -1), weight_rows, cos_rows, sin_rows)
+
+
+def key_tiles(step, tile):
+    return [(t * tile, t == step) for t in range(step + 1)]
+
+
+def causal_tile(tile):
+    key_at = lax.broadcasted_iota(jnp.int32, (tile, tile), 0)
+    query_at = lax.broadcasted_iota(jnp.int32, (tile, tile), 1)
+    return key_at <= query_at
+
+
+def attend(projected, q_heads, kv_heads):
+    rows = projected.shape[1]
+    group = q_heads // kv_heads
+    wide = group * HD
+    tile = 256
+    score_scale = HD ** (-0.5)
+
+    def kernel(query_ref, key_ref, value_ref, heads_ref, heads_t_ref, total_ref):
+        keys = key_ref[...].astype(jnp.float32).T.astype(jnp.bfloat16)
+        visible = causal_tile(tile)
+        for step in range(SEQLEN // tile):
+            here = slice(step * tile, (step + 1) * tile)
+            for h in range(group):
+                query = query_ref[h * HD : (h + 1) * HD, here]
+                parts = []
+                for start, masked in key_tiles(step, tile):
+                    part = jnp.dot(
+                        keys[start : start + tile], query, preferred_element_type=jnp.float32
+                    )
+                    parts.append(jnp.where(visible, part, MASKED) if masked else part)
+                top = functools.reduce(
+                    jnp.maximum, [jnp.max(part, axis=0, keepdims=True) for part in parts]
+                )
+                parts = [jnp.exp((part - top) * score_scale) for part in parts]
+                total = sum(jnp.sum(part, axis=0, keepdims=True) for part in parts)
+                inverse = 1.0 / total
+                mixed = sum(
+                    jnp.dot(
+                        value_ref[:, start : start + tile],
+                        (part * inverse).astype(jnp.bfloat16),
+                        preferred_element_type=jnp.float32,
+                    )
+                    for part, (start, _) in zip(parts, key_tiles(step, tile))
+                )
+                heads_t_ref[h * HD : (h + 1) * HD, here] = mixed.astype(jnp.bfloat16)
+                total_ref[0, h : h + 1, here] = top * score_scale + jnp.log(total)
+        heads_ref[...] = heads_t_ref[...].astype(jnp.float32).T.astype(jnp.bfloat16)
+
+    return pl.pallas_call(
+        kernel,
+        grid=(rows // SEQLEN, kv_heads),
+        in_specs=[
+            pl.BlockSpec((wide, SEQLEN), lambda s, j: (j, s)),
+            pl.BlockSpec((HD, SEQLEN), lambda s, j: (q_heads + j, s)),
+            pl.BlockSpec((HD, SEQLEN), lambda s, j: (q_heads + kv_heads + j, s)),
+        ],
+        out_specs=[
+            pl.BlockSpec((SEQLEN, wide), lambda s, j: (s, j)),
+            pl.BlockSpec((wide, SEQLEN), lambda s, j: (j, s)),
+            pl.BlockSpec((1, group, SEQLEN), lambda s, j: (j, 0, s)),
+        ],
+        out_shape=[
+            jax.ShapeDtypeStruct((rows, q_heads * HD), jnp.bfloat16),
+            jax.ShapeDtypeStruct((q_heads * HD, rows), jnp.bfloat16),
+            jax.ShapeDtypeStruct((kv_heads, group, rows), jnp.float32),
+        ],
+        cost_estimate=pl.CostEstimate(
+            flops=4 * rows * SEQLEN * q_heads * HD,
+            transcendentals=rows * SEQLEN * q_heads,
+            bytes_accessed=4 << 20,
+        ),
+        name="attend",
+    )(projected, projected, projected)
+
+
+def attend_back(projected, d_heads, totals, cos_rows, sin_rows, q_heads, kv_heads):
+    rows = projected.shape[1]
+    group = q_heads // kv_heads
+    wide = group * HD
+    tile = 256
+    score_scale = HD ** (-0.5)
+
+    def kernel(
+        query_ref,
+        key_ref,
+        value_ref,
+        d_heads_ref,
+        total_ref,
+        cos_ref,
+        sin_ref,
+        d_query_ref,
+        d_key_ref,
+        d_value_ref,
+        key_sum,
+        value_sum,
+    ):
+        keys = key_ref[...].astype(jnp.float32).T.astype(jnp.bfloat16)
+        values = value_ref[...].astype(jnp.float32).T.astype(jnp.bfloat16)
+        visible = causal_tile(tile)
+        key_sum[...] = jnp.zeros_like(key_sum)
+        value_sum[...] = jnp.zeros_like(value_sum)
+        for step in range(SEQLEN // tile):
+            here = slice(step * tile, (step + 1) * tile)
+            for h in range(group):
+                query = query_ref[h * HD : (h + 1) * HD, here]
+                d_head = d_heads_ref[h * HD : (h + 1) * HD, here]
+                log_total = total_ref[0, h : h + 1, here]
+                probs, d_probs = [], []
+                for start, masked in key_tiles(step, tile):
+                    span = slice(start, start + tile)
+                    part = jnp.dot(keys[span], query, preferred_element_type=jnp.float32)
+                    part = jnp.exp(part * score_scale - log_total)
+                    if masked:
+                        part = jnp.where(visible, part, 0.0)
+                    probs.append(part)
+                    value_sum[:, span] += dot_lanes(d_head, part.astype(jnp.bfloat16))
+                    d_probs.append(
+                        jnp.dot(values[span], d_head, preferred_element_type=jnp.float32)
+                    )
+                row_sum = sum(
+                    jnp.sum(part * d_part, axis=0, keepdims=True)
+                    for part, d_part in zip(probs, d_probs)
+                )
+                d_query = jnp.zeros((HD, tile), jnp.float32)
+                for (start, _), part, d_part in zip(key_tiles(step, tile), probs, d_probs):
+                    span = slice(start, start + tile)
+                    d_scores = (part * (d_part - row_sum)).astype(jnp.bfloat16)
+                    d_query += jnp.dot(
+                        key_ref[:, span], d_scores, preferred_element_type=jnp.float32
+                    )
+                    key_sum[:, span] += dot_lanes(query, d_scores)
+                d_query_ref[h * HD : (h + 1) * HD, here] = rotate_rows(
+                    d_query * score_scale, cos_ref[:, here], -sin_ref[:, here]
+                ).astype(jnp.bfloat16)
+        d_key_ref[...] = rotate_rows(
+            key_sum[...] * score_scale, cos_ref[...], -sin_ref[...]
+        ).astype(jnp.bfloat16)
+        d_value_ref[...] = value_sum[...].astype(jnp.bfloat16)
+
+    half = HD // 2
+    return pl.pallas_call(
+        kernel,
+        grid=(rows // SEQLEN, kv_heads),
+        in_specs=[
+            pl.BlockSpec((wide, SEQLEN), lambda s, j: (j, s)),
+            pl.BlockSpec((HD, SEQLEN), lambda s, j: (q_heads + j, s)),
+            pl.BlockSpec((HD, SEQLEN), lambda s, j: (q_heads + kv_heads + j, s)),
+            pl.BlockSpec((wide, SEQLEN), lambda s, j: (j, s)),
+            pl.BlockSpec((1, group, SEQLEN), lambda s, j: (j, 0, s)),
+            pl.BlockSpec((half, SEQLEN), lambda s, j: (0, 0)),
+            pl.BlockSpec((half, SEQLEN), lambda s, j: (0, 0)),
+        ],
+        out_specs=[
+            pl.BlockSpec((wide, SEQLEN), lambda s, j: (j, s)),
+            pl.BlockSpec((HD, SEQLEN), lambda s, j: (j, s)),
+            pl.BlockSpec((HD, SEQLEN), lambda s, j: (j, s)),
+        ],
+        out_shape=[
+            jax.ShapeDtypeStruct((q_heads * HD, rows), jnp.bfloat16),
+            jax.ShapeDtypeStruct((kv_heads * HD, rows), jnp.bfloat16),
+            jax.ShapeDtypeStruct((kv_heads * HD, rows), jnp.bfloat16),
+        ],
+        scratch_shapes=[
+            pltpu.VMEM((HD, SEQLEN), jnp.float32),
+            pltpu.VMEM((HD, SEQLEN), jnp.float32),
+        ],
+        cost_estimate=pl.CostEstimate(
+            flops=10 * rows * SEQLEN * q_heads * HD,
+            transcendentals=rows * SEQLEN * q_heads,
+            bytes_accessed=6 << 20,
+        ),
+        name="attend_back",
+    )(projected, projected, projected, d_heads, totals, cos_rows, sin_rows)
+
+
 def project_and_norm(all_heads, weights, all_tokens, gain_vec):
     groups, rows, group_columns = all_heads.shape
     (first, first_offsets), (second, second_offsets) = weights
-    parts, _, part_columns = first.shape
+    parts, depth, part_columns = first.shape
     width = all_tokens.shape[1]
     tile = rows // groups
     places = jnp.stack([lax.axis_index("tensor"), lax.axis_index("dp")])
 
     def kernel(
-        at_ref, heads_ref, first_ref, second_ref, tokens_ref, gain_ref, hidden_ref, normed_ref, acc_ref
+        at_ref, heads_ref, first_ref, second_ref, tokens_ref, gain_ref, hidden_ref, normed_ref, acc_ref, wide_ref
     ):
         step = pl.program_id(0)
+        for g in range(groups):
+            wide_ref[:, g * group_columns : (g + 1) * group_columns] = heads_ref[g]
         acc_ref[...] = tokens_ref[...].astype(jnp.float32)
         for half, (weight_ref, offsets) in enumerate(
             ((first_ref, first_offsets), (second_ref, second_offsets))
@@ -139,12 +359,11 @@
             for part in range(parts):
                 start = (at_ref[1] ^ offsets[part]) * part_columns
                 columns = pl.ds(pl.multiple_of(start, part_columns), part_columns)
-                for g in range(groups // 2):
-                    acc_ref[:, columns] += jnp.dot(
-                        heads_ref[half * (groups // 2) + g],
-                        weight_ref[part, g * group_columns : (g + 1) * group_columns, :],
-                        preferred_element_type=jnp.float32,
-                    )
+                acc_ref[:, columns] += jnp.dot(
+                    wide_ref[:, half * depth : (half + 1) * depth],
+                    weight_ref[part],
+                    preferred_element_type=jnp.float32,
+                )
         hidden = acc_ref[...]
         row_scale = lax.rsqrt(jnp.mean(hidden * hidden, axis=-1, keepdims=True) + EPS)
         normed_ref[...] = (hidden * row_scale * gain_ref[...].astype(jnp.float32)).astype(
@@ -171,7 +390,10 @@
                 pl.BlockSpec((tile, width), lambda i, at_ref: (0, 0)),
                 pl.BlockSpec((tile, width), lambda i, at_ref: (i, 0)),
             ],
-            scratch_shapes=[pltpu.VMEM((tile, width), jnp.float32)],
+            scratch_shapes=[
+                pltpu.VMEM((tile, width), jnp.float32),
+                pltpu.VMEM((tile, groups * group_columns), jnp.bfloat16),
+            ],
         ),
         out_shape=[
             jax.ShapeDtypeStruct((tile, width), jnp.float32),
@@ -184,20 +406,55 @@
     )(places, all_heads, first, second, all_tokens, gain_vec.reshape(1, -1))
 
 
+def gated_up(normed, w_gate, w_up):
+    rows, width = normed.shape
+    columns = w_gate.shape[1]
+    tile = 256
+
+    def kernel(normed_ref, gate_w_ref, up_w_ref, gate_ref, up_ref, active_ref):
+        gate = jnp.dot(normed_ref[...], gate_w_ref[...], preferred_element_type=jnp.float32)
+        up = jnp.dot(normed_ref[...], up_w_ref[...], preferred_element_type=jnp.float32)
+        gate_ref[...] = gate
+        up_ref[...] = up
+        active_ref[...] = (gate * jax.nn.sigmoid(gate) * up).astype(jnp.bfloat16)
+
+    column_block = pl.BlockSpec((rows, tile), lambda j: (0, j))
+    weight_block = pl.BlockSpec((width, tile), lambda j: (0, j))
+    return pl.pallas_call(
+        kernel,
+        grid=(columns // tile,),
+        in_specs=[pl.BlockSpec((rows, width), lambda j: (0, 0)), weight_block, weight_block],
+        out_specs=[column_block] * 3,
+        out_shape=[
+            jax.ShapeDtypeStruct((rows, columns), jnp.float32),
+            jax.ShapeDtypeStruct((rows, columns), jnp.float32),
+            jax.ShapeDtypeStruct((rows, columns), jnp.bfloat16),
+        ],
+        cost_estimate=pl.CostEstimate(
+            flops=4 * rows * width * columns,
+            transcendentals=rows * columns,
+            bytes_accessed=40 << 20,
+        ),
+        name="gated_up",
+    )(normed, w_gate, w_up)
+
+
 def row_major(array):
     return with_layout_constraint(array, Layout(major_to_minor=tuple(range(array.ndim))))
 
 
 def split_columns(array, parts):
-    columns = array.shape[1] // parts
-    return jnp.concatenate(
-        [array[:, p * columns : (p + 1) * columns] for p in range(parts)], axis=0
-    )
+    if parts == 1:
+        return array
+    rows, columns = array.shape[0], array.shape[1] // parts
+    return array.reshape(rows, parts, columns).swapaxes(0, 1).reshape(parts * rows, columns)
 
 
 def join_columns(array, parts):
-    rows = array.shape[0] // parts
-    return jnp.concatenate([array[p * rows : (p + 1) * rows] for p in range(parts)], axis=1)
+    if parts == 1:
+        return array
+    rows, columns = array.shape[0] // parts, array.shape[1]
+    return array.reshape(parts, rows, columns).swapaxes(0, 1).reshape(rows, parts * columns)
 
 
 def block(
@@ -223,58 +480,25 @@
     )
     part_output = gather_rows(own_part, "tensor")
     all_output = cube_gather(part_output, "dp")
-    all_rows = all_tokens.shape[0]
-    seq_count = all_rows // SEQLEN
-    kv_heads = w_key.shape[1] // HD
-    group_size = HQ // KV
-    score_scale = HD ** (-0.5)
+    q_columns, k_columns = w_query.shape[1], w_key.shape[1]
+    q_heads, kv_heads = q_columns // HD, k_columns // HD
     gain_one = norm1_gain.astype(jnp.float32)
     gain_two = norm2_gain.astype(jnp.float32)
-    token_values = all_tokens.astype(jnp.float32)
     own_tokens = tokens.astype(jnp.float32)
-    normed1 = rms_norm(token_values, gain_one).astype(low)
-    query_pre = jnp.dot(normed1, w_query, preferred_element_type=jnp.float32).reshape(
-        seq_count, SEQLEN, kv_heads, group_size, HD
-    )
-    key_pre = jnp.dot(normed1, w_key, preferred_element_type=jnp.float32).reshape(
-        seq_count, SEQLEN, kv_heads, HD
-    )
-    value_all = (
-        jnp.dot(normed1, w_value, preferred_element_type=jnp.float32)
-        .astype(low)
-        .reshape(seq_count, SEQLEN, kv_heads, HD)
-    )
     cos_table, sin_table = rope_tables(SEQLEN, HD)
-    query_rot = rotate(query_pre, cos_table, sin_table).astype(low)
-    key_rot = rotate(key_pre, cos_table, sin_table).astype(low)
-    positions = jnp.arange(SEQLEN)
-    causal = positions[:, None] >= positions[None, :]
-
-    def masked_scores():
-        raw_scores = (
-            jnp.einsum("sqhgd,skhd->shgqk", query_rot, key_rot, preferred_element_type=jnp.float32)
-            * score_scale
-        )
-        return jnp.where(causal, raw_scores, MASKED)
-
-    scores = masked_scores()
-    row_max = jnp.max(scores, axis=-1, keepdims=True)
-    exp_scores = jnp.exp(scores - row_max)
-    row_total = jnp.sum(exp_scores, axis=-1, keepdims=True)
-    attn_probs = exp_scores / row_total
-    log_total = row_max + jnp.log(row_total)
-    mixed_heads = jnp.einsum(
-        "shgqk,skhd->sqhgd", attn_probs.astype(low), value_all, preferred_element_type=jnp.float32
-    )
-    heads_out = mixed_heads.astype(low).reshape(all_rows, kv_heads * group_size * HD)
+    cos_rows, sin_rows = cos_table.T, sin_table.T
+    weight_rows = jnp.concatenate([w_query.T, w_key.T, w_value.T], axis=0)
+    normed1, projected = norm_project(
+        all_tokens, norm1_gain, weight_rows, cos_rows, sin_rows, q_columns + k_columns
+    )
+    heads_out, heads_rows, totals = attend(projected, q_heads, kv_heads)
     all_heads = lax.all_gather(heads_out, "tensor", axis=0)
     all_cot = gather_rows(cotangent, "tensor")
     hidden_state, normed2 = project_and_norm(
         all_heads, all_output, all_tokens, (gain_two + nothing.astype(jnp.float32))
     )
-    gate_proj = jnp.dot(normed2, w_gate, preferred_element_type=jnp.float32)
-    up_proj = jnp.dot(normed2, w_up, preferred_element_type=jnp.float32)
-    activated = gated_unit(gate_proj, up_proj).astype(low)
+    gate_proj, up_proj, activated = gated_up(normed2, w_gate, w_up)
+    mlp_part = jnp.dot(activated, w_down, preferred_element_type=jnp.float32).astype(low)
     d_activated = contract_cols(all_cot, w_down)
     _, pull_gated = jax.vjp(gated_unit, gate_proj, up_proj)
     d_gate, d_up = pull_gated(d_activated)
@@ -293,62 +517,33 @@
         )
     )
     part_gate_up = scatter_sum(gate_up_grads, "dp")
-    mlp_part = jnp.dot(activated, w_down, preferred_element_type=jnp.float32).astype(low)
-    mlp_sum = exchange_sum(mlp_part, "tensor")
-    output = (hidden_state + mlp_sum).astype(low)
+    half_width = mlp_part.shape[1] // 2
+    mlp_sum_a = exchange_sum(mlp_part[:, :half_width], "tensor")
+    mlp_sum_b = exchange_sum(mlp_part[:, half_width:], "tensor")
+    output = (hidden_state + jnp.concatenate([mlp_sum_a, mlp_sum_b], axis=1)).astype(low)
     d_state = cotangent.astype(jnp.float32) + norm_backward(hidden_state, gain_two, d_normed2)
     d_state_low = gather_rows(d_state.astype(low), "tensor")
     gain_two_sum = cube_sum(gain_gradient(hidden_state, d_normed2), ("dp", "tensor"))
-    d_heads = contract_cols(d_state_low, w_output).astype(low)
-    d_heads = d_heads.reshape(seq_count, SEQLEN, kv_heads, group_size, HD)
-    probs_again = jnp.exp(masked_scores() - log_total)
-    probs_low = probs_again.astype(low)
-    d_value = (
-        jnp.einsum("shgqk,sqhgd->skhd", probs_low, d_heads, preferred_element_type=jnp.float32)
-        .astype(low)
-        .reshape(all_rows, kv_heads * HD)
-    )
-    d_probs = jnp.einsum(
-        "sqhgd,skhd->shgqk", d_heads, value_all, preferred_element_type=jnp.float32
-    )
-    d_scores = (
-        probs_again * (d_probs - jnp.sum(probs_again * d_probs, axis=-1, keepdims=True))
-    ).astype(low)
-    d_query = (
-        jnp.einsum("shgqk,skhd->sqhgd", d_scores, key_rot, preferred_element_type=jnp.float32)
-        * score_scale
-    )
-    d_key = (
-        jnp.einsum("shgqk,sqhgd->skhd", d_scores, query_rot, preferred_element_type=jnp.float32)
-        * score_scale
-    )
-    d_query = (
-        rotate(d_query, cos_table, -sin_table)
-        .astype(low)
-        .reshape(all_rows, kv_heads * group_size * HD)
-    )
-    d_key = rotate(d_key, cos_table, -sin_table).astype(low).reshape(all_rows, kv_heads * HD)
-    dn1_part = (
-        contract_cols(d_query, w_query)
-        + contract_cols(d_key, w_key)
-        + contract_cols(d_value, w_value)
-    ).astype(low)
+    d_heads_rows = contract_cols(w_output, d_state_low).astype(low)
+    d_query, d_key, d_value = attend_back(
+        projected, d_heads_rows, totals, cos_rows, sin_rows, q_heads, kv_heads
+    )
+    d_projected = jnp.concatenate([d_query, d_key, d_value], axis=0)
+    dn1_part = contract_rows(d_projected, weight_rows).astype(low)
     d_normed1 = exchange_sum(dn1_part, "tensor")
     gain_one_sum = cube_sum(
-        gain_gradient(token_values, dn1_part.astype(jnp.float32)), ("dp", "tensor")
-    )
-    q_columns, k_columns = w_query.shape[1], w_key.shape[1]
+        gain_gradient(all_tokens.astype(jnp.float32), dn1_part.astype(jnp.float32)), ("dp", "tensor")
+    )
     folds = w_query.shape[0] // w_output.shape[0]
+    grad_qkv = lax.dot_general(
+        normed1,
+        d_projected,
+        (((0,), (1,)), ((), ())),
+        preferred_element_type=jnp.float32,
+    ).astype(low)
+    grad_output = jnp.dot(heads_rows, d_state_low, preferred_element_type=jnp.float32).astype(low)
     low_attn = row_major(
-        jnp.concatenate(
-            [
-                contract_rows(normed1, d_query).astype(low),
-                contract_rows(normed1, d_key).astype(low),
-                contract_rows(normed1, d_value).astype(low),
-                split_columns(contract_rows(heads_out, d_state_low).astype(low), folds),
-            ],
-            axis=1,
-        )
+        jnp.concatenate([grad_qkv, split_columns(grad_output, folds)], axis=1)
     )
     part_attn = scatter_sum(low_attn, "dp")
     shared_ff = row_major(

time: 1150 us -> 1110 us (0.965)
  matrix products: 206 us -> 110 us
  starting transfers between devices: 29 us -> 96.7 us
  Pallas kernels: 18.8 us -> 84.8 us
  other arithmetic: 124 us -> 92.7 us
  waiting for transfers between devices: 700 us -> 671 us
  local copies, waits for them, and re-layouts: 54.2 us -> 29.2 us
    dot_general x11 -> x2, matrix products: 93 us -> 11.3 us  [the longest x1 6.41 us: block(): lax.dot_general(normed1, d_projected, (((0,), (1,)), ((), ())), preferred...]
    pallas_call x0 -> x4, Pallas kernels: none -> 66.1 us  [the longest x1 23.7 us: gated_up(): pl.pallas_call(kernel, grid=(columns // tile,), in_specs=[pl.BlockSpec((r...]
    ppermute x10, waiting for transfers between devices: 75 us -> 26.8 us  [cube_sum(): lax.ppermute(vector, axis, [(i, i ^ bit) for i in range(n)])]
    ppermute x10, starting transfers between devices: 10.1 us -> 51.2 us  [cube_sum(): lax.ppermute(vector, axis, [(i, i ^ bit) for i in range(n)])]
    all_gather x1, waiting for transfers between devices: 30.2 us -> 66.7 us  [block(): all_heads = lax.all_gather(heads_out, 'tensor', axis=0)]
    ppermute x9 -> x12, starting transfers between devices: 12.4 us -> 38.2 us  [exchange_sum(): lax.ppermute(block((me + hop) % n), axis, [(i, (i + hop) % n) for i in ra...]
    concatenate x3 -> x2, other arithmetic: 29.4 us -> 5.74 us  [the longest x1 3.04 us: block(): weight_rows = jnp.concatenate([w_query.T, w_key.T, w_value.T], axis=0)]
    ppermute x9 -> x12, waiting for transfers between devices: 172 us -> 157 us  [exchange_sum(): lax.ppermute(block((me + hop) % n), axis, [(i, (i + hop) % n) for i in ra...]
  transfers between devices with their start and end apart: 36 -> 39, of which waited for: 18 -> 25; matrix products, arithmetic and copies ran while one was open for 16% -> 12% of each run, Pallas kernels for 0% -> 2%
where the time goes in v2:
time: 1110 us; the launch traced here: 1100 us
  waiting for transfers between devices  671 us (60%)
  matrix products  110 us (10%)
  starting transfers between devices  96.7 us (9%)
  other arithmetic  92.7 us (8%)
  Pallas kernels  84.8 us (8%)
  local copies, waits for them, and re-layouts  29.2 us (3%)
  between operations  16.7 us (2%)
    reduce_scatter x4, waiting for transfers between devices, scatter_sum(): return lax.psum_scatter(partial, axis, scatter_dimension=0, tiled=True)  207 us
    all_gather x6, waiting for transfers between devices, gather_rows(): return lax.all_gather(block, axis, axis=0, tiled=True)  180 us
    ppermute x12, waiting for transfers between devices, exchange_sum(): lax.ppermute(block((me + hop) % n), axis, [(i, (i + hop) % n) for i in ra...  157 us
    all_gather x1, waiting for transfers between devices, block(): all_heads = lax.all_gather(heads_out, 'tensor', axis=0)  66.7 us
    ppermute x10, starting transfers between devices, cube_sum(): lax.ppermute(vector, axis, [(i, i ^ bit) for i in range(n)])  51.2 us
    dot_general x4, matrix products, contract_cols(): lax.dot_general(left_side, right_side, (((1,), (1,)), ((), ())), preferre...  46.9 us
    dot_general x4, matrix products, contract_rows(): lax.dot_general(left_side, right_side, (((0,), (0,)), ((), ())), preferre...  40.1 us
    ppermute x12, starting transfers between devices, exchange_sum(): lax.ppermute(block((me + hop) % n), axis, [(i, (i + hop) % n) for i in ra...  38.2 us
  transfers between devices with their start and end apart: 39, of which 25 were waited for; matrix products, arithmetic and copies ran while one was open for 12% of the time, Pallas kernels for 2%

profile of v2, /device:TPU:0, one launch (start us, length us, event | category | flops | bytes accessed | tf_op | source)
XLA Modules:
  0.0 1100.5 jit_solution(3051970462782383329)
XLA Ops:
  25.7 16.0 %all-gather.11.cloned.1.call-done = bf16[2048,256]{1,0:T(8,128)(2,1)} async-done(((bf16[512,256]{1,0:T(8,128)(2,1)}), bf16[2048,256]{1,0:T(8,128)(2,1)}) %all-gather.11.cloned.1.call-update) | async-done | bytes 1048592 | tf_op jit(solution)/shard_map/all_gather | solution.py:60
  44.5 78.9 %all-gather.9.cloned.1.call-done.tokens_ref = bf16[1024,2048]{1,0:T(8,128)(2,1)} async-done(((bf16[256,2048]{1,0:T(8,128)(2,1)}), bf16[1024,2048]{1,0:T(8,128)(2,1)}) %all-gather.9.cloned.1.call-update) | async-done | bytes 4194320 | tf_op jit(solution)/shard_map/all_gather | solution.py:60
  131.8 13.8 %attend.1 = (bf16[1024,512]{1,0:T(8,128)(2,1)}, bf16[512,1024]{1,0:T(8,128)(2,1)}, f32[2,4,1024]{2,1,0:T(4,128)}) custom-call(bf16[768,1024]{1,0:T(8,128)(2,1)} %get-tuple-element.24.query_ref.key_ref.value_ref, bf16[768,1024]{1,0:T(8,128)(2,1)} %get-tuple-element.24.query_ref.key_ref.value_ref, bf16[768,1024]{1,0:T(8,128)(2,1)} %get-tuple-element.24.query_ref.key_ref.value_ref), custom_call_target="tpu_custom_call" | custom-call | flops 1073741824 | bytes 4194304 | tf_op jit(solution)/shard_map/attend/pallas_call | solution.py:214
  149.2 11.6 %collective-permute-done = bf16[1,1024,256]{2,1,0:T(8,128)(2,1)S(1)} collective-permute-done((bf16[1,1024,256]{2,1,0:T(8,128)(2,1)S(1)}, bf16[1,1024,256]{2,1,0:T(8,128)(2,1)S(1)}, u32[]{:S(2)}, u32[]{:S(2)}) %collective-permute-start) | collective-permute-done | bytes 524320 | tf_op jit(solution)/shard_map/ppermute | solution.py:90
  162.5 19.6 %collective-permute-done.4 = bf16[2,1024,256]{2,1,0:T(8,128)(2,1)S(1)} collective-permute-done((bf16[2,1024,256]{2,1,0:T(8,128)(2,1)S(1)}, bf16[2,1024,256]{2,1,0:T(8,128)(2,1)S(1)}, u32[]{:S(2)}, u32[]{:S(2)}) %collective-permute-start.4) | collective-permute-done | bytes 1048608 | tf_op jit(solution)/shard_map/ppermute | solution.py:90
  204.3 14.5 %fusion.20 = f32[1024,2048]{1,0:T(8,128)} fusion(bf16[1024,2048]{1,0:T(8,128)(2,1)} %all-gather.13.cloned.1.call-done, bf16[2048,2048]{1,0:T(8,128)(2,1)} %param.21), kind=kOutput, calls=%fused_computation.93 | convolution fusion | flops 8589934592 | bytes 20971520 | tf_op jit(solution)/shard_map/dot_general | solution.py:50
  218.8 66.7 %all-gather.21.cloned.1.call-done = bf16[4096,512]{1,0:T(8,128)(2,1)} async-done(((bf16[1024,512]{1,0:T(8,128)(2,1)}), bf16[4096,512]{1,0:T(8,128)(2,1)}) %all-gather.21.cloned.1.call-update) | async-done | bytes 4194320 | tf_op jit(solution)/shard_map/all_gather | solution.py:495
  285.5 18.7 %project_and_norm.1 = (f32[256,2048]{1,0:T(8,128)}, bf16[1024,2048]{1,0:T(8,128)(2,1)}) custom-call(s32[2]{0:T(128)} %pad_add_fusion.at_ref, bf16[4,1024,512]{2,1,0:T(8,128)(2,1)} %bitcast.60, bf16[8,1024,256]{2,1,0:T(8,128)(2,1)} %pad_maximum_fusion.2.first_ref, bf16[8,1024,256]{2,1,0:T(8,128)(2,1)} %pad_maximum_fusion.3.second_ref, ...), custom_call_target="tpu_custom_call" | custom-call | flops 8589934592 | bytes 20971520 | tf_op jit(solution)/shard_map/project_and_norm/pallas_call | solution.py:377
  304.2 23.7 %gated_up.1 = (f32[1024,2048]{1,0:T(8,128)}, f32[1024,2048]{1,0:T(8,128)}, bf16[1024,2048]{1,0:T(8,128)(2,1)}) custom-call(bf16[1024,2048]{1,0:T(8,128)(2,1)} %get-tuple-element.27.normed_ref, bf16[2048,2048]{1,0:T(8,128)(2,1)} %gate_w_ref.1, bf16[2048,2048]{1,0:T(8,128)(2,1)} %up_w_ref.1), custom_call_target="tpu_custom_call" | custom-call | flops 17179869184 | bytes 41943040 | tf_op jit(solution)/shard_map/gated_up/pallas_call | solution.py:423
  327.9 10.8 multiply_convert_fusion
  338.7 16.1 %fusion.21 = f32[1024,2048]{1,0:T(8,128)} fusion(bf16[1024,2048]{1,0:T(8,128)(2,1)S(1)} %get-tuple-element.46, bf16[2048,2048]{1,0:T(8,128)(2,1)} %gate_w_ref.1), kind=kOutput, calls=%fused_computation.94 | convolution fusion | flops 8589934592 | bytes 20971520 | tf_op jit(solution)/shard_map/dot_general | solution.py:50
  354.9 12.8 %add_convert_fusion = bf16[1024,2048]{1,0:T(8,128)(2,1)S(1)} fusion(f32[1024,2048]{1,0:T(8,128)} %fusion.21, bf16[1024,2048]{1,0:T(8,128)(2,1)S(1)} %get-tuple-element.45, bf16[2048,2048]{1,0:T(8,128)(2,1)} %up_w_ref.1), kind=kOutput, calls=%fused_computation.13 | convolution fusion | flops 8594128896 | bytes 25165824 | tf_op jit(solution)/shard_map/dot_general | solution.py:50
  377.1 22.5 %collective-permute-done.12 = bf16[256,2048]{1,0:T(8,128)(2,1)} collective-permute-done((bf16[256,2048]{1,0:T(8,128)(2,1)}, bf16[256,2048]{1,0:T(8,128)(2,1)}, u32[]{:S(2)}, u32[]{:S(2)}) %collective-permute-start.12) | collective-permute-done | bytes 1048608 | tf_op jit(solution)/shard_map/ppermute | solution.py:77
  399.6 20.1 %collective-permute-done.14 = bf16[256,2048]{1,0:T(8,128)(2,1)} collective-permute-done((bf16[256,2048]{1,0:T(8,128)(2,1)}, bf16[256,2048]{1,0:T(8,128)(2,1)}, u32[]{:S(2)}, u32[]{:S(2)}) %collective-permute-start.14) | collective-permute-done | bytes 1048608 | tf_op jit(solution)/shard_map/ppermute | solution.py:77
  419.7 44.9 %collective-permute-done.13 = bf16[256,2048]{1,0:T(8,128)(2,1)} collective-permute-done((bf16[256,2048]{1,0:T(8,128)(2,1)}, bf16[256,2048]{1,0:T(8,128)(2,1)}, u32[]{:S(2)}, u32[]{:S(2)}) %collective-permute-start.13) | collective-permute-done | bytes 1048608 | tf_op jit(solution)/shard_map/ppermute | solution.py:77
  471.6 79.5 %all-gather.15.cloned.1.call-done = bf16[1024,2048]{1,0:T(8,128)(2,1)} async-done(((bf16[256,2048]{1,0:T(8,128)(2,1)}), bf16[1024,2048]{1,0:T(8,128)(2,1)}) %all-gather.15.cloned.1.call-update) | async-done | bytes 4194320 | tf_op jit(solution)/shard_map/all_gather | solution.py:60
  562.2 20.3 %attend_back.1 = (bf16[512,1024]{1,0:T(8,128)(2,1)}, bf16[128,1024]{1,0:T(8,128)(2,1)}, bf16[128,1024]{1,0:T(8,128)(2,1)}) custom-call(bf16[768,1024]{1,0:T(8,128)(2,1)} %get-tuple-element.24.query_ref.key_ref.value_ref, bf16[768,1024]{1,0:T(8,128)(2,1)} %get-tuple-element.24.query_ref.key_ref.value_ref, ...), custom_call_target="tpu_custom_call" | custom-call | flops 2684354560 | bytes 6291456 | tf_op jit(solution)/shard_map/attend_back/pallas_call | solution.py:306
  595.2 14.0 %convolution_convert_fusion = bf16[2048,2048]{1,0:T(8,128)(2,1)} fusion(bf16[1024,2048]{1,0:T(8,128)(2,1)} %get-tuple-element.28, bf16[1024,2048]{1,0:T(8,128)(2,1)} %all-gather.13.cloned.1.call-done), kind=kOutput, calls=%fused_computation.16 | convolution fusion | flops 8594128896 | bytes 16777216 | tf_op jit(solution)/shard_map/dot_general | solution.py:44
  609.3 12.2 %convolution_convert_fusion.1 = bf16[2048,2048]{1,0:T(8,128)(2,1)S(1)} fusion(bf16[1024,2048]{1,0:T(8,128)(2,1)} %get-tuple-element.27.normed_ref, bf16[1024,2048]{1,0:T(8,128)(2,1)} %copy-done.19), kind=kOutput, calls=%fused_computation.17 | convolution fusion | flops 8594128896 | bytes 16777216 | tf_op jit(solution)/shard_map/dot_general | solution.py:44
  621.5 9.8 convolution_convert_fusion.2
  638.2 11.6 %reduce-scatter.7.cloned.1.call-done = bf16[256,1280]{1,0:T(8,128)(2,1)} async-done(((bf16[2048,1280]{1,0:T(8,128)(2,1)}), bf16[256,1280]{1,0:T(8,128)(2,1)}) %reduce-scatter.7.cloned.1.call-update) | async-done | bytes 655376 | tf_op jit(solution)/shard_map/reduce_scatter | solution.py:64
  650.3 74.8 %reduce-scatter.11.cloned.1.call-done = bf16[256,2048]{1,0:T(8,128)(2,1)} async-done(((bf16[2048,2048]{1,0:T(8,128)(2,1)}), bf16[256,2048]{1,0:T(8,128)(2,1)}) %reduce-scatter.11.cloned.1.call-update) | async-done | bytes 1048592 | tf_op jit(solution)/shard_map/reduce_scatter | solution.py:64
  725.2 120.2 %reduce-scatter.9.cloned.1.call-done = bf16[256,4096]{1,0:T(8,128)(2,1)} async-done(((bf16[2048,4096]{1,0:T(8,128)(2,1)}), bf16[256,4096]{1,0:T(8,128)(2,1)}) %reduce-scatter.9.cloned.1.call-update) | async-done | bytes 2097168 | tf_op jit(solution)/shard_map/reduce_scatter | solution.py:64
  852.8 11.6 %convolution_convert_fusion.3 = bf16[1024,2048]{1,0:T(8,128)(2,1)S(1)} fusion(bf16[1024,2048]{1,0:T(8,128)(2,1)S(1)} %copy-done.30, bf16[2048,2048]{1,0:T(8,128)(2,1)} %param.21), kind=kOutput, calls=%fused_computation.23 | convolution fusion | flops 8592031744 | bytes 16777216 | tf_op jit(solution)/shard_map/dot_general | solution.py:501
  881.8 13.4 %collective-permute-start.17 = (bf16[256,2048]{1,0:T(8,128)(2,1)S(1)}, bf16[256,2048]{1,0:T(8,128)(2,1)S(1)}, u32[]{:S(2)}, u32[]{:S(2)}) collective-permute-start(bf16[256,2048]{1,0:T(8,128)(2,1)S(1)} %get-tuple-element.52), channel_id=1, source_target_pairs={{0,3},{1,0},{2,1},{3,2},{4,7},{5,4},{6,5},{7,6},{8,11},{9,8},{10,9... | collective-permute-start | bytes 3145736 | tf_op jit(solution)/shard_map/ppermute | solution.py:77
  895.1 9.4 collective-permute-start.16
  904.6 43.1 %collective-permute-done.7 = bf16[256,1024]{1,0:T(8,128)(2,1)S(1)} collective-permute-done((bf16[256,1024]{1,0:T(8,128)(2,1)S(1)}, bf16[256,1024]{1,0:T(8,128)(2,1)S(1)}, u32[]{:S(2)}, u32[]{:S(2)}) %collective-permute-start.7) | collective-permute-done | bytes 524320 | tf_op jit(solution)/shard_map/ppermute | solution.py:77
  967.9 10.9 collective-permute-done.26
  983.2 10.4 collective-permute-done.11
  993.7 43.4 %collective-permute-start.27 = (f32[2048]{0:T(1024)S(1)}, f32[2048]{0:T(1024)S(1)}, u32[]{:S(2)}, u32[]{:S(2)}) collective-permute-start(f32[2048]{0:T(1024)S(1)} %add.234), channel_id=1, source_target_pairs={{0,2},{1,3},{2,0},{3,1},{4,6},{5,7},{6,4},{7,5},{8,10},{9,11},{10,... | collective-permute-start | bytes 24584 | tf_op jit(solution)/shard_map/ppermute | solution.py:102
  1037.1 11.9 %collective-permute-done.10 = bf16[256,1024]{1,0:T(8,128)(2,1)S(1)} collective-permute-done((bf16[256,1024]{1,0:T(8,128)(2,1)S(1)}, bf16[256,1024]{1,0:T(8,128)(2,1)S(1)}, u32[]{:S(2)}, u32[]{:S(2)}) %collective-permute-start.10) | collective-permute-done | bytes 524320 | tf_op jit(solution)/shard_map/ppermute | solution.py:77
  1069.0 24.2 %slice_convert_fusion = (f32[2048,2048]{1,0:T(8,128)}, f32[2048,2048]{1,0:T(8,128)}, f32[2048,2048]{1,0:T(8,128)}) fusion(bf16[2048,6144]{1,0:T(8,128)(2,1)} %all-gather.19.cloned.1.call-done), kind=kLoop, calls=%fused_computation.10 | loop fusion | flops 12582912 | bytes 75497472 | tf_op jit(solution)/shard_map/convert_element_type | solution.py:556
  (196 shorter events, 172.5 us)
Async XLA Ops:
  8.0 33.7 %all-gather.11.cloned.1.call-start = ((), (), s32[]{:S(2)}) async-start(), calls=%async_computation.5 | async-start | bytes 1310720 | tf_op jit(solution)/shard_map/all_gather | solution.py:60
  10.4 113.1 %all-gather.9.cloned.1.call-start = ((), (), s32[]{:S(2)}) async-start(), calls=%async_computation.4 | async-start | bytes 5242880 | tf_op jit(solution)/shard_map/all_gather | solution.py:60
  11.1 177.4 %reduce-scatter.5.cloned.1.call-start = ((), (), s32[]{:S(2)}) async-start(), calls=%async_computation.6 | async-start | bytes 73728 | tf_op jit(solution)/shard_map/reduce_scatter | solution.py:64
  12.7 191.6 %all-gather.13.cloned.1.call-start = ((), (), s32[]{:S(2)}) async-start(), calls=%async_computation.7 | async-start | bytes 5242880 | tf_op jit(solution)/shard_map/all_gather | solution.py:60
  13.4 272.1 %all-gather.21.cloned.1.call-start = ((), (), s32[]{:S(2)}) async-start(), calls=%async_computation.14 | async-start | bytes 5242880 | tf_op jit(solution)/shard_map/all_gather | solution.py:495
  43.0 104.5 %collective-permute-start.3 = (bf16[1,1024,256]{2,1,0:T(8,128)(2,1)S(1)}, bf16[1,1024,256]{2,1,0:T(8,128)(2,1)}, u32[]{:S(2)}, u32[]{:S(2)}) collective-permute-start(bf16[1,1024,256]{2,1,0:T(8,128)(2,1)S(1)} %get-tuple-element.67), channel_id=1, source_target_pairs={{0,16},{4,20},{8,24},{12,28},{16,0},{20,4},{24,8},{28,12},{1,17},{... | collective-permute-start | bytes 1572872 | tf_op jit(solution)/shard_map/ppermute | solution.py:90
  145.6 405.5 %all-gather.15.cloned.1.call-start = ((), (), s32[]{:S(2)}) async-start(), calls=%async_computation.8 | async-start | bytes 5242880 | tf_op jit(solution)/shard_map/all_gather | solution.py:60
  145.9 14.9 %collective-permute-start = (bf16[1,1024,256]{2,1,0:T(8,128)(2,1)S(1)}, bf16[1,1024,256]{2,1,0:T(8,128)(2,1)S(1)}, u32[]{:S(2)}, u32[]{:S(2)}) collective-permute-start(bf16[1,1024,256]{2,1,0:T(8,128)(2,1)S(1)} %get-tuple-element.68), channel_id=1, source_target_pairs={{0,8},{4,12},{8,0},{12,4},{16,24},{20,28},{24,16},{28,20},{1,9},{5... | collective-permute-start | bytes 1572872 | tf_op jit(solution)/shard_map/ppermute | solution.py:90
  148.6 33.4 %collective-permute-start.4 = (bf16[2,1024,256]{2,1,0:T(8,128)(2,1)S(1)}, bf16[2,1024,256]{2,1,0:T(8,128)(2,1)S(1)}, u32[]{:S(2)}, u32[]{:S(2)}) collective-permute-start(bf16[2,1024,256]{2,1,0:T(8,128)(2,1)S(1)} %pad_maximum_fusion.9), channel_id=1, source_target_pairs={{0,8},{4,12},{8,0},{12,4},{16,24},{20,28},{24,16},{28,20},{1,9},{5... | collective-permute-start | bytes 3145736 | tf_op jit(solution)/shard_map/ppermute | solution.py:90
  160.9 24.0 %collective-permute-start.1 = (bf16[2,1024,256]{2,1,0:T(8,128)(2,1)S(1)}, bf16[2,1024,256]{2,1,0:T(8,128)(2,1)S(1)}, u32[]{:S(2)}, u32[]{:S(2)}) collective-permute-start(bf16[2,1024,256]{2,1,0:T(8,128)(2,1)S(1)} %pad_maximum_fusion.8), channel_id=1, source_target_pairs={{0,16},{4,20},{8,24},{12,28},{16,0},{20,4},{24,8},{28,12},{1,17},{... | collective-permute-start | bytes 3145736 | tf_op jit(solution)/shard_map/ppermute | solution.py:90
  185.0 6.1 collective-permute-start.5
  187.5 7.3 collective-permute-start.2
  371.5 28.1 %collective-permute-start.12 = (bf16[256,2048]{1,0:T(8,128)(2,1)}, bf16[256,2048]{1,0:T(8,128)(2,1)}, u32[]{:S(2)}, u32[]{:S(2)}) collective-permute-start(bf16[256,2048]{1,0:T(8,128)(2,1)} %get-tuple-element.54), channel_id=1, source_target_pairs={{0,1},{1,2},{2,3},{3,0},{4,5},{5,6},{6,7},{7,4},{8,9},{9,10},{10,1... | collective-permute-start | bytes 3145736 | tf_op jit(solution)/shard_map/ppermute | solution.py:77
  371.5 48.2 %collective-permute-start.14 = (bf16[256,2048]{1,0:T(8,128)(2,1)}, bf16[256,2048]{1,0:T(8,128)(2,1)}, u32[]{:S(2)}, u32[]{:S(2)}) collective-permute-start(bf16[256,2048]{1,0:T(8,128)(2,1)} %get-tuple-element.55), channel_id=1, source_target_pairs={{0,3},{1,0},{2,1},{3,2},{4,7},{5,4},{6,5},{7,6},{8,11},{9,8},{10,9... | collective-permute-start | bytes 3145736 | tf_op jit(solution)/shard_map/ppermute | solution.py:77
  375.3 89.3 %collective-permute-start.13 = (bf16[256,2048]{1,0:T(8,128)(2,1)}, bf16[256,2048]{1,0:T(8,128)(2,1)}, u32[]{:S(2)}, u32[]{:S(2)}) collective-permute-start(bf16[256,2048]{1,0:T(8,128)(2,1)} %get-tuple-element.56), channel_id=1, source_target_pairs={{0,2},{1,3},{2,0},{3,1},{4,6},{5,7},{6,4},{7,5},{8,10},{9,11},{10,... | collective-permute-start | bytes 3145736 | tf_op jit(solution)/shard_map/ppermute | solution.py:77
  471.4 178.5 %reduce-scatter.7.cloned.1.call-start = ((), (), s32[]{:S(2)}) async-start(), calls=%async_computation.9 | async-start | bytes 5898240 | tf_op jit(solution)/shard_map/reduce_scatter | solution.py:64
  594.9 130.2 %reduce-scatter.11.cloned.1.call-start = ((), (), s32[]{:S(2)}) async-start(), calls=%async_computation.12 | async-start | bytes 9437184 | tf_op jit(solution)/shard_map/reduce_scatter | solution.py:64
  609.2 236.2 %reduce-scatter.9.cloned.1.call-start = ((), (), s32[]{:S(2)}) async-start(), calls=%async_computation.11 | async-start | bytes 18874368 | tf_op jit(solution)/shard_map/reduce_scatter | solution.py:64
  638.2 420.0 %all-gather.17.cloned.1.call-start = ((), (), s32[]{:S(2)}) async-start(), calls=%async_computation.10 | async-start | bytes 5898240 | tf_op jit(solution)/shard_map/all_gather | solution.py:60
  649.9 419.1 %all-gather.19.cloned.1.call-start = ((), (), s32[]{:S(2)}) async-start(), calls=%async_computation.13 | async-start | bytes 28311552 | tf_op jit(solution)/shard_map/all_gather | solution.py:60
  865.1 16.7 %collective-permute-start.6 = (bf16[256,1024]{1,0:T(8,128)(2,1)S(1)}, bf16[256,1024]{1,0:T(8,128)(2,1)S(1)}, u32[]{:S(2)}, u32[]{:S(2)}) collective-permute-start(bf16[256,1024]{1,0:T(8,128)(2,1)S(1)} %get-tuple-element.61), channel_id=1, source_target_pairs={{0,1},{1,2},{2,3},{3,0},{4,5},{5,6},{6,7},{7,4},{8,9},{9,10},{10,1... | collective-permute-start | bytes 1572872 | tf_op jit(solution)/shard_map/ppermute | solution.py:77
  866.5 28.7 %collective-permute-start.8 = (bf16[256,1024]{1,0:T(8,128)(2,1)S(1)}, bf16[256,1024]{1,0:T(8,128)(2,1)S(1)}, u32[]{:S(2)}, u32[]{:S(2)}) collective-permute-start(bf16[256,1024]{1,0:T(8,128)(2,1)S(1)} %get-tuple-element.62), channel_id=1, source_target_pairs={{0,3},{1,0},{2,1},{3,2},{4,7},{5,4},{6,5},{7,6},{8,11},{9,8},{10,9... | collective-permute-start | bytes 1572872 | tf_op jit(solution)/shard_map/ppermute | solution.py:77
  868.9 78.7 %collective-permute-start.7 = (bf16[256,1024]{1,0:T(8,128)(2,1)S(1)}, bf16[256,1024]{1,0:T(8,128)(2,1)S(1)}, u32[]{:S(2)}, u32[]{:S(2)}) collective-permute-start(bf16[256,1024]{1,0:T(8,128)(2,1)S(1)} %get-tuple-element.63), channel_id=1, source_target_pairs={{0,2},{1,3},{2,0},{3,1},{4,6},{5,7},{6,4},{7,5},{8,10},{9,11},{10,... | collective-permute-start | bytes 1572872 | tf_op jit(solution)/shard_map/ppermute | solution.py:77
  869.5 96.4 %collective-permute-start.9 = (bf16[256,1024]{1,0:T(8,128)(2,1)S(1)}, bf16[256,1024]{1,0:T(8,128)(2,1)S(1)}, u32[]{:S(2)}, u32[]{:S(2)}) collective-permute-start(bf16[256,1024]{1,0:T(8,128)(2,1)S(1)} %get-tuple-element.64), channel_id=1, source_target_pairs={{0,1},{1,2},{2,3},{3,0},{4,5},{5,6},{6,7},{7,4},{8,9},{9,10},{10,1... | collective-permute-start | bytes 1572872 | tf_op jit(solution)/shard_map/ppermute | solution.py:77
  875.6 178.5 %collective-permute-start.15 = (bf16[256,2048]{1,0:T(8,128)(2,1)S(1)}, bf16[256,2048]{1,0:T(8,128)(2,1)S(1)}, u32[]{:S(2)}, u32[]{:S(2)}) collective-permute-start(bf16[256,2048]{1,0:T(8,128)(2,1)S(1)} %get-tuple-element.51), channel_id=1, source_target_pairs={{0,1},{1,2},{2,3},{3,0},{4,5},{5,6},{6,7},{7,4},{8,9},{9,10},{10,1... | collective-permute-start | bytes 3145736 | tf_op jit(solution)/shard_map/ppermute | solution.py:77
  881.8 172.4 %collective-permute-start.17 = (bf16[256,2048]{1,0:T(8,128)(2,1)S(1)}, bf16[256,2048]{1,0:T(8,128)(2,1)S(1)}, u32[]{:S(2)}, u32[]{:S(2)}) collective-permute-start(bf16[256,2048]{1,0:T(8,128)(2,1)S(1)} %get-tuple-element.52), channel_id=1, source_target_pairs={{0,3},{1,0},{2,1},{3,2},{4,7},{5,4},{6,5},{7,6},{8,11},{9,8},{10,9... | collective-permute-start | bytes 3145736 | tf_op jit(solution)/shard_map/ppermute | solution.py:77
  895.1 159.0 %collective-permute-start.16 = (bf16[256,2048]{1,0:T(8,128)(2,1)S(1)}, bf16[256,2048]{1,0:T(8,128)(2,1)S(1)}, u32[]{:S(2)}, u32[]{:S(2)}) collective-permute-start(bf16[256,2048]{1,0:T(8,128)(2,1)S(1)} %get-tuple-element.53), channel_id=1, source_target_pairs={{0,2},{1,3},{2,0},{3,1},{4,6},{5,7},{6,4},{7,5},{8,10},{9,11},{10,... | collective-permute-start | bytes 3145736 | tf_op jit(solution)/shard_map/ppermute | solution.py:77
  965.9 12.9 %collective-permute-start.26 = (f32[2048]{0:T(1024)S(1)}, f32[2048]{0:T(1024)S(1)}, u32[]{:S(2)}, u32[]{:S(2)}) collective-permute-start(f32[2048]{0:T(1024)S(1)} %add.233), channel_id=1, source_target_pairs={{0,1},{1,0},{2,3},{3,2},{4,5},{5,4},{6,7},{7,6},{8,9},{9,8},{10,11... | collective-permute-start | bytes 24584 | tf_op jit(solution)/shard_map/ppermute | solution.py:102
  965.9 15.5 %collective-permute-start.21 = (f32[2048]{0:T(1024)S(1)}, f32[2048]{0:T(1024)S(1)}, u32[]{:S(2)}, u32[]{:S(2)}) collective-permute-start(f32[2048]{0:T(1024)S(1)} %add.228), channel_id=1, source_target_pairs={{0,1},{1,0},{2,3},{3,2},{4,5},{5,4},{6,7},{7,6},{8,9},{9,8},{10,11... | collective-permute-start | bytes 24584 | tf_op jit(solution)/shard_map/ppermute | solution.py:102
  978.7 14.9 %collective-permute-start.11 = (bf16[256,1024]{1,0:T(8,128)(2,1)S(1)}, bf16[256,1024]{1,0:T(8,128)(2,1)S(1)}, u32[]{:S(2)}, u32[]{:S(2)}) collective-permute-start(bf16[256,1024]{1,0:T(8,128)(2,1)S(1)} %get-tuple-element.65), channel_id=1, source_target_pairs={{0,3},{1,0},{2,1},{3,2},{4,7},{5,4},{6,5},{7,6},{8,11},{9,8},{10,9... | collective-permute-start | bytes 1572872 | tf_op jit(solution)/shard_map/ppermute | solution.py:77
  981.4 67.6 %collective-permute-start.10 = (bf16[256,1024]{1,0:T(8,128)(2,1)S(1)}, bf16[256,1024]{1,0:T(8,128)(2,1)S(1)}, u32[]{:S(2)}, u32[]{:S(2)}) collective-permute-start(bf16[256,1024]{1,0:T(8,128)(2,1)S(1)} %get-tuple-element.66), channel_id=1, source_target_pairs={{0,2},{1,3},{2,0},{3,1},{4,6},{5,7},{6,4},{7,5},{8,10},{9,11},{10,... | collective-permute-start | bytes 1572872 | tf_op jit(solution)/shard_map/ppermute | solution.py:77
  993.7 55.6 %collective-permute-start.27 = (f32[2048]{0:T(1024)S(1)}, f32[2048]{0:T(1024)S(1)}, u32[]{:S(2)}, u32[]{:S(2)}) collective-permute-start(f32[2048]{0:T(1024)S(1)} %add.234), channel_id=1, source_target_pairs={{0,2},{1,3},{2,0},{3,1},{4,6},{5,7},{6,4},{7,5},{8,10},{9,11},{10,... | collective-permute-start | bytes 24584 | tf_op jit(solution)/shard_map/ppermute | solution.py:102
  (38 other events, 863.4 us)
Sparse Core Ops, SparseCore 0:
  11.0 30.6 all-gather.10
  43.3 80.1 all-gather.8
  125.0 79.2 all-gather.12
  206.3 79.2 all-gather.20
  471.5 79.5 all-gather.14
Sparse Core Ops, SparseCore 1:
  15.2 36.2 reduce-scatter.4
  595.0 54.8 reduce-scatter.6
  653.8 71.3 reduce-scatter.10
  729.3 116.0 reduce-scatter.8
  847.3 40.9 all-gather.16
  890.7 125.7 all-gather.18

commit v3 on v2

--- a/solution.py
+++ b/solution.py
@@ -52,10 +52,6 @@
     )
 
 
-def gated_unit(gate_in, up_in):
-    return jax.nn.silu(gate_in) * up_in
-
-
 def gather_rows(block, axis):
     return lax.all_gather(block, axis, axis=0, tiled=True)
 
@@ -79,12 +75,15 @@
     return total
 
 
-def cube_gather(block, axis):
+def cube_gather(blocks, axis):
     n = lax.axis_size(axis)
     bits = [1 << b for b in range(n.bit_length() - 1)]
-    half = block.shape[0] // 2
+    half = blocks.shape[-1] // 2
     halves = []
-    for part, order in ((block[:half], bits[1:] + bits[:1]), (block[half:], bits[:0:-1] + bits[:1])):
+    for part, order in (
+        (blocks[..., :half], bits[1:] + bits[:1]),
+        (blocks[..., half:], bits[:0:-1] + bits[:1]),
+    ):
         held, offsets = part[None], [0]
         for bit in order:
             moved = lax.ppermute(held, axis, [(i, i ^ bit) for i in range(n)])
@@ -121,13 +120,13 @@
     )
 
 
-def norm_project(all_tokens, gain_vec, weight_rows, cos_rows, sin_rows, rotated):
-    rows, width = all_tokens.shape
+def norm_project(gathered, tile, gain_vec, weight_rows, cos_rows, sin_rows, rotated):
+    groups, _, width = gathered.shape
+    rows = groups * tile
     columns = weight_rows.shape[0]
-    tile = 256
 
     def kernel(tokens_ref, gain_ref, weight_ref, cos_ref, sin_ref, normed_ref, out_ref):
-        values = tokens_ref[...].astype(jnp.float32)
+        values = tokens_ref[0].astype(jnp.float32)
         row_scale = lax.rsqrt(jnp.mean(values * values, axis=-1, keepdims=True) + EPS)
         normed = (values * row_scale * gain_ref[...].astype(jnp.float32)).astype(jnp.bfloat16)
         normed_ref[...] = normed
@@ -142,7 +141,7 @@
         kernel,
         grid=(rows // tile,),
         in_specs=[
-            pl.BlockSpec((tile, width), lambda i: (i, 0)),
+            pl.BlockSpec((1, tile, width), lambda i: (i, 0, 0)),
             pl.BlockSpec((1, width), lambda i: (0, 0)),
             pl.BlockSpec((columns, width), lambda i: (0, 0)),
             pl.BlockSpec((half, tile), lambda i: (0, i % (SEQLEN // tile))),
@@ -160,7 +159,7 @@
             flops=2 * rows * width * columns, transcendentals=rows, bytes_accessed=12 << 20
         ),
         name="norm_project",
-    )(all_tokens, gain_vec.reshape(1, -1), weight_rows, cos_rows, sin_rows)
+    )(gathered, gain_vec.reshape(1, -1), weight_rows, cos_rows, sin_rows)
 
 
 def key_tiles(step, tile):
@@ -338,33 +337,45 @@
     )(projected, projected, projected, d_heads, totals, cos_rows, sin_rows)
 
 
-def project_and_norm(all_heads, weights, all_tokens, gain_vec):
+def project_and_norm(all_heads, weights, gathered, gain_vec):
     groups, rows, group_columns = all_heads.shape
     (first, first_offsets), (second, second_offsets) = weights
-    parts, depth, part_columns = first.shape
-    width = all_tokens.shape[1]
+    parts, _, depth, half = first.shape
+    width = 2 * half
     tile = rows // groups
     places = jnp.stack([lax.axis_index("tensor"), lax.axis_index("dp")])
 
     def kernel(
-        at_ref, heads_ref, first_ref, second_ref, tokens_ref, gain_ref, hidden_ref, normed_ref, acc_ref, wide_ref
+        at_ref,
+        heads_ref,
+        first_ref,
+        second_ref,
+        tokens_ref,
+        gain_ref,
+        hidden_ref,
+        normed_ref,
+        weight_ref,
+        wide_ref,
     ):
         step = pl.program_id(0)
+
+        @pl.when(step == 0)
+        def _():
+            for side, part_ref, offsets in (
+                (0, first_ref, first_offsets),
+                (half, second_ref, second_offsets),
+            ):
+                for part in range(parts):
+                    for g in range(groups):
+                        start = g * group_columns + (at_ref[1] ^ offsets[part]) * depth
+                        at = pl.ds(pl.multiple_of(start, depth), depth)
+                        weight_ref[at, side : side + half] = part_ref[part, g]
+
         for g in range(groups):
             wide_ref[:, g * group_columns : (g + 1) * group_columns] = heads_ref[g]
-        acc_ref[...] = tokens_ref[...].astype(jnp.float32)
-        for half, (weight_ref, offsets) in enumerate(
-            ((first_ref, first_offsets), (second_ref, second_offsets))
-        ):
-            for part in range(parts):
-                start = (at_ref[1] ^ offsets[part]) * part_columns
-                columns = pl.ds(pl.multiple_of(start, part_columns), part_columns)
-                acc_ref[:, columns] += jnp.dot(
-                    wide_ref[:, half * depth : (half + 1) * depth],
-                    weight_ref[part],
-                    preferred_element_type=jnp.float32,
-                )
-        hidden = acc_ref[...]
+        hidden = tokens_ref[0].astype(jnp.float32) + jnp.dot(
+            wide_ref[...], weight_ref[...], preferred_element_type=jnp.float32
+        )
         row_scale = lax.rsqrt(jnp.mean(hidden * hidden, axis=-1, keepdims=True) + EPS)
         normed_ref[...] = (hidden * row_scale * gain_ref[...].astype(jnp.float32)).astype(
             jnp.bfloat16
@@ -381,9 +392,9 @@
             grid=(groups,),
             in_specs=[
                 pl.BlockSpec((groups, tile, group_columns), lambda i, at_ref: (0, i, 0)),
-                pl.BlockSpec(first.shape, lambda i, at_ref: (0, 0, 0)),
-                pl.BlockSpec(second.shape, lambda i, at_ref: (0, 0, 0)),
-                pl.BlockSpec((tile, width), lambda i, at_ref: (i, 0)),
+                pl.BlockSpec(first.shape, lambda i, at_ref: (0, 0, 0, 0)),
+                pl.BlockSpec(second.shape, lambda i, at_ref: (0, 0, 0, 0)),
+                pl.BlockSpec((1, tile, width), lambda i, at_ref: (i, 0, 0)),
                 pl.BlockSpec((1, width), lambda i, at_ref: (0, 0)),
             ],
             out_specs=[
@@ -391,7 +402,7 @@
                 pl.BlockSpec((tile, width), lambda i, at_ref: (i, 0)),
             ],
             scratch_shapes=[
-                pltpu.VMEM((tile, width), jnp.float32),
+                pltpu.VMEM((groups * group_columns, width), jnp.bfloat16),
                 pltpu.VMEM((tile, groups * group_columns), jnp.bfloat16),
             ],
         ),
@@ -403,7 +414,68 @@
             flops=2 * rows * width * width, transcendentals=rows, bytes_accessed=20 << 20
         ),
         name="project_and_norm",
-    )(places, all_heads, first, second, all_tokens, gain_vec.reshape(1, -1))
+    )(places, all_heads, first, second, gathered, gain_vec.reshape(1, -1))
+
+
+def gated_back(all_cot, w_down, gate_proj, up_proj):
+    rows, width = all_cot.shape
+    columns = w_down.shape[0]
+    tile = 256
+
+    def kernel(cot_ref, weight_ref, gate_ref, up_ref, d_gate_ref, d_up_ref):
+        d_active = dot_lanes(cot_ref[...], weight_ref[...])
+        gate = gate_ref[...]
+        chance = jax.nn.sigmoid(gate)
+        smooth = gate * chance
+        d_up_ref[...] = (d_active * smooth).astype(jnp.bfloat16)
+        slope = chance * (1.0 + gate * (1.0 - chance))
+        d_gate_ref[...] = (d_active * up_ref[...] * slope).astype(jnp.bfloat16)
+
+    column_block = pl.BlockSpec((rows, tile), lambda j: (0, j))
+    return pl.pallas_call(
+        kernel,
+        grid=(columns // tile,),
+        in_specs=[
+            pl.BlockSpec((rows, width), lambda j: (0, 0)),
+            pl.BlockSpec((tile, width), lambda j: (j, 0)),
+            column_block,
+            column_block,
+        ],
+        out_specs=[column_block] * 2,
+        out_shape=[jax.ShapeDtypeStruct((rows, columns), jnp.bfloat16)] * 2,
+        cost_estimate=pl.CostEstimate(
+            flops=2 * rows * width * columns,
+            transcendentals=rows * columns,
+            bytes_accessed=36 << 20,
+        ),
+        name="gated_back",
+    )(all_cot, w_down, gate_proj, up_proj)
+
+
+def pair_product(first, first_weight, second, second_weight):
+    rows, depth = first.shape
+    columns = first_weight.shape[0]
+    tile = 256
+
+    def kernel(first_ref, second_ref, first_w_ref, second_w_ref, out_ref):
+        out_ref[...] = (
+            dot_lanes(first_ref[...], first_w_ref[...])
+            + dot_lanes(second_ref[...], second_w_ref[...])
+        ).astype(jnp.bfloat16)
+
+    whole = pl.BlockSpec((rows, depth), lambda j: (0, 0))
+    weight_block = pl.BlockSpec((tile, depth), lambda j: (j, 0))
+    return pl.pallas_call(
+        kernel,
+        grid=(columns // tile,),
+        in_specs=[whole, whole, weight_block, weight_block],
+        out_specs=pl.BlockSpec((rows, tile), lambda j: (0, j)),
+        out_shape=jax.ShapeDtypeStruct((rows, columns), jnp.bfloat16),
+        cost_estimate=pl.CostEstimate(
+            flops=4 * rows * depth * columns, transcendentals=0, bytes_accessed=28 << 20
+        ),
+        name="pair_product",
+    )(first, second, first_weight, second_weight)
 
 
 def gated_up(normed, w_gate, w_up):
@@ -473,13 +545,13 @@
     low = jnp.bfloat16
     n_dp = lax.axis_size("dp")
     nothing = scatter_sum(tokens[:, :128] * 0, "dp")[0, 0]
-    all_tokens = gather_rows(tokens, "tensor")
-    part_columns = w_output.shape[1] // n_dp
-    own_part = lax.dynamic_slice_in_dim(
-        w_output, lax.axis_index("dp") * part_columns, part_columns, 1
-    )
-    part_output = gather_rows(own_part, "tensor")
-    all_output = cube_gather(part_output, "dp")
+    own_rows, width = tokens.shape
+    depth = w_output.shape[0] // n_dp
+    own_part = lax.dynamic_slice_in_dim(w_output, lax.axis_index("dp") * depth, depth, 0)
+    gathered = lax.all_gather(
+        jnp.concatenate([tokens, own_part], axis=0), "tensor", axis=0
+    )
+    all_output = cube_gather(gathered[:, own_rows:], "dp")
     q_columns, k_columns = w_query.shape[1], w_key.shape[1]
     q_heads, kv_heads = q_columns // HD, k_columns // HD
     gain_one = norm1_gain.astype(jnp.float32)
@@ -489,26 +561,22 @@
     cos_rows, sin_rows = cos_table.T, sin_table.T
     weight_rows = jnp.concatenate([w_query.T, w_key.T, w_value.T], axis=0)
     normed1, projected = norm_project(
-        all_tokens, norm1_gain, weight_rows, cos_rows, sin_rows, q_columns + k_columns
+        gathered, own_rows, norm1_gain, weight_rows, cos_rows, sin_rows, q_columns + k_columns
     )
     heads_out, heads_rows, totals = attend(projected, q_heads, kv_heads)
     all_heads = lax.all_gather(heads_out, "tensor", axis=0)
     all_cot = gather_rows(cotangent, "tensor")
     hidden_state, normed2 = project_and_norm(
-        all_heads, all_output, all_tokens, (gain_two + nothing.astype(jnp.float32))
+        all_heads, all_output, gathered, (gain_two + nothing.astype(jnp.float32))
     )
     gate_proj, up_proj, activated = gated_up(normed2, w_gate, w_up)
     mlp_part = jnp.dot(activated, w_down, preferred_element_type=jnp.float32).astype(low)
-    d_activated = contract_cols(all_cot, w_down)
-    _, pull_gated = jax.vjp(gated_unit, gate_proj, up_proj)
-    d_gate, d_up = pull_gated(d_activated)
-    d_gate = d_gate.astype(low)
-    d_up = d_up.astype(low)
     ff_columns = w_gate.shape[1]
     ff_folds = w_gate.shape[0] // w_down.shape[0]
     grad_down = row_major(split_columns(contract_rows(activated, all_cot).astype(low), ff_folds))
     part_down = scatter_sum(grad_down, "dp")
-    dn2_part = (contract_cols(d_gate, w_gate) + contract_cols(d_up, w_up)).astype(low)
+    d_gate, d_up = gated_back(all_cot, w_down, gate_proj, up_proj)
+    dn2_part = pair_product(d_gate, w_gate, d_up, w_up)
     d_normed2 = exchange_sum(dn2_part, "tensor")
     gate_up_grads = row_major(
         jnp.concatenate(
@@ -532,7 +600,10 @@
     dn1_part = contract_rows(d_projected, weight_rows).astype(low)
     d_normed1 = exchange_sum(dn1_part, "tensor")
     gain_one_sum = cube_sum(
-        gain_gradient(all_tokens.astype(jnp.float32), dn1_part.astype(jnp.float32)), ("dp", "tensor")
+        gain_gradient(
+            gathered[:, :own_rows].reshape(-1, width).astype(jnp.float32),
+            dn1_part.astype(jnp.float32),
+        ), ("dp", "tensor")
     )
     folds = w_query.shape[0] // w_output.shape[0]
     grad_qkv = lax.dot_general(

time: 1110 us -> 1080 us (0.973)
  matrix products: 110 us -> 67.7 us
  Pallas kernels: 84.8 us -> 127 us
  waiting for transfers between devices: 671 us -> 644 us
    all_gather x0 -> x1, waiting for transfers between devices: none -> 88.7 us  [block(): lax.all_gather(jnp.concatenate([tokens, own_part], axis=0), 'tensor', axi...]
    all_gather x6 -> x4, waiting for transfers between devices: 180 us -> 119 us  [gather_rows(): return lax.all_gather(block, axis, axis=0, tiled=True)]
    all_gather x1, waiting for transfers between devices: 66.7 us -> 20.5 us  [block(): all_heads = lax.all_gather(heads_out, 'tensor', axis=0)]
    dot_general x4 -> x1, matrix products: 46.9 us -> 3.35 us  [contract_cols(): lax.dot_general(left_side, right_side, (((1,), (1,)), ((), ())), preferre...]
    pallas_call x1 -> x3, Pallas kernels: 8.37 us -> 51.2 us  [the longest x1 24 us: pair_product(): pl.pallas_call(kernel, grid=(columns // tile,), in_specs=[whole, whole, w...]
  transfers between devices with their start and end apart: 39 -> 38, of which waited for: 25 -> 24; matrix products, arithmetic and copies ran while one was open for 12% -> 12% of each run, Pallas kernels for 2% -> 6%
where the time goes in v3:
time: 1080 us; the launch traced here: 1070 us
  waiting for transfers between devices  644 us (60%)
  Pallas kernels  127 us (12%)
  starting transfers between devices  97.8 us (9%)
  other arithmetic  92.3 us (9%)
  matrix products  67.7 us (6%)
  local copies, waits for them, and re-layouts  29.4 us (3%)
  between operations  16.7 us (2%)
    reduce_scatter x4, waiting for transfers between devices, scatter_sum(): return lax.psum_scatter(partial, axis, scatter_dimension=0, tiled=True)  207 us
    ppermute x12, waiting for transfers between devices, exchange_sum(): lax.ppermute(block((me + hop) % n), axis, [(i, (i + hop) % n) for i in ra...  153 us
    all_gather x4, waiting for transfers between devices, gather_rows(): return lax.all_gather(block, axis, axis=0, tiled=True)  119 us
    all_gather x1, waiting for transfers between devices, block(): lax.all_gather(jnp.concatenate([tokens, own_part], axis=0), 'tensor', axi...  88.7 us
    ppermute x10, starting transfers between devices, cube_sum(): lax.ppermute(vector, axis, [(i, i ^ bit) for i in range(n)])  51.6 us
    dot_general x4, matrix products, contract_rows(): lax.dot_general(left_side, right_side, (((0,), (0,)), ((), ())), preferre...  41.8 us
    ppermute x12, starting transfers between devices, exchange_sum(): lax.ppermute(block((me + hop) % n), axis, [(i, (i + hop) % n) for i in ra...  38.2 us
    ppermute x6, waiting for transfers between devices, cube_gather(): moved = lax.ppermute(held, axis, [(i, i ^ bit) for i in range(n)])  30.8 us
  transfers between devices with their start and end apart: 38, of which 24 were waited for; matrix products, arithmetic and copies ran while one was open for 12% of the time, Pallas kernels for 6%

profile of v3, /device:TPU:0, one launch (start us, length us, event | category | flops | bytes accessed | tf_op | source)
XLA Modules:
  0.0 1074.7 jit_solution(8189029548322257379)
XLA Ops:
  24.2 88.7 %all-gather.17.cloned.1.call-done = bf16[1280,2048]{1,0:T(8,128)(2,1)} async-done(((bf16[320,2048]{1,0:T(8,128)(2,1)}), bf16[1280,2048]{1,0:T(8,128)(2,1)}) %all-gather.17.cloned.1.call-update) | async-done | bytes 5242896 | tf_op jit(solution)/shard_map/all_gather | solution.py:551
  113.0 8.3 norm_project.1
  121.3 13.7 %attend.1 = (bf16[1024,512]{1,0:T(8,128)(2,1)}, bf16[512,1024]{1,0:T(8,128)(2,1)}, f32[2,4,1024]{2,1,0:T(4,128)}) custom-call(bf16[768,1024]{1,0:T(8,128)(2,1)} %get-tuple-element.26.query_ref.key_ref.value_ref, bf16[768,1024]{1,0:T(8,128)(2,1)} %get-tuple-element.26.query_ref.key_ref.value_ref, bf16[768,1024]{1,0:T(8,128)(2,1)} %get-tuple-element.26.query_ref.key_ref.value_ref), custom_call_target="tpu_custom_call" | custom-call | flops 1073741824 | bytes 4194304 | tf_op jit(solution)/shard_map/attend/pallas_call | solution.py:213
  139.5 10.7 collective-permute-done.3
  156.5 20.1 %collective-permute-done.4 = bf16[2,4,64,1024]{3,2,1,0:T(8,128)(2,1)} collective-permute-done((bf16[2,4,64,1024]{3,2,1,0:T(8,128)(2,1)}, bf16[2,4,64,1024]{3,2,1,0:T(8,128)(2,1)}, u32[]{:S(2)}, u32[]{:S(2)}) %collective-permute-start.4) | collective-permute-done | bytes 1048608 | tf_op jit(solution)/shard_map/ppermute | solution.py:89
  193.8 20.5 %all-gather.19.cloned.1.call-done = bf16[4096,512]{1,0:T(8,128)(2,1)} async-done(((bf16[1024,512]{1,0:T(8,128)(2,1)}), bf16[4096,512]{1,0:T(8,128)(2,1)}) %all-gather.19.cloned.1.call-update) | async-done | bytes 4194320 | tf_op jit(solution)/shard_map/all_gather | solution.py:567
  214.3 17.6 %project_and_norm.1 = (f32[256,2048]{1,0:T(8,128)}, bf16[1024,2048]{1,0:T(8,128)(2,1)}) custom-call(s32[2]{0:T(128)} %pad_add_fusion.at_ref, bf16[4,1024,512]{2,1,0:T(8,128)(2,1)} %bitcast.70, bf16[8,4,64,1024]{3,2,1,0:T(8,128)(2,1)} %pad_maximum_fusion.2.first_ref, bf16[8,4,64,1024]{3,2,1,0:T(8,128)(2,1)} %pad_maximum_fusion.3.second_ref, ...), custom_call_target="tpu_custom_call" | custom-call | flops 8589934592 | bytes 20971520 | tf_op jit(solution)/shard_map/project_and_norm/pallas_call | solution.py:388
  231.9 23.7 %gated_up.1 = (f32[1024,2048]{1,0:T(8,128)}, f32[1024,2048]{1,0:T(8,128)}, bf16[1024,2048]{1,0:T(8,128)(2,1)}) custom-call(bf16[1024,2048]{1,0:T(8,128)(2,1)} %get-tuple-element.29.normed_ref, bf16[2048,2048]{1,0:T(8,128)(2,1)} %first_w_ref.1, bf16[2048,2048]{1,0:T(8,128)(2,1)} %second_w_ref.1), custom_call_target="tpu_custom_call" | custom-call | flops 17179869184 | bytes 41943040 | tf_op jit(solution)/shard_map/gated_up/pallas_call | solution.py:495
  255.6 39.5 %all-gather.9.cloned.1.call-done.cot_ref = bf16[1024,2048]{1,0:T(8,128)(2,1)} async-done(((bf16[256,2048]{1,0:T(8,128)(2,1)}), bf16[1024,2048]{1,0:T(8,128)(2,1)}) %all-gather.9.cloned.1.call-update) | async-done | bytes 4194320 | tf_op jit(solution)/shard_map/all_gather | solution.py:56
  295.1 18.9 %gated_back.1 = (bf16[1024,2048]{1,0:T(8,128)(2,1)}, bf16[1024,2048]{1,0:T(8,128)(2,1)}) custom-call(bf16[1024,2048]{1,0:T(8,128)(2,1)} %all-gather.9.cloned.1.call-done.cot_ref, bf16[2048,2048]{1,0:T(8,128)(2,1)} %weight_ref.1, f32[1024,2048]{1,0:T(8,128)} %get-tuple-element.31.gate_ref, f32[1024,2048]{1,0:T(8,128)} %get-tuple-element.32.up_ref), custom_call_target="tpu_custom_call" | custom-call | flops 8589934592 | bytes 37748736 | tf_op jit(solution)/shard_map/gated_back/pallas_call | solution.py:435
  314.1 24.0 %pair_product.1 = bf16[1024,2048]{1,0:T(8,128)(2,1)} custom-call(bf16[1024,2048]{1,0:T(8,128)(2,1)} %get-tuple-element.33.first_ref, bf16[1024,2048]{1,0:T(8,128)(2,1)} %get-tuple-element.34.second_ref, bf16[2048,2048]{1,0:T(8,128)(2,1)} %first_w_ref.1, bf16[2048,2048]{1,0:T(8,128)(2,1)} %second_w_ref.1), custom_call_target="tpu_custom_call" | custom-call | flops 17179869184 | bytes 29360128 | tf_op jit(solution)/shard_map/pair_product/pallas_call | solution.py:468
  347.5 22.3 %collective-permute-done.12 = bf16[256,2048]{1,0:T(8,128)(2,1)} collective-permute-done((bf16[256,2048]{1,0:T(8,128)(2,1)}, bf16[256,2048]{1,0:T(8,128)(2,1)}, u32[]{:S(2)}, u32[]{:S(2)}) %collective-permute-start.12) | collective-permute-done | bytes 1048608 | tf_op jit(solution)/shard_map/ppermute | solution.py:73
  369.8 20.0 %collective-permute-done.14 = bf16[256,2048]{1,0:T(8,128)(2,1)} collective-permute-done((bf16[256,2048]{1,0:T(8,128)(2,1)}, bf16[256,2048]{1,0:T(8,128)(2,1)}, u32[]{:S(2)}, u32[]{:S(2)}) %collective-permute-start.14) | collective-permute-done | bytes 1048608 | tf_op jit(solution)/shard_map/ppermute | solution.py:73
  389.9 44.9 %collective-permute-done.13 = bf16[256,2048]{1,0:T(8,128)(2,1)} collective-permute-done((bf16[256,2048]{1,0:T(8,128)(2,1)}, bf16[256,2048]{1,0:T(8,128)(2,1)}, u32[]{:S(2)}, u32[]{:S(2)}) %collective-permute-start.13) | collective-permute-done | bytes 1048608 | tf_op jit(solution)/shard_map/ppermute | solution.py:73
  441.4 79.4 %all-gather.11.cloned.1.call-done = bf16[1024,2048]{1,0:T(8,128)(2,1)} async-done(((bf16[256,2048]{1,0:T(8,128)(2,1)}), bf16[1024,2048]{1,0:T(8,128)(2,1)}) %all-gather.11.cloned.1.call-update) | async-done | bytes 4194320 | tf_op jit(solution)/shard_map/all_gather | solution.py:56
  531.9 20.3 %attend_back.1 = (bf16[512,1024]{1,0:T(8,128)(2,1)}, bf16[128,1024]{1,0:T(8,128)(2,1)}, bf16[128,1024]{1,0:T(8,128)(2,1)}) custom-call(bf16[768,1024]{1,0:T(8,128)(2,1)} %get-tuple-element.26.query_ref.key_ref.value_ref, bf16[768,1024]{1,0:T(8,128)(2,1)} %get-tuple-element.26.query_ref.key_ref.value_ref, ...), custom_call_target="tpu_custom_call" | custom-call | flops 2684354560 | bytes 6291456 | tf_op jit(solution)/shard_map/attend_back/pallas_call | solution.py:305
  565.0 14.0 %convolution_convert_fusion = bf16[2048,2048]{1,0:T(8,128)(2,1)} fusion(bf16[1024,2048]{1,0:T(8,128)(2,1)} %get-tuple-element.30, bf16[1024,2048]{1,0:T(8,128)(2,1)} %all-gather.9.cloned.1.call-done.cot_ref), kind=kOutput, calls=%fused_computation.8 | convolution fusion | flops 8594128896 | bytes 16777216 | tf_op jit(solution)/shard_map/dot_general | solution.py:44
  579.2 12.2 %convolution_convert_fusion.1 = bf16[2048,2048]{1,0:T(8,128)(2,1)S(1)} fusion(bf16[1024,2048]{1,0:T(8,128)(2,1)} %get-tuple-element.29.normed_ref, bf16[1024,2048]{1,0:T(8,128)(2,1)} %get-tuple-element.34.second_ref), kind=kOutput, calls=%fused_computation.9 | convolution fusion | flops 8594128896 | bytes 16777216 | tf_op jit(solution)/shard_map/dot_general | solution.py:44
  591.4 9.8 convolution_convert_fusion.2
  601.2 6.9 pad_maximum_fusion
  608.1 11.4 %reduce-scatter.7.cloned.1.call-done = bf16[256,1280]{1,0:T(8,128)(2,1)} async-done(((bf16[2048,1280]{1,0:T(8,128)(2,1)}), bf16[256,1280]{1,0:T(8,128)(2,1)}) %reduce-scatter.7.cloned.1.call-update) | async-done | bytes 655376 | tf_op jit(solution)/shard_map/reduce_scatter | solution.py:60
  619.8 75.0 %reduce-scatter.11.cloned.1.call-done = bf16[256,2048]{1,0:T(8,128)(2,1)} async-done(((bf16[2048,2048]{1,0:T(8,128)(2,1)}), bf16[256,2048]{1,0:T(8,128)(2,1)}) %reduce-scatter.11.cloned.1.call-update) | async-done | bytes 1048592 | tf_op jit(solution)/shard_map/reduce_scatter | solution.py:60
  694.8 120.2 %reduce-scatter.9.cloned.1.call-done = bf16[256,4096]{1,0:T(8,128)(2,1)} async-done(((bf16[2048,4096]{1,0:T(8,128)(2,1)}), bf16[256,4096]{1,0:T(8,128)(2,1)}) %reduce-scatter.9.cloned.1.call-update) | async-done | bytes 2097168 | tf_op jit(solution)/shard_map/reduce_scatter | solution.py:60
  826.2 11.3 %convolution_convert_fusion.3 = bf16[1024,2048]{1,0:T(8,128)(2,1)S(1)} fusion(bf16[1024,2048]{1,0:T(8,128)(2,1)S(1)} %copy-done.27, bf16[2048,2048]{1,0:T(8,128)(2,1)} %weight_ref.1), kind=kOutput, calls=%fused_computation.16 | convolution fusion | flops 8592031744 | bytes 16777216 | tf_op jit(solution)/shard_map/dot_general | solution.py:573
  855.7 13.3 %collective-permute-start.17 = (bf16[256,2048]{1,0:T(8,128)(2,1)S(1)}, bf16[256,2048]{1,0:T(8,128)(2,1)S(1)}, u32[]{:S(2)}, u32[]{:S(2)}) collective-permute-start(bf16[256,2048]{1,0:T(8,128)(2,1)S(1)} %get-tuple-element.56), channel_id=1, source_target_pairs={{0,3},{1,0},{2,1},{3,2},{4,7},{5,4},{6,5},{7,6},{8,11},{9,8},{10,9... | collective-permute-start | bytes 3145736 | tf_op jit(solution)/shard_map/ppermute | solution.py:73
  869.0 9.6 collective-permute-start.16
  878.6 43.1 %collective-permute-done.7 = bf16[256,1024]{1,0:T(8,128)(2,1)} collective-permute-done((bf16[256,1024]{1,0:T(8,128)(2,1)}, bf16[256,1024]{1,0:T(8,128)(2,1)}, u32[]{:S(2)}, u32[]{:S(2)}) %collective-permute-start.7) | collective-permute-done | bytes 524320 | tf_op jit(solution)/shard_map/ppermute | solution.py:73
  941.9 10.9 %collective-permute-done.26 = f32[2048]{0:T(1024)S(1)} collective-permute-done((f32[2048]{0:T(1024)S(1)}, f32[2048]{0:T(1024)S(1)}, u32[]{:S(2)}, u32[]{:S(2)}) %collective-permute-start.26) | collective-permute-done | bytes 8224 | tf_op jit(solution)/shard_map/ppermute | solution.py:101
  958.7 8.9 collective-permute-done.11
  967.7 43.4 %collective-permute-start.27 = (f32[2048]{0:T(1024)S(1)}, f32[2048]{0:T(1024)S(1)}, u32[]{:S(2)}, u32[]{:S(2)}) collective-permute-start(f32[2048]{0:T(1024)S(1)} %add.226), channel_id=1, source_target_pairs={{0,2},{1,3},{2,0},{3,1},{4,6},{5,7},{6,4},{7,5},{8,10},{9,11},{10,... | collective-permute-start | bytes 24584 | tf_op jit(solution)/shard_map/ppermute | solution.py:101
  1011.0 11.9 %collective-permute-done.10 = bf16[256,1024]{1,0:T(8,128)(2,1)S(1)} collective-permute-done((bf16[256,1024]{1,0:T(8,128)(2,1)S(1)}, bf16[256,1024]{1,0:T(8,128)(2,1)S(1)}, u32[]{:S(2)}, u32[]{:S(2)}) %collective-permute-start.10) | collective-permute-done | bytes 524320 | tf_op jit(solution)/shard_map/ppermute | solution.py:73
  1043.2 24.2 %slice_convert_fusion = (f32[2048,2048]{1,0:T(8,128)}, f32[2048,2048]{1,0:T(8,128)}, f32[2048,2048]{1,0:T(8,128)}) fusion(bf16[2048,6144]{1,0:T(8,128)(2,1)} %all-gather.15.cloned.1.call-done), kind=kLoop, calls=%fused_computation.1 | loop fusion | flops 12582912 | bytes 75497472 | tf_op jit(solution)/shard_map/convert_element_type | solution.py:627
  (188 shorter events, 159.2 us)
Async XLA Ops:
  8.0 104.9 %all-gather.17.cloned.1.call-start = ((), (), s32[]{:S(2)}) async-start(), calls=%async_computation.12 | async-start | bytes 6553600 | tf_op jit(solution)/shard_map/all_gather | solution.py:551
  12.1 172.0 %reduce-scatter.5.cloned.1.call-start = ((), (), s32[]{:S(2)}) async-start(), calls=%async_computation.4 | async-start | bytes 73728 | tf_op jit(solution)/shard_map/reduce_scatter | solution.py:60
  13.6 200.7 %all-gather.19.cloned.1.call-start = ((), (), s32[]{:S(2)}) async-start(), calls=%async_computation.13 | async-start | bytes 5242880 | tf_op jit(solution)/shard_map/all_gather | solution.py:567
  135.1 160.1 %all-gather.9.cloned.1.call-start = ((), (), s32[]{:S(2)}) async-start(), calls=%async_computation.5 | async-start | bytes 5242880 | tf_op jit(solution)/shard_map/all_gather | solution.py:56
  136.5 13.7 %collective-permute-start.3 = (bf16[1,4,64,1024]{3,2,1,0:T(8,128)(2,1)S(1)}, bf16[1,4,64,1024]{3,2,1,0:T(8,128)(2,1)S(1)}, u32[]{:S(2)}, u32[]{:S(2)}) collective-permute-start(bf16[1,4,64,1024]{3,2,1,0:T(8,128)(2,1)S(1)} %get-tuple-element.53), channel_id=1, source_target_pairs={{0,16},{4,20},{8,24},{12,28},{16,0},{20,4},{24,8},{28,12},{1,17},{... | collective-permute-start | bytes 1572872 | tf_op jit(solution)/shard_map/ppermute | solution.py:89
  138.0 15.8 %collective-permute-start = (bf16[1,4,64,1024]{3,2,1,0:T(8,128)(2,1)S(1)}, bf16[1,4,64,1024]{3,2,1,0:T(8,128)(2,1)}, u32[]{:S(2)}, u32[]{:S(2)}) collective-permute-start(bf16[1,4,64,1024]{3,2,1,0:T(8,128)(2,1)S(1)} %get-tuple-element.54), channel_id=1, source_target_pairs={{0,8},{4,12},{8,0},{12,4},{16,24},{20,28},{24,16},{28,20},{1,9},{5... | collective-permute-start | bytes 1572872 | tf_op jit(solution)/shard_map/ppermute | solution.py:89
  152.1 24.5 %collective-permute-start.4 = (bf16[2,4,64,1024]{3,2,1,0:T(8,128)(2,1)}, bf16[2,4,64,1024]{3,2,1,0:T(8,128)(2,1)}, u32[]{:S(2)}, u32[]{:S(2)}) collective-permute-start(bf16[2,4,64,1024]{3,2,1,0:T(8,128)(2,1)} %pad_maximum_fusion.10), channel_id=1, source_target_pairs={{0,8},{4,12},{8,0},{12,4},{16,24},{20,28},{24,16},{28,20},{1,9},{5... | collective-permute-start | bytes 3145736 | tf_op jit(solution)/shard_map/ppermute | solution.py:89
  153.5 367.2 %all-gather.11.cloned.1.call-start = ((), (), s32[]{:S(2)}) async-start(), calls=%async_computation.6 | async-start | bytes 5242880 | tf_op jit(solution)/shard_map/all_gather | solution.py:56
  154.9 24.5 %collective-permute-start.1 = (bf16[2,4,64,1024]{3,2,1,0:T(8,128)(2,1)S(1)}, bf16[2,4,64,1024]{3,2,1,0:T(8,128)(2,1)S(1)}, u32[]{:S(2)}, u32[]{:S(2)}) collective-permute-start(bf16[2,4,64,1024]{3,2,1,0:T(8,128)(2,1)S(1)} %pad_maximum_fusion.9), channel_id=1, source_target_pairs={{0,16},{4,20},{8,24},{12,28},{16,0},{20,4},{24,8},{28,12},{1,17},{... | collective-permute-start | bytes 3145736 | tf_op jit(solution)/shard_map/ppermute | solution.py:89
  179.4 7.1 collective-permute-start.5
  183.0 7.3 collective-permute-start.2
  341.7 28.1 %collective-permute-start.12 = (bf16[256,2048]{1,0:T(8,128)(2,1)}, bf16[256,2048]{1,0:T(8,128)(2,1)}, u32[]{:S(2)}, u32[]{:S(2)}) collective-permute-start(bf16[256,2048]{1,0:T(8,128)(2,1)} %get-tuple-element.58), channel_id=1, source_target_pairs={{0,1},{1,2},{2,3},{3,0},{4,5},{5,6},{6,7},{7,4},{8,9},{9,10},{10,1... | collective-permute-start | bytes 3145736 | tf_op jit(solution)/shard_map/ppermute | solution.py:73
  341.7 48.2 %collective-permute-start.14 = (bf16[256,2048]{1,0:T(8,128)(2,1)}, bf16[256,2048]{1,0:T(8,128)(2,1)}, u32[]{:S(2)}, u32[]{:S(2)}) collective-permute-start(bf16[256,2048]{1,0:T(8,128)(2,1)} %get-tuple-element.59), channel_id=1, source_target_pairs={{0,3},{1,0},{2,1},{3,2},{4,7},{5,4},{6,5},{7,6},{8,11},{9,8},{10,9... | collective-permute-start | bytes 3145736 | tf_op jit(solution)/shard_map/ppermute | solution.py:73
  345.5 89.3 %collective-permute-start.13 = (bf16[256,2048]{1,0:T(8,128)(2,1)}, bf16[256,2048]{1,0:T(8,128)(2,1)}, u32[]{:S(2)}, u32[]{:S(2)}) collective-permute-start(bf16[256,2048]{1,0:T(8,128)(2,1)} %get-tuple-element.60), channel_id=1, source_target_pairs={{0,2},{1,3},{2,0},{3,1},{4,6},{5,7},{6,4},{7,5},{8,10},{9,11},{10,... | collective-permute-start | bytes 3145736 | tf_op jit(solution)/shard_map/ppermute | solution.py:73
  441.1 178.4 %reduce-scatter.7.cloned.1.call-start = ((), (), s32[]{:S(2)}) async-start(), calls=%async_computation.7 | async-start | bytes 5898240 | tf_op jit(solution)/shard_map/reduce_scatter | solution.py:60
  564.6 130.2 %reduce-scatter.11.cloned.1.call-start = ((), (), s32[]{:S(2)}) async-start(), calls=%async_computation.10 | async-start | bytes 9437184 | tf_op jit(solution)/shard_map/reduce_scatter | solution.py:60
  579.1 236.0 %reduce-scatter.9.cloned.1.call-start = ((), (), s32[]{:S(2)}) async-start(), calls=%async_computation.9 | async-start | bytes 18874368 | tf_op jit(solution)/shard_map/reduce_scatter | solution.py:60
  608.1 424.2 %all-gather.13.cloned.1.call-start = ((), (), s32[]{:S(2)}) async-start(), calls=%async_computation.8 | async-start | bytes 5898240 | tf_op jit(solution)/shard_map/all_gather | solution.py:56
  619.6 423.6 %all-gather.15.cloned.1.call-start = ((), (), s32[]{:S(2)}) async-start(), calls=%async_computation.11 | async-start | bytes 28311552 | tf_op jit(solution)/shard_map/all_gather | solution.py:56
  839.0 16.7 %collective-permute-start.6 = (bf16[256,1024]{1,0:T(8,128)(2,1)S(1)}, bf16[256,1024]{1,0:T(8,128)(2,1)}, u32[]{:S(2)}, u32[]{:S(2)}) collective-permute-start(bf16[256,1024]{1,0:T(8,128)(2,1)S(1)} %get-tuple-element.65), channel_id=1, source_target_pairs={{0,1},{1,2},{2,3},{3,0},{4,5},{5,6},{6,7},{7,4},{8,9},{9,10},{10,1... | collective-permute-start | bytes 1572872 | tf_op jit(solution)/shard_map/ppermute | solution.py:73
  840.3 28.7 %collective-permute-start.8 = (bf16[256,1024]{1,0:T(8,128)(2,1)S(1)}, bf16[256,1024]{1,0:T(8,128)(2,1)}, u32[]{:S(2)}, u32[]{:S(2)}) collective-permute-start(bf16[256,1024]{1,0:T(8,128)(2,1)S(1)} %get-tuple-element.66), channel_id=1, source_target_pairs={{0,3},{1,0},{2,1},{3,2},{4,7},{5,4},{6,5},{7,6},{8,11},{9,8},{10,9... | collective-permute-start | bytes 1572872 | tf_op jit(solution)/shard_map/ppermute | solution.py:73
  842.8 78.9 %collective-permute-start.7 = (bf16[256,1024]{1,0:T(8,128)(2,1)}, bf16[256,1024]{1,0:T(8,128)(2,1)}, u32[]{:S(2)}, u32[]{:S(2)}) collective-permute-start(bf16[256,1024]{1,0:T(8,128)(2,1)} %get-tuple-element.67), channel_id=1, source_target_pairs={{0,2},{1,3},{2,0},{3,1},{4,6},{5,7},{6,4},{7,5},{8,10},{9,11},{10,... | collective-permute-start | bytes 1572872 | tf_op jit(solution)/shard_map/ppermute | solution.py:73
  844.4 95.4 %collective-permute-start.9 = (bf16[256,1024]{1,0:T(8,128)(2,1)}, bf16[256,1024]{1,0:T(8,128)(2,1)}, u32[]{:S(2)}, u32[]{:S(2)}) collective-permute-start(bf16[256,1024]{1,0:T(8,128)(2,1)} %get-tuple-element.68), channel_id=1, source_target_pairs={{0,1},{1,2},{2,3},{3,0},{4,5},{5,6},{6,7},{7,4},{8,9},{9,10},{10,1... | collective-permute-start | bytes 1572872 | tf_op jit(solution)/shard_map/ppermute | solution.py:73
  852.1 176.0 %collective-permute-start.15 = (bf16[256,2048]{1,0:T(8,128)(2,1)S(1)}, bf16[256,2048]{1,0:T(8,128)(2,1)S(1)}, u32[]{:S(2)}, u32[]{:S(2)}) collective-permute-start(bf16[256,2048]{1,0:T(8,128)(2,1)S(1)} %get-tuple-element.55), channel_id=1, source_target_pairs={{0,1},{1,2},{2,3},{3,0},{4,5},{5,6},{6,7},{7,4},{8,9},{9,10},{10,1... | collective-permute-start | bytes 3145736 | tf_op jit(solution)/shard_map/ppermute | solution.py:73
  855.7 172.4 %collective-permute-start.17 = (bf16[256,2048]{1,0:T(8,128)(2,1)S(1)}, bf16[256,2048]{1,0:T(8,128)(2,1)S(1)}, u32[]{:S(2)}, u32[]{:S(2)}) collective-permute-start(bf16[256,2048]{1,0:T(8,128)(2,1)S(1)} %get-tuple-element.56), channel_id=1, source_target_pairs={{0,3},{1,0},{2,1},{3,2},{4,7},{5,4},{6,5},{7,6},{8,11},{9,8},{10,9... | collective-permute-start | bytes 3145736 | tf_op jit(solution)/shard_map/ppermute | solution.py:73
  869.0 159.1 %collective-permute-start.16 = (bf16[256,2048]{1,0:T(8,128)(2,1)S(1)}, bf16[256,2048]{1,0:T(8,128)(2,1)S(1)}, u32[]{:S(2)}, u32[]{:S(2)}) collective-permute-start(bf16[256,2048]{1,0:T(8,128)(2,1)S(1)} %get-tuple-element.57), channel_id=1, source_target_pairs={{0,2},{1,3},{2,0},{3,1},{4,6},{5,7},{6,4},{7,5},{8,10},{9,11},{10,... | collective-permute-start | bytes 3145736 | tf_op jit(solution)/shard_map/ppermute | solution.py:73
  939.9 12.9 %collective-permute-start.26 = (f32[2048]{0:T(1024)S(1)}, f32[2048]{0:T(1024)S(1)}, u32[]{:S(2)}, u32[]{:S(2)}) collective-permute-start(f32[2048]{0:T(1024)S(1)} %add.225), channel_id=1, source_target_pairs={{0,1},{1,0},{2,3},{3,2},{4,5},{5,4},{6,7},{7,6},{8,9},{9,8},{10,11... | collective-permute-start | bytes 24584 | tf_op jit(solution)/shard_map/ppermute | solution.py:101
  939.9 15.5 %collective-permute-start.21 = (f32[2048]{0:T(1024)S(1)}, f32[2048]{0:T(1024)S(1)}, u32[]{:S(2)}, u32[]{:S(2)}) collective-permute-start(f32[2048]{0:T(1024)S(1)} %add.220), channel_id=1, source_target_pairs={{0,1},{1,0},{2,3},{3,2},{4,5},{5,4},{6,7},{7,6},{8,9},{9,8},{10,11... | collective-permute-start | bytes 24584 | tf_op jit(solution)/shard_map/ppermute | solution.py:101
  952.8 14.9 %collective-permute-start.11 = (bf16[256,1024]{1,0:T(8,128)(2,1)S(1)}, bf16[256,1024]{1,0:T(8,128)(2,1)S(1)}, u32[]{:S(2)}, u32[]{:S(2)}) collective-permute-start(bf16[256,1024]{1,0:T(8,128)(2,1)S(1)} %copy-done.19), channel_id=1, source_target_pairs={{0,3},{1,0},{2,1},{3,2},{4,7},{5,4},{6,5},{7,6},{8,11},{9,8},{10,9... | collective-permute-start | bytes 1572872 | tf_op jit(solution)/shard_map/ppermute | solution.py:73
  955.4 67.5 %collective-permute-start.10 = (bf16[256,1024]{1,0:T(8,128)(2,1)S(1)}, bf16[256,1024]{1,0:T(8,128)(2,1)S(1)}, u32[]{:S(2)}, u32[]{:S(2)}) collective-permute-start(bf16[256,1024]{1,0:T(8,128)(2,1)S(1)} %copy-done.18), channel_id=1, source_target_pairs={{0,2},{1,3},{2,0},{3,1},{4,6},{5,7},{6,4},{7,5},{8,10},{9,11},{10,... | collective-permute-start | bytes 1572872 | tf_op jit(solution)/shard_map/ppermute | solution.py:73
  967.7 56.6 %collective-permute-start.27 = (f32[2048]{0:T(1024)S(1)}, f32[2048]{0:T(1024)S(1)}, u32[]{:S(2)}, u32[]{:S(2)}) collective-permute-start(f32[2048]{0:T(1024)S(1)} %add.226), channel_id=1, source_target_pairs={{0,2},{1,3},{2,0},{3,1},{4,6},{5,7},{6,4},{7,5},{8,10},{9,11},{10,... | collective-permute-start | bytes 24584 | tf_op jit(solution)/shard_map/ppermute | solution.py:101
  1022.9 4.5 collective-permute-start.22
  (34 other events, 726.2 us)
Sparse Core Ops, SparseCore 0:
  12.2 100.7 all-gather.16
  135.2 79.0 all-gather.18
  215.9 79.2 all-gather.8
  441.2 79.4 all-gather.10
Sparse Core Ops, SparseCore 1:
  16.1 36.2 reduce-scatter.4
  564.7 54.8 reduce-scatter.6
  623.4 71.3 reduce-scatter.10
  699.0 116.0 reduce-scatter.8
  817.0 40.8 all-gather.12
  860.4 125.7 all-gather.14

commit v4 on v3

--- a/solution.py
+++ b/solution.py
@@ -511,6 +511,76 @@
     )(normed, w_gate, w_up)
 
 
+def place_blocks(halves, axis):
+    (first, first_offsets), (second, second_offsets) = halves
+    parts, rows, half = first.shape
+
+    def kernel(at_ref, first_ref, second_ref, out_ref):
+        out_ref[:, :half] = first_ref[0].astype(jnp.float32)
+        out_ref[:, half:] = second_ref[0].astype(jnp.float32)
+
+    def entry(offsets):
+        where = [offsets.index(k) for k in range(parts)]
+
+        def index(k, at_ref):
+            found = where[0]
+            for candidate in range(1, parts):
+                found = jnp.where(k == candidate, where[candidate], found)
+            return (found, 0, 0)
+
+        return pl.BlockSpec((1, rows, half), index)
+
+    return pl.pallas_call(
+        kernel,
+        grid_spec=pltpu.PrefetchScalarGridSpec(
+            num_scalar_prefetch=1,
+            grid=(parts,),
+            in_specs=[entry(first_offsets), entry(second_offsets)],
+            out_specs=pl.BlockSpec((rows, 2 * half), lambda k, at_ref: (at_ref[0] ^ k, 0)),
+        ),
+        out_shape=jax.ShapeDtypeStruct((parts * rows, 2 * half), jnp.float32),
+        cost_estimate=pl.CostEstimate(
+            flops=0, transcendentals=0, bytes_accessed=12 * parts * rows * half
+        ),
+        name="place_blocks",
+    )(lax.axis_index(axis).reshape(1), first, second)
+
+
+def unpack_attention(shared, q_columns, k_columns, folds):
+    rows, columns = shared.shape
+    block = rows // folds
+    ends = (q_columns, q_columns + k_columns, q_columns + 2 * k_columns)
+
+    def kernel(shared_ref, query_ref, key_ref, value_ref, output_ref):
+        query_ref[...] = shared_ref[:, : ends[0]].astype(jnp.float32)
+        key_ref[...] = shared_ref[:, ends[0] : ends[1]].astype(jnp.float32)
+        value_ref[...] = shared_ref[:, ends[1] : ends[2]].astype(jnp.float32)
+        output_ref[...] = shared_ref[:, ends[2] :].astype(jnp.float32)
+
+    narrow = pl.BlockSpec((block, k_columns), lambda p: (p, 0))
+    return pl.pallas_call(
+        kernel,
+        grid=(folds,),
+        in_specs=[pl.BlockSpec((block, columns), lambda p: (p, 0))],
+        out_specs=[
+            pl.BlockSpec((block, q_columns), lambda p: (p, 0)),
+            narrow,
+            narrow,
+            pl.BlockSpec((block, columns - ends[2]), lambda p: (0, p)),
+        ],
+        out_shape=[
+            jax.ShapeDtypeStruct((rows, q_columns), jnp.float32),
+            jax.ShapeDtypeStruct((rows, k_columns), jnp.float32),
+            jax.ShapeDtypeStruct((rows, k_columns), jnp.float32),
+            jax.ShapeDtypeStruct((block, (columns - ends[2]) * folds), jnp.float32),
+        ],
+        cost_estimate=pl.CostEstimate(
+            flops=0, transcendentals=0, bytes_accessed=6 * rows * columns
+        ),
+        name="unpack_attention",
+    )(shared)
+
+
 def row_major(array):
     return with_layout_constraint(array, Layout(major_to_minor=tuple(range(array.ndim))))
 
@@ -547,11 +617,10 @@
     nothing = scatter_sum(tokens[:, :128] * 0, "dp")[0, 0]
     own_rows, width = tokens.shape
     depth = w_output.shape[0] // n_dp
+    gathered = lax.all_gather(tokens, "tensor", axis=0)
     own_part = lax.dynamic_slice_in_dim(w_output, lax.axis_index("dp") * depth, depth, 0)
-    gathered = lax.all_gather(
-        jnp.concatenate([tokens, own_part], axis=0), "tensor", axis=0
-    )
-    all_output = cube_gather(gathered[:, own_rows:], "dp")
+    output_part = lax.all_gather(own_part, "tensor", axis=0)
+    all_output = cube_gather(output_part, "dp")
     q_columns, k_columns = w_query.shape[1], w_key.shape[1]
     q_heads, kv_heads = q_columns // HD, k_columns // HD
     gain_one = norm1_gain.astype(jnp.float32)
@@ -601,7 +670,7 @@
     d_normed1 = exchange_sum(dn1_part, "tensor")
     gain_one_sum = cube_sum(
         gain_gradient(
-            gathered[:, :own_rows].reshape(-1, width).astype(jnp.float32),
+            gathered.reshape(-1, width).astype(jnp.float32),
             dn1_part.astype(jnp.float32),
         ), ("dp", "tensor")
     )
@@ -617,19 +686,16 @@
         jnp.concatenate([grad_qkv, split_columns(grad_output, folds)], axis=1)
     )
     part_attn = scatter_sum(low_attn, "dp")
-    shared_ff = row_major(
-        gather_rows(row_major(jnp.concatenate([part_gate_up, part_down], axis=1)), "dp")
-    )
+    down_halves = cube_gather(part_down, "dp")
+    full_down = join_columns(place_blocks(down_halves, "dp"), ff_folds)
+    shared_ff = row_major(gather_rows(part_gate_up, "dp"))
     shared_attn = row_major(gather_rows(part_attn, "dp"))
     input_grad = (d_state + norm_backward(own_tokens, gain_one, d_normed1)).astype(low)
     full_gate = shared_ff[:, :ff_columns].astype(jnp.float32)
-    full_up = shared_ff[:, ff_columns : 2 * ff_columns].astype(jnp.float32)
-    full_down = join_columns(shared_ff[:, 2 * ff_columns :], ff_folds).astype(jnp.float32)
-    ends = (q_columns, q_columns + k_columns, q_columns + 2 * k_columns)
-    full_query = shared_attn[:, : ends[0]].astype(jnp.float32)
-    full_key = shared_attn[:, ends[0] : ends[1]].astype(jnp.float32)
-    full_value = shared_attn[:, ends[1] : ends[2]].astype(jnp.float32)
-    full_output = join_columns(shared_attn[:, ends[2] :], folds).astype(jnp.float32)
+    full_up = shared_ff[:, ff_columns:].astype(jnp.float32)
+    full_query, full_key, full_value, full_output = unpack_attention(
+        shared_attn, q_columns, k_columns, folds
+    )
     return (
         output,
         input_grad,

time: 1080 us -> 1090 us (level)
  waiting for transfers between devices: 644 us -> 676 us
  other arithmetic: 92.3 us -> 73 us
  Pallas kernels: 127 us -> 144 us
  starting transfers between devices: 97.8 us -> 83.7 us
    ppermute x10, waiting for transfers between devices: 25.3 us -> 89.8 us  [cube_sum(): lax.ppermute(vector, axis, [(i, i ^ bit) for i in range(n)])]
    ppermute x10, starting transfers between devices: 51.6 us -> 5.06 us  [cube_sum(): lax.ppermute(vector, axis, [(i, i ^ bit) for i in range(n)])]
    ppermute x12, starting transfers between devices: 38.2 us -> 66.5 us  [exchange_sum(): lax.ppermute(block((me + hop) % n), axis, [(i, (i + hop) % n) for i in ra...]
    ppermute x12, waiting for transfers between devices: 153 us -> 134 us  [exchange_sum(): lax.ppermute(block((me + hop) % n), axis, [(i, (i + hop) % n) for i in ra...]
    pallas_call x0 -> x2, Pallas kernels: none -> 17.1 us  [the longest x1 10.2 us: place_blocks(): pl.pallas_call(kernel, grid_spec=pltpu.PrefetchScalarGridSpec(num_scalar_...]
    reduce_scatter x4, waiting for transfers between devices: 207 us -> 190 us  [scatter_sum(): return lax.psum_scatter(partial, axis, scatter_dimension=0, tiled=True)]
    convert_element_type x3 -> x1, other arithmetic: 30.6 us -> 17.2 us  [block(): full_up = shared_ff[:, ff_columns:].astype(jnp.float32)]
    all_gather x1 -> x2, waiting for transfers between devices: 88.7 us -> 76.2 us  [the longest x1 69.7 us: block(): gathered = lax.all_gather(tokens, 'tensor', axis=0)]
  transfers between devices with their start and end apart: 38 -> 45, of which waited for: 24 -> 22; matrix products, arithmetic and copies ran while one was open for 12% -> 11% of each run, Pallas kernels for 6% -> 7%
where the time goes in v4:
time: 1090 us
  waiting for transfers between devices  676 us (62%)
  Pallas kernels  144 us (13%)
  starting transfers between devices  83.7 us (8%)
  other arithmetic  73 us (7%)
  matrix products  65.2 us (6%)
  local copies, waits for them, and re-layouts  26.5 us (2%)
  between operations  16.8 us (2%)
    reduce_scatter x4, waiting for transfers between devices, scatter_sum(): return lax.psum_scatter(partial, axis, scatter_dimension=0, tiled=True)  190 us
    ppermute x12, waiting for transfers between devices, exchange_sum(): lax.ppermute(block((me + hop) % n), axis, [(i, (i + hop) % n) for i in ra...  134 us
    all_gather x4, waiting for transfers between devices, gather_rows(): return lax.all_gather(block, axis, axis=0, tiled=True)  120 us
    ppermute x10, waiting for transfers between devices, cube_sum(): lax.ppermute(vector, axis, [(i, i ^ bit) for i in range(n)])  89.8 us
    all_gather x1, waiting for transfers between devices, block(): gathered = lax.all_gather(tokens, 'tensor', axis=0)  69.7 us
    ppermute x12, starting transfers between devices, exchange_sum(): lax.ppermute(block((me + hop) % n), axis, [(i, (i + hop) % n) for i in ra...  66.5 us
    ppermute x12, waiting for transfers between devices, cube_gather(): moved = lax.ppermute(held, axis, [(i, i ^ bit) for i in range(n)])  40.7 us
    dot_general x4, matrix products, contract_rows(): lax.dot_general(left_side, right_side, (((0,), (0,)), ((), ())), preferre...  40.2 us
  transfers between devices with their start and end apart: 45, of which 22 were waited for; matrix products, arithmetic and copies ran while one was open for 11% of the time, Pallas kernels for 7%

profile of v4, /device:TPU:0, one launch (start us, length us, event | category | flops | bytes accessed | tf_op | source)
XLA Modules:
  0.0 1085.0 jit_solution(11979866102415388742)
XLA Ops:
  24.2 69.7 %all-gather.19.cloned.1.call-done = bf16[1024,2048]{1,0:T(8,128)(2,1)} async-done(((bf16[256,2048]{1,0:T(8,128)(2,1)}), bf16[1024,2048]{1,0:T(8,128)(2,1)}) %all-gather.19.cloned.1.call-update) | async-done | bytes 4194320 | tf_op jit(solution)/shard_map/all_gather | solution.py:620
  93.9 8.3 norm_project.1
  102.2 13.8 %attend.1 = (bf16[1024,512]{1,0:T(8,128)(2,1)}, bf16[512,1024]{1,0:T(8,128)(2,1)}, f32[2,4,1024]{2,1,0:T(4,128)}) custom-call(bf16[768,1024]{1,0:T(8,128)(2,1)} %get-tuple-element.30.query_ref.key_ref.value_ref, bf16[768,1024]{1,0:T(8,128)(2,1)} %get-tuple-element.30.query_ref.key_ref.value_ref, bf16[768,1024]{1,0:T(8,128)(2,1)} %get-tuple-element.30.query_ref.key_ref.value_ref), custom_call_target="tpu_custom_call" | custom-call | flops 1073741824 | bytes 4194304 | tf_op jit(solution)/shard_map/attend/pallas_call | solution.py:213
  126.9 10.3 collective-permute-done
  143.7 19.5 %collective-permute-done.1 = bf16[2,4,64,1024]{3,2,1,0:T(8,128)(2,1)} collective-permute-done((bf16[2,4,64,1024]{3,2,1,0:T(8,128)(2,1)}, bf16[2,4,64,1024]{3,2,1,0:T(8,128)(2,1)}, u32[]{:S(2)}, u32[]{:S(2)}) %collective-permute-start.1) | collective-permute-done | bytes 1048608 | tf_op jit(solution)/shard_map/ppermute | solution.py:89
  180.4 24.4 %all-gather.21.cloned.1.call-done = bf16[4096,512]{1,0:T(8,128)(2,1)} async-done(((bf16[1024,512]{1,0:T(8,128)(2,1)}), bf16[4096,512]{1,0:T(8,128)(2,1)}) %all-gather.21.cloned.1.call-update) | async-done | bytes 4194320 | tf_op jit(solution)/shard_map/all_gather | solution.py:636
  204.8 17.6 %project_and_norm.1 = (f32[256,2048]{1,0:T(8,128)}, bf16[1024,2048]{1,0:T(8,128)(2,1)}) custom-call(s32[2]{0:T(128)} %pad_add_fusion.at_ref, bf16[4,1024,512]{2,1,0:T(8,128)(2,1)} %bitcast.67, bf16[8,4,64,1024]{3,2,1,0:T(8,128)(2,1)} %pad_maximum_fusion.2.first_ref, bf16[8,4,64,1024]{3,2,1,0:T(8,128)(2,1)} %pad_maximum_fusion.3.second_ref, ...), custom_call_target="tpu_custom_call" | custom-call | flops 8589934592 | bytes 20971520 | tf_op jit(solution)/shard_map/project_and_norm/pallas_call | solution.py:388
  222.4 23.7 %gated_up.1 = (f32[1024,2048]{1,0:T(8,128)}, f32[1024,2048]{1,0:T(8,128)}, bf16[1024,2048]{1,0:T(8,128)(2,1)}) custom-call(bf16[1024,2048]{1,0:T(8,128)(2,1)} %get-tuple-element.33.normed_ref, bf16[2048,2048]{1,0:T(8,128)(2,1)} %first_w_ref.1, bf16[2048,2048]{1,0:T(8,128)(2,1)} %second_w_ref.1), custom_call_target="tpu_custom_call" | custom-call | flops 17179869184 | bytes 41943040 | tf_op jit(solution)/shard_map/gated_up/pallas_call | solution.py:495
  246.2 39.3 %all-gather.11.cloned.1.call-done.cot_ref = bf16[1024,2048]{1,0:T(8,128)(2,1)} async-done(((bf16[256,2048]{1,0:T(8,128)(2,1)}), bf16[1024,2048]{1,0:T(8,128)(2,1)}) %all-gather.11.cloned.1.call-update) | async-done | bytes 4194320 | tf_op jit(solution)/shard_map/all_gather | solution.py:56
  285.5 18.9 %gated_back.1 = (bf16[1024,2048]{1,0:T(8,128)(2,1)}, bf16[1024,2048]{1,0:T(8,128)(2,1)}) custom-call(bf16[1024,2048]{1,0:T(8,128)(2,1)} %all-gather.11.cloned.1.call-done.cot_ref, bf16[2048,2048]{1,0:T(8,128)(2,1)} %weight_ref.1, f32[1024,2048]{1,0:T(8,128)} %get-tuple-element.35.gate_ref, f32[1024,2048]{1,0:T(8,128)} %get-tuple-element.36.up_ref), custom_call_target="tpu_custom_call" | custom-call | flops 8589934592 | bytes 37748736 | tf_op jit(solution)/shard_map/gated_back/pallas_call | solution.py:435
  304.4 24.0 %pair_product.1 = bf16[1024,2048]{1,0:T(8,128)(2,1)} custom-call(bf16[1024,2048]{1,0:T(8,128)(2,1)} %get-tuple-element.37.first_ref, bf16[1024,2048]{1,0:T(8,128)(2,1)} %get-tuple-element.38.second_ref, bf16[2048,2048]{1,0:T(8,128)(2,1)} %first_w_ref.1, bf16[2048,2048]{1,0:T(8,128)(2,1)} %second_w_ref.1), custom_call_target="tpu_custom_call" | custom-call | flops 17179869184 | bytes 29360128 | tf_op jit(solution)/shard_map/pair_product/pallas_call | solution.py:468
  337.0 21.1 %collective-permute-done.14 = bf16[256,2048]{1,0:T(8,128)(2,1)} collective-permute-done((bf16[256,2048]{1,0:T(8,128)(2,1)}, bf16[256,2048]{1,0:T(8,128)(2,1)}, u32[]{:S(2)}, u32[]{:S(2)}) %collective-permute-start.14) | collective-permute-done | bytes 1048608 | tf_op jit(solution)/shard_map/ppermute | solution.py:73
  358.1 65.6 %collective-permute-done.13 = bf16[256,2048]{1,0:T(8,128)(2,1)} collective-permute-done((bf16[256,2048]{1,0:T(8,128)(2,1)}, bf16[256,2048]{1,0:T(8,128)(2,1)}, u32[]{:S(2)}, u32[]{:S(2)}) %collective-permute-start.13) | collective-permute-done | bytes 1048608 | tf_op jit(solution)/shard_map/ppermute | solution.py:73
  430.2 81.1 %all-gather.13.cloned.1.call-done = bf16[1024,2048]{1,0:T(8,128)(2,1)} async-done(((bf16[256,2048]{1,0:T(8,128)(2,1)}), bf16[1024,2048]{1,0:T(8,128)(2,1)}) %all-gather.13.cloned.1.call-update) | async-done | bytes 4194320 | tf_op jit(solution)/shard_map/all_gather | solution.py:56
  516.9 20.4 %attend_back.1 = (bf16[512,1024]{1,0:T(8,128)(2,1)}, bf16[128,1024]{1,0:T(8,128)(2,1)}, bf16[128,1024]{1,0:T(8,128)(2,1)}) custom-call(bf16[768,1024]{1,0:T(8,128)(2,1)} %get-tuple-element.30.query_ref.key_ref.value_ref, bf16[768,1024]{1,0:T(8,128)(2,1)} %get-tuple-element.30.query_ref.key_ref.value_ref, ...), custom_call_target="tpu_custom_call" | custom-call | flops 2684354560 | bytes 6291456 | tf_op jit(solution)/shard_map/attend_back/pallas_call | solution.py:305
  553.0 12.2 %convolution_convert_fusion.1 = bf16[2048,2048]{1,0:T(8,128)(2,1)S(1)} fusion(bf16[1024,2048]{1,0:T(8,128)(2,1)} %get-tuple-element.33.normed_ref, bf16[1024,2048]{1,0:T(8,128)(2,1)} %get-tuple-element.38.second_ref), kind=kOutput, calls=%fused_computation.8 | convolution fusion | flops 8594128896 | bytes 16777216 | tf_op jit(solution)/shard_map/dot_general | solution.py:44
  565.2 9.8 convolution_convert_fusion.2
  575.0 6.9 pad_maximum_fusion
  581.9 14.0 %convolution_convert_fusion = bf16[2048,2048]{1,0:T(8,128)(2,1)} fusion(bf16[1024,2048]{1,0:T(8,128)(2,1)} %get-tuple-element.34, bf16[1024,2048]{1,0:T(8,128)(2,1)} %all-gather.11.cloned.1.call-done.cot_ref), kind=kOutput, calls=%fused_computation.7 | convolution fusion | flops 8594128896 | bytes 16777216 | tf_op jit(solution)/shard_map/dot_general | solution.py:44
  596.0 11.4 %reduce-scatter.7.cloned.1.call-done = bf16[256,1280]{1,0:T(8,128)(2,1)} async-done(((bf16[2048,1280]{1,0:T(8,128)(2,1)}), bf16[256,1280]{1,0:T(8,128)(2,1)}) %reduce-scatter.7.cloned.1.call-update) | async-done | bytes 655376 | tf_op jit(solution)/shard_map/reduce_scatter | solution.py:60
  607.7 119.8 %reduce-scatter.9.cloned.1.call-done = bf16[256,4096]{1,0:T(8,128)(2,1)} async-done(((bf16[2048,4096]{1,0:T(8,128)(2,1)}), bf16[256,4096]{1,0:T(8,128)(2,1)}) %reduce-scatter.9.cloned.1.call-update) | async-done | bytes 2097168 | tf_op jit(solution)/shard_map/reduce_scatter | solution.py:60
  731.0 11.2 %convolution_convert_fusion.3 = bf16[1024,2048]{1,0:T(8,128)(2,1)S(1)} fusion(bf16[1024,2048]{1,0:T(8,128)(2,1)S(1)} %copy-done.32, bf16[2048,2048]{1,0:T(8,128)(2,1)} %weight_ref.1), kind=kOutput, calls=%fused_computation.15 | convolution fusion | flops 8592031744 | bytes 16777216 | tf_op jit(solution)/shard_map/dot_general | solution.py:642
  744.0 58.9 %reduce-scatter.11.cloned.1.call-done = bf16[256,2048]{1,0:T(8,128)(2,1)} async-done(((bf16[2048,2048]{1,0:T(8,128)(2,1)}), bf16[256,2048]{1,0:T(8,128)(2,1)}) %reduce-scatter.11.cloned.1.call-update) | async-done | bytes 1048592 | tf_op jit(solution)/shard_map/reduce_scatter | solution.py:60
  811.3 10.9 %collective-permute-done.28 = bf16[1,256,1024]{2,1,0:T(8,128)(2,1)S(1)} collective-permute-done((bf16[1,256,1024]{2,1,0:T(8,128)(2,1)S(1)}, bf16[1,256,1024]{2,1,0:T(8,128)(2,1)S(1)}, u32[]{:S(2)}, u32[]{:S(2)}) %collective-permute-start.28) | collective-permute-done | bytes 524320 | tf_op jit(solution)/shard_map/ppermute | solution.py:89
  826.9 40.5 %collective-permute-done.10 = bf16[256,1024]{1,0:T(8,128)(2,1)} collective-permute-done((bf16[256,1024]{1,0:T(8,128)(2,1)S(1)}, bf16[256,1024]{1,0:T(8,128)(2,1)}, u32[]{:S(2)}, u32[]{:S(2)}) %collective-permute-start.10) | collective-permute-done | bytes 524320 | tf_op jit(solution)/shard_map/ppermute | solution.py:73
  876.4 25.1 %collective-permute-done.24 = f32[2048]{0:T(1024)S(1)} collective-permute-done((f32[2048]{0:T(1024)S(1)}, f32[2048]{0:T(1024)S(1)}, u32[]{:S(2)}, u32[]{:S(2)}) %collective-permute-start.24) | collective-permute-done | bytes 8224 | tf_op jit(solution)/shard_map/ppermute | solution.py:101
  913.2 15.7 %collective-permute-start.6 = (bf16[256,1024]{1,0:T(8,128)(2,1)S(1)}, bf16[256,1024]{1,0:T(8,128)(2,1)S(1)}, u32[]{:S(2)}, u32[]{:S(2)}) collective-permute-start(bf16[256,1024]{1,0:T(8,128)(2,1)S(1)} %get-tuple-element.66), channel_id=1, source_target_pairs={{0,1},{1,2},{2,3},{3,0},{4,5},{5,6},{6,7},{7,4},{8,9},{9,10},{10,1... | collective-permute-start | bytes 1572872 | tf_op jit(solution)/shard_map/ppermute | solution.py:73
  940.8 33.6 %collective-permute-start.16 = (bf16[256,2048]{1,0:T(8,128)(2,1)S(1)}, bf16[256,2048]{1,0:T(8,128)(2,1)S(1)}, u32[]{:S(2)}, u32[]{:S(2)}) collective-permute-start(bf16[256,2048]{1,0:T(8,128)(2,1)S(1)} %get-tuple-element.58), channel_id=1, source_target_pairs={{0,2},{1,3},{2,0},{3,1},{4,6},{5,7},{6,4},{7,5},{8,10},{9,11},{10,... | collective-permute-start | bytes 3145736 | tf_op jit(solution)/shard_map/ppermute | solution.py:73
  977.1 48.9 %collective-permute-done.27 = f32[2048]{0:T(1024)S(1)} collective-permute-done((f32[2048]{0:T(1024)S(1)}, f32[2048]{0:T(1024)S(1)}, u32[]{:S(2)}, u32[]{:S(2)}) %collective-permute-start.27) | collective-permute-done | bytes 8224 | tf_op jit(solution)/shard_map/ppermute | solution.py:101
  1043.3 10.2 place_blocks.1
  1053.6 6.9 unpack_attention.1
  1060.5 17.2 %slice_convert_fusion = (f32[2048,2048]{1,0:T(8,128)}, f32[2048,2048]{1,0:T(8,128)}) fusion(bf16[2048,4096]{1,0:T(8,128)(2,1)} %all-gather.17.cloned.1.call-done), kind=kLoop, calls=%fused_computation.1 | loop fusion | flops 8388608 | bytes 50331648 | tf_op jit(solution)/shard_map/convert_element_type | solution.py:695
  (215 shorter events, 157.2 us)
Async XLA Ops:
  8.0 85.9 %all-gather.19.cloned.1.call-start = ((), (), s32[]{:S(2)}) async-start(), calls=%async_computation.12 | async-start | bytes 5242880 | tf_op jit(solution)/shard_map/all_gather | solution.py:620
  8.8 113.8 %all-gather.23.cloned.1.call-start = ((), (), s32[]{:S(2)}) async-start(), calls=%async_computation.14 | async-start | bytes 1310720 | tf_op jit(solution)/shard_map/all_gather | solution.py:622
  10.4 160.4 %reduce-scatter.5.cloned.1.call-start = ((), (), s32[]{:S(2)}) async-start(), calls=%async_computation.4 | async-start | bytes 73728 | tf_op jit(solution)/shard_map/reduce_scatter | solution.py:60
  11.9 192.9 %all-gather.21.cloned.1.call-start = ((), (), s32[]{:S(2)}) async-start(), calls=%async_computation.13 | async-start | bytes 5242880 | tf_op jit(solution)/shard_map/all_gather | solution.py:636
  116.0 169.5 %all-gather.11.cloned.1.call-start = ((), (), s32[]{:S(2)}) async-start(), calls=%async_computation.5 | async-start | bytes 5242880 | tf_op jit(solution)/shard_map/all_gather | solution.py:56
  139.3 23.9 %collective-permute-start.1 = (bf16[2,4,64,1024]{3,2,1,0:T(8,128)(2,1)}, bf16[2,4,64,1024]{3,2,1,0:T(8,128)(2,1)}, u32[]{:S(2)}, u32[]{:S(2)}) collective-permute-start(bf16[2,4,64,1024]{3,2,1,0:T(8,128)(2,1)} %pad_maximum_fusion.11), channel_id=1, source_target_pairs={{0,16},{4,20},{8,24},{12,28},{16,0},{20,4},{24,8},{28,12},{1,17},{... | collective-permute-start | bytes 3145736 | tf_op jit(solution)/shard_map/ppermute | solution.py:89
  140.8 370.5 %all-gather.13.cloned.1.call-start = ((), (), s32[]{:S(2)}) async-start(), calls=%async_computation.6 | async-start | bytes 5242880 | tf_op jit(solution)/shard_map/all_gather | solution.py:56
  142.2 23.9 %collective-permute-start.4 = (bf16[2,4,64,1024]{3,2,1,0:T(8,128)(2,1)S(1)}, bf16[2,4,64,1024]{3,2,1,0:T(8,128)(2,1)S(1)}, u32[]{:S(2)}, u32[]{:S(2)}) collective-permute-start(bf16[2,4,64,1024]{3,2,1,0:T(8,128)(2,1)S(1)} %pad_maximum_fusion.12), channel_id=1, source_target_pairs={{0,8},{4,12},{8,0},{12,4},{16,24},{20,28},{24,16},{28,20},{1,9},{5... | collective-permute-start | bytes 3145736 | tf_op jit(solution)/shard_map/ppermute | solution.py:89
  332.0 26.0 %collective-permute-start.14 = (bf16[256,2048]{1,0:T(8,128)(2,1)}, bf16[256,2048]{1,0:T(8,128)(2,1)}, u32[]{:S(2)}, u32[]{:S(2)}) collective-permute-start(bf16[256,2048]{1,0:T(8,128)(2,1)} %get-tuple-element.60), channel_id=1, source_target_pairs={{0,3},{1,0},{2,1},{3,2},{4,7},{5,4},{6,5},{7,6},{8,11},{9,8},{10,9... | collective-permute-start | bytes 3145736 | tf_op jit(solution)/shard_map/ppermute | solution.py:73
  332.6 91.0 %collective-permute-start.13 = (bf16[256,2048]{1,0:T(8,128)(2,1)}, bf16[256,2048]{1,0:T(8,128)(2,1)}, u32[]{:S(2)}, u32[]{:S(2)}) collective-permute-start(bf16[256,2048]{1,0:T(8,128)(2,1)} %get-tuple-element.61), channel_id=1, source_target_pairs={{0,2},{1,3},{2,0},{3,1},{4,6},{5,7},{6,4},{7,5},{8,10},{9,11},{10,... | collective-permute-start | bytes 3145736 | tf_op jit(solution)/shard_map/ppermute | solution.py:73
  333.0 90.7 %collective-permute-start.12 = (bf16[256,2048]{1,0:T(8,128)(2,1)}, bf16[256,2048]{1,0:T(8,128)(2,1)}, u32[]{:S(2)}, u32[]{:S(2)}) collective-permute-start(bf16[256,2048]{1,0:T(8,128)(2,1)} %get-tuple-element.59), channel_id=1, source_target_pairs={{0,1},{1,2},{2,3},{3,0},{4,5},{5,6},{6,7},{7,4},{8,9},{9,10},{10,1... | collective-permute-start | bytes 3145736 | tf_op jit(solution)/shard_map/ppermute | solution.py:73
  430.0 177.5 %reduce-scatter.7.cloned.1.call-start = ((), (), s32[]{:S(2)}) async-start(), calls=%async_computation.7 | async-start | bytes 5898240 | tf_op jit(solution)/shard_map/reduce_scatter | solution.py:60
  552.5 175.0 %reduce-scatter.9.cloned.1.call-start = ((), (), s32[]{:S(2)}) async-start(), calls=%async_computation.9 | async-start | bytes 18874368 | tf_op jit(solution)/shard_map/reduce_scatter | solution.py:60
  581.9 221.1 %reduce-scatter.11.cloned.1.call-start = ((), (), s32[]{:S(2)}) async-start(), calls=%async_computation.11 | async-start | bytes 9437184 | tf_op jit(solution)/shard_map/reduce_scatter | solution.py:60
  596.0 457.6 %all-gather.15.cloned.1.call-start = ((), (), s32[]{:S(2)}) async-start(), calls=%async_computation.8 | async-start | bytes 5898240 | tf_op jit(solution)/shard_map/all_gather | solution.py:56
  607.5 453.0 %all-gather.17.cloned.1.call-start = ((), (), s32[]{:S(2)}) async-start(), calls=%async_computation.10 | async-start | bytes 18874368 | tf_op jit(solution)/shard_map/all_gather | solution.py:56
  805.9 19.5 %collective-permute-start.31 = (bf16[1,256,1024]{2,1,0:T(8,128)(2,1)S(1)}, bf16[1,256,1024]{2,1,0:T(8,128)(2,1)S(1)}, u32[]{:S(2)}, u32[]{:S(2)}) collective-permute-start(bf16[1,256,1024]{2,1,0:T(8,128)(2,1)S(1)} %get-tuple-element.72), channel_id=1, source_target_pairs={{0,16},{4,20},{8,24},{12,28},{16,0},{20,4},{24,8},{28,12},{1,17},{... | collective-permute-start | bytes 1572872 | tf_op jit(solution)/shard_map/ppermute | solution.py:89
  806.6 20.2 %collective-permute-start.11 = (bf16[256,1024]{1,0:T(8,128)(2,1)S(1)}, bf16[256,1024]{1,0:T(8,128)(2,1)S(1)}, u32[]{:S(2)}, u32[]{:S(2)}) collective-permute-start(bf16[256,1024]{1,0:T(8,128)(2,1)S(1)} %get-tuple-element.70), channel_id=1, source_target_pairs={{0,3},{1,0},{2,1},{3,2},{4,7},{5,4},{6,5},{7,6},{8,11},{9,8},{10,9... | collective-permute-start | bytes 1572872 | tf_op jit(solution)/shard_map/ppermute | solution.py:73
  810.0 57.4 %collective-permute-start.10 = (bf16[256,1024]{1,0:T(8,128)(2,1)S(1)}, bf16[256,1024]{1,0:T(8,128)(2,1)}, u32[]{:S(2)}, u32[]{:S(2)}) collective-permute-start(bf16[256,1024]{1,0:T(8,128)(2,1)S(1)} %get-tuple-element.71), channel_id=1, source_target_pairs={{0,2},{1,3},{2,0},{3,1},{4,6},{5,7},{6,4},{7,5},{8,10},{9,11},{10,... | collective-permute-start | bytes 1572872 | tf_op jit(solution)/shard_map/ppermute | solution.py:73
  810.0 58.9 %collective-permute-start.9 = (bf16[256,1024]{1,0:T(8,128)(2,1)S(1)}, bf16[256,1024]{1,0:T(8,128)(2,1)S(1)}, u32[]{:S(2)}, u32[]{:S(2)}) collective-permute-start(bf16[256,1024]{1,0:T(8,128)(2,1)S(1)} %get-tuple-element.69), channel_id=1, source_target_pairs={{0,1},{1,2},{2,3},{3,0},{4,5},{5,6},{6,7},{7,4},{8,9},{9,10},{10,1... | collective-permute-start | bytes 1572872 | tf_op jit(solution)/shard_map/ppermute | solution.py:73
  822.2 106.7 %collective-permute-start.8 = (bf16[256,1024]{1,0:T(8,128)(2,1)S(1)}, bf16[256,1024]{1,0:T(8,128)(2,1)}, u32[]{:S(2)}, u32[]{:S(2)}) collective-permute-start(bf16[256,1024]{1,0:T(8,128)(2,1)S(1)} %get-tuple-element.67), channel_id=1, source_target_pairs={{0,3},{1,0},{2,1},{3,2},{4,7},{5,4},{6,5},{7,6},{8,11},{9,8},{10,9... | collective-permute-start | bytes 1572872 | tf_op jit(solution)/shard_map/ppermute | solution.py:73
  825.4 105.0 %collective-permute-start.7 = (bf16[256,1024]{1,0:T(8,128)(2,1)S(1)}, bf16[256,1024]{1,0:T(8,128)(2,1)}, u32[]{:S(2)}, u32[]{:S(2)}) collective-permute-start(bf16[256,1024]{1,0:T(8,128)(2,1)S(1)} %get-tuple-element.68), channel_id=1, source_target_pairs={{0,2},{1,3},{2,0},{3,1},{4,6},{5,7},{6,4},{7,5},{8,10},{9,11},{10,... | collective-permute-start | bytes 1572872 | tf_op jit(solution)/shard_map/ppermute | solution.py:73
  826.8 47.0 %collective-permute-start.23 = (f32[2048]{0:T(1024)S(1)}, f32[2048]{0:T(1024)S(1)}, u32[]{:S(2)}, u32[]{:S(2)}) collective-permute-start(f32[2048]{0:T(1024)S(1)} %get-tuple-element.49), channel_id=1, source_target_pairs={{0,4},{4,0},{8,12},{12,8},{16,20},{20,16},{24,28},{28,24},{1,5},{5... | collective-permute-start | bytes 24584 | tf_op jit(solution)/shard_map/ppermute | solution.py:101
  867.4 109.3 %collective-permute-start.29 = (bf16[2,256,1024]{2,1,0:T(8,128)(2,1)S(1)}, bf16[2,256,1024]{2,1,0:T(8,128)(2,1)S(1)}, u32[]{:S(2)}, u32[]{:S(2)}) collective-permute-start(bf16[2,256,1024]{2,1,0:T(8,128)(2,1)S(1)} %pad_maximum_fusion.13), channel_id=1, source_target_pairs={{0,16},{4,20},{8,24},{12,28},{16,0},{20,4},{24,8},{28,12},{1,17},{... | collective-permute-start | bytes 3145736 | tf_op jit(solution)/shard_map/ppermute | solution.py:89
  868.9 157.1 %collective-permute-start.32 = (bf16[2,256,1024]{2,1,0:T(8,128)(2,1)S(1)}, bf16[2,256,1024]{2,1,0:T(8,128)(2,1)S(1)}, u32[]{:S(2)}, u32[]{:S(2)}) collective-permute-start(bf16[2,256,1024]{2,1,0:T(8,128)(2,1)S(1)} %pad_maximum_fusion.14), channel_id=1, source_target_pairs={{0,8},{4,12},{8,0},{12,4},{16,24},{20,28},{24,16},{28,20},{1,9},{5... | collective-permute-start | bytes 3145736 | tf_op jit(solution)/shard_map/ppermute | solution.py:89
  875.1 26.4 %collective-permute-start.24 = (f32[2048]{0:T(1024)S(1)}, f32[2048]{0:T(1024)S(1)}, u32[]{:S(2)}, u32[]{:S(2)}) collective-permute-start(f32[2048]{0:T(1024)S(1)} %add.223), channel_id=1, source_target_pairs={{0,8},{4,12},{8,0},{12,4},{16,24},{20,28},{24,16},{28,20},{1,9},{5... | collective-permute-start | bytes 24584 | tf_op jit(solution)/shard_map/ppermute | solution.py:101
  913.2 24.4 %collective-permute-start.6 = (bf16[256,1024]{1,0:T(8,128)(2,1)S(1)}, bf16[256,1024]{1,0:T(8,128)(2,1)S(1)}, u32[]{:S(2)}, u32[]{:S(2)}) collective-permute-start(bf16[256,1024]{1,0:T(8,128)(2,1)S(1)} %get-tuple-element.66), channel_id=1, source_target_pairs={{0,1},{1,2},{2,3},{3,0},{4,5},{5,6},{6,7},{7,4},{8,9},{9,10},{10,1... | collective-permute-start | bytes 1572872 | tf_op jit(solution)/shard_map/ppermute | solution.py:73
  930.4 44.0 %collective-permute-start.21 = (f32[2048]{0:T(1024)S(1)}, f32[2048]{0:T(1024)S(1)}, u32[]{:S(2)}, u32[]{:S(2)}) collective-permute-start(f32[2048]{0:T(1024)S(1)} %add.220), channel_id=1, source_target_pairs={{0,1},{1,0},{2,3},{3,2},{4,5},{5,4},{6,7},{7,6},{8,9},{9,8},{10,11... | collective-permute-start | bytes 24584 | tf_op jit(solution)/shard_map/ppermute | solution.py:101
  937.6 97.2 %collective-permute-start.17 = (bf16[256,2048]{1,0:T(8,128)(2,1)S(1)}, bf16[256,2048]{1,0:T(8,128)(2,1)S(1)}, u32[]{:S(2)}, u32[]{:S(2)}) collective-permute-start(bf16[256,2048]{1,0:T(8,128)(2,1)S(1)} %get-tuple-element.57), channel_id=1, source_target_pairs={{0,3},{1,0},{2,1},{3,2},{4,7},{5,4},{6,5},{7,6},{8,11},{9,8},{10,9... | collective-permute-start | bytes 3145736 | tf_op jit(solution)/shard_map/ppermute | solution.py:73
  940.8 94.1 %collective-permute-start.16 = (bf16[256,2048]{1,0:T(8,128)(2,1)S(1)}, bf16[256,2048]{1,0:T(8,128)(2,1)S(1)}, u32[]{:S(2)}, u32[]{:S(2)}) collective-permute-start(bf16[256,2048]{1,0:T(8,128)(2,1)S(1)} %get-tuple-element.58), channel_id=1, source_target_pairs={{0,2},{1,3},{2,0},{3,1},{4,6},{5,7},{6,4},{7,5},{8,10},{9,11},{10,... | collective-permute-start | bytes 3145736 | tf_op jit(solution)/shard_map/ppermute | solution.py:73
  974.5 60.4 %collective-permute-start.15 = (bf16[256,2048]{1,0:T(8,128)(2,1)S(1)}, bf16[256,2048]{1,0:T(8,128)(2,1)S(1)}, u32[]{:S(2)}, u32[]{:S(2)}) collective-permute-start(bf16[256,2048]{1,0:T(8,128)(2,1)S(1)} %get-tuple-element.56), channel_id=1, source_target_pairs={{0,1},{1,2},{2,3},{3,0},{4,5},{5,6},{6,7},{7,4},{8,9},{9,10},{10,1... | collective-permute-start | bytes 3145736 | tf_op jit(solution)/shard_map/ppermute | solution.py:73
  976.7 49.3 %collective-permute-start.27 = (f32[2048]{0:T(1024)S(1)}, f32[2048]{0:T(1024)S(1)}, u32[]{:S(2)}, u32[]{:S(2)}) collective-permute-start(f32[2048]{0:T(1024)S(1)} %add.226), channel_id=1, source_target_pairs={{0,2},{1,3},{2,0},{3,1},{4,6},{5,7},{6,4},{7,5},{8,10},{9,11},{10,... | collective-permute-start | bytes 24584 | tf_op jit(solution)/shard_map/ppermute | solution.py:101
  (46 other events, 984.8 us)
Sparse Core Ops, SparseCore 0:
  10.4 83.4 all-gather.18
  96.0 26.4 all-gather.22
  124.7 80.1 all-gather.20
  206.3 79.2 all-gather.10
  430.1 81.2 all-gather.12
Sparse Core Ops, SparseCore 1:
  14.4 36.2 reduce-scatter.4
  552.6 54.8 reduce-scatter.6
  611.5 116.0 reduce-scatter.8
  731.6 71.3 reduce-scatter.10
  804.9 44.5 all-gather.14
  851.3 99.8 all-gather.16

commit v5 on v4

v5 whole, which is shorter than its diff:
```python
import functools

import jax
import jax.numpy as jnp
from jax import lax
from jax.experimental import pallas as pl
from jax.experimental.pallas import tpu as pltpu
from jax.experimental.layout import Layout, with_layout_constraint
from jax.sharding import PartitionSpec as P


LOW = jnp.bfloat16
DP, TP = "dp", "tensor"

HD = 64
SEQLEN = 512


EPS = 1e-05
ROPE_BASE = 500000.0
MASKED = -1e30


def rope_tables(length, columns):
    half_width = columns // 2
    frequency = ROPE_BASE ** (-(jnp.arange(half_width, dtype=jnp.float32) * 2.0 / columns))
    angles = jnp.arange(length, dtype=jnp.float32)[:, None] * frequency[None, :]
    return (jnp.cos(angles), jnp.sin(angles))


def contract_rows(left_side, right_side):
    return lax.dot_general(
        left_side, right_side, (((0,), (0,)), ((), ())), preferred_element_type=jnp.float32
    )


def contract_cols(left_side, right_side):
    return lax.dot_general(
        left_side, right_side, (((1,), (1,)), ((), ())), preferred_element_type=jnp.float32
    )


def gather_rows(block, axis):
    return lax.all_gather(block, axis, axis=0, tiled=True)


def scatter_sum(partial, axis):
    return lax.psum_scatter(partial, axis, scatter_dimension=0, tiled=True)


def cube_gather(blocks, axis):
    n = lax.axis_size(axis)
    bits = [1 << b for b in range(n.bit_length() - 1)]
    half = blocks.shape[-1] // 2
    halves = []
    for part, order in (
        (blocks[..., :half], bits[1:] + bits[:1]),
        (blocks[..., half:], bits[:0:-1] + bits[:1]),
    ):
        held, offsets = part[None], [0]
        for bit in order:
            moved = lax.ppermute(held, axis, [(i, i ^ bit) for i in range(n)])
            held = jnp.concatenate([held, moved], axis=0)
            offsets = offsets + [o ^ bit for o in offsets]
        halves.append((held, tuple(offsets)))
    return halves


def cube_sum(vector, axes):
    for axis in axes:
        n = lax.axis_size(axis)
        bit = 1
        while bit < n:
            vector = vector + lax.ppermute(vector, axis, [(i, i ^ bit) for i in range(n)])
            bit *= 2
    return vector


def rotate_rows(values, cos_rows, sin_rows):
    half = HD // 2
    heads = []
    for h in range(values.shape[0] // HD):
        upper = values[h * HD : h * HD + half]
        lower = values[h * HD + half : (h + 1) * HD]
        heads.append(upper * cos_rows - lower * sin_rows)
        heads.append(lower * cos_rows + upper * sin_rows)
    return jnp.concatenate(heads, axis=0)


def dot_lanes(left_side, right_side):
    return lax.dot_general(
        left_side, right_side, (((1,), (1,)), ((), ())), preferred_element_type=jnp.float32
    )


def norm_project(gathered, gain_vec, weight_rows, cos_rows, sin_rows, group):
    blocks, tile, width = gathered.shape
    rows = blocks * tile
    columns = weight_rows.shape[0]
    packed = (group + 2) * HD

    def kernel(tokens_ref, gain_ref, weight_ref, cos_ref, sin_ref, normed_ref, out_ref):
        values = tokens_ref[0].astype(jnp.float32)
        row_scale = lax.rsqrt(jnp.mean(values * values, axis=-1, keepdims=True) + EPS)
        normed = (values * row_scale * gain_ref[...].astype(jnp.float32)).astype(LOW)
        normed_ref[...] = normed
        projected = dot_lanes(weight_ref[...], normed)
        for start in range(0, columns, packed):
            turned = start + packed - HD
            out_ref[start:turned] = rotate_rows(
                projected[start:turned], cos_ref[...], sin_ref[...]
            ).astype(LOW)
            out_ref[turned : turned + HD] = projected[turned : turned + HD].astype(LOW)

    half = HD // 2
    return pl.pallas_call(
        kernel,
        grid=(blocks,),
        in_specs=[
            pl.BlockSpec((1, tile, width), lambda i: (i, 0, 0)),
            pl.BlockSpec((1, width), lambda i: (0, 0)),
            pl.BlockSpec((columns, width), lambda i: (0, 0)),
            pl.BlockSpec((half, tile), lambda i: (0, i % (SEQLEN // tile))),
            pl.BlockSpec((half, tile), lambda i: (0, i % (SEQLEN // tile))),
        ],
        out_specs=[
            pl.BlockSpec((tile, width), lambda i: (i, 0)),
            pl.BlockSpec((columns, tile), lambda i: (0, i)),
        ],
        out_shape=[
            jax.ShapeDtypeStruct((rows, width), LOW),
            jax.ShapeDtypeStruct((columns, rows), LOW),
        ],
        cost_estimate=pl.CostEstimate(
            flops=2 * rows * width * columns, transcendentals=rows, bytes_accessed=12 << 20
        ),
        name="norm_project",
    )(gathered, gain_vec.reshape(1, -1), weight_rows, cos_rows, sin_rows)


def key_tiles(step, tile):
    return [(t * tile, t == step) for t in range(step + 1)]


def causal_tile(tile):
    key_at = lax.broadcasted_iota(jnp.int32, (tile, tile), 0)
    query_at = lax.broadcasted_iota(jnp.int32, (tile, tile), 1)
    return key_at <= query_at


def attend(projected, group):
    columns, rows = projected.shape
    packed = (group + 2) * HD
    kv_heads = columns // packed
    wide = group * HD
    tile = 256
    score_scale = HD ** (-0.5)

    def kernel(packed_ref, heads_ref, heads_t_ref, total_ref):
        keys = packed_ref[wide : wide + HD].astype(jnp.float32).T.astype(LOW)
        visible = causal_tile(tile)
        for step in range(SEQLEN // tile):
            here = slice(step * tile, (step + 1) * tile)
            for h in range(group):
                query = packed_ref[h * HD : (h + 1) * HD, here]
                parts = []
                for start, masked in key_tiles(step, tile):
                    part = jnp.dot(
                        keys[start : start + tile], query, preferred_element_type=jnp.float32
                    )
                    parts.append(jnp.where(visible, part, MASKED) if masked else part)
                top = functools.reduce(
                    jnp.maximum, [jnp.max(part, axis=0, keepdims=True) for part in parts]
                )
                parts = [jnp.exp((part - top) * score_scale) for part in parts]
                total = sum(jnp.sum(part, axis=0, keepdims=True) for part in parts)
                inverse = 1.0 / total
                mixed = sum(
                    jnp.dot(
                        packed_ref[wide + HD : packed, start : start + tile],
                        (part * inverse).astype(LOW),
                        preferred_element_type=jnp.float32,
                    )
                    for part, (start, _) in zip(parts, key_tiles(step, tile))
                )
                heads_t_ref[h * HD : (h + 1) * HD, here] = mixed.astype(LOW)
                total_ref[0, h : h + 1, here] = top * score_scale + jnp.log(total)
        heads_ref[...] = heads_t_ref[...].astype(jnp.float32).T.astype(LOW)

    return pl.pallas_call(
        kernel,
        grid=(rows // SEQLEN, kv_heads),
        in_specs=[pl.BlockSpec((packed, SEQLEN), lambda s, j: (j, s))],
        out_specs=[
            pl.BlockSpec((SEQLEN, wide), lambda s, j: (s, j)),
            pl.BlockSpec((wide, SEQLEN), lambda s, j: (j, s)),
            pl.BlockSpec((1, group, SEQLEN), lambda s, j: (j, 0, s)),
        ],
        out_shape=[
            jax.ShapeDtypeStruct((rows, kv_heads * wide), LOW),
            jax.ShapeDtypeStruct((kv_heads * wide, rows), LOW),
            jax.ShapeDtypeStruct((kv_heads, group, rows), jnp.float32),
        ],
        cost_estimate=pl.CostEstimate(
            flops=4 * rows * SEQLEN * kv_heads * wide,
            transcendentals=rows * SEQLEN * kv_heads * group,
            bytes_accessed=4 << 20,
        ),
        name="attend",
    )(projected)


def attend_back(projected, d_heads, totals, cos_rows, sin_rows):
    columns, rows = projected.shape
    kv_heads, group, _ = totals.shape
    packed = (group + 2) * HD
    wide = group * HD
    tile = 256
    score_scale = HD ** (-0.5)

    def kernel(
        packed_ref, d_heads_ref, total_ref, cos_ref, sin_ref, out_ref, key_sum, value_sum
    ):
        keys = packed_ref[wide : wide + HD].astype(jnp.float32).T.astype(LOW)
        values = packed_ref[wide + HD : packed].astype(jnp.float32).T.astype(LOW)
        visible = causal_tile(tile)
        key_sum[...] = jnp.zeros_like(key_sum)
        value_sum[...] = jnp.zeros_like(value_sum)
        for step in range(SEQLEN // tile):
            here = slice(step * tile, (step + 1) * tile)
            for h in range(group):
                query = packed_ref[h * HD : (h + 1) * HD, here]
                d_head = d_heads_ref[h * HD : (h + 1) * HD, here]
                log_total = total_ref[0, h : h + 1, here]
                probs, d_probs = [], []
                for start, masked in key_tiles(step, tile):
                    span = slice(start, start + tile)
                    part = jnp.dot(keys[span], query, preferred_element_type=jnp.float32)
                    part = jnp.exp(part * score_scale - log_total)
                    if masked:
                        part = jnp.where(visible, part, 0.0)
                    probs.append(part)
                    value_sum[:, span] += dot_lanes(d_head, part.astype(LOW))
                    d_probs.append(
                        jnp.dot(values[span], d_head, preferred_element_type=jnp.float32)
                    )
                row_sum = sum(
                    jnp.sum(part * d_part, axis=0, keepdims=True)
                    for part, d_part in zip(probs, d_probs)
                )
                d_query = jnp.zeros((HD, tile), jnp.float32)
                for (start, _), part, d_part in zip(key_tiles(step, tile), probs, d_probs):
                    span = slice(start, start + tile)
                    d_scores = (part * (d_part - row_sum)).astype(LOW)
                    d_query += jnp.dot(
                        packed_ref[wide : wide + HD, span],
                        d_scores,
                        preferred_element_type=jnp.float32,
                    )
                    key_sum[:, span] += dot_lanes(query, d_scores)
                out_ref[h * HD : (h + 1) * HD, here] = rotate_rows(
                    d_query * score_scale, cos_ref[:, here], -sin_ref[:, here]
                ).astype(LOW)
        out_ref[wide : wide + HD] = rotate_rows(
            key_sum[...] * score_scale, cos_ref[...], -sin_ref[...]
        ).astype(LOW)
        out_ref[wide + HD : packed] = value_sum[...].astype(LOW)

    half = HD // 2
    return pl.pallas_call(
        kernel,
        grid=(rows // SEQLEN, kv_heads),
        in_specs=[
            pl.BlockSpec((packed, SEQLEN), lambda s, j: (j, s)),
            pl.BlockSpec((wide, SEQLEN), lambda s, j: (j, s)),
            pl.BlockSpec((1, group, SEQLEN), lambda s, j: (j, 0, s)),
            pl.BlockSpec((half, SEQLEN), lambda s, j: (0, 0)),
            pl.BlockSpec((half, SEQLEN), lambda s, j: (0, 0)),
        ],
        out_specs=pl.BlockSpec((packed, SEQLEN), lambda s, j: (j, s)),
        out_shape=jax.ShapeDtypeStruct((columns, rows), LOW),
        scratch_shapes=[
            pltpu.VMEM((HD, SEQLEN), jnp.float32),
            pltpu.VMEM((HD, SEQLEN), jnp.float32),
        ],
        cost_estimate=pl.CostEstimate(
            flops=10 * rows * SEQLEN * kv_heads * wide,
            transcendentals=rows * SEQLEN * kv_heads * group,
            bytes_accessed=6 << 20,
        ),
        name="attend_back",
    )(projected, d_heads, totals, cos_rows, sin_rows)


def project_and_norm(all_heads, weights, gathered, gain_vec):
    groups, rows, group_columns = all_heads.shape
    (first, first_offsets), (second, second_offsets) = weights
    parts, _, depth, half = first.shape
    width = 2 * half
    tile = rows // groups
    places = jnp.stack([lax.axis_index(TP), lax.axis_index(DP)])

    def kernel(
        at_ref,
        heads_ref,
        first_ref,
        second_ref,
        tokens_ref,
        gain_ref,
        hidden_ref,
        normed_ref,
        weight_ref,
        wide_ref,
    ):
        step = pl.program_id(0)

        @pl.when(step == 0)
        def _():
            for side, part_ref, offsets in (
                (0, first_ref, first_offsets),
                (half, second_ref, second_offsets),
            ):
                for part in range(parts):
                    for g in range(groups):
                        start = g * group_columns + (at_ref[1] ^ offsets[part]) * depth
                        at = pl.ds(pl.multiple_of(start, depth), depth)
                        weight_ref[at, side : side + half] = part_ref[part, g]

        for g in range(groups):
            wide_ref[:, g * group_columns : (g + 1) * group_columns] = heads_ref[g]
        hidden = tokens_ref[0].astype(jnp.float32) + jnp.dot(
            wide_ref[...], weight_ref[...], preferred_element_type=jnp.float32
        )
        row_scale = lax.rsqrt(jnp.mean(hidden * hidden, axis=-1, keepdims=True) + EPS)
        normed_ref[...] = (hidden * row_scale * gain_ref[...].astype(jnp.float32)).astype(
            LOW
        )

        @pl.when(step == at_ref[0])
        def _():
            hidden_ref[...] = hidden

    return pl.pallas_call(
        kernel,
        grid_spec=pltpu.PrefetchScalarGridSpec(
            num_scalar_prefetch=1,
            grid=(groups,),
            in_specs=[
                pl.BlockSpec((groups, tile, group_columns), lambda i, at_ref: (0, i, 0)),
                pl.BlockSpec(first.shape, lambda i, at_ref: (0, 0, 0, 0)),
                pl.BlockSpec(second.shape, lambda i, at_ref: (0, 0, 0, 0)),
                pl.BlockSpec((1, tile, width), lambda i, at_ref: (i, 0, 0)),
                pl.BlockSpec((1, width), lambda i, at_ref: (0, 0)),
            ],
            out_specs=[
                pl.BlockSpec((tile, width), lambda i, at_ref: (0, 0)),
                pl.BlockSpec((tile, width), lambda i, at_ref: (i, 0)),
            ],
            scratch_shapes=[
                pltpu.VMEM((groups * group_columns, width), LOW),
                pltpu.VMEM((tile, groups * group_columns), LOW),
            ],
        ),
        out_shape=[
            jax.ShapeDtypeStruct((tile, width), jnp.float32),
            jax.ShapeDtypeStruct((rows, width), LOW),
        ],
        cost_estimate=pl.CostEstimate(
            flops=2 * rows * width * width, transcendentals=rows, bytes_accessed=20 << 20
        ),
        name="project_and_norm",
    )(places, all_heads, first, second, gathered, gain_vec.reshape(1, -1))


def gated_up(normed, w_gate, w_up):
    rows, width = normed.shape
    columns = w_gate.shape[1]
    tile = 256

    def kernel(normed_ref, gate_w_ref, up_w_ref, gate_ref, up_ref, active_ref):
        gate = jnp.dot(normed_ref[...], gate_w_ref[...], preferred_element_type=jnp.float32)
        up = jnp.dot(normed_ref[...], up_w_ref[...], preferred_element_type=jnp.float32)
        gate_ref[...] = gate
        up_ref[...] = up
        active_ref[...] = (gate * jax.nn.sigmoid(gate) * up).astype(LOW)

    column_block = pl.BlockSpec((rows, tile), lambda j: (0, j))
    weight_block = pl.BlockSpec((width, tile), lambda j: (0, j))
    return pl.pallas_call(
        kernel,
        grid=(columns // tile,),
        in_specs=[pl.BlockSpec((rows, width), lambda j: (0, 0)), weight_block, weight_block],
        out_specs=[column_block] * 3,
        out_shape=[
            jax.ShapeDtypeStruct((rows, columns), jnp.float32),
            jax.ShapeDtypeStruct((rows, columns), jnp.float32),
            jax.ShapeDtypeStruct((rows, columns), LOW),
        ],
        cost_estimate=pl.CostEstimate(
            flops=4 * rows * width * columns,
            transcendentals=rows * columns,
            bytes_accessed=40 << 20,
        ),
        name="gated_up",
    )(normed, w_gate, w_up)


def gated_back(all_cot, w_down, gate_proj, up_proj):
    rows, width = all_cot.shape
    columns = w_down.shape[0]
    tile = 256

    def kernel(cot_ref, weight_ref, gate_ref, up_ref, d_gate_ref, d_up_ref):
        d_active = dot_lanes(cot_ref[...], weight_ref[...])
        gate = gate_ref[...]
        chance = jax.nn.sigmoid(gate)
        smooth = gate * chance
        d_up_ref[...] = (d_active * smooth).astype(LOW)
        slope = chance * (1.0 + gate * (1.0 - chance))
        d_gate_ref[...] = (d_active * up_ref[...] * slope).astype(LOW)

    column_block = pl.BlockSpec((rows, tile), lambda j: (0, j))
    return pl.pallas_call(
        kernel,
        grid=(columns // tile,),
        in_specs=[
            pl.BlockSpec((rows, width), lambda j: (0, 0)),
            pl.BlockSpec((tile, width), lambda j: (j, 0)),
            column_block,
            column_block,
        ],
        out_specs=[column_block] * 2,
        out_shape=[jax.ShapeDtypeStruct((rows, columns), LOW)] * 2,
        cost_estimate=pl.CostEstimate(
            flops=2 * rows * width * columns,
            transcendentals=rows * columns,
            bytes_accessed=36 << 20,
        ),
        name="gated_back",
    )(all_cot, w_down, gate_proj, up_proj)


def pair_product(place, tile, first, first_weight, second, second_weight):
    depth = first.shape[1]
    columns = first_weight.shape[0]
    part = min(columns, 512)

    def kernel(at_ref, first_ref, second_ref, first_w_ref, second_w_ref, out_ref):
        out_ref[...] = (
            dot_lanes(first_ref[...], first_w_ref[...])
            + dot_lanes(second_ref[...], second_w_ref[...])
        ).astype(LOW)

    here = pl.BlockSpec((tile, depth), lambda j, at_ref: (at_ref[0], 0))
    weight_block = pl.BlockSpec((part, depth), lambda j, at_ref: (j, 0))
    return pl.pallas_call(
        kernel,
        grid_spec=pltpu.PrefetchScalarGridSpec(
            num_scalar_prefetch=1,
            grid=(columns // part,),
            in_specs=[here, here, weight_block, weight_block],
            out_specs=pl.BlockSpec((tile, part), lambda j, at_ref: (0, j)),
        ),
        out_shape=jax.ShapeDtypeStruct((tile, columns), LOW),
        cost_estimate=pl.CostEstimate(
            flops=4 * tile * depth * columns, transcendentals=0, bytes_accessed=20 << 20
        ),
        name="pair_product",
    )(place.reshape(1), first, second, first_weight, second_weight)


def projection_back(place, d_projected, weight_rows, gathered):
    columns, width = weight_rows.shape
    tile = gathered.shape[1]
    part = 128

    def kernel(at_ref, d_ref, weight_ref, tokens_ref, out_ref, gain_ref):
        step = pl.program_id(0)
        grads = d_ref[...].astype(jnp.float32).T.astype(LOW)
        block = jnp.dot(grads, weight_ref[...], preferred_element_type=jnp.float32).astype(LOW)
        out_ref[...] = block
        values = tokens_ref[0].astype(jnp.float32)
        row_scale = lax.rsqrt(jnp.mean(values * values, axis=-1, keepdims=True) + EPS)
        added = jnp.sum(block.astype(jnp.float32) * values * row_scale, axis=0, keepdims=True)
        gain_ref[...] = jnp.where(step == 0, added, gain_ref[...] + added)

    return pl.pallas_call(
        kernel,
        grid_spec=pltpu.PrefetchScalarGridSpec(
            num_scalar_prefetch=1,
            grid=(tile // part,),
            in_specs=[
                pl.BlockSpec(
                    (columns, part), lambda i, at_ref: (0, at_ref[0] * (tile // part) + i)
                ),
                pl.BlockSpec((columns, width), lambda i, at_ref: (0, 0)),
                pl.BlockSpec((1, part, width), lambda i, at_ref: (at_ref[0], i, 0)),
            ],
            out_specs=[
                pl.BlockSpec((part, width), lambda i, at_ref: (i, 0)),
                pl.BlockSpec((1, width), lambda i, at_ref: (0, 0)),
            ],
        ),
        out_shape=[
            jax.ShapeDtypeStruct((tile, width), LOW),
            jax.ShapeDtypeStruct((1, width), jnp.float32),
        ],
        cost_estimate=pl.CostEstimate(
            flops=2 * tile * columns * width, transcendentals=0, bytes_accessed=6 << 20
        ),
        name="projection_back",
    )(place.reshape(1), d_projected, weight_rows, gathered)


def norm_back(values, gain_vec, base, blocks):
    rows, width = values.shape
    part = 64
    count = len(blocks)

    def kernel(values_ref, gain_ref, base_ref, *refs):
        wide_ref, low_ref, sum_ref = refs[count:]
        step = pl.program_id(0)
        upstream = sum(ref[...].astype(jnp.float32) for ref in refs[:count])
        held = values_ref[...].astype(jnp.float32)
        row_scale = lax.rsqrt(jnp.mean(held * held, axis=-1, keepdims=True) + EPS)
        scaled = held * row_scale
        added = jnp.sum(upstream * scaled, axis=0, keepdims=True)
        sum_ref[...] = jnp.where(step == 0, added, sum_ref[...] + added)
        weighted = upstream * gain_ref[...].astype(jnp.float32)
        inner = jnp.mean(weighted * scaled, axis=-1, keepdims=True)
        result = base_ref[...].astype(jnp.float32) + row_scale * (weighted - scaled * inner)
        wide_ref[...] = result
        low_ref[...] = result.astype(LOW)

    tile_block = pl.BlockSpec((part, width), lambda i: (i, 0))
    line = pl.BlockSpec((1, width), lambda i: (0, 0))
    return pl.pallas_call(
        kernel,
        grid=(rows // part,),
        in_specs=[tile_block, line, tile_block] + [tile_block] * count,
        out_specs=[tile_block, tile_block, line],
        out_shape=[
            jax.ShapeDtypeStruct((rows, width), jnp.float32),
            jax.ShapeDtypeStruct((rows, width), LOW),
            jax.ShapeDtypeStruct((1, width), jnp.float32),
        ],
        cost_estimate=pl.CostEstimate(
            flops=16 * rows * width, transcendentals=rows, bytes_accessed=10 << 20
        ),
        name="norm_back",
    )(values, gain_vec.reshape(1, -1), base, *blocks)


def exchange(make_block, axis):
    n = lax.axis_size(axis)
    me = lax.axis_index(axis)
    blocks = []
    for hop in range(1, n):
        made = make_block((me + hop) % n)
        blocks.append(lax.ppermute(made, axis, [(i, (i + hop) % n) for i in range(n)]))
    blocks.append(make_block(me))
    return blocks


def place_blocks(halves, axis):
    (first, first_offsets), (second, second_offsets) = halves
    parts, rows, half = first.shape

    def kernel(at_ref, first_ref, second_ref, out_ref):
        out_ref[:, :half] = first_ref[0].astype(jnp.float32)
        out_ref[:, half:] = second_ref[0].astype(jnp.float32)

    def entry(offsets):
        where = [offsets.index(k) for k in range(parts)]

        def index(k, at_ref):
            found = where[0]
            for candidate in range(1, parts):
                found = jnp.where(k == candidate, where[candidate], found)
            return (found, 0, 0)

        return pl.BlockSpec((1, rows, half), index)

    return pl.pallas_call(
        kernel,
        grid_spec=pltpu.PrefetchScalarGridSpec(
            num_scalar_prefetch=1,
            grid=(parts,),
            in_specs=[entry(first_offsets), entry(second_offsets)],
            out_specs=pl.BlockSpec((rows, 2 * half), lambda k, at_ref: (at_ref[0] ^ k, 0)),
        ),
        out_shape=jax.ShapeDtypeStruct((parts * rows, 2 * half), jnp.float32),
        cost_estimate=pl.CostEstimate(
            flops=0, transcendentals=0, bytes_accessed=12 * parts * rows * half
        ),
        name="place_blocks",
    )(lax.axis_index(axis).reshape(1), first, second)


def unpack_attention(shared, q_columns, k_columns, folds):
    rows, columns = shared.shape
    block = rows // folds
    kv_heads = k_columns // HD
    wide = q_columns // kv_heads
    packed = wide + 2 * HD
    end = kv_heads * packed

    def kernel(shared_ref, query_ref, key_ref, value_ref, output_ref):
        for j in range(kv_heads):
            start = j * packed
            query_ref[:, j * wide : (j + 1) * wide] = shared_ref[
                :, start : start + wide
            ].astype(jnp.float32)
            for at, ref in ((start + wide, key_ref), (start + wide + HD, value_ref)):
                ref[:, j * HD : (j + 1) * HD] = shared_ref[:, at : at + HD].astype(jnp.float32)
        output_ref[...] = shared_ref[:, end:].astype(jnp.float32)

    narrow = pl.BlockSpec((block, k_columns), lambda p: (p, 0))
    return pl.pallas_call(
        kernel,
        grid=(folds,),
        in_specs=[pl.BlockSpec((block, columns), lambda p: (p, 0))],
        out_specs=[
            pl.BlockSpec((block, q_columns), lambda p: (p, 0)),
            narrow,
            narrow,
            pl.BlockSpec((block, columns - end), lambda p: (0, p)),
        ],
        out_shape=[
            jax.ShapeDtypeStruct((rows, q_columns), jnp.float32),
            jax.ShapeDtypeStruct((rows, k_columns), jnp.float32),
            jax.ShapeDtypeStruct((rows, k_columns), jnp.float32),
            jax.ShapeDtypeStruct((block, (columns - end) * folds), jnp.float32),
        ],
        cost_estimate=pl.CostEstimate(
            flops=0, transcendentals=0, bytes_accessed=6 * rows * columns
        ),
        name="unpack_attention",
    )(shared)


def add_all(blocks):
    return sum(block.astype(jnp.float32) for block in blocks)


def row_major(array):
    return with_layout_constraint(array, Layout(major_to_minor=tuple(range(array.ndim))))


def split_columns(array, parts):
    if parts == 1:
        return array
    rows, columns = array.shape[0], array.shape[1] // parts
    return array.reshape(rows, parts, columns).swapaxes(0, 1).reshape(parts * rows, columns)


def join_columns(array, parts):
    if parts == 1:
        return array
    rows, columns = array.shape[0] // parts, array.shape[1]
    return array.reshape(parts, rows, columns).swapaxes(0, 1).reshape(rows, parts * columns)


def block(
    tokens,
    cotangent,
    norm1_gain,
    w_query,
    w_key,
    w_value,
    w_output,
    norm2_gain,
    w_gate,
    w_up,
    w_down,
):
    n_dp = lax.axis_size(DP)
    own_rows, width = tokens.shape
    depth = w_output.shape[0] // n_dp
    q_columns, k_columns = w_query.shape[1], w_key.shape[1]
    kv_heads = k_columns // HD
    group = q_columns // k_columns
    ff_columns = w_gate.shape[1]
    ff_folds = width // w_down.shape[0]
    folds = width // w_output.shape[0]
    nothing = scatter_sum(tokens[:, :128] * 0, DP)[0, 0]
    gathered = lax.all_gather(tokens, TP, axis=0)
    own_part = lax.dynamic_slice_in_dim(w_output, lax.axis_index(DP) * depth, depth, 0)
    output_part = lax.all_gather(own_part, TP, axis=0)
    all_output = cube_gather(output_part, DP)
    cos_table, sin_table = rope_tables(SEQLEN, HD)
    cos_rows, sin_rows = cos_table.T, sin_table.T
    pieces = []
    for j in range(kv_heads):
        pieces.append(w_query[:, j * group * HD : (j + 1) * group * HD].T)
        pieces.append(w_key[:, j * HD : (j + 1) * HD].T)
        pieces.append(w_value[:, j * HD : (j + 1) * HD].T)
    weight_rows = jnp.concatenate(pieces, axis=0)
    normed1, projected = norm_project(
        gathered, norm1_gain, weight_rows, cos_rows, sin_rows, group
    )
    heads_out, heads_rows, totals = attend(projected, group)
    all_heads = lax.all_gather(heads_out, TP, axis=0)
    all_cot = gather_rows(cotangent, TP)
    hidden_state, normed2 = project_and_norm(
        all_heads, all_output, gathered, norm2_gain.astype(jnp.float32) + nothing.astype(jnp.float32)
    )
    gate_proj, up_proj, activated = gated_up(normed2, w_gate, w_up)
    mlp_part = jnp.dot(activated, w_down, preferred_element_type=jnp.float32).astype(LOW)
    half_width = width // 2

    def part_of(columns):
        return lambda place: lax.dynamic_slice(
            mlp_part, (place * own_rows, columns), (own_rows, half_width)
        )

    first_half = exchange(part_of(0), TP)
    second_half = exchange(part_of(half_width), TP)
    output = (
        hidden_state
        + jnp.concatenate([add_all(first_half), add_all(second_half)], axis=1)
    ).astype(LOW)
    d_gate, d_up = gated_back(all_cot, w_down, gate_proj, up_proj)
    grad_down = row_major(split_columns(contract_rows(activated, all_cot).astype(LOW), ff_folds))
    part_down = scatter_sum(grad_down, DP)
    dn2_blocks = exchange(
        lambda place: pair_product(place, own_rows, d_gate, w_gate, d_up, w_up), TP
    )
    gate_up_grads = row_major(
        jnp.concatenate(
            [contract_rows(normed2, d_gate).astype(LOW), contract_rows(normed2, d_up).astype(LOW)],
            axis=1,
        )
    )
    part_gate_up = scatter_sum(gate_up_grads, DP)
    d_state, state_low, gain_two = norm_back(hidden_state, norm2_gain, cotangent, dn2_blocks)
    d_state_low = gather_rows(state_low, TP)
    gain_two_sum = cube_sum(gain_two[0], (DP, TP))
    d_heads_rows = contract_cols(w_output, d_state_low).astype(LOW)
    d_projected = attend_back(projected, d_heads_rows, totals, cos_rows, sin_rows)
    gains = []

    def dn1_block(place):
        made, gain = projection_back(place, d_projected, weight_rows, gathered)
        gains.append(gain)
        return made

    dn1_blocks = exchange(dn1_block, TP)
    gain_one_sum = cube_sum(sum(gains)[0], (DP, TP))
    grad_qkv = lax.dot_general(
        normed1,
        d_projected,
        (((0,), (1,)), ((), ())),
        preferred_element_type=jnp.float32,
    ).astype(LOW)
    grad_output = jnp.dot(heads_rows, d_state_low, preferred_element_type=jnp.float32).astype(LOW)
    low_attn = row_major(
        jnp.concatenate([grad_qkv, split_columns(grad_output, folds)], axis=1)
    )
    part_attn = scatter_sum(low_attn, DP)
    down_halves = cube_gather(part_down, DP)
    full_down = join_columns(place_blocks(down_halves, DP), ff_folds)
    shared_ff = row_major(gather_rows(part_gate_up, DP))
    shared_attn = row_major(gather_rows(part_attn, DP))
    _, input_grad, _ = norm_back(tokens, norm1_gain, d_state, dn1_blocks)
    full_gate = shared_ff[:, :ff_columns].astype(jnp.float32)
    full_up = shared_ff[:, ff_columns:].astype(jnp.float32)
    full_query, full_key, full_value, full_output = unpack_attention(
        shared_attn, q_columns, k_columns, folds
    )
    return (
        output,
        input_grad,
        gain_one_sum,
        full_query,
        full_key,
        full_value,
        full_output,
        gain_two_sum,
        full_gate,
        full_up,
        full_down,
    )


ROWS, COLUMNS, HIDDEN = P((DP, TP), None), P(None, TP), P(TP, None)


def solution(mesh):
    return jax.shard_map(
        block,
        mesh=mesh,
        in_specs=(ROWS, ROWS, P(), COLUMNS, COLUMNS, COLUMNS, HIDDEN, P(), COLUMNS, COLUMNS, HIDDEN),
        out_specs=(ROWS, ROWS, P(), COLUMNS, COLUMNS, COLUMNS, HIDDEN, P(), COLUMNS, COLUMNS, HIDDEN),
        check_vma=False,
    )
```

time: 1090 us -> 1080 us (level); the launches traced: 1090 us -> 1060 us
  waiting for transfers between devices: 676 us -> 627 us
  Pallas kernels: 144 us -> 191 us
  starting transfers between devices: 83.7 us -> 65.5 us
    ppermute x12, waiting for transfers between devices: 134 us -> 73.8 us  [exchange(): lax.ppermute(made, axis, [(i, (i + hop) % n) for i in range(n)])]
    pallas_call x2 -> x11, Pallas kernels: 32.3 us -> 79.8 us  [the longest x4 39.8 us: pair_product(): pl.pallas_call(kernel, grid_spec=pltpu.PrefetchScalarGridSpec(num_scalar_...]
    ppermute x10, waiting for transfers between devices: 89.8 us -> 52.6 us  [cube_sum(): lax.ppermute(vector, axis, [(i, i ^ bit) for i in range(n)])]
    ppermute x12, starting transfers between devices: 66.5 us -> 32 us  [exchange(): lax.ppermute(made, axis, [(i, (i + hop) % n) for i in range(n)])]
    ppermute x12, waiting for transfers between devices: 40.7 us -> 65.5 us  [cube_gather(): moved = lax.ppermute(held, axis, [(i, i ^ bit) for i in range(n)])]
    all_gather x4, waiting for transfers between devices: 120 us -> 141 us  [gather_rows(): return lax.all_gather(block, axis, axis=0, tiled=True)]
    ppermute x10, starting transfers between devices: 5.06 us -> 22.1 us  [cube_sum(): lax.ppermute(vector, axis, [(i, i ^ bit) for i in range(n)])]
    reduce_scatter x4, waiting for transfers between devices: 190 us -> 207 us  [scatter_sum(): return lax.psum_scatter(partial, axis, scatter_dimension=0, tiled=True)]
  transfers between devices with their start and end apart: 45 -> 45, of which waited for: 22 -> 27; matrix products, arithmetic and copies ran while one was open for 11% -> 12% of each run, Pallas kernels for 7% -> 13%
where the time goes in v5:
time: 1080 us; the launch traced here: 1060 us
  waiting for transfers between devices  627 us (58%)
  Pallas kernels  191 us (18%)
  starting transfers between devices  65.5 us (6%)
  other arithmetic  63.2 us (6%)
  matrix products  63.1 us (6%)
  local copies, waits for them, and re-layouts  36.3 us (3%)
  between operations  16.6 us (2%)
    reduce_scatter x4, waiting for transfers between devices, scatter_sum(): return lax.psum_scatter(partial, axis, scatter_dimension=0, tiled=True)  207 us
    all_gather x4, waiting for transfers between devices, gather_rows(): return lax.all_gather(block, axis, axis=0, tiled=True)  141 us
    ppermute x12, waiting for transfers between devices, exchange(): lax.ppermute(made, axis, [(i, (i + hop) % n) for i in range(n)])  73.8 us
    ppermute x12, waiting for transfers between devices, cube_gather(): moved = lax.ppermute(held, axis, [(i, i ^ bit) for i in range(n)])  65.5 us
    all_gather x1, waiting for transfers between devices, block(): gathered = lax.all_gather(tokens, TP, axis=0)  56.2 us
    ppermute x10, waiting for transfers between devices, cube_sum(): lax.ppermute(vector, axis, [(i, i ^ bit) for i in range(n)])  52.6 us
    pallas_call x4, Pallas kernels, pair_product(): pl.pallas_call(kernel, grid_spec=pltpu.PrefetchScalarGridSpec(num_scalar_...  39.8 us
    dot_general x3, matrix products, contract_rows(): lax.dot_general(left_side, right_side, (((0,), (0,)), ((), ())), preferre...  36 us
  transfers between devices with their start and end apart: 45, of which 27 were waited for; matrix products, arithmetic and copies ran while one was open for 12% of the time, Pallas kernels for 13%

profile of v5, /device:TPU:0, one launch (start us, length us, event | category | flops | bytes accessed | tf_op | source)
XLA Modules:
  0.0 1062.7 jit_solution(9071498704532485505)
XLA Ops:
  37.7 56.2 %all-gather.19.cloned.1.call-done = bf16[1024,2048]{1,0:T(8,128)(2,1)} async-done(((bf16[256,2048]{1,0:T(8,128)(2,1)}), bf16[1024,2048]{1,0:T(8,128)(2,1)}) %all-gather.19.cloned.1.call-update) | async-done | bytes 4194320 | tf_op jit(solution)/shard_map/all_gather | solution.py:687
  93.9 8.3 norm_project.1
  102.2 13.7 %attend.1 = (bf16[1024,512]{1,0:T(8,128)(2,1)}, bf16[512,1024]{1,0:T(8,128)(2,1)}, f32[2,4,1024]{2,1,0:T(4,128)}) custom-call(bf16[768,1024]{1,0:T(8,128)(2,1)} %get-tuple-element.39.packed_ref), custom_call_target="tpu_custom_call" | custom-call | flops 1073741824 | bytes 4194304 | tf_op jit(solution)/shard_map/attend/pallas_call | solution.py:190
  126.9 10.4 collective-permute-done
  143.7 19.5 %collective-permute-done.1 = bf16[2,4,64,1024]{3,2,1,0:T(8,128)(2,1)} collective-permute-done((bf16[2,4,64,1024]{3,2,1,0:T(8,128)(2,1)}, bf16[2,4,64,1024]{3,2,1,0:T(8,128)(2,1)}, u32[]{:S(2)}, u32[]{:S(2)}) %collective-permute-start.1) | collective-permute-done | bytes 1048608 | tf_op jit(solution)/shard_map/ppermute | solution.py:62
  180.5 24.4 %all-gather.21.cloned.1.call-done = bf16[4096,512]{1,0:T(8,128)(2,1)} async-done(((bf16[1024,512]{1,0:T(8,128)(2,1)}), bf16[4096,512]{1,0:T(8,128)(2,1)}) %all-gather.21.cloned.1.call-update) | async-done | bytes 4194320 | tf_op jit(solution)/shard_map/all_gather | solution.py:703
  204.8 17.6 %project_and_norm.1 = (f32[256,2048]{1,0:T(8,128)}, bf16[1024,2048]{1,0:T(8,128)(2,1)}) custom-call(s32[2]{0:T(128)} %pad_add_fusion.at_ref, bf16[4,1024,512]{2,1,0:T(8,128)(2,1)} %bitcast.70, bf16[8,4,64,1024]{3,2,1,0:T(8,128)(2,1)} %pad_maximum_fusion.2.first_ref, bf16[8,4,64,1024]{3,2,1,0:T(8,128)(2,1)} %pad_maximum_fusion.3.second_ref, ...), custom_call_target="tpu_custom_call" | custom-call | flops 8589934592 | bytes 20971520 | tf_op jit(solution)/shard_map/project_and_norm/pallas_call | solution.py:343
  222.4 23.7 %gated_up.1 = (f32[1024,2048]{1,0:T(8,128)}, f32[1024,2048]{1,0:T(8,128)}, bf16[1024,2048]{1,0:T(8,128)(2,1)}) custom-call(bf16[1024,2048]{1,0:T(8,128)(2,1)} %get-tuple-element.42.normed_ref, bf16[2048,2048]{1,0:T(8,128)(2,1)} %first_w_ref.7, bf16[2048,2048]{1,0:T(8,128)(2,1)} %second_w_ref.7), custom_call_target="tpu_custom_call" | custom-call | flops 17179869184 | bytes 41943040 | tf_op jit(solution)/shard_map/gated_up/pallas_call | solution.py:389
  246.2 39.4 %all-gather.11.cloned.1.call-done.cot_ref = bf16[1024,2048]{1,0:T(8,128)(2,1)} async-done(((bf16[256,2048]{1,0:T(8,128)(2,1)}), bf16[1024,2048]{1,0:T(8,128)(2,1)}) %all-gather.11.cloned.1.call-update) | async-done | bytes 4194320 | tf_op jit(solution)/shard_map/all_gather | solution.py:44
  285.5 18.9 %gated_back.1 = (bf16[1024,2048]{1,0:T(8,128)(2,1)}, bf16[1024,2048]{1,0:T(8,128)(2,1)}) custom-call(bf16[1024,2048]{1,0:T(8,128)(2,1)} %all-gather.11.cloned.1.call-done.cot_ref, bf16[2048,2048]{1,0:T(8,128)(2,1)} %weight_ref.1, f32[1024,2048]{1,0:T(8,128)} %get-tuple-element.44.gate_ref, f32[1024,2048]{1,0:T(8,128)} %get-tuple-element.45.up_ref), custom_call_target="tpu_custom_call" | custom-call | flops 8589934592 | bytes 37748736 | tf_op jit(solution)/shard_map/gated_back/pallas_call | solution.py:423
  304.4 10.0 pair_product.4
  314.4 10.0 pair_product.5
  325.5 10.0 pair_product.6
  338.8 10.0 pair_product.7.refs_3_
  348.7 37.6 %collective-permute-done.13.refs_1_ = bf16[256,2048]{1,0:T(8,128)(2,1)} collective-permute-done((bf16[256,2048]{1,0:T(8,128)(2,1)}, bf16[256,2048]{1,0:T(8,128)(2,1)}, u32[]{:S(2)}, u32[]{:S(2)}) %collective-permute-start.13) | collective-permute-done | bytes 1048608 | tf_op jit(solution)/shard_map/ppermute | solution.py:560
  392.7 101.1 %all-gather.13.cloned.1.call-done = bf16[1024,2048]{1,0:T(8,128)(2,1)} async-done(((bf16[256,2048]{1,0:T(8,128)(2,1)}), bf16[1024,2048]{1,0:T(8,128)(2,1)}) %all-gather.13.cloned.1.call-update) | async-done | bytes 4194320 | tf_op jit(solution)/shard_map/all_gather | solution.py:44
  505.0 20.2 %attend_back.1.d_ref = bf16[768,1024]{1,0:T(8,128)(2,1)} custom-call(bf16[768,1024]{1,0:T(8,128)(2,1)} %get-tuple-element.39.packed_ref, bf16[512,1024]{1,0:T(8,128)(2,1)} %fusion.1.d_heads_ref, f32[2,4,1024]{2,1,0:T(4,128)} %get-tuple-element.50.total_ref, f32[32,512]{1,0:T(8,128)} %get-tuple-element.88.cos_ref, f32[32,512]{1,0:T(8,128)} %get-tuple-element.87.sin_ref), custom_call_target="tpu_custom_call" | custom-call | flops 2684354560 | bytes 6291456 | tf_op jit(solution)/shard_map/attend_back/pallas_call | solution.py:270
  534.8 12.2 %convolution_convert_fusion.1 = bf16[2048,2048]{1,0:T(8,128)(2,1)S(1)} fusion(bf16[1024,2048]{1,0:T(8,128)(2,1)} %get-tuple-element.42.normed_ref, bf16[1024,2048]{1,0:T(8,128)(2,1)} %get-tuple-element.47.second_ref), kind=kOutput, calls=%fused_computation.4 | convolution fusion | flops 8594128896 | bytes 16777216 | tf_op jit(solution)/shard_map/dot_general | solution.py:32
  547.0 9.8 convolution_convert_fusion.2
  563.8 14.0 %convolution_convert_fusion = bf16[2048,2048]{1,0:T(8,128)(2,1)} fusion(bf16[1024,2048]{1,0:T(8,128)(2,1)} %get-tuple-element.43, bf16[1024,2048]{1,0:T(8,128)(2,1)} %all-gather.11.cloned.1.call-done.cot_ref), kind=kOutput, calls=%fused_computation.3 | convolution fusion | flops 8594128896 | bytes 16777216 | tf_op jit(solution)/shard_map/dot_general | solution.py:32
  577.9 11.4 %reduce-scatter.7.cloned.1.call-done = bf16[256,1280]{1,0:T(8,128)(2,1)} async-done(((bf16[2048,1280]{1,0:T(8,128)(2,1)}), bf16[256,1280]{1,0:T(8,128)(2,1)}) %reduce-scatter.7.cloned.1.call-update) | async-done | bytes 655376 | tf_op jit(solution)/shard_map/reduce_scatter | solution.py:48
  589.5 119.8 %reduce-scatter.9.cloned.1.call-done = bf16[256,4096]{1,0:T(8,128)(2,1)} async-done(((bf16[2048,4096]{1,0:T(8,128)(2,1)}), bf16[256,4096]{1,0:T(8,128)(2,1)}) %reduce-scatter.9.cloned.1.call-update) | async-done | bytes 2097168 | tf_op jit(solution)/shard_map/reduce_scatter | solution.py:48
  709.4 75.4 %reduce-scatter.11.cloned.1.call-done = bf16[256,2048]{1,0:T(8,128)(2,1)} async-done(((bf16[2048,2048]{1,0:T(8,128)(2,1)}), bf16[256,2048]{1,0:T(8,128)(2,1)}) %reduce-scatter.11.cloned.1.call-update) | async-done | bytes 1048592 | tf_op jit(solution)/shard_map/reduce_scatter | solution.py:48
  788.1 15.9 %collective-permute-done.28 = bf16[1,256,1024]{2,1,0:T(8,128)(2,1)S(1)} collective-permute-done((bf16[1,256,1024]{2,1,0:T(8,128)(2,1)S(1)}, bf16[1,256,1024]{2,1,0:T(8,128)(2,1)S(1)}, u32[]{:S(2)}, u32[]{:S(2)}) %collective-permute-start.28) | collective-permute-done | bytes 524320 | tf_op jit(solution)/shard_map/ppermute | solution.py:62
  807.1 12.5 %convolution_convert_fusion.3 = bf16[1024,2048]{1,0:T(8,128)(2,1)S(1)} fusion(bf16[1024,2048]{1,0:T(8,128)(2,1)} %get-tuple-element.43, bf16[2048,2048]{1,0:T(8,128)(2,1)} %weight_ref.1), kind=kOutput, calls=%fused_computation.11 | convolution fusion | flops 8592031744 | bytes 16777216 | tf_op jit(solution)/shard_map/dot_general | solution.py:709
  825.8 18.1 %collective-permute-done.29 = bf16[2,256,1024]{2,1,0:T(8,128)(2,1)S(1)} collective-permute-done((bf16[2,256,1024]{2,1,0:T(8,128)(2,1)S(1)}, bf16[2,256,1024]{2,1,0:T(8,128)(2,1)S(1)}, u32[]{:S(2)}, u32[]{:S(2)}) %collective-permute-start.29) | collective-permute-done | bytes 1048608 | tf_op jit(solution)/shard_map/ppermute | solution.py:62
  871.1 18.1 %collective-permute-start.9 = (bf16[256,1024]{1,0:T(8,128)(2,1)}, bf16[256,1024]{1,0:T(8,128)(2,1)}, u32[]{:S(2)}, u32[]{:S(2)}) collective-permute-start(bf16[256,1024]{1,0:T(8,128)(2,1)} %get-tuple-element.74), channel_id=1, source_target_pairs={{0,1},{1,2},{2,3},{3,0},{4,5},{5,6},{6,7},{7,4},{8,9},{9,10},{10,1... | collective-permute-start | bytes 1572872 | tf_op jit(solution)/shard_map/ppermute | solution.py:560
  912.7 10.5 collective-permute-start.26
  933.4 38.3 %collective-permute-done.27 = f32[2048]{0:T(1024)S(1)} collective-permute-done((f32[2048]{0:T(1024)S(1)}, f32[2048]{0:T(1024)S(1)}, u32[]{:S(2)}, u32[]{:S(2)}) %collective-permute-start.27) | collective-permute-done | bytes 8224 | tf_op jit(solution)/shard_map/ppermute | solution.py:74
  977.8 24.0 %collective-permute-done.16.refs_1_ = bf16[256,2048]{1,0:T(8,128)(2,1)} collective-permute-done((bf16[256,2048]{1,0:T(8,128)(2,1)}, bf16[256,2048]{1,0:T(8,128)(2,1)}, u32[]{:S(2)}, u32[]{:S(2)}) %collective-permute-start.16) | collective-permute-done | bytes 1048608 | tf_op jit(solution)/shard_map/ppermute | solution.py:560
  1021.0 10.2 place_blocks.1
  1038.2 17.2 %slice_convert_fusion = (f32[2048,2048]{1,0:T(8,128)}, f32[2048,2048]{1,0:T(8,128)}) fusion(bf16[2048,4096]{1,0:T(8,128)(2,1)} %all-gather.17.cloned.1.call-done), kind=kLoop, calls=%fused_computation.1 | loop fusion | flops 8388608 | bytes 50331648 | tf_op jit(solution)/shard_map/convert_element_type | solution.py:767
  (196 shorter events, 207.9 us)
Async XLA Ops:
  8.0 85.9 %all-gather.19.cloned.1.call-start = ((), (), s32[]{:S(2)}) async-start(), calls=%async_computation.12 | async-start | bytes 5242880 | tf_op jit(solution)/shard_map/all_gather | solution.py:687
  8.8 113.8 %all-gather.23.cloned.1.call-start = ((), (), s32[]{:S(2)}) async-start(), calls=%async_computation.14 | async-start | bytes 1310720 | tf_op jit(solution)/shard_map/all_gather | solution.py:689
  10.4 160.4 %reduce-scatter.5.cloned.1.call-start = ((), (), s32[]{:S(2)}) async-start(), calls=%async_computation.4 | async-start | bytes 73728 | tf_op jit(solution)/shard_map/reduce_scatter | solution.py:48
  11.9 192.9 %all-gather.21.cloned.1.call-start = ((), (), s32[]{:S(2)}) async-start(), calls=%async_computation.13 | async-start | bytes 5242880 | tf_op jit(solution)/shard_map/all_gather | solution.py:703
  116.0 169.6 %all-gather.11.cloned.1.call-start = ((), (), s32[]{:S(2)}) async-start(), calls=%async_computation.5 | async-start | bytes 5242880 | tf_op jit(solution)/shard_map/all_gather | solution.py:44
  139.3 23.9 %collective-permute-start.1 = (bf16[2,4,64,1024]{3,2,1,0:T(8,128)(2,1)}, bf16[2,4,64,1024]{3,2,1,0:T(8,128)(2,1)}, u32[]{:S(2)}, u32[]{:S(2)}) collective-permute-start(bf16[2,4,64,1024]{3,2,1,0:T(8,128)(2,1)} %pad_maximum_fusion.10), channel_id=1, source_target_pairs={{0,16},{4,20},{8,24},{12,28},{16,0},{20,4},{24,8},{28,12},{1,17},{... | collective-permute-start | bytes 3145736 | tf_op jit(solution)/shard_map/ppermute | solution.py:62
  140.8 353.1 %all-gather.13.cloned.1.call-start = ((), (), s32[]{:S(2)}) async-start(), calls=%async_computation.6 | async-start | bytes 5242880 | tf_op jit(solution)/shard_map/all_gather | solution.py:44
  142.2 23.9 %collective-permute-start.4 = (bf16[2,4,64,1024]{3,2,1,0:T(8,128)(2,1)S(1)}, bf16[2,4,64,1024]{3,2,1,0:T(8,128)(2,1)S(1)}, u32[]{:S(2)}, u32[]{:S(2)}) collective-permute-start(bf16[2,4,64,1024]{3,2,1,0:T(8,128)(2,1)S(1)} %pad_maximum_fusion.11), channel_id=1, source_target_pairs={{0,8},{4,12},{8,0},{12,4},{16,24},{20,28},{24,16},{28,20},{1,9},{5... | collective-permute-start | bytes 3145736 | tf_op jit(solution)/shard_map/ppermute | solution.py:62
  314.4 34.3 %collective-permute-start.12 = (bf16[256,2048]{1,0:T(8,128)(2,1)}, bf16[256,2048]{1,0:T(8,128)(2,1)S(1)}, u32[]{:S(2)}, u32[]{:S(2)}) collective-permute-start(bf16[256,2048]{1,0:T(8,128)(2,1)} %pair_product.4), channel_id=1, source_target_pairs={{0,1},{1,2},{2,3},{3,0},{4,5},{5,6},{6,7},{7,4},{8,9},{9,10},{10,1... | collective-permute-start | bytes 3145736 | tf_op jit(solution)/shard_map/ppermute | solution.py:560
  324.4 61.9 %collective-permute-start.13 = (bf16[256,2048]{1,0:T(8,128)(2,1)}, bf16[256,2048]{1,0:T(8,128)(2,1)}, u32[]{:S(2)}, u32[]{:S(2)}) collective-permute-start(bf16[256,2048]{1,0:T(8,128)(2,1)} %pair_product.5), channel_id=1, source_target_pairs={{0,2},{1,3},{2,0},{3,1},{4,6},{5,7},{6,4},{7,5},{8,10},{9,11},{10,... | collective-permute-start | bytes 3145736 | tf_op jit(solution)/shard_map/ppermute | solution.py:560
  335.5 50.9 %collective-permute-start.14 = (bf16[256,2048]{1,0:T(8,128)(2,1)}, bf16[256,2048]{1,0:T(8,128)(2,1)}, u32[]{:S(2)}, u32[]{:S(2)}) collective-permute-start(bf16[256,2048]{1,0:T(8,128)(2,1)} %pair_product.6), channel_id=1, source_target_pairs={{0,3},{1,0},{2,1},{3,2},{4,7},{5,4},{6,5},{7,6},{8,11},{9,8},{10,9... | collective-permute-start | bytes 3145736 | tf_op jit(solution)/shard_map/ppermute | solution.py:560
  392.5 196.8 %reduce-scatter.7.cloned.1.call-start = ((), (), s32[]{:S(2)}) async-start(), calls=%async_computation.7 | async-start | bytes 5898240 | tf_op jit(solution)/shard_map/reduce_scatter | solution.py:48
  534.3 175.0 %reduce-scatter.9.cloned.1.call-start = ((), (), s32[]{:S(2)}) async-start(), calls=%async_computation.9 | async-start | bytes 18874368 | tf_op jit(solution)/shard_map/reduce_scatter | solution.py:48
  563.7 221.0 %reduce-scatter.11.cloned.1.call-start = ((), (), s32[]{:S(2)}) async-start(), calls=%async_computation.11 | async-start | bytes 9437184 | tf_op jit(solution)/shard_map/reduce_scatter | solution.py:48
  577.8 453.4 %all-gather.15.cloned.1.call-start = ((), (), s32[]{:S(2)}) async-start(), calls=%async_computation.8 | async-start | bytes 5898240 | tf_op jit(solution)/shard_map/all_gather | solution.py:44
  589.3 448.9 %all-gather.17.cloned.1.call-start = ((), (), s32[]{:S(2)}) async-start(), calls=%async_computation.10 | async-start | bytes 18874368 | tf_op jit(solution)/shard_map/all_gather | solution.py:44
  787.6 19.4 %collective-permute-start.31 = (bf16[1,256,1024]{2,1,0:T(8,128)(2,1)S(1)}, bf16[1,256,1024]{2,1,0:T(8,128)(2,1)S(1)}, u32[]{:S(2)}, u32[]{:S(2)}) collective-permute-start(bf16[1,256,1024]{2,1,0:T(8,128)(2,1)S(1)} %get-tuple-element.79), channel_id=1, source_target_pairs={{0,16},{4,20},{8,24},{12,28},{16,0},{20,4},{24,8},{28,12},{1,17},{... | collective-permute-start | bytes 1572872 | tf_op jit(solution)/shard_map/ppermute | solution.py:62
  804.1 39.8 %collective-permute-start.29 = (bf16[2,256,1024]{2,1,0:T(8,128)(2,1)S(1)}, bf16[2,256,1024]{2,1,0:T(8,128)(2,1)S(1)}, u32[]{:S(2)}, u32[]{:S(2)}) collective-permute-start(bf16[2,256,1024]{2,1,0:T(8,128)(2,1)S(1)} %pad_maximum_fusion.12), channel_id=1, source_target_pairs={{0,16},{4,20},{8,24},{12,28},{16,0},{20,4},{24,8},{28,12},{1,17},{... | collective-permute-start | bytes 3145736 | tf_op jit(solution)/shard_map/ppermute | solution.py:62
  807.0 38.5 %collective-permute-start.32 = (bf16[2,256,1024]{2,1,0:T(8,128)(2,1)S(1)}, bf16[2,256,1024]{2,1,0:T(8,128)(2,1)S(1)}, u32[]{:S(2)}, u32[]{:S(2)}) collective-permute-start(bf16[2,256,1024]{2,1,0:T(8,128)(2,1)S(1)} %pad_maximum_fusion.13), channel_id=1, source_target_pairs={{0,8},{4,12},{8,0},{12,4},{16,24},{20,28},{24,16},{28,20},{1,9},{5... | collective-permute-start | bytes 3145736 | tf_op jit(solution)/shard_map/ppermute | solution.py:62
  821.3 33.6 %collective-permute-start.8 = (bf16[256,1024]{1,0:T(8,128)(2,1)}, bf16[256,1024]{1,0:T(8,128)(2,1)}, u32[]{:S(2)}, u32[]{:S(2)}) collective-permute-start(bf16[256,1024]{1,0:T(8,128)(2,1)} %get-tuple-element.75), channel_id=1, source_target_pairs={{0,3},{1,0},{2,1},{3,2},{4,7},{5,4},{6,5},{7,6},{8,11},{9,8},{10,9... | collective-permute-start | bytes 1572872 | tf_op jit(solution)/shard_map/ppermute | solution.py:560
  824.7 46.3 %collective-permute-start.7 = (bf16[256,1024]{1,0:T(8,128)(2,1)}, bf16[256,1024]{1,0:T(8,128)(2,1)}, u32[]{:S(2)}, u32[]{:S(2)}) collective-permute-start(bf16[256,1024]{1,0:T(8,128)(2,1)} %get-tuple-element.76), channel_id=1, source_target_pairs={{0,2},{1,3},{2,0},{3,1},{4,6},{5,7},{6,4},{7,5},{8,10},{9,11},{10,... | collective-permute-start | bytes 1572872 | tf_op jit(solution)/shard_map/ppermute | solution.py:560
  824.7 46.3 %collective-permute-start.6 = (bf16[256,1024]{1,0:T(8,128)(2,1)}, bf16[256,1024]{1,0:T(8,128)(2,1)}, u32[]{:S(2)}, u32[]{:S(2)}) collective-permute-start(bf16[256,1024]{1,0:T(8,128)(2,1)} %get-tuple-element.71), channel_id=1, source_target_pairs={{0,1},{1,2},{2,3},{3,0},{4,5},{5,6},{6,7},{7,4},{8,9},{9,10},{10,1... | collective-permute-start | bytes 1572872 | tf_op jit(solution)/shard_map/ppermute | solution.py:560
  845.5 168.2 %collective-permute-start.30 = (bf16[4,256,1024]{2,1,0:T(8,128)(2,1)}, bf16[4,256,1024]{2,1,0:T(8,128)(2,1)}, u32[]{:S(2)}, u32[]{:S(2)}) collective-permute-start(bf16[4,256,1024]{2,1,0:T(8,128)(2,1)} %pad_maximum_fusion.8), channel_id=1, source_target_pairs={{0,4},{4,0},{8,12},{12,8},{16,20},{20,16},{24,28},{28,24},{1,5},{5... | collective-permute-start | bytes 6291464 | tf_op jit(solution)/shard_map/ppermute | solution.py:62
  845.6 48.9 %collective-permute-start.11 = (bf16[256,1024]{1,0:T(8,128)(2,1)}, bf16[256,1024]{1,0:T(8,128)(2,1)}, u32[]{:S(2)}, u32[]{:S(2)}) collective-permute-start(bf16[256,1024]{1,0:T(8,128)(2,1)} %get-tuple-element.72), channel_id=1, source_target_pairs={{0,3},{1,0},{2,1},{3,2},{4,7},{5,4},{6,5},{7,6},{8,11},{9,8},{10,9... | collective-permute-start | bytes 1572872 | tf_op jit(solution)/shard_map/ppermute | solution.py:560
  854.9 162.6 %collective-permute-start.33 = (bf16[4,256,1024]{2,1,0:T(8,128)(2,1)}, bf16[4,256,1024]{2,1,0:T(8,128)(2,1)}, u32[]{:S(2)}, u32[]{:S(2)}) collective-permute-start(bf16[4,256,1024]{2,1,0:T(8,128)(2,1)} %pad_maximum_fusion.9), channel_id=1, source_target_pairs={{0,4},{4,0},{8,12},{12,8},{16,20},{20,16},{24,28},{28,24},{1,5},{5... | collective-permute-start | bytes 6291464 | tf_op jit(solution)/shard_map/ppermute | solution.py:62
  871.0 58.5 %collective-permute-start.10 = (bf16[256,1024]{1,0:T(8,128)(2,1)}, bf16[256,1024]{1,0:T(8,128)(2,1)}, u32[]{:S(2)}, u32[]{:S(2)}) collective-permute-start(bf16[256,1024]{1,0:T(8,128)(2,1)} %get-tuple-element.73), channel_id=1, source_target_pairs={{0,2},{1,3},{2,0},{3,1},{4,6},{5,7},{6,4},{7,5},{8,10},{9,11},{10,... | collective-permute-start | bytes 1572872 | tf_op jit(solution)/shard_map/ppermute | solution.py:560
  871.1 60.4 %collective-permute-start.9 = (bf16[256,1024]{1,0:T(8,128)(2,1)}, bf16[256,1024]{1,0:T(8,128)(2,1)}, u32[]{:S(2)}, u32[]{:S(2)}) collective-permute-start(bf16[256,1024]{1,0:T(8,128)(2,1)} %get-tuple-element.74), channel_id=1, source_target_pairs={{0,1},{1,2},{2,3},{3,0},{4,5},{5,6},{6,7},{7,4},{8,9},{9,10},{10,1... | collective-permute-start | bytes 1572872 | tf_op jit(solution)/shard_map/ppermute | solution.py:560
  928.5 43.2 %collective-permute-start.27 = (f32[2048]{0:T(1024)S(1)}, f32[2048]{0:T(1024)S(1)}, u32[]{:S(2)}, u32[]{:S(2)}) collective-permute-start(f32[2048]{0:T(1024)S(1)} %add.161), channel_id=1, source_target_pairs={{0,2},{1,3},{2,0},{3,1},{4,6},{5,7},{6,4},{7,5},{8,10},{9,11},{10,... | collective-permute-start | bytes 24584 | tf_op jit(solution)/shard_map/ppermute | solution.py:74
  929.5 42.6 %collective-permute-start.22 = (f32[2048]{0:T(1024)S(1)}, f32[2048]{0:T(1024)S(1)}, u32[]{:S(2)}, u32[]{:S(2)}) collective-permute-start(f32[2048]{0:T(1024)S(1)} %add.156), channel_id=1, source_target_pairs={{0,2},{1,3},{2,0},{3,1},{4,6},{5,7},{6,4},{7,5},{8,10},{9,11},{10,... | collective-permute-start | bytes 24584 | tf_op jit(solution)/shard_map/ppermute | solution.py:74
  931.4 46.3 %collective-permute-start.15 = (bf16[256,2048]{1,0:T(8,128)(2,1)}, bf16[256,2048]{1,0:T(8,128)(2,1)}, u32[]{:S(2)}, u32[]{:S(2)}) collective-permute-start(bf16[256,2048]{1,0:T(8,128)(2,1)} %get-tuple-element.51), channel_id=1, source_target_pairs={{0,1},{1,2},{2,3},{3,0},{4,5},{5,6},{6,7},{7,4},{8,9},{9,10},{10,1... | collective-permute-start | bytes 3145736 | tf_op jit(solution)/shard_map/ppermute | solution.py:560
  971.7 30.1 %collective-permute-start.16 = (bf16[256,2048]{1,0:T(8,128)(2,1)}, bf16[256,2048]{1,0:T(8,128)(2,1)}, u32[]{:S(2)}, u32[]{:S(2)}) collective-permute-start(bf16[256,2048]{1,0:T(8,128)(2,1)} %get-tuple-element.52), channel_id=1, source_target_pairs={{0,2},{1,3},{2,0},{3,1},{4,6},{5,7},{6,4},{7,5},{8,10},{9,11},{10,... | collective-permute-start | bytes 3145736 | tf_op jit(solution)/shard_map/ppermute | solution.py:560
  972.1 35.5 %collective-permute-start.17 = (bf16[256,2048]{1,0:T(8,128)(2,1)}, bf16[256,2048]{1,0:T(8,128)(2,1)}, u32[]{:S(2)}, u32[]{:S(2)}) collective-permute-start(bf16[256,2048]{1,0:T(8,128)(2,1)} %get-tuple-element.53), channel_id=1, source_target_pairs={{0,3},{1,0},{2,1},{3,2},{4,7},{5,4},{6,5},{7,6},{8,11},{9,8},{10,9... | collective-permute-start | bytes 3145736 | tf_op jit(solution)/shard_map/ppermute | solution.py:560
  (36 other events, 562.0 us)
Sparse Core Ops, SparseCore 0:
  10.4 83.4 all-gather.18
  96.0 26.4 all-gather.22
  124.7 80.1 all-gather.20
  206.3 79.2 all-gather.10
  392.6 101.2 all-gather.12
Sparse Core Ops, SparseCore 1:
  14.4 36.2 reduce-scatter.4
  534.4 54.8 reduce-scatter.6
  593.3 116.0 reduce-scatter.8
  713.4 71.3 reduce-scatter.10
  786.7 59.3 all-gather.14
  847.9 89.9 all-gather.16

commit v6 on v5

--- a/solution.py
+++ b/solution.py
@@ -440,76 +440,88 @@
     )(all_cot, w_down, gate_proj, up_proj)
 
 
-def pair_product(place, tile, first, first_weight, second, second_weight):
-    depth = first.shape[1]
+def pair_product(places, tile, first, first_weight, second, second_weight):
+    rows, depth = first.shape
     columns = first_weight.shape[0]
-    part = min(columns, 512)
-
-    def kernel(at_ref, first_ref, second_ref, first_w_ref, second_w_ref, out_ref):
-        out_ref[...] = (
-            dot_lanes(first_ref[...], first_w_ref[...])
-            + dot_lanes(second_ref[...], second_w_ref[...])
-        ).astype(LOW)
-
-    here = pl.BlockSpec((tile, depth), lambda j, at_ref: (at_ref[0], 0))
+    count = len(places)
+    part = 512 if count == 1 else 256
+    at = jnp.stack(places)
+
+    def kernel(at_ref, first_ref, second_ref, first_w_ref, second_w_ref, *out_refs):
+        for k, out_ref in enumerate(out_refs):
+            here = (
+                slice(None)
+                if count == 1
+                else pl.ds(pl.multiple_of(at_ref[k] * tile, tile), tile)
+            )
+            out_ref[...] = (
+                dot_lanes(first_ref[here, :], first_w_ref[...])
+                + dot_lanes(second_ref[here, :], second_w_ref[...])
+            ).astype(LOW)
+
+    held = (
+        pl.BlockSpec((tile, depth), lambda j, at_ref: (at_ref[0], 0))
+        if count == 1
+        else pl.BlockSpec((rows, depth), lambda j, at_ref: (0, 0))
+    )
     weight_block = pl.BlockSpec((part, depth), lambda j, at_ref: (j, 0))
     return pl.pallas_call(
         kernel,
         grid_spec=pltpu.PrefetchScalarGridSpec(
             num_scalar_prefetch=1,
             grid=(columns // part,),
-            in_specs=[here, here, weight_block, weight_block],
-            out_specs=pl.BlockSpec((tile, part), lambda j, at_ref: (0, j)),
-        ),
-        out_shape=jax.ShapeDtypeStruct((tile, columns), LOW),
-        cost_estimate=pl.CostEstimate(
-            flops=4 * tile * depth * columns, transcendentals=0, bytes_accessed=20 << 20
+            in_specs=[held, held, weight_block, weight_block],
+            out_specs=[pl.BlockSpec((tile, part), lambda j, at_ref: (0, j))] * count,
+        ),
+        out_shape=[jax.ShapeDtypeStruct((tile, columns), LOW)] * count,
+        cost_estimate=pl.CostEstimate(
+            flops=4 * count * tile * depth * columns, transcendentals=0, bytes_accessed=20 << 20
         ),
         name="pair_product",
-    )(place.reshape(1), first, second, first_weight, second_weight)
-
-
-def projection_back(place, d_projected, weight_rows, gathered):
+    )(at, first, second, first_weight, second_weight)
+
+
+def projection_back(places, d_projected, weight_rows, gathered):
     columns, width = weight_rows.shape
     tile = gathered.shape[1]
-    part = 128
-
-    def kernel(at_ref, d_ref, weight_ref, tokens_ref, out_ref, gain_ref):
+    count = len(places)
+    at = jnp.stack(places)
+
+    def kernel(at_ref, d_ref, weight_ref, tokens_ref, *out_refs):
         step = pl.program_id(0)
         grads = d_ref[...].astype(jnp.float32).T.astype(LOW)
-        block = jnp.dot(grads, weight_ref[...], preferred_element_type=jnp.float32).astype(LOW)
-        out_ref[...] = block
+        made = jnp.dot(grads, weight_ref[...], preferred_element_type=jnp.float32).astype(LOW)
         values = tokens_ref[0].astype(jnp.float32)
         row_scale = lax.rsqrt(jnp.mean(values * values, axis=-1, keepdims=True) + EPS)
-        added = jnp.sum(block.astype(jnp.float32) * values * row_scale, axis=0, keepdims=True)
+        added = jnp.sum(made.astype(jnp.float32) * values * row_scale, axis=0, keepdims=True)
+        gain_ref = out_refs[count]
         gain_ref[...] = jnp.where(step == 0, added, gain_ref[...] + added)
+        for k in range(count):
+
+            @pl.when(step == k)
+            def _():
+                out_refs[k][...] = made
 
     return pl.pallas_call(
         kernel,
         grid_spec=pltpu.PrefetchScalarGridSpec(
             num_scalar_prefetch=1,
-            grid=(tile // part,),
+            grid=(count,),
             in_specs=[
-                pl.BlockSpec(
-                    (columns, part), lambda i, at_ref: (0, at_ref[0] * (tile // part) + i)
-                ),
+                pl.BlockSpec((columns, tile), lambda i, at_ref: (0, at_ref[i])),
                 pl.BlockSpec((columns, width), lambda i, at_ref: (0, 0)),
-                pl.BlockSpec((1, part, width), lambda i, at_ref: (at_ref[0], i, 0)),
+                pl.BlockSpec((1, tile, width), lambda i, at_ref: (at_ref[i], 0, 0)),
             ],
-            out_specs=[
-                pl.BlockSpec((part, width), lambda i, at_ref: (i, 0)),
-                pl.BlockSpec((1, width), lambda i, at_ref: (0, 0)),
-            ],
-        ),
-        out_shape=[
-            jax.ShapeDtypeStruct((tile, width), LOW),
-            jax.ShapeDtypeStruct((1, width), jnp.float32),
-        ],
-        cost_estimate=pl.CostEstimate(
-            flops=2 * tile * columns * width, transcendentals=0, bytes_accessed=6 << 20
+            out_specs=[pl.BlockSpec((tile, width), lambda i, at_ref: (0, 0))] * count
+            + [pl.BlockSpec((1, width), lambda i, at_ref: (0, 0))],
+        ),
+        out_shape=[jax.ShapeDtypeStruct((tile, width), LOW)] * count
+        + [jax.ShapeDtypeStruct((1, width), jnp.float32)],
+        cost_estimate=pl.CostEstimate(
+            flops=2 * count * tile * columns * width, transcendentals=0, bytes_accessed=8 << 20
         ),
         name="projection_back",
-    )(place.reshape(1), d_projected, weight_rows, gathered)
+    )(at, d_projected, weight_rows, gathered)
 
 
 def norm_back(values, gain_vec, base, blocks):
@@ -551,15 +563,18 @@
     )(values, gain_vec.reshape(1, -1), base, *blocks)
 
 
-def exchange(make_block, axis):
+def exchange(make_blocks, axis):
     n = lax.axis_size(axis)
     me = lax.axis_index(axis)
-    blocks = []
+    places = [(me + hop) % n for hop in range(1, n)] + [me]
+    made = list(make_blocks(places[:1]))
+    moved = []
     for hop in range(1, n):
-        made = make_block((me + hop) % n)
-        blocks.append(lax.ppermute(made, axis, [(i, (i + hop) % n) for i in range(n)]))
-    blocks.append(make_block(me))
-    return blocks
+        if hop == 2:
+            made += make_blocks(places[1:])
+        pairs = [(i, (i + hop) % n) for i in range(n)]
+        moved.append(lax.ppermute(made[hop - 1], axis, pairs))
+    return moved + made[n - 1 :]
 
 
 def place_blocks(halves, axis):
@@ -710,9 +725,10 @@
     half_width = width // 2
 
     def part_of(columns):
-        return lambda place: lax.dynamic_slice(
-            mlp_part, (place * own_rows, columns), (own_rows, half_width)
-        )
+        return lambda places: [
+            lax.dynamic_slice(mlp_part, (place * own_rows, columns), (own_rows, half_width))
+            for place in places
+        ]
 
     first_half = exchange(part_of(0), TP)
     second_half = exchange(part_of(half_width), TP)
@@ -724,7 +740,7 @@
     grad_down = row_major(split_columns(contract_rows(activated, all_cot).astype(LOW), ff_folds))
     part_down = scatter_sum(grad_down, DP)
     dn2_blocks = exchange(
-        lambda place: pair_product(place, own_rows, d_gate, w_gate, d_up, w_up), TP
+        lambda places: pair_product(places, own_rows, d_gate, w_gate, d_up, w_up), TP
     )
     gate_up_grads = row_major(
         jnp.concatenate(
@@ -740,12 +756,12 @@
     d_projected = attend_back(projected, d_heads_rows, totals, cos_rows, sin_rows)
     gains = []
 
-    def dn1_block(place):
-        made, gain = projection_back(place, d_projected, weight_rows, gathered)
+    def dn1_blocks_of(places):
+        *made, gain = projection_back(places, d_projected, weight_rows, gathered)
         gains.append(gain)
         return made
 
-    dn1_blocks = exchange(dn1_block, TP)
+    dn1_blocks = exchange(dn1_blocks_of, TP)
     gain_one_sum = cube_sum(sum(gains)[0], (DP, TP))
     grad_qkv = lax.dot_general(
         normed1,

time: 1080 us -> 1090 us (level)
  waiting for transfers between devices: 627 us -> 666 us
  starting transfers between devices: 65.5 us -> 43.8 us
  Pallas kernels: 191 us -> 177 us
    ppermute x12, waiting for transfers between devices: 73.8 us -> 114 us  [exchange(): moved.append(lax.ppermute(made[hop - 1], axis, pairs))]
    ppermute x12, starting transfers between devices: 32 us -> 13.9 us  [exchange(): moved.append(lax.ppermute(made[hop - 1], axis, pairs))]
    pallas_call x4 -> x2, Pallas kernels: 39.8 us -> 30.2 us  [pair_product(): pl.pallas_call(kernel, grid_spec=pltpu.PrefetchScalarGridSpec(num_scalar_...]
  transfers between devices with their start and end apart: 45 -> 45, of which waited for: 27 -> 27; matrix products, arithmetic and copies ran while one was open for 12% -> 12% of each run, Pallas kernels for 13% -> 11%
where the time goes in v6:
time: 1090 us; the launch traced here: 1070 us
  waiting for transfers between devices  666 us (61%)
  Pallas kernels  177 us (16%)
  other arithmetic  64 us (6%)
  matrix products  63.1 us (6%)
  starting transfers between devices  43.8 us (4%)
  local copies, waits for them, and re-layouts  36.9 us (3%)
  between operations  16.6 us (2%)
    reduce_scatter x4, waiting for transfers between devices, scatter_sum(): return lax.psum_scatter(partial, axis, scatter_dimension=0, tiled=True)  207 us
    all_gather x4, waiting for transfers between devices, gather_rows(): return lax.all_gather(block, axis, axis=0, tiled=True)  141 us
    ppermute x12, waiting for transfers between devices, exchange(): moved.append(lax.ppermute(made[hop - 1], axis, pairs))  114 us
    ppermute x12, waiting for transfers between devices, cube_gather(): moved = lax.ppermute(held, axis, [(i, i ^ bit) for i in range(n)])  65.7 us
    all_gather x1, waiting for transfers between devices, block(): gathered = lax.all_gather(tokens, TP, axis=0)  56.2 us
    ppermute x10, waiting for transfers between devices, cube_sum(): lax.ppermute(vector, axis, [(i, i ^ bit) for i in range(n)])  52.4 us
    dot_general x3, matrix products, contract_rows(): lax.dot_general(left_side, right_side, (((0,), (0,)), ((), ())), preferre...  36 us
    pallas_call x2, Pallas kernels, pair_product(): pl.pallas_call(kernel, grid_spec=pltpu.PrefetchScalarGridSpec(num_scalar_...  30.2 us
  transfers between devices with their start and end apart: 45, of which 27 were waited for; matrix products, arithmetic and copies ran while one was open for 12% of the time, Pallas kernels for 11%

profile of v6, /device:TPU:0, one launch (start us, length us, event | category | flops | bytes accessed | tf_op | source)
XLA Modules:
  0.0 1067.4 jit_solution(10575019880736637462)
XLA Ops:
  37.7 56.2 %all-gather.19.cloned.1.call-done = bf16[1024,2048]{1,0:T(8,128)(2,1)} async-done(((bf16[256,2048]{1,0:T(8,128)(2,1)}), bf16[1024,2048]{1,0:T(8,128)(2,1)}) %all-gather.19.cloned.1.call-update) | async-done | bytes 4194320 | tf_op jit(solution)/shard_map/all_gather | solution.py:702
  93.9 8.3 norm_project.1
  102.2 13.7 %attend.1 = (bf16[1024,512]{1,0:T(8,128)(2,1)}, bf16[512,1024]{1,0:T(8,128)(2,1)}, f32[2,4,1024]{2,1,0:T(4,128)}) custom-call(bf16[768,1024]{1,0:T(8,128)(2,1)} %get-tuple-element.40.packed_ref), custom_call_target="tpu_custom_call" | custom-call | flops 1073741824 | bytes 4194304 | tf_op jit(solution)/shard_map/attend/pallas_call | solution.py:190
  126.9 10.4 collective-permute-done
  143.7 19.5 %collective-permute-done.1 = bf16[2,4,64,1024]{3,2,1,0:T(8,128)(2,1)} collective-permute-done((bf16[2,4,64,1024]{3,2,1,0:T(8,128)(2,1)}, bf16[2,4,64,1024]{3,2,1,0:T(8,128)(2,1)}, u32[]{:S(2)}, u32[]{:S(2)}) %collective-permute-start.1) | collective-permute-done | bytes 1048608 | tf_op jit(solution)/shard_map/ppermute | solution.py:62
  181.1 23.7 %all-gather.21.cloned.1.call-done = bf16[4096,512]{1,0:T(8,128)(2,1)} async-done(((bf16[1024,512]{1,0:T(8,128)(2,1)}), bf16[4096,512]{1,0:T(8,128)(2,1)}) %all-gather.21.cloned.1.call-update) | async-done | bytes 4194320 | tf_op jit(solution)/shard_map/all_gather | solution.py:718
  204.8 17.6 %project_and_norm.1 = (f32[256,2048]{1,0:T(8,128)}, bf16[1024,2048]{1,0:T(8,128)(2,1)}) custom-call(s32[2]{0:T(128)} %pad_add_fusion.at_ref, bf16[4,1024,512]{2,1,0:T(8,128)(2,1)} %bitcast.68, bf16[8,4,64,1024]{3,2,1,0:T(8,128)(2,1)} %pad_maximum_fusion.2.first_ref, bf16[8,4,64,1024]{3,2,1,0:T(8,128)(2,1)} %pad_maximum_fusion.3.second_ref, ...), custom_call_target="tpu_custom_call" | custom-call | flops 8589934592 | bytes 20971520 | tf_op jit(solution)/shard_map/project_and_norm/pallas_call | solution.py:343
  222.4 23.7 %gated_up.1 = (f32[1024,2048]{1,0:T(8,128)}, f32[1024,2048]{1,0:T(8,128)}, bf16[1024,2048]{1,0:T(8,128)(2,1)}) custom-call(bf16[1024,2048]{1,0:T(8,128)(2,1)} %get-tuple-element.43.normed_ref, bf16[2048,2048]{1,0:T(8,128)(2,1)} %first_w_ref.3, bf16[2048,2048]{1,0:T(8,128)(2,1)} %second_w_ref.3), custom_call_target="tpu_custom_call" | custom-call | flops 17179869184 | bytes 41943040 | tf_op jit(solution)/shard_map/gated_up/pallas_call | solution.py:389
  246.1 39.4 %all-gather.11.cloned.1.call-done.cot_ref = bf16[1024,2048]{1,0:T(8,128)(2,1)} async-done(((bf16[256,2048]{1,0:T(8,128)(2,1)}), bf16[1024,2048]{1,0:T(8,128)(2,1)}) %all-gather.11.cloned.1.call-update) | async-done | bytes 4194320 | tf_op jit(solution)/shard_map/all_gather | solution.py:44
  285.5 18.9 %gated_back.1 = (bf16[1024,2048]{1,0:T(8,128)(2,1)}, bf16[1024,2048]{1,0:T(8,128)(2,1)}) custom-call(bf16[1024,2048]{1,0:T(8,128)(2,1)} %all-gather.11.cloned.1.call-done.cot_ref, bf16[2048,2048]{1,0:T(8,128)(2,1)} %weight_ref.1, f32[1024,2048]{1,0:T(8,128)} %get-tuple-element.45.gate_ref, f32[1024,2048]{1,0:T(8,128)} %get-tuple-element.46.up_ref), custom_call_target="tpu_custom_call" | custom-call | flops 8589934592 | bytes 37748736 | tf_op jit(solution)/shard_map/gated_back/pallas_call | solution.py:423
  304.4 10.0 pair_product.2
  314.4 20.2 %pair_product.3 = (bf16[256,2048]{1,0:T(8,128)(2,1)}, bf16[256,2048]{1,0:T(8,128)(2,1)}, bf16[256,2048]{1,0:T(8,128)(2,1)}) custom-call(s32[3]{0:T(128)} %pad_add_fusion.1.at_ref, bf16[1024,2048]{1,0:T(8,128)(2,1)} %get-tuple-element.47.first_ref, bf16[1024,2048]{1,0:T(8,128)(2,1)} %get-tuple-element.48.second_ref, bf16[2048,2048]{1,0:T(8,128)(2,1)} %first_w_ref.3, ...), custom_call_target="tpu_custom_call" | custom-call | flops 12884901888 | bytes 20971520 | tf_op jit(solution)/shard_map/pair_product/pallas_call | solution.py:468
  342.5 43.8 %collective-permute-done.13.refs_1_ = bf16[256,2048]{1,0:T(8,128)(2,1)} collective-permute-done((bf16[256,2048]{1,0:T(8,128)(2,1)}, bf16[256,2048]{1,0:T(8,128)(2,1)}, u32[]{:S(2)}, u32[]{:S(2)}) %collective-permute-start.13) | collective-permute-done | bytes 1048608 | tf_op jit(solution)/shard_map/ppermute | solution.py:576
  392.7 101.1 %all-gather.13.cloned.1.call-done = bf16[1024,2048]{1,0:T(8,128)(2,1)} async-done(((bf16[256,2048]{1,0:T(8,128)(2,1)}), bf16[1024,2048]{1,0:T(8,128)(2,1)}) %all-gather.13.cloned.1.call-update) | async-done | bytes 4194320 | tf_op jit(solution)/shard_map/all_gather | solution.py:44
  505.0 20.2 %attend_back.1.d_ref = bf16[768,1024]{1,0:T(8,128)(2,1)} custom-call(bf16[768,1024]{1,0:T(8,128)(2,1)} %get-tuple-element.40.packed_ref, bf16[512,1024]{1,0:T(8,128)(2,1)} %fusion.1.d_heads_ref, f32[2,4,1024]{2,1,0:T(4,128)} %get-tuple-element.54.total_ref, f32[32,512]{1,0:T(8,128)} %get-tuple-element.90.cos_ref, f32[32,512]{1,0:T(8,128)} %get-tuple-element.89.sin_ref), custom_call_target="tpu_custom_call" | custom-call | flops 2684354560 | bytes 6291456 | tf_op jit(solution)/shard_map/attend_back/pallas_call | solution.py:270
  534.8 12.2 %convolution_convert_fusion.1 = bf16[2048,2048]{1,0:T(8,128)(2,1)S(1)} fusion(bf16[1024,2048]{1,0:T(8,128)(2,1)} %get-tuple-element.43.normed_ref, bf16[1024,2048]{1,0:T(8,128)(2,1)} %get-tuple-element.48.second_ref), kind=kOutput, calls=%fused_computation.4 | convolution fusion | flops 8594128896 | bytes 16777216 | tf_op jit(solution)/shard_map/dot_general | solution.py:32
  547.0 9.8 convolution_convert_fusion.2
  556.8 6.9 pad_maximum_fusion
  563.8 14.0 %convolution_convert_fusion = bf16[2048,2048]{1,0:T(8,128)(2,1)} fusion(bf16[1024,2048]{1,0:T(8,128)(2,1)} %get-tuple-element.44, bf16[1024,2048]{1,0:T(8,128)(2,1)} %all-gather.11.cloned.1.call-done.cot_ref), kind=kOutput, calls=%fused_computation.3 | convolution fusion | flops 8594128896 | bytes 16777216 | tf_op jit(solution)/shard_map/dot_general | solution.py:32
  577.9 11.5 %reduce-scatter.7.cloned.1.call-done = bf16[256,1280]{1,0:T(8,128)(2,1)} async-done(((bf16[2048,1280]{1,0:T(8,128)(2,1)}), bf16[256,1280]{1,0:T(8,128)(2,1)}) %reduce-scatter.7.cloned.1.call-update) | async-done | bytes 655376 | tf_op jit(solution)/shard_map/reduce_scatter | solution.py:48
  589.6 119.8 %reduce-scatter.9.cloned.1.call-done = bf16[256,4096]{1,0:T(8,128)(2,1)} async-done(((bf16[2048,4096]{1,0:T(8,128)(2,1)}), bf16[256,4096]{1,0:T(8,128)(2,1)}) %reduce-scatter.9.cloned.1.call-update) | async-done | bytes 2097168 | tf_op jit(solution)/shard_map/reduce_scatter | solution.py:48
  709.4 75.4 %reduce-scatter.11.cloned.1.call-done = bf16[256,2048]{1,0:T(8,128)(2,1)} async-done(((bf16[2048,2048]{1,0:T(8,128)(2,1)}), bf16[256,2048]{1,0:T(8,128)(2,1)}) %reduce-scatter.11.cloned.1.call-update) | async-done | bytes 1048592 | tf_op jit(solution)/shard_map/reduce_scatter | solution.py:48
  788.2 15.9 %collective-permute-done.28 = bf16[1,256,1024]{2,1,0:T(8,128)(2,1)S(1)} collective-permute-done((bf16[1,256,1024]{2,1,0:T(8,128)(2,1)S(1)}, bf16[1,256,1024]{2,1,0:T(8,128)(2,1)S(1)}, u32[]{:S(2)}, u32[]{:S(2)}) %collective-permute-start.28) | collective-permute-done | bytes 524320 | tf_op jit(solution)/shard_map/ppermute | solution.py:62
  807.2 12.5 %convolution_convert_fusion.3 = bf16[1024,2048]{1,0:T(8,128)(2,1)S(1)} fusion(bf16[1024,2048]{1,0:T(8,128)(2,1)} %get-tuple-element.44, bf16[2048,2048]{1,0:T(8,128)(2,1)} %weight_ref.1), kind=kOutput, calls=%fused_computation.11 | convolution fusion | flops 8592031744 | bytes 16777216 | tf_op jit(solution)/shard_map/dot_general | solution.py:724
  825.7 18.2 %collective-permute-done.29 = bf16[2,256,1024]{2,1,0:T(8,128)(2,1)S(1)} collective-permute-done((bf16[2,256,1024]{2,1,0:T(8,128)(2,1)S(1)}, bf16[2,256,1024]{2,1,0:T(8,128)(2,1)S(1)}, u32[]{:S(2)}, u32[]{:S(2)}) %collective-permute-start.29) | collective-permute-done | bytes 1048608 | tf_op jit(solution)/shard_map/ppermute | solution.py:62
  851.0 36.7 %collective-permute-done.7 = bf16[256,1024]{1,0:T(8,128)(2,1)} collective-permute-done((bf16[256,1024]{1,0:T(8,128)(2,1)S(1)}, bf16[256,1024]{1,0:T(8,128)(2,1)}, u32[]{:S(2)}, u32[]{:S(2)}) %collective-permute-start.7) | collective-permute-done | bytes 524320 | tf_op jit(solution)/shard_map/ppermute | solution.py:576
  887.8 10.1 projection_back.3
  938.1 38.3 %collective-permute-done.27 = f32[2048]{0:T(1024)S(1)} collective-permute-done((f32[2048]{0:T(1024)S(1)}, f32[2048]{0:T(1024)S(1)}, u32[]{:S(2)}, u32[]{:S(2)}) %collective-permute-start.27) | collective-permute-done | bytes 8224 | tf_op jit(solution)/shard_map/ppermute | solution.py:74
  982.5 24.0 %collective-permute-done.16.refs_1_ = bf16[256,2048]{1,0:T(8,128)(2,1)} collective-permute-done((bf16[256,2048]{1,0:T(8,128)(2,1)}, bf16[256,2048]{1,0:T(8,128)(2,1)}, u32[]{:S(2)}, u32[]{:S(2)}) %collective-permute-start.16) | collective-permute-done | bytes 1048608 | tf_op jit(solution)/shard_map/ppermute | solution.py:576
  1025.7 10.2 place_blocks.1
  1035.9 7.0 unpack_attention.1
  1042.9 17.2 %slice_convert_fusion = (f32[2048,2048]{1,0:T(8,128)}, f32[2048,2048]{1,0:T(8,128)}) fusion(bf16[2048,4096]{1,0:T(8,128)(2,1)} %all-gather.17.cloned.1.call-done), kind=kLoop, calls=%fused_computation.1 | loop fusion | flops 8388608 | bytes 50331648 | tf_op jit(solution)/shard_map/convert_element_type | solution.py:783
  (191 shorter events, 184.6 us)
Async XLA Ops:
  8.0 85.9 %all-gather.19.cloned.1.call-start = ((), (), s32[]{:S(2)}) async-start(), calls=%async_computation.12 | async-start | bytes 5242880 | tf_op jit(solution)/shard_map/all_gather | solution.py:702
  8.8 113.8 %all-gather.23.cloned.1.call-start = ((), (), s32[]{:S(2)}) async-start(), calls=%async_computation.14 | async-start | bytes 1310720 | tf_op jit(solution)/shard_map/all_gather | solution.py:704
  10.4 161.0 %reduce-scatter.5.cloned.1.call-start = ((), (), s32[]{:S(2)}) async-start(), calls=%async_computation.4 | async-start | bytes 73728 | tf_op jit(solution)/shard_map/reduce_scatter | solution.py:48
  11.9 192.9 %all-gather.21.cloned.1.call-start = ((), (), s32[]{:S(2)}) async-start(), calls=%async_computation.13 | async-start | bytes 5242880 | tf_op jit(solution)/shard_map/all_gather | solution.py:718
  116.0 169.6 %all-gather.11.cloned.1.call-start = ((), (), s32[]{:S(2)}) async-start(), calls=%async_computation.5 | async-start | bytes 5242880 | tf_op jit(solution)/shard_map/all_gather | solution.py:44
  139.3 23.9 %collective-permute-start.1 = (bf16[2,4,64,1024]{3,2,1,0:T(8,128)(2,1)}, bf16[2,4,64,1024]{3,2,1,0:T(8,128)(2,1)}, u32[]{:S(2)}, u32[]{:S(2)}) collective-permute-start(bf16[2,4,64,1024]{3,2,1,0:T(8,128)(2,1)} %pad_maximum_fusion.10), channel_id=1, source_target_pairs={{0,16},{4,20},{8,24},{12,28},{16,0},{20,4},{24,8},{28,12},{1,17},{... | collective-permute-start | bytes 3145736 | tf_op jit(solution)/shard_map/ppermute | solution.py:62
  140.8 353.1 %all-gather.13.cloned.1.call-start = ((), (), s32[]{:S(2)}) async-start(), calls=%async_computation.6 | async-start | bytes 5242880 | tf_op jit(solution)/shard_map/all_gather | solution.py:44
  142.2 23.9 %collective-permute-start.4 = (bf16[2,4,64,1024]{3,2,1,0:T(8,128)(2,1)S(1)}, bf16[2,4,64,1024]{3,2,1,0:T(8,128)(2,1)S(1)}, u32[]{:S(2)}, u32[]{:S(2)}) collective-permute-start(bf16[2,4,64,1024]{3,2,1,0:T(8,128)(2,1)S(1)} %pad_maximum_fusion.11), channel_id=1, source_target_pairs={{0,8},{4,12},{8,0},{12,4},{16,24},{20,28},{24,16},{28,20},{1,9},{5... | collective-permute-start | bytes 3145736 | tf_op jit(solution)/shard_map/ppermute | solution.py:62
  314.4 28.1 %collective-permute-start.12 = (bf16[256,2048]{1,0:T(8,128)(2,1)}, bf16[256,2048]{1,0:T(8,128)(2,1)S(1)}, u32[]{:S(2)}, u32[]{:S(2)}) collective-permute-start(bf16[256,2048]{1,0:T(8,128)(2,1)} %pair_product.2), channel_id=1, source_target_pairs={{0,1},{1,2},{2,3},{3,0},{4,5},{5,6},{6,7},{7,4},{8,9},{9,10},{10,1... | collective-permute-start | bytes 3145736 | tf_op jit(solution)/shard_map/ppermute | solution.py:576
  334.6 51.7 %collective-permute-start.13 = (bf16[256,2048]{1,0:T(8,128)(2,1)}, bf16[256,2048]{1,0:T(8,128)(2,1)}, u32[]{:S(2)}, u32[]{:S(2)}) collective-permute-start(bf16[256,2048]{1,0:T(8,128)(2,1)} %get-tuple-element.49), channel_id=1, source_target_pairs={{0,2},{1,3},{2,0},{3,1},{4,6},{5,7},{6,4},{7,5},{8,10},{9,11},{10,... | collective-permute-start | bytes 3145736 | tf_op jit(solution)/shard_map/ppermute | solution.py:576
  335.8 50.5 %collective-permute-start.14 = (bf16[256,2048]{1,0:T(8,128)(2,1)}, bf16[256,2048]{1,0:T(8,128)(2,1)}, u32[]{:S(2)}, u32[]{:S(2)}) collective-permute-start(bf16[256,2048]{1,0:T(8,128)(2,1)} %get-tuple-element.50), channel_id=1, source_target_pairs={{0,3},{1,0},{2,1},{3,2},{4,7},{5,4},{6,5},{7,6},{8,11},{9,8},{10,9... | collective-permute-start | bytes 3145736 | tf_op jit(solution)/shard_map/ppermute | solution.py:576
  392.5 196.9 %reduce-scatter.7.cloned.1.call-start = ((), (), s32[]{:S(2)}) async-start(), calls=%async_computation.7 | async-start | bytes 5898240 | tf_op jit(solution)/shard_map/reduce_scatter | solution.py:48
  534.3 175.0 %reduce-scatter.9.cloned.1.call-start = ((), (), s32[]{:S(2)}) async-start(), calls=%async_computation.9 | async-start | bytes 18874368 | tf_op jit(solution)/shard_map/reduce_scatter | solution.py:48
  563.7 221.1 %reduce-scatter.11.cloned.1.call-start = ((), (), s32[]{:S(2)}) async-start(), calls=%async_computation.11 | async-start | bytes 9437184 | tf_op jit(solution)/shard_map/reduce_scatter | solution.py:48
  577.8 458.1 %all-gather.15.cloned.1.call-start = ((), (), s32[]{:S(2)}) async-start(), calls=%async_computation.8 | async-start | bytes 5898240 | tf_op jit(solution)/shard_map/all_gather | solution.py:44
  589.3 453.5 %all-gather.17.cloned.1.call-start = ((), (), s32[]{:S(2)}) async-start(), calls=%async_computation.10 | async-start | bytes 18874368 | tf_op jit(solution)/shard_map/all_gather | solution.py:44
  787.6 19.4 %collective-permute-start.31 = (bf16[1,256,1024]{2,1,0:T(8,128)(2,1)S(1)}, bf16[1,256,1024]{2,1,0:T(8,128)(2,1)S(1)}, u32[]{:S(2)}, u32[]{:S(2)}) collective-permute-start(bf16[1,256,1024]{2,1,0:T(8,128)(2,1)S(1)} %get-tuple-element.81), channel_id=1, source_target_pairs={{0,16},{4,20},{8,24},{12,28},{16,0},{20,4},{24,8},{28,12},{1,17},{... | collective-permute-start | bytes 1572872 | tf_op jit(solution)/shard_map/ppermute | solution.py:62
  804.1 39.8 %collective-permute-start.29 = (bf16[2,256,1024]{2,1,0:T(8,128)(2,1)S(1)}, bf16[2,256,1024]{2,1,0:T(8,128)(2,1)S(1)}, u32[]{:S(2)}, u32[]{:S(2)}) collective-permute-start(bf16[2,256,1024]{2,1,0:T(8,128)(2,1)S(1)} %pad_maximum_fusion.12), channel_id=1, source_target_pairs={{0,16},{4,20},{8,24},{12,28},{16,0},{20,4},{24,8},{28,12},{1,17},{... | collective-permute-start | bytes 3145736 | tf_op jit(solution)/shard_map/ppermute | solution.py:62
  807.1 38.5 %collective-permute-start.32 = (bf16[2,256,1024]{2,1,0:T(8,128)(2,1)S(1)}, bf16[2,256,1024]{2,1,0:T(8,128)(2,1)S(1)}, u32[]{:S(2)}, u32[]{:S(2)}) collective-permute-start(bf16[2,256,1024]{2,1,0:T(8,128)(2,1)S(1)} %pad_maximum_fusion.13), channel_id=1, source_target_pairs={{0,8},{4,12},{8,0},{12,4},{16,24},{20,28},{24,16},{28,20},{1,9},{5... | collective-permute-start | bytes 3145736 | tf_op jit(solution)/shard_map/ppermute | solution.py:62
  821.3 26.5 %collective-permute-start.8 = (bf16[256,1024]{1,0:T(8,128)(2,1)S(1)}, bf16[256,1024]{1,0:T(8,128)(2,1)}, u32[]{:S(2)}, u32[]{:S(2)}) collective-permute-start(bf16[256,1024]{1,0:T(8,128)(2,1)S(1)} %get-tuple-element.77), channel_id=1, source_target_pairs={{0,3},{1,0},{2,1},{3,2},{4,7},{5,4},{6,5},{7,6},{8,11},{9,8},{10,9... | collective-permute-start | bytes 1572872 | tf_op jit(solution)/shard_map/ppermute | solution.py:576
  824.6 63.1 %collective-permute-start.7 = (bf16[256,1024]{1,0:T(8,128)(2,1)S(1)}, bf16[256,1024]{1,0:T(8,128)(2,1)}, u32[]{:S(2)}, u32[]{:S(2)}) collective-permute-start(bf16[256,1024]{1,0:T(8,128)(2,1)S(1)} %get-tuple-element.78), channel_id=1, source_target_pairs={{0,2},{1,3},{2,0},{3,1},{4,6},{5,7},{6,4},{7,5},{8,10},{9,11},{10,... | collective-permute-start | bytes 1572872 | tf_op jit(solution)/shard_map/ppermute | solution.py:576
  824.6 63.1 %collective-permute-start.6 = (bf16[256,1024]{1,0:T(8,128)(2,1)S(1)}, bf16[256,1024]{1,0:T(8,128)(2,1)}, u32[]{:S(2)}, u32[]{:S(2)}) collective-permute-start(bf16[256,1024]{1,0:T(8,128)(2,1)S(1)} %get-tuple-element.73), channel_id=1, source_target_pairs={{0,1},{1,2},{2,3},{3,0},{4,5},{5,6},{6,7},{7,4},{8,9},{9,10},{10,1... | collective-permute-start | bytes 1572872 | tf_op jit(solution)/shard_map/ppermute | solution.py:576
  845.6 172.9 %collective-permute-start.30 = (bf16[4,256,1024]{2,1,0:T(8,128)(2,1)}, bf16[4,256,1024]{2,1,0:T(8,128)(2,1)}, u32[]{:S(2)}, u32[]{:S(2)}) collective-permute-start(bf16[4,256,1024]{2,1,0:T(8,128)(2,1)} %pad_maximum_fusion.8), channel_id=1, source_target_pairs={{0,4},{4,0},{8,12},{12,8},{16,20},{20,16},{24,28},{28,24},{1,5},{5... | collective-permute-start | bytes 6291464 | tf_op jit(solution)/shard_map/ppermute | solution.py:62
  847.3 175.0 %collective-permute-start.33 = (bf16[4,256,1024]{2,1,0:T(8,128)(2,1)}, bf16[4,256,1024]{2,1,0:T(8,128)(2,1)}, u32[]{:S(2)}, u32[]{:S(2)}) collective-permute-start(bf16[4,256,1024]{2,1,0:T(8,128)(2,1)} %pad_maximum_fusion.9), channel_id=1, source_target_pairs={{0,4},{4,0},{8,12},{12,8},{16,20},{20,16},{24,28},{28,24},{1,5},{5... | collective-permute-start | bytes 6291464 | tf_op jit(solution)/shard_map/ppermute | solution.py:62
  847.8 50.2 %collective-permute-start.11 = (bf16[256,1024]{1,0:T(8,128)(2,1)}, bf16[256,1024]{1,0:T(8,128)(2,1)S(1)}, u32[]{:S(2)}, u32[]{:S(2)}) collective-permute-start(bf16[256,1024]{1,0:T(8,128)(2,1)} %get-tuple-element.74), channel_id=1, source_target_pairs={{0,3},{1,0},{2,1},{3,2},{4,7},{5,4},{6,5},{7,6},{8,11},{9,8},{10,9... | collective-permute-start | bytes 1572872 | tf_op jit(solution)/shard_map/ppermute | solution.py:576
  887.7 46.9 %collective-permute-start.10 = (bf16[256,1024]{1,0:T(8,128)(2,1)}, bf16[256,1024]{1,0:T(8,128)(2,1)}, u32[]{:S(2)}, u32[]{:S(2)}) collective-permute-start(bf16[256,1024]{1,0:T(8,128)(2,1)} %get-tuple-element.75), channel_id=1, source_target_pairs={{0,2},{1,3},{2,0},{3,1},{4,6},{5,7},{6,4},{7,5},{8,10},{9,11},{10,... | collective-permute-start | bytes 1572872 | tf_op jit(solution)/shard_map/ppermute | solution.py:576
  887.8 48.3 %collective-permute-start.9 = (bf16[256,1024]{1,0:T(8,128)(2,1)}, bf16[256,1024]{1,0:T(8,128)(2,1)}, u32[]{:S(2)}, u32[]{:S(2)}) collective-permute-start(bf16[256,1024]{1,0:T(8,128)(2,1)} %get-tuple-element.76), channel_id=1, source_target_pairs={{0,1},{1,2},{2,3},{3,0},{4,5},{5,6},{6,7},{7,4},{8,9},{9,10},{10,1... | collective-permute-start | bytes 1572872 | tf_op jit(solution)/shard_map/ppermute | solution.py:576
  933.2 43.3 %collective-permute-start.27 = (f32[2048]{0:T(1024)S(1)}, f32[2048]{0:T(1024)S(1)}, u32[]{:S(2)}, u32[]{:S(2)}) collective-permute-start(f32[2048]{0:T(1024)S(1)} %add.153), channel_id=1, source_target_pairs={{0,2},{1,3},{2,0},{3,1},{4,6},{5,7},{6,4},{7,5},{8,10},{9,11},{10,... | collective-permute-start | bytes 24584 | tf_op jit(solution)/shard_map/ppermute | solution.py:74
  934.6 42.1 %collective-permute-start.22 = (f32[2048]{0:T(1024)S(1)}, f32[2048]{0:T(1024)S(1)}, u32[]{:S(2)}, u32[]{:S(2)}) collective-permute-start(f32[2048]{0:T(1024)S(1)} %add.148), channel_id=1, source_target_pairs={{0,2},{1,3},{2,0},{3,1},{4,6},{5,7},{6,4},{7,5},{8,10},{9,11},{10,... | collective-permute-start | bytes 24584 | tf_op jit(solution)/shard_map/ppermute | solution.py:74
  936.1 46.4 %collective-permute-start.15 = (bf16[256,2048]{1,0:T(8,128)(2,1)}, bf16[256,2048]{1,0:T(8,128)(2,1)}, u32[]{:S(2)}, u32[]{:S(2)}) collective-permute-start(bf16[256,2048]{1,0:T(8,128)(2,1)} %get-tuple-element.55), channel_id=1, source_target_pairs={{0,1},{1,2},{2,3},{3,0},{4,5},{5,6},{6,7},{7,4},{8,9},{9,10},{10,1... | collective-permute-start | bytes 3145736 | tf_op jit(solution)/shard_map/ppermute | solution.py:576
  976.4 30.1 %collective-permute-start.16 = (bf16[256,2048]{1,0:T(8,128)(2,1)}, bf16[256,2048]{1,0:T(8,128)(2,1)}, u32[]{:S(2)}, u32[]{:S(2)}) collective-permute-start(bf16[256,2048]{1,0:T(8,128)(2,1)} %get-tuple-element.56), channel_id=1, source_target_pairs={{0,2},{1,3},{2,0},{3,1},{4,6},{5,7},{6,4},{7,5},{8,10},{9,11},{10,... | collective-permute-start | bytes 3145736 | tf_op jit(solution)/shard_map/ppermute | solution.py:576
  976.8 35.5 %collective-permute-start.17 = (bf16[256,2048]{1,0:T(8,128)(2,1)}, bf16[256,2048]{1,0:T(8,128)(2,1)}, u32[]{:S(2)}, u32[]{:S(2)}) collective-permute-start(bf16[256,2048]{1,0:T(8,128)(2,1)} %get-tuple-element.57), channel_id=1, source_target_pairs={{0,3},{1,0},{2,1},{3,2},{4,7},{5,4},{6,5},{7,6},{8,11},{9,8},{10,9... | collective-permute-start | bytes 3145736 | tf_op jit(solution)/shard_map/ppermute | solution.py:576
  (35 other events, 529.5 us)
Sparse Core Ops, SparseCore 0:
  10.4 83.4 all-gather.18
  96.0 26.4 all-gather.22
  124.7 80.1 all-gather.20
  206.3 79.2 all-gather.10
  392.6 101.2 all-gather.12
Sparse Core Ops, SparseCore 1:
  14.4 36.2 reduce-scatter.4
  534.4 54.8 reduce-scatter.6
  593.3 116.0 reduce-scatter.8
  713.4 71.3 reduce-scatter.10
  786.7 59.3 all-gather.14
  848.0 89.9 all-gather.16

commit v7 on v6

--- a/solution.py
+++ b/solution.py
@@ -28,12 +28,6 @@
     return (jnp.cos(angles), jnp.sin(angles))
 
 
-def contract_rows(left_side, right_side):
-    return lax.dot_general(
-        left_side, right_side, (((0,), (0,)), ((), ())), preferred_element_type=jnp.float32
-    )
-
-
 def contract_cols(left_side, right_side):
     return lax.dot_general(
         left_side, right_side, (((1,), (1,)), ((), ())), preferred_element_type=jnp.float32
@@ -48,7 +42,7 @@
     return lax.psum_scatter(partial, axis, scatter_dimension=0, tiled=True)
 
 
-def cube_gather(blocks, axis):
+def cube_gather(blocks, axis, join=True):
     n = lax.axis_size(axis)
     bits = [1 << b for b in range(n.bit_length() - 1)]
     half = blocks.shape[-1] // 2
@@ -60,9 +54,10 @@
         held, offsets = part[None], [0]
         for bit in order:
             moved = lax.ppermute(held, axis, [(i, i ^ bit) for i in range(n)])
-            held = jnp.concatenate([held, moved], axis=0)
             offsets = offsets + [o ^ bit for o in offsets]
-        halves.append((held, tuple(offsets)))
+            if join or bit != order[-1]:
+                held = jnp.concatenate([held, moved], axis=0)
+        halves.append((held if join else (held, moved), tuple(offsets)))
     return halves
 
 
@@ -309,6 +304,7 @@
         gain_ref,
         hidden_ref,
         normed_ref,
+        turned_ref,
         weight_ref,
         wide_ref,
     ):
@@ -332,9 +328,9 @@
             wide_ref[...], weight_ref[...], preferred_element_type=jnp.float32
         )
         row_scale = lax.rsqrt(jnp.mean(hidden * hidden, axis=-1, keepdims=True) + EPS)
-        normed_ref[...] = (hidden * row_scale * gain_ref[...].astype(jnp.float32)).astype(
-            LOW
-        )
+        normed = hidden * row_scale * gain_ref[...].astype(jnp.float32)
+        normed_ref[...] = normed.astype(LOW)
+        turned_ref[...] = normed.T.astype(LOW)
 
         @pl.when(step == at_ref[0])
         def _():
@@ -355,6 +351,7 @@
             out_specs=[
                 pl.BlockSpec((tile, width), lambda i, at_ref: (0, 0)),
                 pl.BlockSpec((tile, width), lambda i, at_ref: (i, 0)),
+                pl.BlockSpec((width, tile), lambda i, at_ref: (0, i)),
             ],
             scratch_shapes=[
                 pltpu.VMEM((groups * group_columns, width), LOW),
@@ -364,9 +361,10 @@
         out_shape=[
             jax.ShapeDtypeStruct((tile, width), jnp.float32),
             jax.ShapeDtypeStruct((rows, width), LOW),
-        ],
-        cost_estimate=pl.CostEstimate(
-            flops=2 * rows * width * width, transcendentals=rows, bytes_accessed=20 << 20
+            jax.ShapeDtypeStruct((width, rows), LOW),
+        ],
+        cost_estimate=pl.CostEstimate(
+            flops=2 * rows * width * width, transcendentals=rows, bytes_accessed=24 << 20
         ),
         name="project_and_norm",
     )(places, all_heads, first, second, gathered, gain_vec.reshape(1, -1))
@@ -377,47 +375,49 @@
     columns = w_gate.shape[1]
     tile = 256
 
-    def kernel(normed_ref, gate_w_ref, up_w_ref, gate_ref, up_ref, active_ref):
+    def kernel(normed_ref, gate_w_ref, up_w_ref, active_ref, turned_ref, smooth_ref, slope_ref):
         gate = jnp.dot(normed_ref[...], gate_w_ref[...], preferred_element_type=jnp.float32)
         up = jnp.dot(normed_ref[...], up_w_ref[...], preferred_element_type=jnp.float32)
-        gate_ref[...] = gate
-        up_ref[...] = up
-        active_ref[...] = (gate * jax.nn.sigmoid(gate) * up).astype(LOW)
+        chance = jax.nn.sigmoid(gate)
+        smooth = gate * chance
+        active = smooth * up
+        active_ref[...] = active.astype(LOW)
+        turned_ref[...] = active.T.astype(LOW)
+        smooth_ref[...] = smooth.astype(LOW)
+        slope_ref[...] = (up * (chance * (1.0 + gate * (1.0 - chance)))).astype(LOW)
 
     column_block = pl.BlockSpec((rows, tile), lambda j: (0, j))
     weight_block = pl.BlockSpec((width, tile), lambda j: (0, j))
+    flat = jax.ShapeDtypeStruct((rows, columns), LOW)
     return pl.pallas_call(
         kernel,
         grid=(columns // tile,),
         in_specs=[pl.BlockSpec((rows, width), lambda j: (0, 0)), weight_block, weight_block],
-        out_specs=[column_block] * 3,
-        out_shape=[
-            jax.ShapeDtypeStruct((rows, columns), jnp.float32),
-            jax.ShapeDtypeStruct((rows, columns), jnp.float32),
-            jax.ShapeDtypeStruct((rows, columns), LOW),
-        ],
+        out_specs=[
+            column_block,
+            pl.BlockSpec((tile, rows), lambda j: (j, 0)),
+            column_block,
+            column_block,
+        ],
+        out_shape=[flat, jax.ShapeDtypeStruct((columns, rows), LOW), flat, flat],
         cost_estimate=pl.CostEstimate(
             flops=4 * rows * width * columns,
             transcendentals=rows * columns,
-            bytes_accessed=40 << 20,
+            bytes_accessed=36 << 20,
         ),
         name="gated_up",
     )(normed, w_gate, w_up)
 
 
-def gated_back(all_cot, w_down, gate_proj, up_proj):
+def gated_back(all_cot, w_down, smooth, slope):
     rows, width = all_cot.shape
     columns = w_down.shape[0]
     tile = 256
 
-    def kernel(cot_ref, weight_ref, gate_ref, up_ref, d_gate_ref, d_up_ref):
+    def kernel(cot_ref, weight_ref, smooth_ref, slope_ref, d_gate_ref, d_up_ref):
         d_active = dot_lanes(cot_ref[...], weight_ref[...])
-        gate = gate_ref[...]
-        chance = jax.nn.sigmoid(gate)
-        smooth = gate * chance
-        d_up_ref[...] = (d_active * smooth).astype(LOW)
-        slope = chance * (1.0 + gate * (1.0 - chance))
-        d_gate_ref[...] = (d_active * up_ref[...] * slope).astype(LOW)
+        d_up_ref[...] = (d_active * smooth_ref[...].astype(jnp.float32)).astype(LOW)
+        d_gate_ref[...] = (d_active * slope_ref[...].astype(jnp.float32)).astype(LOW)
 
     column_block = pl.BlockSpec((rows, tile), lambda j: (0, j))
     return pl.pallas_call(
@@ -432,12 +432,55 @@
         out_specs=[column_block] * 2,
         out_shape=[jax.ShapeDtypeStruct((rows, columns), LOW)] * 2,
         cost_estimate=pl.CostEstimate(
-            flops=2 * rows * width * columns,
-            transcendentals=rows * columns,
-            bytes_accessed=36 << 20,
+            flops=2 * rows * width * columns, transcendentals=0, bytes_accessed=28 << 20
         ),
         name="gated_back",
-    )(all_cot, w_down, gate_proj, up_proj)
+    )(all_cot, w_down, smooth, slope)
+
+
+def product(left, rights, folds):
+    rows, depth = left.shape
+    each = rights[0].shape[1]
+    tile = 512
+    row_steps, column_steps = rows // tile, each // tile
+    count = len(rights)
+    per = count * column_steps // folds
+
+    def kernel(left_ref, *refs):
+        out_ref = refs[count]
+        for k in range(count):
+
+            def _(k=k):
+                out_ref[...] = jnp.dot(
+                    left_ref[...], refs[k][...], preferred_element_type=jnp.float32
+                ).astype(LOW)
+
+            if count == 1:
+                _()
+            else:
+                pl.when(pl.program_id(1) // column_steps == k)(_)
+
+    def right_block(k):
+        return pl.BlockSpec(
+            (depth, tile), lambda i, j: (0, jnp.clip(j - k * column_steps, 0, column_steps - 1))
+        )
+
+    return pl.pallas_call(
+        kernel,
+        grid=(row_steps, count * column_steps),
+        in_specs=[pl.BlockSpec((tile, depth), lambda i, j: (i, 0))]
+        + [right_block(k) for k in range(count)],
+        out_specs=pl.BlockSpec(
+            (tile, tile), lambda i, j: (i + (j // per) * row_steps, j % per)
+        ),
+        out_shape=jax.ShapeDtypeStruct((rows * folds, count * each // folds), LOW),
+        cost_estimate=pl.CostEstimate(
+            flops=2 * rows * depth * count * each,
+            transcendentals=0,
+            bytes_accessed=2 * (rows * depth + (depth + rows) * count * each),
+        ),
+        name="product",
+    )(left, *rights)
 
 
 def pair_product(places, tile, first, first_weight, second, second_weight):
@@ -579,29 +622,38 @@
 
 def place_blocks(halves, axis):
     (first, first_offsets), (second, second_offsets) = halves
-    parts, rows, half = first.shape
-
-    def kernel(at_ref, first_ref, second_ref, out_ref):
-        out_ref[:, :half] = first_ref[0].astype(jnp.float32)
-        out_ref[:, half:] = second_ref[0].astype(jnp.float32)
+    some, rows, half = first[0].shape
+    parts = 2 * some
+
+    def kernel(at_ref, *refs):
+        out_ref = refs[4]
+        k = pl.program_id(0)
+        for side, offsets in enumerate((first_offsets, second_offsets)):
+            columns = slice(side * half, (side + 1) * half)
+            late = functools.reduce(
+                jnp.logical_or, [k == offset for offset in offsets[some:]]
+            )
+            early_ref, late_ref = refs[2 * side : 2 * side + 2]
+            out_ref[:, columns] = jnp.where(late, late_ref[0], early_ref[0]).astype(jnp.float32)
 
     def entry(offsets):
-        where = [offsets.index(k) for k in range(parts)]
-
         def index(k, at_ref):
-            found = where[0]
-            for candidate in range(1, parts):
-                found = jnp.where(k == candidate, where[candidate], found)
+            found = 0
+            for at, offset in enumerate(offsets):
+                found = jnp.where(k == offset, at, found)
             return (found, 0, 0)
 
         return pl.BlockSpec((1, rows, half), index)
 
+    specs = []
+    for offsets in (first_offsets, second_offsets):
+        specs += [entry(offsets[:some]), entry(offsets[some:])]
     return pl.pallas_call(
         kernel,
         grid_spec=pltpu.PrefetchScalarGridSpec(
             num_scalar_prefetch=1,
             grid=(parts,),
-            in_specs=[entry(first_offsets), entry(second_offsets)],
+            in_specs=specs,
             out_specs=pl.BlockSpec((rows, 2 * half), lambda k, at_ref: (at_ref[0] ^ k, 0)),
         ),
         out_shape=jax.ShapeDtypeStruct((parts * rows, 2 * half), jnp.float32),
@@ -609,7 +661,7 @@
             flops=0, transcendentals=0, bytes_accessed=12 * parts * rows * half
         ),
         name="place_blocks",
-    )(lax.axis_index(axis).reshape(1), first, second)
+    )(lax.axis_index(axis).reshape(1), *first, *second)
 
 
 def unpack_attention(shared, q_columns, k_columns, folds):
@@ -717,11 +769,11 @@
     heads_out, heads_rows, totals = attend(projected, group)
     all_heads = lax.all_gather(heads_out, TP, axis=0)
     all_cot = gather_rows(cotangent, TP)
-    hidden_state, normed2 = project_and_norm(
+    hidden_state, normed2, normed2_rows = project_and_norm(
         all_heads, all_output, gathered, norm2_gain.astype(jnp.float32) + nothing.astype(jnp.float32)
     )
-    gate_proj, up_proj, activated = gated_up(normed2, w_gate, w_up)
-    mlp_part = jnp.dot(activated, w_down, preferred_element_type=jnp.float32).astype(LOW)
+    activated, active_rows, smooth, slope = gated_up(normed2, w_gate, w_up)
+    mlp_part = product(activated, [w_down], 1)
     half_width = width // 2
 
     def part_of(columns):
@@ -736,18 +788,13 @@
         hidden_state
         + jnp.concatenate([add_all(first_half), add_all(second_half)], axis=1)
     ).astype(LOW)
-    d_gate, d_up = gated_back(all_cot, w_down, gate_proj, up_proj)
-    grad_down = row_major(split_columns(contract_rows(activated, all_cot).astype(LOW), ff_folds))
+    d_gate, d_up = gated_back(all_cot, w_down, smooth, slope)
+    grad_down = product(active_rows, [all_cot], ff_folds)
     part_down = scatter_sum(grad_down, DP)
     dn2_blocks = exchange(
         lambda places: pair_product(places, own_rows, d_gate, w_gate, d_up, w_up), TP
     )
-    gate_up_grads = row_major(
-        jnp.concatenate(
-            [contract_rows(normed2, d_gate).astype(LOW), contract_rows(normed2, d_up).astype(LOW)],
-            axis=1,
-        )
-    )
+    gate_up_grads = product(normed2_rows, [d_gate, d_up], 1)
     part_gate_up = scatter_sum(gate_up_grads, DP)
     d_state, state_low, gain_two = norm_back(hidden_state, norm2_gain, cotangent, dn2_blocks)
     d_state_low = gather_rows(state_low, TP)
@@ -774,7 +821,7 @@
         jnp.concatenate([grad_qkv, split_columns(grad_output, folds)], axis=1)
     )
     part_attn = scatter_sum(low_attn, DP)
-    down_halves = cube_gather(part_down, DP)
+    down_halves = cube_gather(part_down, DP, join=False)
     full_down = join_columns(place_blocks(down_halves, DP), ff_folds)
     shared_ff = row_major(gather_rows(part_gate_up, DP))
     shared_attn = row_major(gather_rows(part_attn, DP))

time: 1090 us -> 1090 us (level)
  Pallas kernels: 177 us -> 255 us
  matrix products: 63.1 us -> 14.6 us
  waiting for transfers between devices: 666 us -> 647 us
  other arithmetic: 64 us -> 52.1 us
    pallas_call x0 -> x3, Pallas kernels: none -> 75.5 us  [product(): pl.pallas_call(kernel, grid=(row_steps, count * column_steps), in_specs=[...]
    dot_general x4 -> x0, matrix products: 48.5 us -> none  [the longest x3 36 us: contract_rows(): lax.dot_general(left_side, right_side, (((0,), (0,)), ((), ())), preferre...]
    reduce_scatter x4, waiting for transfers between devices: 207 us -> 190 us  [scatter_sum(): return lax.psum_scatter(partial, axis, scatter_dimension=0, tiled=True)]
    concatenate x12 -> x10, other arithmetic: 26.6 us -> 21.6 us  [cube_gather(): held = jnp.concatenate([held, moved], axis=0)]
  transfers between devices with their start and end apart: 45 -> 45, of which waited for: 27 -> 26; matrix products, arithmetic and copies ran while one was open for 12% -> 6% of each run, Pallas kernels for 11% -> 19%
where the time goes in v7:
time: 1090 us; the launch traced here: 1070 us
  waiting for transfers between devices  647 us (59%)
  Pallas kernels  255 us (23%)
  other arithmetic  52.1 us (5%)
  starting transfers between devices  46.7 us (4%)
  local copies, waits for them, and re-layouts  35.4 us (3%)
  between operations  16.5 us (2%)
  matrix products  14.6 us (1%)
    reduce_scatter x4, waiting for transfers between devices, scatter_sum(): return lax.psum_scatter(partial, axis, scatter_dimension=0, tiled=True)  190 us
    all_gather x4, waiting for transfers between devices, gather_rows(): return lax.all_gather(block, axis, axis=0, tiled=True)  138 us
    ppermute x12, waiting for transfers between devices, exchange(): moved.append(lax.ppermute(made[hop - 1], axis, pairs))  116 us
    pallas_call x3, Pallas kernels, product(): pl.pallas_call(kernel, grid=(row_steps, count * column_steps), in_specs=[...  75.5 us
    all_gather x1, waiting for transfers between devices, block(): gathered = lax.all_gather(tokens, TP, axis=0)  59.3 us
    ppermute x12, waiting for transfers between devices, cube_gather(): moved = lax.ppermute(held, axis, [(i, i ^ bit) for i in range(n)])  59.2 us
    ppermute x10, waiting for transfers between devices, cube_sum(): lax.ppermute(vector, axis, [(i, i ^ bit) for i in range(n)])  52.1 us
    pallas_call x2, Pallas kernels, pair_product(): pl.pallas_call(kernel, grid_spec=pltpu.PrefetchScalarGridSpec(num_scalar_...  30.2 us
  transfers between devices with their start and end apart: 45, of which 26 were waited for; matrix products, arithmetic and copies ran while one was open for 6% of the time, Pallas kernels for 19%

profile of v7, /device:TPU:0, one launch (start us, length us, event | category | flops | bytes accessed | tf_op | source)
XLA Modules:
  0.0 1067.7 jit_solution(12706460643529788927)
XLA Ops:
  34.6 59.3 %all-gather.19.cloned.1.call-done = bf16[1024,2048]{1,0:T(8,128)(2,1)} async-done(((bf16[256,2048]{1,0:T(8,128)(2,1)}), bf16[1024,2048]{1,0:T(8,128)(2,1)}) %all-gather.19.cloned.1.call-update) | async-done | bytes 4194320 | tf_op jit(solution)/shard_map/all_gather | solution.py:754
  93.9 8.4 norm_project.1
  102.3 13.7 %attend.1 = (bf16[1024,512]{1,0:T(8,128)(2,1)}, bf16[512,1024]{1,0:T(8,128)(2,1)}, f32[2,4,1024]{2,1,0:T(4,128)}) custom-call(bf16[768,1024]{1,0:T(8,128)(2,1)} %get-tuple-element.42.packed_ref), custom_call_target="tpu_custom_call" | custom-call | flops 1073741824 | bytes 4194304 | tf_op jit(solution)/shard_map/attend/pallas_call | solution.py:185
  116.0 6.5 all-gather.23.cloned.1.call-done
  126.9 10.2 collective-permute-done
  143.7 19.3 %collective-permute-done.1 = bf16[2,4,64,1024]{3,2,1,0:T(8,128)(2,1)} collective-permute-done((bf16[2,4,64,1024]{3,2,1,0:T(8,128)(2,1)}, bf16[2,4,64,1024]{3,2,1,0:T(8,128)(2,1)}, u32[]{:S(2)}, u32[]{:S(2)}) %collective-permute-start.1) | collective-permute-done | bytes 1048608 | tf_op jit(solution)/shard_map/ppermute | solution.py:56
  180.8 24.0 %all-gather.21.cloned.1.call-done = bf16[4096,512]{1,0:T(8,128)(2,1)} async-done(((bf16[1024,512]{1,0:T(8,128)(2,1)}), bf16[4096,512]{1,0:T(8,128)(2,1)}) %all-gather.21.cloned.1.call-update) | async-done | bytes 4194320 | tf_op jit(solution)/shard_map/all_gather | solution.py:770
  204.8 18.8 %project_and_norm.1 = (f32[256,2048]{1,0:T(8,128)}, bf16[1024,2048]{1,0:T(8,128)(2,1)}, bf16[2048,1024]{1,0:T(8,128)(2,1)}) custom-call(s32[2]{0:T(128)} %pad_add_fusion.at_ref, bf16[4,1024,512]{2,1,0:T(8,128)(2,1)} %bitcast.60, bf16[8,4,64,1024]{3,2,1,0:T(8,128)(2,1)} %pad_maximum_fusion.1.first_ref, bf16[8,4,64,1024]{3,2,1,0:T(8,128)(2,1)} %pad_maximum_fusion.2.second_ref, ...), custom_call_target="tpu_custom_call" | custom-call | flops 8589934592 | bytes 25165824 | tf_op jit(solution)/shard_map/project_and_norm/pallas_call | solution.py:339
  223.6 25.1 %gated_up.1 = (bf16[1024,2048]{1,0:T(8,128)(2,1)}, bf16[2048,1024]{1,0:T(8,128)(2,1)}, bf16[1024,2048]{1,0:T(8,128)(2,1)}, bf16[1024,2048]{1,0:T(8,128)(2,1)}) custom-call(bf16[1024,2048]{1,0:T(8,128)(2,1)} %get-tuple-element.45.normed_ref, bf16[2048,2048]{1,0:T(8,128)(2,1)} %first_w_ref.3, bf16[2048,2048]{1,0:T(8,128)(2,1)} %second_w_ref.3), custom_call_target="tpu_custom_call" | custom-call | flops 17179869184 | bytes 37748736 | tf_op jit(solution)/shard_map/gated_up/pallas_call | solution.py:392
  248.7 36.8 %all-gather.11.cloned.1.call-done.cot_ref.refs_0_ = bf16[1024,2048]{1,0:T(8,128)(2,1)} async-done(((bf16[256,2048]{1,0:T(8,128)(2,1)}), bf16[1024,2048]{1,0:T(8,128)(2,1)}) %all-gather.11.cloned.1.call-update) | async-done | bytes 4194320 | tf_op jit(solution)/shard_map/all_gather | solution.py:38
  285.5 17.0 %gated_back.1 = (bf16[1024,2048]{1,0:T(8,128)(2,1)}, bf16[1024,2048]{1,0:T(8,128)(2,1)}) custom-call(bf16[1024,2048]{1,0:T(8,128)(2,1)} %all-gather.11.cloned.1.call-done.cot_ref.refs_0_, bf16[2048,2048]{1,0:T(8,128)(2,1)} %weight_ref.1, bf16[1024,2048]{1,0:T(8,128)(2,1)} %get-tuple-element.47.smooth_ref, bf16[1024,2048]{1,0:T(8,128)(2,1)} %get-tuple-element.48.slope_ref), custom_call_target="tpu_custom_call" | custom-call | flops 8589934592 | bytes 29360128 | tf_op jit(solution)/shard_map/gated_back/pallas_call | solution.py:423
  302.5 10.0 pair_product.2
  312.5 20.2 %pair_product.3 = (bf16[256,2048]{1,0:T(8,128)(2,1)}, bf16[256,2048]{1,0:T(8,128)(2,1)}, bf16[256,2048]{1,0:T(8,128)(2,1)}) custom-call(s32[3]{0:T(128)} %pad_add_fusion.1.at_ref, bf16[1024,2048]{1,0:T(8,128)(2,1)} %get-tuple-element.49.first_ref.refs_0_, bf16[1024,2048]{1,0:T(8,128)(2,1)} %get-tuple-element.50.second_ref.refs_1_, ...), custom_call_target="tpu_custom_call" | custom-call | flops 12884901888 | bytes 20971520 | tf_op jit(solution)/shard_map/pair_product/pallas_call | solution.py:511
  340.6 43.8 %collective-permute-done.13.refs_1_ = bf16[256,2048]{1,0:T(8,128)(2,1)} collective-permute-done((bf16[256,2048]{1,0:T(8,128)(2,1)}, bf16[256,2048]{1,0:T(8,128)(2,1)}, u32[]{:S(2)}, u32[]{:S(2)}) %collective-permute-start.13) | collective-permute-done | bytes 1048608 | tf_op jit(solution)/shard_map/ppermute | solution.py:619
  390.8 101.2 %all-gather.13.cloned.1.call-done = bf16[1024,2048]{1,0:T(8,128)(2,1)} async-done(((bf16[256,2048]{1,0:T(8,128)(2,1)}), bf16[1024,2048]{1,0:T(8,128)(2,1)}) %all-gather.13.cloned.1.call-update) | async-done | bytes 4194320 | tf_op jit(solution)/shard_map/all_gather | solution.py:38
  503.1 20.2 %attend_back.1.d_ref = bf16[768,1024]{1,0:T(8,128)(2,1)} custom-call(bf16[768,1024]{1,0:T(8,128)(2,1)} %get-tuple-element.42.packed_ref, bf16[512,1024]{1,0:T(8,128)(2,1)} %fusion.1.d_heads_ref, f32[2,4,1024]{2,1,0:T(4,128)} %get-tuple-element.56.total_ref, f32[32,512]{1,0:T(8,128)} %get-tuple-element.94.cos_ref, f32[32,512]{1,0:T(8,128)} %get-tuple-element.93.sin_ref), custom_call_target="tpu_custom_call" | custom-call | flops 2684354560 | bytes 6291456 | tf_op jit(solution)/shard_map/attend_back/pallas_call | solution.py:265
  523.3 6.4 convolution_convert_fusion
  532.5 38.6 %product.4 = bf16[2048,4096]{1,0:T(8,128)(2,1)} custom-call(bf16[2048,1024]{1,0:T(8,128)(2,1)} %get-tuple-element.71.left_ref, bf16[1024,2048]{1,0:T(8,128)(2,1)} %get-tuple-element.49.first_ref.refs_0_, bf16[1024,2048]{1,0:T(8,128)(2,1)} %get-tuple-element.50.second_ref.refs_1_), custom_call_target="tpu_custom_call" | custom-call | flops 17179869184 | bytes 29360128 | tf_op jit(solution)/shard_map/product/pallas_call | solution.py:468
  571.4 20.5 %product.5 = bf16[2048,2048]{1,0:T(8,128)(2,1)} custom-call(bf16[2048,1024]{1,0:T(8,128)(2,1)} %get-tuple-element.72.left_ref, bf16[1024,2048]{1,0:T(8,128)(2,1)} %all-gather.11.cloned.1.call-done.cot_ref.refs_0_), custom_call_target="tpu_custom_call" | custom-call | flops 8589934592 | bytes 16777216 | tf_op jit(solution)/shard_map/product/pallas_call | solution.py:468
  592.7 114.7 %reduce-scatter.9.cloned.1.call-done = bf16[256,4096]{1,0:T(8,128)(2,1)} async-done(((bf16[2048,4096]{1,0:T(8,128)(2,1)}), bf16[256,4096]{1,0:T(8,128)(2,1)}) %reduce-scatter.9.cloned.1.call-update) | async-done | bytes 2097168 | tf_op jit(solution)/shard_map/reduce_scatter | solution.py:42
  707.5 75.4 %reduce-scatter.11.cloned.1.call-done = bf16[256,2048]{1,0:T(8,128)(2,1)} async-done(((bf16[2048,2048]{1,0:T(8,128)(2,1)}), bf16[256,2048]{1,0:T(8,128)(2,1)}) %reduce-scatter.11.cloned.1.call-update) | async-done | bytes 1048592 | tf_op jit(solution)/shard_map/reduce_scatter | solution.py:42
  786.3 15.6 %collective-permute-done.28 = bf16[1,256,1024]{2,1,0:T(8,128)(2,1)S(1)} collective-permute-done((bf16[1,256,1024]{2,1,0:T(8,128)(2,1)S(1)}, bf16[1,256,1024]{2,1,0:T(8,128)(2,1)S(1)}, u32[]{:S(2)}, u32[]{:S(2)}) %collective-permute-start.28) | collective-permute-done | bytes 524320 | tf_op jit(solution)/shard_map/ppermute | solution.py:56
  805.6 16.4 %product.3 = bf16[1024,2048]{1,0:T(8,128)(2,1)} custom-call(bf16[1024,2048]{1,0:T(8,128)(2,1)} %get-tuple-element.46.left_ref, bf16[2048,2048]{1,0:T(8,128)(2,1)} %weight_ref.1), custom_call_target="tpu_custom_call" | custom-call | flops 8589934592 | bytes 16777216 | tf_op jit(solution)/shard_map/product/pallas_call | solution.py:468
  828.9 13.6 %collective-permute-done.29 = bf16[2,256,1024]{2,1,0:T(8,128)(2,1)} collective-permute-done((bf16[2,256,1024]{2,1,0:T(8,128)(2,1)}, bf16[2,256,1024]{2,1,0:T(8,128)(2,1)}, u32[]{:S(2)}, u32[]{:S(2)}) %collective-permute-start.29) | collective-permute-done | bytes 1048608 | tf_op jit(solution)/shard_map/ppermute | solution.py:56
  852.0 39.0 %collective-permute-done.7 = bf16[256,1024]{1,0:T(8,128)(2,1)} collective-permute-done((bf16[256,1024]{1,0:T(8,128)(2,1)S(1)}, bf16[256,1024]{1,0:T(8,128)(2,1)}, u32[]{:S(2)}, u32[]{:S(2)}) %collective-permute-start.7) | collective-permute-done | bytes 524320 | tf_op jit(solution)/shard_map/ppermute | solution.py:619
  891.0 8.8 projection_back.3
  922.7 8.3 collective-permute-start.26
  941.3 39.0 %collective-permute-done.27 = f32[2048]{0:T(1024)S(1)} collective-permute-done((f32[2048]{0:T(1024)S(1)}, f32[2048]{0:T(1024)S(1)}, u32[]{:S(2)}, u32[]{:S(2)}) %collective-permute-start.27) | collective-permute-done | bytes 8224 | tf_op jit(solution)/shard_map/ppermute | solution.py:69
  986.4 23.7 %collective-permute-done.16.refs_1_ = bf16[256,2048]{1,0:T(8,128)(2,1)} collective-permute-done((bf16[256,2048]{1,0:T(8,128)(2,1)}, bf16[256,2048]{1,0:T(8,128)(2,1)}, u32[]{:S(2)}, u32[]{:S(2)}) %collective-permute-start.16) | collective-permute-done | bytes 1048608 | tf_op jit(solution)/shard_map/ppermute | solution.py:619
  1022.3 13.9 %place_blocks.1 = f32[2048,2048]{1,0:T(8,128)} custom-call(s32[1]{0:T(128)} %bitcast.1.at_ref, bf16[4,256,1024]{2,1,0:T(8,128)(2,1)} %pad_maximum_fusion.5.refs_0_, bf16[4,256,1024]{2,1,0:T(8,128)(2,1)} %collective-permute-done.30.refs_1_, bf16[4,256,1024]{2,1,0:T(8,128)(2,1)} %pad_maximum_fusion.6.refs_2_, bf16[4,256,1024]{2,1,0:T(8,128)(2,1)} %collective-permute-done.33.refs_3_), custom_call_target="tpu_custom_call" | custom-call | bytes 25165824 | tf_op jit(solution)/shard_map/place_blocks/pallas_call | solution.py:651
  1036.2 7.0 unpack_attention.1
  1043.1 17.2 %slice_convert_fusion = (f32[2048,2048]{1,0:T(8,128)}, f32[2048,2048]{1,0:T(8,128)}) fusion(bf16[2048,4096]{1,0:T(8,128)(2,1)} %all-gather.17.cloned.1.call-done), kind=kLoop, calls=%fused_computation | loop fusion | flops 8388608 | bytes 50331648 | tf_op jit(solution)/shard_map/convert_element_type | solution.py:830
  (181 shorter events, 158.8 us)
Async XLA Ops:
  8.0 85.9 %all-gather.19.cloned.1.call-start = ((), (), s32[]{:S(2)}) async-start(), calls=%async_computation.12 | async-start | bytes 5242880 | tf_op jit(solution)/shard_map/all_gather | solution.py:754
  8.8 113.8 %all-gather.23.cloned.1.call-start = ((), (), s32[]{:S(2)}) async-start(), calls=%async_computation.14 | async-start | bytes 1310720 | tf_op jit(solution)/shard_map/all_gather | solution.py:756
  10.4 160.7 %reduce-scatter.5.cloned.1.call-start = ((), (), s32[]{:S(2)}) async-start(), calls=%async_computation.4 | async-start | bytes 73728 | tf_op jit(solution)/shard_map/reduce_scatter | solution.py:42
  11.9 192.9 %all-gather.21.cloned.1.call-start = ((), (), s32[]{:S(2)}) async-start(), calls=%async_computation.13 | async-start | bytes 5242880 | tf_op jit(solution)/shard_map/all_gather | solution.py:770
  116.0 169.5 %all-gather.11.cloned.1.call-start = ((), (), s32[]{:S(2)}) async-start(), calls=%async_computation.5 | async-start | bytes 5242880 | tf_op jit(solution)/shard_map/all_gather | solution.py:38
  139.0 24.0 %collective-permute-start.1 = (bf16[2,4,64,1024]{3,2,1,0:T(8,128)(2,1)}, bf16[2,4,64,1024]{3,2,1,0:T(8,128)(2,1)}, u32[]{:S(2)}, u32[]{:S(2)}) collective-permute-start(bf16[2,4,64,1024]{3,2,1,0:T(8,128)(2,1)} %pad_maximum_fusion.7), channel_id=1, source_target_pairs={{0,16},{4,20},{8,24},{12,28},{16,0},{20,4},{24,8},{28,12},{1,17},{... | collective-permute-start | bytes 3145736 | tf_op jit(solution)/shard_map/ppermute | solution.py:56
  140.5 351.5 %all-gather.13.cloned.1.call-start = ((), (), s32[]{:S(2)}) async-start(), calls=%async_computation.6 | async-start | bytes 5242880 | tf_op jit(solution)/shard_map/all_gather | solution.py:38
  142.1 23.7 %collective-permute-start.4 = (bf16[2,4,64,1024]{3,2,1,0:T(8,128)(2,1)S(1)}, bf16[2,4,64,1024]{3,2,1,0:T(8,128)(2,1)S(1)}, u32[]{:S(2)}, u32[]{:S(2)}) collective-permute-start(bf16[2,4,64,1024]{3,2,1,0:T(8,128)(2,1)S(1)} %pad_maximum_fusion.8), channel_id=1, source_target_pairs={{0,8},{4,12},{8,0},{12,4},{16,24},{20,28},{24,16},{28,20},{1,9},{5... | collective-permute-start | bytes 3145736 | tf_op jit(solution)/shard_map/ppermute | solution.py:56
  312.4 28.1 %collective-permute-start.12 = (bf16[256,2048]{1,0:T(8,128)(2,1)}, bf16[256,2048]{1,0:T(8,128)(2,1)S(1)}, u32[]{:S(2)}, u32[]{:S(2)}) collective-permute-start(bf16[256,2048]{1,0:T(8,128)(2,1)} %pair_product.2), channel_id=1, source_target_pairs={{0,1},{1,2},{2,3},{3,0},{4,5},{5,6},{6,7},{7,4},{8,9},{9,10},{10,1... | collective-permute-start | bytes 3145736 | tf_op jit(solution)/shard_map/ppermute | solution.py:619
  332.7 51.7 %collective-permute-start.13 = (bf16[256,2048]{1,0:T(8,128)(2,1)}, bf16[256,2048]{1,0:T(8,128)(2,1)}, u32[]{:S(2)}, u32[]{:S(2)}) collective-permute-start(bf16[256,2048]{1,0:T(8,128)(2,1)} %get-tuple-element.51), channel_id=1, source_target_pairs={{0,2},{1,3},{2,0},{3,1},{4,6},{5,7},{6,4},{7,5},{8,10},{9,11},{10,... | collective-permute-start | bytes 3145736 | tf_op jit(solution)/shard_map/ppermute | solution.py:619
  333.8 50.5 %collective-permute-start.14 = (bf16[256,2048]{1,0:T(8,128)(2,1)}, bf16[256,2048]{1,0:T(8,128)(2,1)}, u32[]{:S(2)}, u32[]{:S(2)}) collective-permute-start(bf16[256,2048]{1,0:T(8,128)(2,1)} %get-tuple-element.52), channel_id=1, source_target_pairs={{0,3},{1,0},{2,1},{3,2},{4,7},{5,4},{6,5},{7,6},{8,11},{9,8},{10,9... | collective-permute-start | bytes 3145736 | tf_op jit(solution)/shard_map/ppermute | solution.py:619
  390.6 201.4 %reduce-scatter.7.cloned.1.call-start = ((), (), s32[]{:S(2)}) async-start(), calls=%async_computation.7 | async-start | bytes 5898240 | tf_op jit(solution)/shard_map/reduce_scatter | solution.py:42
  532.4 175.0 %reduce-scatter.9.cloned.1.call-start = ((), (), s32[]{:S(2)}) async-start(), calls=%async_computation.9 | async-start | bytes 18874368 | tf_op jit(solution)/shard_map/reduce_scatter | solution.py:42
  571.1 211.8 %reduce-scatter.11.cloned.1.call-start = ((), (), s32[]{:S(2)}) async-start(), calls=%async_computation.11 | async-start | bytes 9437184 | tf_op jit(solution)/shard_map/reduce_scatter | solution.py:42
  591.9 444.2 %all-gather.15.cloned.1.call-start = ((), (), s32[]{:S(2)}) async-start(), calls=%async_computation.8 | async-start | bytes 5898240 | tf_op jit(solution)/shard_map/all_gather | solution.py:38
  592.7 450.4 %all-gather.17.cloned.1.call-start = ((), (), s32[]{:S(2)}) async-start(), calls=%async_computation.10 | async-start | bytes 18874368 | tf_op jit(solution)/shard_map/all_gather | solution.py:38
  785.7 19.0 %collective-permute-start.31 = (bf16[1,256,1024]{2,1,0:T(8,128)(2,1)S(1)}, bf16[1,256,1024]{2,1,0:T(8,128)(2,1)S(1)}, u32[]{:S(2)}, u32[]{:S(2)}) collective-permute-start(bf16[1,256,1024]{2,1,0:T(8,128)(2,1)S(1)} %get-tuple-element.85), channel_id=1, source_target_pairs={{0,16},{4,20},{8,24},{12,28},{16,0},{20,4},{24,8},{28,12},{1,17},{... | collective-permute-start | bytes 1572872 | tf_op jit(solution)/shard_map/ppermute | solution.py:56
  802.9 39.6 %collective-permute-start.29 = (bf16[2,256,1024]{2,1,0:T(8,128)(2,1)}, bf16[2,256,1024]{2,1,0:T(8,128)(2,1)}, u32[]{:S(2)}, u32[]{:S(2)}) collective-permute-start(bf16[2,256,1024]{2,1,0:T(8,128)(2,1)} %pad_maximum_fusion.9), channel_id=1, source_target_pairs={{0,16},{4,20},{8,24},{12,28},{16,0},{20,4},{24,8},{28,12},{1,17},{... | collective-permute-start | bytes 3145736 | tf_op jit(solution)/shard_map/ppermute | solution.py:56
  804.8 40.5 %collective-permute-start.32 = (bf16[2,256,1024]{2,1,0:T(8,128)(2,1)S(1)}, bf16[2,256,1024]{2,1,0:T(8,128)(2,1)}, u32[]{:S(2)}, u32[]{:S(2)}) collective-permute-start(bf16[2,256,1024]{2,1,0:T(8,128)(2,1)S(1)} %pad_maximum_fusion.10), channel_id=1, source_target_pairs={{0,8},{4,12},{8,0},{12,4},{16,24},{20,28},{24,16},{28,20},{1,9},{5... | collective-permute-start | bytes 3145736 | tf_op jit(solution)/shard_map/ppermute | solution.py:56
  825.1 23.5 %collective-permute-start.8 = (bf16[256,1024]{1,0:T(8,128)(2,1)S(1)}, bf16[256,1024]{1,0:T(8,128)(2,1)}, u32[]{:S(2)}, u32[]{:S(2)}) collective-permute-start(bf16[256,1024]{1,0:T(8,128)(2,1)S(1)} %get-tuple-element.81), channel_id=1, source_target_pairs={{0,3},{1,0},{2,1},{3,2},{4,7},{5,4},{6,5},{7,6},{8,11},{9,8},{10,9... | collective-permute-start | bytes 1572872 | tf_op jit(solution)/shard_map/ppermute | solution.py:619
  827.8 63.1 %collective-permute-start.7 = (bf16[256,1024]{1,0:T(8,128)(2,1)S(1)}, bf16[256,1024]{1,0:T(8,128)(2,1)}, u32[]{:S(2)}, u32[]{:S(2)}) collective-permute-start(bf16[256,1024]{1,0:T(8,128)(2,1)S(1)} %get-tuple-element.82), channel_id=1, source_target_pairs={{0,2},{1,3},{2,0},{3,1},{4,6},{5,7},{6,4},{7,5},{8,10},{9,11},{10,... | collective-permute-start | bytes 1572872 | tf_op jit(solution)/shard_map/ppermute | solution.py:619
  827.8 63.1 %collective-permute-start.6 = (bf16[256,1024]{1,0:T(8,128)(2,1)S(1)}, bf16[256,1024]{1,0:T(8,128)(2,1)}, u32[]{:S(2)}, u32[]{:S(2)}) collective-permute-start(bf16[256,1024]{1,0:T(8,128)(2,1)S(1)} %get-tuple-element.77), channel_id=1, source_target_pairs={{0,1},{1,2},{2,3},{3,0},{4,5},{5,6},{6,7},{7,4},{8,9},{9,10},{10,1... | collective-permute-start | bytes 1572872 | tf_op jit(solution)/shard_map/ppermute | solution.py:619
  845.4 176.9 %collective-permute-start.30 = (bf16[4,256,1024]{2,1,0:T(8,128)(2,1)}, bf16[4,256,1024]{2,1,0:T(8,128)(2,1)}, u32[]{:S(2)}, u32[]{:S(2)}) collective-permute-start(bf16[4,256,1024]{2,1,0:T(8,128)(2,1)} %pad_maximum_fusion.5.refs_0_), channel_id=1, source_target_pairs={{0,4},{4,0},{8,12},{12,8},{16,20},{20,16},{24,28},{28,24},{1,5},{5... | collective-permute-start | bytes 6291464 | tf_op jit(solution)/shard_map/ppermute | solution.py:56
  848.1 174.2 %collective-permute-start.33 = (bf16[4,256,1024]{2,1,0:T(8,128)(2,1)}, bf16[4,256,1024]{2,1,0:T(8,128)(2,1)}, u32[]{:S(2)}, u32[]{:S(2)}) collective-permute-start(bf16[4,256,1024]{2,1,0:T(8,128)(2,1)} %pad_maximum_fusion.6.refs_2_), channel_id=1, source_target_pairs={{0,4},{4,0},{8,12},{12,8},{16,20},{20,16},{24,28},{28,24},{1,5},{5... | collective-permute-start | bytes 6291464 | tf_op jit(solution)/shard_map/ppermute | solution.py:56
  848.6 51.1 %collective-permute-start.11 = (bf16[256,1024]{1,0:T(8,128)(2,1)}, bf16[256,1024]{1,0:T(8,128)(2,1)S(1)}, u32[]{:S(2)}, u32[]{:S(2)}) collective-permute-start(bf16[256,1024]{1,0:T(8,128)(2,1)} %get-tuple-element.78), channel_id=1, source_target_pairs={{0,3},{1,0},{2,1},{3,2},{4,7},{5,4},{6,5},{7,6},{8,11},{9,8},{10,9... | collective-permute-start | bytes 1572872 | tf_op jit(solution)/shard_map/ppermute | solution.py:619
  890.9 46.5 %collective-permute-start.10 = (bf16[256,1024]{1,0:T(8,128)(2,1)}, bf16[256,1024]{1,0:T(8,128)(2,1)S(1)}, u32[]{:S(2)}, u32[]{:S(2)}) collective-permute-start(bf16[256,1024]{1,0:T(8,128)(2,1)} %get-tuple-element.79), channel_id=1, source_target_pairs={{0,2},{1,3},{2,0},{3,1},{4,6},{5,7},{6,4},{7,5},{8,10},{9,11},{10,... | collective-permute-start | bytes 1572872 | tf_op jit(solution)/shard_map/ppermute | solution.py:619
  890.9 48.4 %collective-permute-start.9 = (bf16[256,1024]{1,0:T(8,128)(2,1)}, bf16[256,1024]{1,0:T(8,128)(2,1)S(1)}, u32[]{:S(2)}, u32[]{:S(2)}) collective-permute-start(bf16[256,1024]{1,0:T(8,128)(2,1)} %get-tuple-element.80), channel_id=1, source_target_pairs={{0,1},{1,2},{2,3},{3,0},{4,5},{5,6},{6,7},{7,4},{8,9},{9,10},{10,1... | collective-permute-start | bytes 1572872 | tf_op jit(solution)/shard_map/ppermute | solution.py:619
  936.4 44.0 %collective-permute-start.27 = (f32[2048]{0:T(1024)S(1)}, f32[2048]{0:T(1024)S(1)}, u32[]{:S(2)}, u32[]{:S(2)}) collective-permute-start(f32[2048]{0:T(1024)S(1)} %add.153), channel_id=1, source_target_pairs={{0,2},{1,3},{2,0},{3,1},{4,6},{5,7},{6,4},{7,5},{8,10},{9,11},{10,... | collective-permute-start | bytes 24584 | tf_op jit(solution)/shard_map/ppermute | solution.py:69
  937.4 43.3 %collective-permute-start.22 = (f32[2048]{0:T(1024)S(1)}, f32[2048]{0:T(1024)S(1)}, u32[]{:S(2)}, u32[]{:S(2)}) collective-permute-start(f32[2048]{0:T(1024)S(1)} %add.148), channel_id=1, source_target_pairs={{0,2},{1,3},{2,0},{3,1},{4,6},{5,7},{6,4},{7,5},{8,10},{9,11},{10,... | collective-permute-start | bytes 24584 | tf_op jit(solution)/shard_map/ppermute | solution.py:69
  939.4 47.0 %collective-permute-start.15 = (bf16[256,2048]{1,0:T(8,128)(2,1)}, bf16[256,2048]{1,0:T(8,128)(2,1)S(1)}, u32[]{:S(2)}, u32[]{:S(2)}) collective-permute-start(bf16[256,2048]{1,0:T(8,128)(2,1)} %get-tuple-element.57), channel_id=1, source_target_pairs={{0,1},{1,2},{2,3},{3,0},{4,5},{5,6},{6,7},{7,4},{8,9},{9,10},{10,1... | collective-permute-start | bytes 3145736 | tf_op jit(solution)/shard_map/ppermute | solution.py:619
  980.4 29.7 %collective-permute-start.16 = (bf16[256,2048]{1,0:T(8,128)(2,1)}, bf16[256,2048]{1,0:T(8,128)(2,1)}, u32[]{:S(2)}, u32[]{:S(2)}) collective-permute-start(bf16[256,2048]{1,0:T(8,128)(2,1)} %get-tuple-element.58), channel_id=1, source_target_pairs={{0,2},{1,3},{2,0},{3,1},{4,6},{5,7},{6,4},{7,5},{8,10},{9,11},{10,... | collective-permute-start | bytes 3145736 | tf_op jit(solution)/shard_map/ppermute | solution.py:619
  980.7 35.5 %collective-permute-start.17 = (bf16[256,2048]{1,0:T(8,128)(2,1)}, bf16[256,2048]{1,0:T(8,128)(2,1)}, u32[]{:S(2)}, u32[]{:S(2)}) collective-permute-start(bf16[256,2048]{1,0:T(8,128)(2,1)} %get-tuple-element.59), channel_id=1, source_target_pairs={{0,3},{1,0},{2,1},{3,2},{4,7},{5,4},{6,5},{7,6},{8,11},{9,8},{10,9... | collective-permute-start | bytes 3145736 | tf_op jit(solution)/shard_map/ppermute | solution.py:619
  (32 other events, 332.0 us)
Sparse Core Ops, SparseCore 0:
  10.4 83.4 all-gather.18
  96.0 26.4 all-gather.22
  124.7 80.1 all-gather.20
  206.3 79.2 all-gather.10
  390.7 101.2 all-gather.12
Sparse Core Ops, SparseCore 1:
  14.4 36.2 reduce-scatter.4
  532.5 54.8 reduce-scatter.6
  591.4 116.0 reduce-scatter.8
  711.5 71.3 reduce-scatter.10
  784.8 59.1 all-gather.14
  845.9 90.0 all-gather.16

commit v8 on v7

--- a/solution.py
+++ b/solution.py
@@ -412,12 +412,14 @@
 def gated_back(all_cot, w_down, smooth, slope):
     rows, width = all_cot.shape
     columns = w_down.shape[0]
-    tile = 256
+    tile = 512
 
     def kernel(cot_ref, weight_ref, smooth_ref, slope_ref, d_gate_ref, d_up_ref):
-        d_active = dot_lanes(cot_ref[...], weight_ref[...])
-        d_up_ref[...] = (d_active * smooth_ref[...].astype(jnp.float32)).astype(LOW)
-        d_gate_ref[...] = (d_active * slope_ref[...].astype(jnp.float32)).astype(LOW)
+        for start in range(0, tile, 256):
+            here = slice(start, start + 256)
+            d_active = dot_lanes(cot_ref[...], weight_ref[here, :])
+            d_up_ref[:, here] = (d_active * smooth_ref[:, here].astype(jnp.float32)).astype(LOW)
+            d_gate_ref[:, here] = (d_active * slope_ref[:, here].astype(jnp.float32)).astype(LOW)
 
     column_block = pl.BlockSpec((rows, tile), lambda j: (0, j))
     return pl.pallas_call(
@@ -442,7 +444,7 @@
     rows, depth = left.shape
     each = rights[0].shape[1]
     tile = 512
-    row_steps, column_steps = rows // tile, each // tile
+    column_steps = each // tile
     count = len(rights)
     per = count * column_steps // folds
 
@@ -458,21 +460,19 @@
             if count == 1:
                 _()
             else:
-                pl.when(pl.program_id(1) // column_steps == k)(_)
+                pl.when(pl.program_id(0) // column_steps == k)(_)
 
     def right_block(k):
         return pl.BlockSpec(
-            (depth, tile), lambda i, j: (0, jnp.clip(j - k * column_steps, 0, column_steps - 1))
+            (depth, tile), lambda j: (0, jnp.clip(j - k * column_steps, 0, column_steps - 1))
         )
 
     return pl.pallas_call(
         kernel,
-        grid=(row_steps, count * column_steps),
-        in_specs=[pl.BlockSpec((tile, depth), lambda i, j: (i, 0))]
+        grid=(count * column_steps,),
+        in_specs=[pl.BlockSpec((rows, depth), lambda j: (0, 0))]
         + [right_block(k) for k in range(count)],
-        out_specs=pl.BlockSpec(
-            (tile, tile), lambda i, j: (i + (j // per) * row_steps, j % per)
-        ),
+        out_specs=pl.BlockSpec((rows, tile), lambda j: (j // per, j % per)),
         out_shape=jax.ShapeDtypeStruct((rows * folds, count * each // folds), LOW),
         cost_estimate=pl.CostEstimate(
             flops=2 * rows * depth * count * each,
@@ -799,6 +799,9 @@
     d_state, state_low, gain_two = norm_back(hidden_state, norm2_gain, cotangent, dn2_blocks)
     d_state_low = gather_rows(state_low, TP)
     gain_two_sum = cube_sum(gain_two[0], (DP, TP))
+    grad_output = jnp.dot(heads_rows, d_state_low, preferred_element_type=jnp.float32)
+    output_grads = row_major(split_columns(grad_output.astype(LOW), folds))
+    part_out = scatter_sum(output_grads, DP)
     d_heads_rows = contract_cols(w_output, d_state_low).astype(LOW)
     d_projected = attend_back(projected, d_heads_rows, totals, cos_rows, sin_rows)
     gains = []
@@ -810,21 +813,21 @@
 
     dn1_blocks = exchange(dn1_blocks_of, TP)
     gain_one_sum = cube_sum(sum(gains)[0], (DP, TP))
-    grad_qkv = lax.dot_general(
-        normed1,
-        d_projected,
-        (((0,), (1,)), ((), ())),
-        preferred_element_type=jnp.float32,
-    ).astype(LOW)
-    grad_output = jnp.dot(heads_rows, d_state_low, preferred_element_type=jnp.float32).astype(LOW)
-    low_attn = row_major(
-        jnp.concatenate([grad_qkv, split_columns(grad_output, folds)], axis=1)
-    )
-    part_attn = scatter_sum(low_attn, DP)
+    packed_grads = row_major(
+        lax.dot_general(
+            normed1,
+            d_projected,
+            (((0,), (1,)), ((), ())),
+            preferred_element_type=jnp.float32,
+        ).astype(LOW)
+    )
+    part_attn = scatter_sum(packed_grads, DP)
     down_halves = cube_gather(part_down, DP, join=False)
     full_down = join_columns(place_blocks(down_halves, DP), ff_folds)
     shared_ff = row_major(gather_rows(part_gate_up, DP))
-    shared_attn = row_major(gather_rows(part_attn, DP))
+    shared_attn = row_major(
+        gather_rows(row_major(jnp.concatenate([part_attn, part_out], axis=1)), DP)
+    )
     _, input_grad, _ = norm_back(tokens, norm1_gain, d_state, dn1_blocks)
     full_gate = shared_ff[:, :ff_columns].astype(jnp.float32)
     full_up = shared_ff[:, ff_columns:].astype(jnp.float32)

time: 1090 us -> 1080 us (level)
  Pallas kernels: 255 us -> 229 us
  waiting for transfers between devices: 647 us -> 667 us
    pallas_call x3, Pallas kernels: 75.5 us -> 50.2 us  [product(): pl.pallas_call(kernel, grid=(count * column_steps,), in_specs=[pl.BlockSp...]
    reduce_scatter x4 -> x5, waiting for transfers between devices: 190 us -> 211 us  [scatter_sum(): return lax.psum_scatter(partial, axis, scatter_dimension=0, tiled=True)]
  transfers between devices with their start and end apart: 45 -> 46, of which waited for: 26 -> 27; matrix products, arithmetic and copies ran while one was open for 6% -> 7% of each run, Pallas kernels for 19% -> 19%
where the time goes in v8:
time: 1080 us; the launch traced here: 1060 us
  waiting for transfers between devices  667 us (62%)
  Pallas kernels  229 us (21%)
  other arithmetic  51.3 us (5%)
  starting transfers between devices  47.4 us (4%)
  local copies, waits for them, and re-layouts  33.8 us (3%)
  matrix products  18.3 us (2%)
  between operations  16.5 us (2%)
    reduce_scatter x5, waiting for transfers between devices, scatter_sum(): return lax.psum_scatter(partial, axis, scatter_dimension=0, tiled=True)  211 us
    all_gather x4, waiting for transfers between devices, gather_rows(): return lax.all_gather(block, axis, axis=0, tiled=True)  138 us
    ppermute x12, waiting for transfers between devices, exchange(): moved.append(lax.ppermute(made[hop - 1], axis, pairs))  113 us
    ppermute x12, waiting for transfers between devices, cube_gather(): moved = lax.ppermute(held, axis, [(i, i ^ bit) for i in range(n)])  61.8 us
    all_gather x1, waiting for transfers between devices, block(): gathered = lax.all_gather(tokens, TP, axis=0)  59.4 us
    ppermute x10, waiting for transfers between devices, cube_sum(): lax.ppermute(vector, axis, [(i, i ^ bit) for i in range(n)])  51.7 us
    pallas_call x3, Pallas kernels, product(): pl.pallas_call(kernel, grid=(count * column_steps,), in_specs=[pl.BlockSp...  50.2 us
    pallas_call x2, Pallas kernels, pair_product(): pl.pallas_call(kernel, grid_spec=pltpu.PrefetchScalarGridSpec(num_scalar_...  30.2 us
  transfers between devices with their start and end apart: 46, of which 27 were waited for; matrix products, arithmetic and copies ran while one was open for 7% of the time, Pallas kernels for 19%

profile of v8, /device:TPU:0, one launch (start us, length us, event | category | flops | bytes accessed | tf_op | source)
XLA Modules:
  0.0 1063.2 jit_solution(8236347055701356021)
XLA Ops:
  34.5 59.4 %all-gather.19.cloned.1.call-done = bf16[1024,2048]{1,0:T(8,128)(2,1)} async-done(((bf16[256,2048]{1,0:T(8,128)(2,1)}), bf16[1024,2048]{1,0:T(8,128)(2,1)}) %all-gather.19.cloned.1.call-update) | async-done | bytes 4194320 | tf_op jit(solution)/shard_map/all_gather | solution.py:754
  93.9 8.4 norm_project.1
  102.3 13.7 %attend.1 = (bf16[1024,512]{1,0:T(8,128)(2,1)}, bf16[512,1024]{1,0:T(8,128)(2,1)}, f32[2,4,1024]{2,1,0:T(4,128)}) custom-call(bf16[768,1024]{1,0:T(8,128)(2,1)} %get-tuple-element.42.packed_ref), custom_call_target="tpu_custom_call" | custom-call | flops 1073741824 | bytes 4194304 | tf_op jit(solution)/shard_map/attend/pallas_call | solution.py:185
  126.9 10.2 collective-permute-done
  143.7 19.2 %collective-permute-done.1 = bf16[2,4,64,1024]{3,2,1,0:T(8,128)(2,1)} collective-permute-done((bf16[2,4,64,1024]{3,2,1,0:T(8,128)(2,1)}, bf16[2,4,64,1024]{3,2,1,0:T(8,128)(2,1)}, u32[]{:S(2)}, u32[]{:S(2)}) %collective-permute-start.1) | collective-permute-done | bytes 1048608 | tf_op jit(solution)/shard_map/ppermute | solution.py:56
  180.8 24.0 %all-gather.21.cloned.1.call-done = bf16[4096,512]{1,0:T(8,128)(2,1)} async-done(((bf16[1024,512]{1,0:T(8,128)(2,1)}), bf16[4096,512]{1,0:T(8,128)(2,1)}) %all-gather.21.cloned.1.call-update) | async-done | bytes 4194320 | tf_op jit(solution)/shard_map/all_gather | solution.py:770
  204.8 18.7 %project_and_norm.1 = (f32[256,2048]{1,0:T(8,128)}, bf16[1024,2048]{1,0:T(8,128)(2,1)}, bf16[2048,1024]{1,0:T(8,128)(2,1)}) custom-call(s32[2]{0:T(128)} %pad_add_fusion.at_ref, bf16[4,1024,512]{2,1,0:T(8,128)(2,1)} %bitcast.60, bf16[8,4,64,1024]{3,2,1,0:T(8,128)(2,1)} %pad_maximum_fusion.first_ref, bf16[8,4,64,1024]{3,2,1,0:T(8,128)(2,1)} %pad_maximum_fusion.1.second_ref, ...), custom_call_target="tpu_custom_call" | custom-call | flops 8589934592 | bytes 25165824 | tf_op jit(solution)/shard_map/project_and_norm/pallas_call | solution.py:339
  223.5 25.1 %gated_up.1 = (bf16[1024,2048]{1,0:T(8,128)(2,1)}, bf16[2048,1024]{1,0:T(8,128)(2,1)}, bf16[1024,2048]{1,0:T(8,128)(2,1)}, bf16[1024,2048]{1,0:T(8,128)(2,1)}) custom-call(bf16[1024,2048]{1,0:T(8,128)(2,1)} %get-tuple-element.45.normed_ref, bf16[2048,2048]{1,0:T(8,128)(2,1)} %first_w_ref.3, bf16[2048,2048]{1,0:T(8,128)(2,1)} %second_w_ref.3), custom_call_target="tpu_custom_call" | custom-call | flops 17179869184 | bytes 37748736 | tf_op jit(solution)/shard_map/gated_up/pallas_call | solution.py:392
  248.6 36.9 %all-gather.11.cloned.1.call-done.cot_ref.refs_0_ = bf16[1024,2048]{1,0:T(8,128)(2,1)} async-done(((bf16[256,2048]{1,0:T(8,128)(2,1)}), bf16[1024,2048]{1,0:T(8,128)(2,1)}) %all-gather.11.cloned.1.call-update) | async-done | bytes 4194320 | tf_op jit(solution)/shard_map/all_gather | solution.py:38
  285.5 16.2 %gated_back.1 = (bf16[1024,2048]{1,0:T(8,128)(2,1)}, bf16[1024,2048]{1,0:T(8,128)(2,1)}) custom-call(bf16[1024,2048]{1,0:T(8,128)(2,1)} %all-gather.11.cloned.1.call-done.cot_ref.refs_0_, bf16[2048,2048]{1,0:T(8,128)(2,1)} %weight_ref.1, bf16[1024,2048]{1,0:T(8,128)(2,1)} %get-tuple-element.47.smooth_ref, bf16[1024,2048]{1,0:T(8,128)(2,1)} %get-tuple-element.48.slope_ref), custom_call_target="tpu_custom_call" | custom-call | flops 8589934592 | bytes 29360128 | tf_op jit(solution)/shard_map/gated_back/pallas_call | solution.py:425
  301.7 10.0 pair_product.2
  311.7 20.2 %pair_product.3 = (bf16[256,2048]{1,0:T(8,128)(2,1)}, bf16[256,2048]{1,0:T(8,128)(2,1)}, bf16[256,2048]{1,0:T(8,128)(2,1)}) custom-call(s32[3]{0:T(128)} %pad_add_fusion.1.at_ref, bf16[1024,2048]{1,0:T(8,128)(2,1)} %get-tuple-element.49.first_ref.refs_0_, bf16[1024,2048]{1,0:T(8,128)(2,1)} %get-tuple-element.50.second_ref.refs_1_, ...), custom_call_target="tpu_custom_call" | custom-call | flops 12884901888 | bytes 20971520 | tf_op jit(solution)/shard_map/pair_product/pallas_call | solution.py:511
  339.8 43.8 %collective-permute-done.13.refs_1_ = bf16[256,2048]{1,0:T(8,128)(2,1)} collective-permute-done((bf16[256,2048]{1,0:T(8,128)(2,1)}, bf16[256,2048]{1,0:T(8,128)(2,1)}, u32[]{:S(2)}, u32[]{:S(2)}) %collective-permute-start.13) | collective-permute-done | bytes 1048608 | tf_op jit(solution)/shard_map/ppermute | solution.py:619
  390.0 101.2 %all-gather.13.cloned.1.call-done = bf16[1024,2048]{1,0:T(8,128)(2,1)} async-done(((bf16[256,2048]{1,0:T(8,128)(2,1)}), bf16[1024,2048]{1,0:T(8,128)(2,1)}) %all-gather.13.cloned.1.call-update) | async-done | bytes 4194320 | tf_op jit(solution)/shard_map/all_gather | solution.py:38
  503.2 20.2 %attend_back.1.d_ref = bf16[768,1024]{1,0:T(8,128)(2,1)} custom-call(bf16[768,1024]{1,0:T(8,128)(2,1)} %get-tuple-element.42.packed_ref, bf16[512,1024]{1,0:T(8,128)(2,1)} %fusion.1.d_heads_ref, f32[2,4,1024]{2,1,0:T(4,128)} %get-tuple-element.56.total_ref, f32[32,512]{1,0:T(8,128)} %get-tuple-element.94.cos_ref, f32[32,512]{1,0:T(8,128)} %get-tuple-element.93.sin_ref), custom_call_target="tpu_custom_call" | custom-call | flops 2684354560 | bytes 6291456 | tf_op jit(solution)/shard_map/attend_back/pallas_call | solution.py:265
  523.4 8.0 convolution_convert_fusion
  531.6 23.5 %product.4 = bf16[2048,4096]{1,0:T(8,128)(2,1)} custom-call(bf16[2048,1024]{1,0:T(8,128)(2,1)} %get-tuple-element.71.left_ref, bf16[1024,2048]{1,0:T(8,128)(2,1)} %get-tuple-element.49.first_ref.refs_0_, bf16[1024,2048]{1,0:T(8,128)(2,1)} %get-tuple-element.50.second_ref.refs_1_), custom_call_target="tpu_custom_call" | custom-call | flops 17179869184 | bytes 29360128 | tf_op jit(solution)/shard_map/product/pallas_call | solution.py:470
  555.2 13.4 %product.5 = bf16[2048,2048]{1,0:T(8,128)(2,1)} custom-call(bf16[2048,1024]{1,0:T(8,128)(2,1)} %get-tuple-element.72.left_ref, bf16[1024,2048]{1,0:T(8,128)(2,1)} %all-gather.11.cloned.1.call-done.cot_ref.refs_0_), custom_call_target="tpu_custom_call" | custom-call | flops 8589934592 | bytes 16777216 | tf_op jit(solution)/shard_map/product/pallas_call | solution.py:470
  568.7 17.7 %reduce-scatter.8.cloned.1.call-done = bf16[256,768]{1,0:T(8,128)(2,1)} async-done(((bf16[2048,768]{1,0:T(8,128)(2,1)}), bf16[256,768]{1,0:T(8,128)(2,1)}) %reduce-scatter.8.cloned.1.call-update) | async-done | bytes 393232 | tf_op jit(solution)/shard_map/reduce_scatter | solution.py:42
  588.4 118.2 %reduce-scatter.12.cloned.1.call-done = bf16[256,4096]{1,0:T(8,128)(2,1)} async-done(((bf16[2048,4096]{1,0:T(8,128)(2,1)}), bf16[256,4096]{1,0:T(8,128)(2,1)}) %reduce-scatter.12.cloned.1.call-update) | async-done | bytes 2097168 | tf_op jit(solution)/shard_map/reduce_scatter | solution.py:42
  706.6 75.4 %reduce-scatter.14.cloned.1.call-done = bf16[256,2048]{1,0:T(8,128)(2,1)} async-done(((bf16[2048,2048]{1,0:T(8,128)(2,1)}), bf16[256,2048]{1,0:T(8,128)(2,1)}) %reduce-scatter.14.cloned.1.call-update) | async-done | bytes 1048592 | tf_op jit(solution)/shard_map/reduce_scatter | solution.py:42
  785.4 15.0 %collective-permute-done.28 = bf16[1,256,1024]{2,1,0:T(8,128)(2,1)S(1)} collective-permute-done((bf16[1,256,1024]{2,1,0:T(8,128)(2,1)S(1)}, bf16[1,256,1024]{2,1,0:T(8,128)(2,1)S(1)}, u32[]{:S(2)}, u32[]{:S(2)}) %collective-permute-start.28) | collective-permute-done | bytes 524320 | tf_op jit(solution)/shard_map/ppermute | solution.py:56
  804.1 13.3 %product.3 = bf16[1024,2048]{1,0:T(8,128)(2,1)} custom-call(bf16[1024,2048]{1,0:T(8,128)(2,1)} %get-tuple-element.46.left_ref, bf16[2048,2048]{1,0:T(8,128)(2,1)} %weight_ref.1), custom_call_target="tpu_custom_call" | custom-call | flops 8589934592 | bytes 16777216 | tf_op jit(solution)/shard_map/product/pallas_call | solution.py:470
  824.7 16.8 %collective-permute-done.29 = bf16[2,256,1024]{2,1,0:T(8,128)(2,1)} collective-permute-done((bf16[2,256,1024]{2,1,0:T(8,128)(2,1)}, bf16[2,256,1024]{2,1,0:T(8,128)(2,1)}, u32[]{:S(2)}, u32[]{:S(2)}) %collective-permute-start.29) | collective-permute-done | bytes 1048608 | tf_op jit(solution)/shard_map/ppermute | solution.py:56
  850.8 35.8 %collective-permute-done.7 = bf16[256,1024]{1,0:T(8,128)(2,1)} collective-permute-done((bf16[256,1024]{1,0:T(8,128)(2,1)S(1)}, bf16[256,1024]{1,0:T(8,128)(2,1)}, u32[]{:S(2)}, u32[]{:S(2)}) %collective-permute-start.7) | collective-permute-done | bytes 524320 | tf_op jit(solution)/shard_map/ppermute | solution.py:619
  887.0 8.8 projection_back.3
  918.6 8.0 collective-permute-start.26
  937.0 38.8 %collective-permute-done.27 = f32[2048]{0:T(1024)S(1)} collective-permute-done((f32[2048]{0:T(1024)S(1)}, f32[2048]{0:T(1024)S(1)}, u32[]{:S(2)}, u32[]{:S(2)}) %collective-permute-start.27) | collective-permute-done | bytes 8224 | tf_op jit(solution)/shard_map/ppermute | solution.py:69
  981.8 23.8 %collective-permute-done.16.refs_1_ = bf16[256,2048]{1,0:T(8,128)(2,1)} collective-permute-done((bf16[256,2048]{1,0:T(8,128)(2,1)}, bf16[256,2048]{1,0:T(8,128)(2,1)}, u32[]{:S(2)}, u32[]{:S(2)}) %collective-permute-start.16) | collective-permute-done | bytes 1048608 | tf_op jit(solution)/shard_map/ppermute | solution.py:619
  1017.8 13.9 %place_blocks.1 = f32[2048,2048]{1,0:T(8,128)} custom-call(s32[1]{0:T(128)} %bitcast.1.at_ref, bf16[4,256,1024]{2,1,0:T(8,128)(2,1)} %pad_maximum_fusion.4.refs_0_, bf16[4,256,1024]{2,1,0:T(8,128)(2,1)} %collective-permute-done.30.refs_1_, bf16[4,256,1024]{2,1,0:T(8,128)(2,1)} %pad_maximum_fusion.5.refs_2_, bf16[4,256,1024]{2,1,0:T(8,128)(2,1)} %collective-permute-done.33.refs_3_), custom_call_target="tpu_custom_call" | custom-call | bytes 25165824 | tf_op jit(solution)/shard_map/place_blocks/pallas_call | solution.py:651
  1031.7 7.0 unpack_attention.1
  1038.6 17.2 %slice_convert_fusion = (f32[2048,2048]{1,0:T(8,128)}, f32[2048,2048]{1,0:T(8,128)}) fusion(bf16[2048,4096]{1,0:T(8,128)(2,1)} %all-gather.17.cloned.1.call-done), kind=kLoop, calls=%fused_computation | loop fusion | flops 8388608 | bytes 50331648 | tf_op jit(solution)/shard_map/convert_element_type | solution.py:833
  (180 shorter events, 165.0 us)
Async XLA Ops:
  8.0 85.9 %all-gather.19.cloned.1.call-start = ((), (), s32[]{:S(2)}) async-start(), calls=%async_computation.14 | async-start | bytes 5242880 | tf_op jit(solution)/shard_map/all_gather | solution.py:754
  8.8 113.8 %all-gather.23.cloned.1.call-start = ((), (), s32[]{:S(2)}) async-start(), calls=%async_computation.16 | async-start | bytes 1310720 | tf_op jit(solution)/shard_map/all_gather | solution.py:756
  10.4 160.7 %reduce-scatter.6.cloned.1.call-start = ((), (), s32[]{:S(2)}) async-start(), calls=%async_computation.5 | async-start | bytes 73728 | tf_op jit(solution)/shard_map/reduce_scatter | solution.py:42
  11.9 192.9 %all-gather.21.cloned.1.call-start = ((), (), s32[]{:S(2)}) async-start(), calls=%async_computation.15 | async-start | bytes 5242880 | tf_op jit(solution)/shard_map/all_gather | solution.py:770
  116.0 169.5 %all-gather.11.cloned.1.call-start = ((), (), s32[]{:S(2)}) async-start(), calls=%async_computation.6 | async-start | bytes 5242880 | tf_op jit(solution)/shard_map/all_gather | solution.py:38
  139.0 24.0 %collective-permute-start.1 = (bf16[2,4,64,1024]{3,2,1,0:T(8,128)(2,1)}, bf16[2,4,64,1024]{3,2,1,0:T(8,128)(2,1)}, u32[]{:S(2)}, u32[]{:S(2)}) collective-permute-start(bf16[2,4,64,1024]{3,2,1,0:T(8,128)(2,1)} %pad_maximum_fusion.6), channel_id=1, source_target_pairs={{0,16},{4,20},{8,24},{12,28},{16,0},{20,4},{24,8},{28,12},{1,17},{... | collective-permute-start | bytes 3145736 | tf_op jit(solution)/shard_map/ppermute | solution.py:56
  140.5 350.8 %all-gather.13.cloned.1.call-start = ((), (), s32[]{:S(2)}) async-start(), calls=%async_computation.7 | async-start | bytes 5242880 | tf_op jit(solution)/shard_map/all_gather | solution.py:38
  142.2 23.6 %collective-permute-start.4 = (bf16[2,4,64,1024]{3,2,1,0:T(8,128)(2,1)S(1)}, bf16[2,4,64,1024]{3,2,1,0:T(8,128)(2,1)S(1)}, u32[]{:S(2)}, u32[]{:S(2)}) collective-permute-start(bf16[2,4,64,1024]{3,2,1,0:T(8,128)(2,1)S(1)} %pad_maximum_fusion.7), channel_id=1, source_target_pairs={{0,8},{4,12},{8,0},{12,4},{16,24},{20,28},{24,16},{28,20},{1,9},{5... | collective-permute-start | bytes 3145736 | tf_op jit(solution)/shard_map/ppermute | solution.py:56
  311.7 28.1 %collective-permute-start.12 = (bf16[256,2048]{1,0:T(8,128)(2,1)}, bf16[256,2048]{1,0:T(8,128)(2,1)S(1)}, u32[]{:S(2)}, u32[]{:S(2)}) collective-permute-start(bf16[256,2048]{1,0:T(8,128)(2,1)} %pair_product.2), channel_id=1, source_target_pairs={{0,1},{1,2},{2,3},{3,0},{4,5},{5,6},{6,7},{7,4},{8,9},{9,10},{10,1... | collective-permute-start | bytes 3145736 | tf_op jit(solution)/shard_map/ppermute | solution.py:619
  331.9 51.7 %collective-permute-start.13 = (bf16[256,2048]{1,0:T(8,128)(2,1)}, bf16[256,2048]{1,0:T(8,128)(2,1)}, u32[]{:S(2)}, u32[]{:S(2)}) collective-permute-start(bf16[256,2048]{1,0:T(8,128)(2,1)} %get-tuple-element.51), channel_id=1, source_target_pairs={{0,2},{1,3},{2,0},{3,1},{4,6},{5,7},{6,4},{7,5},{8,10},{9,11},{10,... | collective-permute-start | bytes 3145736 | tf_op jit(solution)/shard_map/ppermute | solution.py:619
  333.0 50.5 %collective-permute-start.14 = (bf16[256,2048]{1,0:T(8,128)(2,1)}, bf16[256,2048]{1,0:T(8,128)(2,1)}, u32[]{:S(2)}, u32[]{:S(2)}) collective-permute-start(bf16[256,2048]{1,0:T(8,128)(2,1)} %get-tuple-element.52), channel_id=1, source_target_pairs={{0,3},{1,0},{2,1},{3,2},{4,7},{5,4},{6,5},{7,6},{8,11},{9,8},{10,9... | collective-permute-start | bytes 3145736 | tf_op jit(solution)/shard_map/ppermute | solution.py:619
  389.8 178.9 %reduce-scatter.10.cloned.1.call-start = ((), (), s32[]{:S(2)}) async-start(), calls=%async_computation.9 | async-start | bytes 2359296 | tf_op jit(solution)/shard_map/reduce_scatter | solution.py:42
  497.6 88.8 %reduce-scatter.8.cloned.1.call-start = ((), (), s32[]{:S(2)}) async-start(), calls=%async_computation.8 | async-start | bytes 3538944 | tf_op jit(solution)/shard_map/reduce_scatter | solution.py:42
  531.4 175.2 %reduce-scatter.12.cloned.1.call-start = ((), (), s32[]{:S(2)}) async-start(), calls=%async_computation.11 | async-start | bytes 18874368 | tf_op jit(solution)/shard_map/reduce_scatter | solution.py:42
  555.2 226.9 %reduce-scatter.14.cloned.1.call-start = ((), (), s32[]{:S(2)}) async-start(), calls=%async_computation.13 | async-start | bytes 9437184 | tf_op jit(solution)/shard_map/reduce_scatter | solution.py:42
  568.6 463.1 %all-gather.15.cloned.1.call-start = ((), (), s32[]{:S(2)}) async-start(), calls=%async_computation.10 | async-start | bytes 5898240 | tf_op jit(solution)/shard_map/all_gather | solution.py:38
  588.4 450.3 %all-gather.17.cloned.1.call-start = ((), (), s32[]{:S(2)}) async-start(), calls=%async_computation.12 | async-start | bytes 18874368 | tf_op jit(solution)/shard_map/all_gather | solution.py:38
  801.5 40.0 %collective-permute-start.29 = (bf16[2,256,1024]{2,1,0:T(8,128)(2,1)}, bf16[2,256,1024]{2,1,0:T(8,128)(2,1)}, u32[]{:S(2)}, u32[]{:S(2)}) collective-permute-start(bf16[2,256,1024]{2,1,0:T(8,128)(2,1)} %pad_maximum_fusion.8), channel_id=1, source_target_pairs={{0,16},{4,20},{8,24},{12,28},{16,0},{20,4},{24,8},{28,12},{1,17},{... | collective-permute-start | bytes 3145736 | tf_op jit(solution)/shard_map/ppermute | solution.py:56
  803.4 40.9 %collective-permute-start.32 = (bf16[2,256,1024]{2,1,0:T(8,128)(2,1)S(1)}, bf16[2,256,1024]{2,1,0:T(8,128)(2,1)}, u32[]{:S(2)}, u32[]{:S(2)}) collective-permute-start(bf16[2,256,1024]{2,1,0:T(8,128)(2,1)S(1)} %pad_maximum_fusion.9), channel_id=1, source_target_pairs={{0,8},{4,12},{8,0},{12,4},{16,24},{20,28},{24,16},{28,20},{1,9},{5... | collective-permute-start | bytes 3145736 | tf_op jit(solution)/shard_map/ppermute | solution.py:56
  820.6 27.0 %collective-permute-start.8 = (bf16[256,1024]{1,0:T(8,128)(2,1)S(1)}, bf16[256,1024]{1,0:T(8,128)(2,1)}, u32[]{:S(2)}, u32[]{:S(2)}) collective-permute-start(bf16[256,1024]{1,0:T(8,128)(2,1)S(1)} %get-tuple-element.81), channel_id=1, source_target_pairs={{0,3},{1,0},{2,1},{3,2},{4,7},{5,4},{6,5},{7,6},{8,11},{9,8},{10,9... | collective-permute-start | bytes 1572872 | tf_op jit(solution)/shard_map/ppermute | solution.py:619
  823.5 63.1 %collective-permute-start.7 = (bf16[256,1024]{1,0:T(8,128)(2,1)S(1)}, bf16[256,1024]{1,0:T(8,128)(2,1)}, u32[]{:S(2)}, u32[]{:S(2)}) collective-permute-start(bf16[256,1024]{1,0:T(8,128)(2,1)S(1)} %get-tuple-element.82), channel_id=1, source_target_pairs={{0,2},{1,3},{2,0},{3,1},{4,6},{5,7},{6,4},{7,5},{8,10},{9,11},{10,... | collective-permute-start | bytes 1572872 | tf_op jit(solution)/shard_map/ppermute | solution.py:619
  823.5 63.1 %collective-permute-start.6 = (bf16[256,1024]{1,0:T(8,128)(2,1)S(1)}, bf16[256,1024]{1,0:T(8,128)(2,1)}, u32[]{:S(2)}, u32[]{:S(2)}) collective-permute-start(bf16[256,1024]{1,0:T(8,128)(2,1)S(1)} %get-tuple-element.77), channel_id=1, source_target_pairs={{0,1},{1,2},{2,3},{3,0},{4,5},{5,6},{6,7},{7,4},{8,9},{9,10},{10,1... | collective-permute-start | bytes 1572872 | tf_op jit(solution)/shard_map/ppermute | solution.py:619
  844.3 173.5 %collective-permute-start.30 = (bf16[4,256,1024]{2,1,0:T(8,128)(2,1)}, bf16[4,256,1024]{2,1,0:T(8,128)(2,1)}, u32[]{:S(2)}, u32[]{:S(2)}) collective-permute-start(bf16[4,256,1024]{2,1,0:T(8,128)(2,1)} %pad_maximum_fusion.4.refs_0_), channel_id=1, source_target_pairs={{0,4},{4,0},{8,12},{12,8},{16,20},{20,16},{24,28},{28,24},{1,5},{5... | collective-permute-start | bytes 6291464 | tf_op jit(solution)/shard_map/ppermute | solution.py:56
  847.0 170.8 %collective-permute-start.33 = (bf16[4,256,1024]{2,1,0:T(8,128)(2,1)}, bf16[4,256,1024]{2,1,0:T(8,128)(2,1)}, u32[]{:S(2)}, u32[]{:S(2)}) collective-permute-start(bf16[4,256,1024]{2,1,0:T(8,128)(2,1)} %pad_maximum_fusion.5.refs_2_), channel_id=1, source_target_pairs={{0,4},{4,0},{8,12},{12,8},{16,20},{20,16},{24,28},{28,24},{1,5},{5... | collective-permute-start | bytes 6291464 | tf_op jit(solution)/shard_map/ppermute | solution.py:56
  847.5 48.2 %collective-permute-start.11 = (bf16[256,1024]{1,0:T(8,128)(2,1)}, bf16[256,1024]{1,0:T(8,128)(2,1)S(1)}, u32[]{:S(2)}, u32[]{:S(2)}) collective-permute-start(bf16[256,1024]{1,0:T(8,128)(2,1)} %get-tuple-element.78), channel_id=1, source_target_pairs={{0,3},{1,0},{2,1},{3,2},{4,7},{5,4},{6,5},{7,6},{8,11},{9,8},{10,9... | collective-permute-start | bytes 1572872 | tf_op jit(solution)/shard_map/ppermute | solution.py:619
  886.6 46.3 %collective-permute-start.10 = (bf16[256,1024]{1,0:T(8,128)(2,1)}, bf16[256,1024]{1,0:T(8,128)(2,1)S(1)}, u32[]{:S(2)}, u32[]{:S(2)}) collective-permute-start(bf16[256,1024]{1,0:T(8,128)(2,1)} %get-tuple-element.79), channel_id=1, source_target_pairs={{0,2},{1,3},{2,0},{3,1},{4,6},{5,7},{6,4},{7,5},{8,10},{9,11},{10,... | collective-permute-start | bytes 1572872 | tf_op jit(solution)/shard_map/ppermute | solution.py:619
  886.7 48.3 %collective-permute-start.9 = (bf16[256,1024]{1,0:T(8,128)(2,1)}, bf16[256,1024]{1,0:T(8,128)(2,1)S(1)}, u32[]{:S(2)}, u32[]{:S(2)}) collective-permute-start(bf16[256,1024]{1,0:T(8,128)(2,1)} %get-tuple-element.80), channel_id=1, source_target_pairs={{0,1},{1,2},{2,3},{3,0},{4,5},{5,6},{6,7},{7,4},{8,9},{9,10},{10,1... | collective-permute-start | bytes 1572872 | tf_op jit(solution)/shard_map/ppermute | solution.py:619
  931.9 43.9 %collective-permute-start.27 = (f32[2048]{0:T(1024)S(1)}, f32[2048]{0:T(1024)S(1)}, u32[]{:S(2)}, u32[]{:S(2)}) collective-permute-start(f32[2048]{0:T(1024)S(1)} %add.155), channel_id=1, source_target_pairs={{0,2},{1,3},{2,0},{3,1},{4,6},{5,7},{6,4},{7,5},{8,10},{9,11},{10,... | collective-permute-start | bytes 24584 | tf_op jit(solution)/shard_map/ppermute | solution.py:69
  932.9 43.2 %collective-permute-start.22 = (f32[2048]{0:T(1024)S(1)}, f32[2048]{0:T(1024)S(1)}, u32[]{:S(2)}, u32[]{:S(2)}) collective-permute-start(f32[2048]{0:T(1024)S(1)} %add.150), channel_id=1, source_target_pairs={{0,2},{1,3},{2,0},{3,1},{4,6},{5,7},{6,4},{7,5},{8,10},{9,11},{10,... | collective-permute-start | bytes 24584 | tf_op jit(solution)/shard_map/ppermute | solution.py:69
  934.9 46.9 %collective-permute-start.15 = (bf16[256,2048]{1,0:T(8,128)(2,1)}, bf16[256,2048]{1,0:T(8,128)(2,1)S(1)}, u32[]{:S(2)}, u32[]{:S(2)}) collective-permute-start(bf16[256,2048]{1,0:T(8,128)(2,1)} %get-tuple-element.57), channel_id=1, source_target_pairs={{0,1},{1,2},{2,3},{3,0},{4,5},{5,6},{6,7},{7,4},{8,9},{9,10},{10,1... | collective-permute-start | bytes 3145736 | tf_op jit(solution)/shard_map/ppermute | solution.py:619
  975.8 29.8 %collective-permute-start.16 = (bf16[256,2048]{1,0:T(8,128)(2,1)}, bf16[256,2048]{1,0:T(8,128)(2,1)}, u32[]{:S(2)}, u32[]{:S(2)}) collective-permute-start(bf16[256,2048]{1,0:T(8,128)(2,1)} %get-tuple-element.58), channel_id=1, source_target_pairs={{0,2},{1,3},{2,0},{3,1},{4,6},{5,7},{6,4},{7,5},{8,10},{9,11},{10,... | collective-permute-start | bytes 3145736 | tf_op jit(solution)/shard_map/ppermute | solution.py:619
  976.1 35.5 %collective-permute-start.17 = (bf16[256,2048]{1,0:T(8,128)(2,1)}, bf16[256,2048]{1,0:T(8,128)(2,1)}, u32[]{:S(2)}, u32[]{:S(2)}) collective-permute-start(bf16[256,2048]{1,0:T(8,128)(2,1)} %get-tuple-element.59), channel_id=1, source_target_pairs={{0,3},{1,0},{2,1},{3,2},{4,7},{5,4},{6,5},{7,6},{8,11},{9,8},{10,9... | collective-permute-start | bytes 3145736 | tf_op jit(solution)/shard_map/ppermute | solution.py:619
  (31 other events, 339.6 us)
Sparse Core Ops, SparseCore 0:
  10.4 83.4 all-gather.18
  96.0 26.4 all-gather.22
  124.7 80.1 all-gather.20
  206.3 79.2 all-gather.10
  389.9 101.2 all-gather.12
Sparse Core Ops, SparseCore 1:
  14.4 36.2 reduce-scatter.5
  497.7 39.5 reduce-scatter.9
  540.4 45.9 reduce-scatter.7
  590.5 116.0 reduce-scatter.11
  710.7 71.3 reduce-scatter.13
  784.5 58.7 all-gather.14
  845.1 89.9 all-gather.16

commit v9 on v7

--- a/solution.py
+++ b/solution.py
@@ -412,12 +412,14 @@
 def gated_back(all_cot, w_down, smooth, slope):
     rows, width = all_cot.shape
     columns = w_down.shape[0]
-    tile = 256
+    tile = 512
 
     def kernel(cot_ref, weight_ref, smooth_ref, slope_ref, d_gate_ref, d_up_ref):
-        d_active = dot_lanes(cot_ref[...], weight_ref[...])
-        d_up_ref[...] = (d_active * smooth_ref[...].astype(jnp.float32)).astype(LOW)
-        d_gate_ref[...] = (d_active * slope_ref[...].astype(jnp.float32)).astype(LOW)
+        for start in range(0, tile, 256):
+            here = slice(start, start + 256)
+            d_active = dot_lanes(cot_ref[...], weight_ref[here, :])
+            d_up_ref[:, here] = (d_active * smooth_ref[:, here].astype(jnp.float32)).astype(LOW)
+            d_gate_ref[:, here] = (d_active * slope_ref[:, here].astype(jnp.float32)).astype(LOW)
 
     column_block = pl.BlockSpec((rows, tile), lambda j: (0, j))
     return pl.pallas_call(
@@ -442,7 +444,7 @@
     rows, depth = left.shape
     each = rights[0].shape[1]
     tile = 512
-    row_steps, column_steps = rows // tile, each // tile
+    column_steps = each // tile
     count = len(rights)
     per = count * column_steps // folds
 
@@ -458,21 +460,19 @@
             if count == 1:
                 _()
             else:
-                pl.when(pl.program_id(1) // column_steps == k)(_)
+                pl.when(pl.program_id(0) // column_steps == k)(_)
 
     def right_block(k):
         return pl.BlockSpec(
-            (depth, tile), lambda i, j: (0, jnp.clip(j - k * column_steps, 0, column_steps - 1))
+            (depth, tile), lambda j: (0, jnp.clip(j - k * column_steps, 0, column_steps - 1))
         )
 
     return pl.pallas_call(
         kernel,
-        grid=(row_steps, count * column_steps),
-        in_specs=[pl.BlockSpec((tile, depth), lambda i, j: (i, 0))]
+        grid=(count * column_steps,),
+        in_specs=[pl.BlockSpec((rows, depth), lambda j: (0, 0))]
         + [right_block(k) for k in range(count)],
-        out_specs=pl.BlockSpec(
-            (tile, tile), lambda i, j: (i + (j // per) * row_steps, j % per)
-        ),
+        out_specs=pl.BlockSpec((rows, tile), lambda j: (j // per, j % per)),
         out_shape=jax.ShapeDtypeStruct((rows * folds, count * each // folds), LOW),
         cost_estimate=pl.CostEstimate(
             flops=2 * rows * depth * count * each,

time: 1090 us -> 1080 us (level)
  Pallas kernels: 255 us -> 229 us
  waiting for transfers between devices: 647 us -> 669 us
    pallas_call x3, Pallas kernels: 75.5 us -> 50.1 us  [product(): pl.pallas_call(kernel, grid=(count * column_steps,), in_specs=[pl.BlockSp...]
    reduce_scatter x4, waiting for transfers between devices: 190 us -> 213 us  [scatter_sum(): return lax.psum_scatter(partial, axis, scatter_dimension=0, tiled=True)]
  transfers between devices with their start and end apart: 45 -> 45, of which waited for: 26 -> 27; matrix products, arithmetic and copies ran while one was open for 6% -> 6% of each run, Pallas kernels for 19% -> 17%
where the time goes in v9:
time: 1080 us; the launch traced here: 1060 us
  waiting for transfers between devices  669 us (62%)
  Pallas kernels  229 us (21%)
  other arithmetic  52.1 us (5%)
  starting transfers between devices  47.1 us (4%)
  local copies, waits for them, and re-layouts  35.4 us (3%)
  between operations  16.5 us (2%)
  matrix products  14.6 us (1%)
    reduce_scatter x4, waiting for transfers between devices, scatter_sum(): return lax.psum_scatter(partial, axis, scatter_dimension=0, tiled=True)  213 us
    all_gather x4, waiting for transfers between devices, gather_rows(): return lax.all_gather(block, axis, axis=0, tiled=True)  138 us
    ppermute x12, waiting for transfers between devices, exchange(): moved.append(lax.ppermute(made[hop - 1], axis, pairs))  113 us
    ppermute x12, waiting for transfers between devices, cube_gather(): moved = lax.ppermute(held, axis, [(i, i ^ bit) for i in range(n)])  61.8 us
    all_gather x1, waiting for transfers between devices, block(): gathered = lax.all_gather(tokens, TP, axis=0)  59.3 us
    ppermute x10, waiting for transfers between devices, cube_sum(): lax.ppermute(vector, axis, [(i, i ^ bit) for i in range(n)])  51.9 us
    pallas_call x3, Pallas kernels, product(): pl.pallas_call(kernel, grid=(count * column_steps,), in_specs=[pl.BlockSp...  50.1 us
    pallas_call x2, Pallas kernels, pair_product(): pl.pallas_call(kernel, grid_spec=pltpu.PrefetchScalarGridSpec(num_scalar_...  30.2 us
  transfers between devices with their start and end apart: 45, of which 27 were waited for; matrix products, arithmetic and copies ran while one was open for 6% of the time, Pallas kernels for 17%

profile of v9, /device:TPU:0, one launch (start us, length us, event | category | flops | bytes accessed | tf_op | source)
XLA Modules:
  0.0 1063.6 jit_solution(1519484533342675756)
XLA Ops:
  34.6 59.3 %all-gather.19.cloned.1.call-done = bf16[1024,2048]{1,0:T(8,128)(2,1)} async-done(((bf16[256,2048]{1,0:T(8,128)(2,1)}), bf16[1024,2048]{1,0:T(8,128)(2,1)}) %all-gather.19.cloned.1.call-update) | async-done | bytes 4194320 | tf_op jit(solution)/shard_map/all_gather | solution.py:754
  93.9 8.4 norm_project.1
  102.3 13.7 %attend.1 = (bf16[1024,512]{1,0:T(8,128)(2,1)}, bf16[512,1024]{1,0:T(8,128)(2,1)}, f32[2,4,1024]{2,1,0:T(4,128)}) custom-call(bf16[768,1024]{1,0:T(8,128)(2,1)} %get-tuple-element.42.packed_ref), custom_call_target="tpu_custom_call" | custom-call | flops 1073741824 | bytes 4194304 | tf_op jit(solution)/shard_map/attend/pallas_call | solution.py:185
  116.0 6.5 all-gather.23.cloned.1.call-done
  126.9 10.2 collective-permute-done
  143.7 19.2 %collective-permute-done.1 = bf16[2,4,64,1024]{3,2,1,0:T(8,128)(2,1)} collective-permute-done((bf16[2,4,64,1024]{3,2,1,0:T(8,128)(2,1)}, bf16[2,4,64,1024]{3,2,1,0:T(8,128)(2,1)}, u32[]{:S(2)}, u32[]{:S(2)}) %collective-permute-start.1) | collective-permute-done | bytes 1048608 | tf_op jit(solution)/shard_map/ppermute | solution.py:56
  180.8 24.0 %all-gather.21.cloned.1.call-done = bf16[4096,512]{1,0:T(8,128)(2,1)} async-done(((bf16[1024,512]{1,0:T(8,128)(2,1)}), bf16[4096,512]{1,0:T(8,128)(2,1)}) %all-gather.21.cloned.1.call-update) | async-done | bytes 4194320 | tf_op jit(solution)/shard_map/all_gather | solution.py:770
  204.8 18.8 %project_and_norm.1 = (f32[256,2048]{1,0:T(8,128)}, bf16[1024,2048]{1,0:T(8,128)(2,1)}, bf16[2048,1024]{1,0:T(8,128)(2,1)}) custom-call(s32[2]{0:T(128)} %pad_add_fusion.at_ref, bf16[4,1024,512]{2,1,0:T(8,128)(2,1)} %bitcast.60, bf16[8,4,64,1024]{3,2,1,0:T(8,128)(2,1)} %pad_maximum_fusion.1.first_ref, bf16[8,4,64,1024]{3,2,1,0:T(8,128)(2,1)} %pad_maximum_fusion.2.second_ref, ...), custom_call_target="tpu_custom_call" | custom-call | flops 8589934592 | bytes 25165824 | tf_op jit(solution)/shard_map/project_and_norm/pallas_call | solution.py:339
  223.6 25.1 %gated_up.1 = (bf16[1024,2048]{1,0:T(8,128)(2,1)}, bf16[2048,1024]{1,0:T(8,128)(2,1)}, bf16[1024,2048]{1,0:T(8,128)(2,1)}, bf16[1024,2048]{1,0:T(8,128)(2,1)}) custom-call(bf16[1024,2048]{1,0:T(8,128)(2,1)} %get-tuple-element.45.normed_ref, bf16[2048,2048]{1,0:T(8,128)(2,1)} %first_w_ref.3, bf16[2048,2048]{1,0:T(8,128)(2,1)} %second_w_ref.3), custom_call_target="tpu_custom_call" | custom-call | flops 17179869184 | bytes 37748736 | tf_op jit(solution)/shard_map/gated_up/pallas_call | solution.py:392
  248.7 36.8 %all-gather.11.cloned.1.call-done.cot_ref.refs_0_ = bf16[1024,2048]{1,0:T(8,128)(2,1)} async-done(((bf16[256,2048]{1,0:T(8,128)(2,1)}), bf16[1024,2048]{1,0:T(8,128)(2,1)}) %all-gather.11.cloned.1.call-update) | async-done | bytes 4194320 | tf_op jit(solution)/shard_map/all_gather | solution.py:38
  285.5 16.2 %gated_back.1 = (bf16[1024,2048]{1,0:T(8,128)(2,1)}, bf16[1024,2048]{1,0:T(8,128)(2,1)}) custom-call(bf16[1024,2048]{1,0:T(8,128)(2,1)} %all-gather.11.cloned.1.call-done.cot_ref.refs_0_, bf16[2048,2048]{1,0:T(8,128)(2,1)} %weight_ref.1, bf16[1024,2048]{1,0:T(8,128)(2,1)} %get-tuple-element.47.smooth_ref, bf16[1024,2048]{1,0:T(8,128)(2,1)} %get-tuple-element.48.slope_ref), custom_call_target="tpu_custom_call" | custom-call | flops 8589934592 | bytes 29360128 | tf_op jit(solution)/shard_map/gated_back/pallas_call | solution.py:425
  301.8 10.0 pair_product.2
  311.7 20.2 %pair_product.3 = (bf16[256,2048]{1,0:T(8,128)(2,1)}, bf16[256,2048]{1,0:T(8,128)(2,1)}, bf16[256,2048]{1,0:T(8,128)(2,1)}) custom-call(s32[3]{0:T(128)} %pad_add_fusion.1.at_ref, bf16[1024,2048]{1,0:T(8,128)(2,1)} %get-tuple-element.49.first_ref.refs_0_, bf16[1024,2048]{1,0:T(8,128)(2,1)} %get-tuple-element.50.second_ref.refs_1_, ...), custom_call_target="tpu_custom_call" | custom-call | flops 12884901888 | bytes 20971520 | tf_op jit(solution)/shard_map/pair_product/pallas_call | solution.py:511
  339.9 43.8 %collective-permute-done.13.refs_1_ = bf16[256,2048]{1,0:T(8,128)(2,1)} collective-permute-done((bf16[256,2048]{1,0:T(8,128)(2,1)}, bf16[256,2048]{1,0:T(8,128)(2,1)}, u32[]{:S(2)}, u32[]{:S(2)}) %collective-permute-start.13) | collective-permute-done | bytes 1048608 | tf_op jit(solution)/shard_map/ppermute | solution.py:619
  390.0 101.2 %all-gather.13.cloned.1.call-done = bf16[1024,2048]{1,0:T(8,128)(2,1)} async-done(((bf16[256,2048]{1,0:T(8,128)(2,1)}), bf16[1024,2048]{1,0:T(8,128)(2,1)}) %all-gather.13.cloned.1.call-update) | async-done | bytes 4194320 | tf_op jit(solution)/shard_map/all_gather | solution.py:38
  502.3 20.2 %attend_back.1.d_ref = bf16[768,1024]{1,0:T(8,128)(2,1)} custom-call(bf16[768,1024]{1,0:T(8,128)(2,1)} %get-tuple-element.42.packed_ref, bf16[512,1024]{1,0:T(8,128)(2,1)} %fusion.1.d_heads_ref, f32[2,4,1024]{2,1,0:T(4,128)} %get-tuple-element.56.total_ref, f32[32,512]{1,0:T(8,128)} %get-tuple-element.94.cos_ref, f32[32,512]{1,0:T(8,128)} %get-tuple-element.93.sin_ref), custom_call_target="tpu_custom_call" | custom-call | flops 2684354560 | bytes 6291456 | tf_op jit(solution)/shard_map/attend_back/pallas_call | solution.py:265
  531.9 23.5 %product.4 = bf16[2048,4096]{1,0:T(8,128)(2,1)} custom-call(bf16[2048,1024]{1,0:T(8,128)(2,1)} %get-tuple-element.71.left_ref, bf16[1024,2048]{1,0:T(8,128)(2,1)} %get-tuple-element.49.first_ref.refs_0_, bf16[1024,2048]{1,0:T(8,128)(2,1)} %get-tuple-element.50.second_ref.refs_1_), custom_call_target="tpu_custom_call" | custom-call | flops 17179869184 | bytes 29360128 | tf_op jit(solution)/shard_map/product/pallas_call | solution.py:470
  555.5 13.4 %product.5 = bf16[2048,2048]{1,0:T(8,128)(2,1)} custom-call(bf16[2048,1024]{1,0:T(8,128)(2,1)} %get-tuple-element.72.left_ref, bf16[1024,2048]{1,0:T(8,128)(2,1)} %all-gather.11.cloned.1.call-done.cot_ref.refs_0_), custom_call_target="tpu_custom_call" | custom-call | flops 8589934592 | bytes 16777216 | tf_op jit(solution)/shard_map/product/pallas_call | solution.py:470
  568.9 17.7 %reduce-scatter.7.cloned.1.call-done = bf16[256,1280]{1,0:T(8,128)(2,1)} async-done(((bf16[2048,1280]{1,0:T(8,128)(2,1)}), bf16[256,1280]{1,0:T(8,128)(2,1)}) %reduce-scatter.7.cloned.1.call-update) | async-done | bytes 655376 | tf_op jit(solution)/shard_map/reduce_scatter | solution.py:42
  586.7 120.0 %reduce-scatter.9.cloned.1.call-done = bf16[256,4096]{1,0:T(8,128)(2,1)} async-done(((bf16[2048,4096]{1,0:T(8,128)(2,1)}), bf16[256,4096]{1,0:T(8,128)(2,1)}) %reduce-scatter.9.cloned.1.call-update) | async-done | bytes 2097168 | tf_op jit(solution)/shard_map/reduce_scatter | solution.py:42
  706.7 75.4 %reduce-scatter.11.cloned.1.call-done = bf16[256,2048]{1,0:T(8,128)(2,1)} async-done(((bf16[2048,2048]{1,0:T(8,128)(2,1)}), bf16[256,2048]{1,0:T(8,128)(2,1)}) %reduce-scatter.11.cloned.1.call-update) | async-done | bytes 1048592 | tf_op jit(solution)/shard_map/reduce_scatter | solution.py:42
  785.5 15.6 %collective-permute-done.28 = bf16[1,256,1024]{2,1,0:T(8,128)(2,1)S(1)} collective-permute-done((bf16[1,256,1024]{2,1,0:T(8,128)(2,1)S(1)}, bf16[1,256,1024]{2,1,0:T(8,128)(2,1)S(1)}, u32[]{:S(2)}, u32[]{:S(2)}) %collective-permute-start.28) | collective-permute-done | bytes 524320 | tf_op jit(solution)/shard_map/ppermute | solution.py:56
  804.8 13.2 %product.3 = bf16[1024,2048]{1,0:T(8,128)(2,1)} custom-call(bf16[1024,2048]{1,0:T(8,128)(2,1)} %get-tuple-element.46.left_ref, bf16[2048,2048]{1,0:T(8,128)(2,1)} %weight_ref.1), custom_call_target="tpu_custom_call" | custom-call | flops 8589934592 | bytes 16777216 | tf_op jit(solution)/shard_map/product/pallas_call | solution.py:470
  825.4 16.3 %collective-permute-done.29 = bf16[2,256,1024]{2,1,0:T(8,128)(2,1)} collective-permute-done((bf16[2,256,1024]{2,1,0:T(8,128)(2,1)}, bf16[2,256,1024]{2,1,0:T(8,128)(2,1)}, u32[]{:S(2)}, u32[]{:S(2)}) %collective-permute-start.29) | collective-permute-done | bytes 1048608 | tf_op jit(solution)/shard_map/ppermute | solution.py:56
  851.1 36.3 %collective-permute-done.7 = bf16[256,1024]{1,0:T(8,128)(2,1)} collective-permute-done((bf16[256,1024]{1,0:T(8,128)(2,1)S(1)}, bf16[256,1024]{1,0:T(8,128)(2,1)}, u32[]{:S(2)}, u32[]{:S(2)}) %collective-permute-start.7) | collective-permute-done | bytes 524320 | tf_op jit(solution)/shard_map/ppermute | solution.py:619
  887.8 8.8 projection_back.3
  919.2 8.1 collective-permute-start.26
  937.6 38.6 %collective-permute-done.27 = f32[2048]{0:T(1024)S(1)} collective-permute-done((f32[2048]{0:T(1024)S(1)}, f32[2048]{0:T(1024)S(1)}, u32[]{:S(2)}, u32[]{:S(2)}) %collective-permute-start.27) | collective-permute-done | bytes 8224 | tf_op jit(solution)/shard_map/ppermute | solution.py:69
  982.2 23.9 %collective-permute-done.16.refs_1_ = bf16[256,2048]{1,0:T(8,128)(2,1)} collective-permute-done((bf16[256,2048]{1,0:T(8,128)(2,1)}, bf16[256,2048]{1,0:T(8,128)(2,1)}, u32[]{:S(2)}, u32[]{:S(2)}) %collective-permute-start.16) | collective-permute-done | bytes 1048608 | tf_op jit(solution)/shard_map/ppermute | solution.py:619
  1018.2 13.9 %place_blocks.1 = f32[2048,2048]{1,0:T(8,128)} custom-call(s32[1]{0:T(128)} %bitcast.1.at_ref, bf16[4,256,1024]{2,1,0:T(8,128)(2,1)} %pad_maximum_fusion.5.refs_0_, bf16[4,256,1024]{2,1,0:T(8,128)(2,1)} %collective-permute-done.30.refs_1_, bf16[4,256,1024]{2,1,0:T(8,128)(2,1)} %pad_maximum_fusion.6.refs_2_, bf16[4,256,1024]{2,1,0:T(8,128)(2,1)} %collective-permute-done.33.refs_3_), custom_call_target="tpu_custom_call" | custom-call | bytes 25165824 | tf_op jit(solution)/shard_map/place_blocks/pallas_call | solution.py:651
  1032.0 7.0 unpack_attention.1
  1039.0 17.2 %slice_convert_fusion = (f32[2048,2048]{1,0:T(8,128)}, f32[2048,2048]{1,0:T(8,128)}) fusion(bf16[2048,4096]{1,0:T(8,128)(2,1)} %all-gather.17.cloned.1.call-done), kind=kLoop, calls=%fused_computation | loop fusion | flops 8388608 | bytes 50331648 | tf_op jit(solution)/shard_map/convert_element_type | solution.py:830
  (181 shorter events, 164.8 us)
Async XLA Ops:
  8.0 85.9 %all-gather.19.cloned.1.call-start = ((), (), s32[]{:S(2)}) async-start(), calls=%async_computation.12 | async-start | bytes 5242880 | tf_op jit(solution)/shard_map/all_gather | solution.py:754
  8.8 113.8 %all-gather.23.cloned.1.call-start = ((), (), s32[]{:S(2)}) async-start(), calls=%async_computation.14 | async-start | bytes 1310720 | tf_op jit(solution)/shard_map/all_gather | solution.py:756
  10.4 160.7 %reduce-scatter.5.cloned.1.call-start = ((), (), s32[]{:S(2)}) async-start(), calls=%async_computation.4 | async-start | bytes 73728 | tf_op jit(solution)/shard_map/reduce_scatter | solution.py:42
  11.9 192.9 %all-gather.21.cloned.1.call-start = ((), (), s32[]{:S(2)}) async-start(), calls=%async_computation.13 | async-start | bytes 5242880 | tf_op jit(solution)/shard_map/all_gather | solution.py:770
  116.0 169.5 %all-gather.11.cloned.1.call-start = ((), (), s32[]{:S(2)}) async-start(), calls=%async_computation.5 | async-start | bytes 5242880 | tf_op jit(solution)/shard_map/all_gather | solution.py:38
  139.0 24.0 %collective-permute-start.1 = (bf16[2,4,64,1024]{3,2,1,0:T(8,128)(2,1)}, bf16[2,4,64,1024]{3,2,1,0:T(8,128)(2,1)}, u32[]{:S(2)}, u32[]{:S(2)}) collective-permute-start(bf16[2,4,64,1024]{3,2,1,0:T(8,128)(2,1)} %pad_maximum_fusion.7), channel_id=1, source_target_pairs={{0,16},{4,20},{8,24},{12,28},{16,0},{20,4},{24,8},{28,12},{1,17},{... | collective-permute-start | bytes 3145736 | tf_op jit(solution)/shard_map/ppermute | solution.py:56
  140.5 350.7 %all-gather.13.cloned.1.call-start = ((), (), s32[]{:S(2)}) async-start(), calls=%async_computation.6 | async-start | bytes 5242880 | tf_op jit(solution)/shard_map/all_gather | solution.py:38
  142.2 23.7 %collective-permute-start.4 = (bf16[2,4,64,1024]{3,2,1,0:T(8,128)(2,1)S(1)}, bf16[2,4,64,1024]{3,2,1,0:T(8,128)(2,1)S(1)}, u32[]{:S(2)}, u32[]{:S(2)}) collective-permute-start(bf16[2,4,64,1024]{3,2,1,0:T(8,128)(2,1)S(1)} %pad_maximum_fusion.8), channel_id=1, source_target_pairs={{0,8},{4,12},{8,0},{12,4},{16,24},{20,28},{24,16},{28,20},{1,9},{5... | collective-permute-start | bytes 3145736 | tf_op jit(solution)/shard_map/ppermute | solution.py:56
  311.7 28.1 %collective-permute-start.12 = (bf16[256,2048]{1,0:T(8,128)(2,1)}, bf16[256,2048]{1,0:T(8,128)(2,1)S(1)}, u32[]{:S(2)}, u32[]{:S(2)}) collective-permute-start(bf16[256,2048]{1,0:T(8,128)(2,1)} %pair_product.2), channel_id=1, source_target_pairs={{0,1},{1,2},{2,3},{3,0},{4,5},{5,6},{6,7},{7,4},{8,9},{9,10},{10,1... | collective-permute-start | bytes 3145736 | tf_op jit(solution)/shard_map/ppermute | solution.py:619
  331.9 51.7 %collective-permute-start.13 = (bf16[256,2048]{1,0:T(8,128)(2,1)}, bf16[256,2048]{1,0:T(8,128)(2,1)}, u32[]{:S(2)}, u32[]{:S(2)}) collective-permute-start(bf16[256,2048]{1,0:T(8,128)(2,1)} %get-tuple-element.51), channel_id=1, source_target_pairs={{0,2},{1,3},{2,0},{3,1},{4,6},{5,7},{6,4},{7,5},{8,10},{9,11},{10,... | collective-permute-start | bytes 3145736 | tf_op jit(solution)/shard_map/ppermute | solution.py:619
  333.1 50.5 %collective-permute-start.14 = (bf16[256,2048]{1,0:T(8,128)(2,1)}, bf16[256,2048]{1,0:T(8,128)(2,1)}, u32[]{:S(2)}, u32[]{:S(2)}) collective-permute-start(bf16[256,2048]{1,0:T(8,128)(2,1)} %get-tuple-element.52), channel_id=1, source_target_pairs={{0,3},{1,0},{2,1},{3,2},{4,7},{5,4},{6,5},{7,6},{8,11},{9,8},{10,9... | collective-permute-start | bytes 3145736 | tf_op jit(solution)/shard_map/ppermute | solution.py:619
  389.8 196.8 %reduce-scatter.7.cloned.1.call-start = ((), (), s32[]{:S(2)}) async-start(), calls=%async_computation.7 | async-start | bytes 5898240 | tf_op jit(solution)/shard_map/reduce_scatter | solution.py:42
  531.7 175.0 %reduce-scatter.9.cloned.1.call-start = ((), (), s32[]{:S(2)}) async-start(), calls=%async_computation.9 | async-start | bytes 18874368 | tf_op jit(solution)/shard_map/reduce_scatter | solution.py:42
  555.4 226.7 %reduce-scatter.11.cloned.1.call-start = ((), (), s32[]{:S(2)}) async-start(), calls=%async_computation.11 | async-start | bytes 9437184 | tf_op jit(solution)/shard_map/reduce_scatter | solution.py:42
  568.9 463.1 %all-gather.15.cloned.1.call-start = ((), (), s32[]{:S(2)}) async-start(), calls=%async_computation.8 | async-start | bytes 5898240 | tf_op jit(solution)/shard_map/all_gather | solution.py:38
  586.7 452.3 %all-gather.17.cloned.1.call-start = ((), (), s32[]{:S(2)}) async-start(), calls=%async_computation.10 | async-start | bytes 18874368 | tf_op jit(solution)/shard_map/all_gather | solution.py:38
  784.9 19.0 %collective-permute-start.31 = (bf16[1,256,1024]{2,1,0:T(8,128)(2,1)S(1)}, bf16[1,256,1024]{2,1,0:T(8,128)(2,1)S(1)}, u32[]{:S(2)}, u32[]{:S(2)}) collective-permute-start(bf16[1,256,1024]{2,1,0:T(8,128)(2,1)S(1)} %get-tuple-element.85), channel_id=1, source_target_pairs={{0,16},{4,20},{8,24},{12,28},{16,0},{20,4},{24,8},{28,12},{1,17},{... | collective-permute-start | bytes 1572872 | tf_op jit(solution)/shard_map/ppermute | solution.py:56
  802.1 39.6 %collective-permute-start.29 = (bf16[2,256,1024]{2,1,0:T(8,128)(2,1)}, bf16[2,256,1024]{2,1,0:T(8,128)(2,1)}, u32[]{:S(2)}, u32[]{:S(2)}) collective-permute-start(bf16[2,256,1024]{2,1,0:T(8,128)(2,1)} %pad_maximum_fusion.9), channel_id=1, source_target_pairs={{0,16},{4,20},{8,24},{12,28},{16,0},{20,4},{24,8},{28,12},{1,17},{... | collective-permute-start | bytes 3145736 | tf_op jit(solution)/shard_map/ppermute | solution.py:56
  804.0 40.5 %collective-permute-start.32 = (bf16[2,256,1024]{2,1,0:T(8,128)(2,1)S(1)}, bf16[2,256,1024]{2,1,0:T(8,128)(2,1)}, u32[]{:S(2)}, u32[]{:S(2)}) collective-permute-start(bf16[2,256,1024]{2,1,0:T(8,128)(2,1)S(1)} %pad_maximum_fusion.10), channel_id=1, source_target_pairs={{0,8},{4,12},{8,0},{12,4},{16,24},{20,28},{24,16},{28,20},{1,9},{5... | collective-permute-start | bytes 3145736 | tf_op jit(solution)/shard_map/ppermute | solution.py:56
  821.1 26.7 %collective-permute-start.8 = (bf16[256,1024]{1,0:T(8,128)(2,1)S(1)}, bf16[256,1024]{1,0:T(8,128)(2,1)}, u32[]{:S(2)}, u32[]{:S(2)}) collective-permute-start(bf16[256,1024]{1,0:T(8,128)(2,1)S(1)} %get-tuple-element.81), channel_id=1, source_target_pairs={{0,3},{1,0},{2,1},{3,2},{4,7},{5,4},{6,5},{7,6},{8,11},{9,8},{10,9... | collective-permute-start | bytes 1572872 | tf_op jit(solution)/shard_map/ppermute | solution.py:619
  824.3 63.1 %collective-permute-start.7 = (bf16[256,1024]{1,0:T(8,128)(2,1)S(1)}, bf16[256,1024]{1,0:T(8,128)(2,1)}, u32[]{:S(2)}, u32[]{:S(2)}) collective-permute-start(bf16[256,1024]{1,0:T(8,128)(2,1)S(1)} %get-tuple-element.82), channel_id=1, source_target_pairs={{0,2},{1,3},{2,0},{3,1},{4,6},{5,7},{6,4},{7,5},{8,10},{9,11},{10,... | collective-permute-start | bytes 1572872 | tf_op jit(solution)/shard_map/ppermute | solution.py:619
  824.3 63.1 %collective-permute-start.6 = (bf16[256,1024]{1,0:T(8,128)(2,1)S(1)}, bf16[256,1024]{1,0:T(8,128)(2,1)}, u32[]{:S(2)}, u32[]{:S(2)}) collective-permute-start(bf16[256,1024]{1,0:T(8,128)(2,1)S(1)} %get-tuple-element.77), channel_id=1, source_target_pairs={{0,1},{1,2},{2,3},{3,0},{4,5},{5,6},{6,7},{7,4},{8,9},{9,10},{10,1... | collective-permute-start | bytes 1572872 | tf_op jit(solution)/shard_map/ppermute | solution.py:619
  844.5 173.6 %collective-permute-start.30 = (bf16[4,256,1024]{2,1,0:T(8,128)(2,1)}, bf16[4,256,1024]{2,1,0:T(8,128)(2,1)}, u32[]{:S(2)}, u32[]{:S(2)}) collective-permute-start(bf16[4,256,1024]{2,1,0:T(8,128)(2,1)} %pad_maximum_fusion.5.refs_0_), channel_id=1, source_target_pairs={{0,4},{4,0},{8,12},{12,8},{16,20},{20,16},{24,28},{28,24},{1,5},{5... | collective-permute-start | bytes 6291464 | tf_op jit(solution)/shard_map/ppermute | solution.py:56
  847.3 170.9 %collective-permute-start.33 = (bf16[4,256,1024]{2,1,0:T(8,128)(2,1)}, bf16[4,256,1024]{2,1,0:T(8,128)(2,1)}, u32[]{:S(2)}, u32[]{:S(2)}) collective-permute-start(bf16[4,256,1024]{2,1,0:T(8,128)(2,1)} %pad_maximum_fusion.6.refs_2_), channel_id=1, source_target_pairs={{0,4},{4,0},{8,12},{12,8},{16,20},{20,16},{24,28},{28,24},{1,5},{5... | collective-permute-start | bytes 6291464 | tf_op jit(solution)/shard_map/ppermute | solution.py:56
  847.8 48.7 %collective-permute-start.11 = (bf16[256,1024]{1,0:T(8,128)(2,1)}, bf16[256,1024]{1,0:T(8,128)(2,1)S(1)}, u32[]{:S(2)}, u32[]{:S(2)}) collective-permute-start(bf16[256,1024]{1,0:T(8,128)(2,1)} %get-tuple-element.78), channel_id=1, source_target_pairs={{0,3},{1,0},{2,1},{3,2},{4,7},{5,4},{6,5},{7,6},{8,11},{9,8},{10,9... | collective-permute-start | bytes 1572872 | tf_op jit(solution)/shard_map/ppermute | solution.py:619
  887.4 46.2 %collective-permute-start.10 = (bf16[256,1024]{1,0:T(8,128)(2,1)}, bf16[256,1024]{1,0:T(8,128)(2,1)S(1)}, u32[]{:S(2)}, u32[]{:S(2)}) collective-permute-start(bf16[256,1024]{1,0:T(8,128)(2,1)} %get-tuple-element.79), channel_id=1, source_target_pairs={{0,2},{1,3},{2,0},{3,1},{4,6},{5,7},{6,4},{7,5},{8,10},{9,11},{10,... | collective-permute-start | bytes 1572872 | tf_op jit(solution)/shard_map/ppermute | solution.py:619
  887.4 48.1 %collective-permute-start.9 = (bf16[256,1024]{1,0:T(8,128)(2,1)}, bf16[256,1024]{1,0:T(8,128)(2,1)S(1)}, u32[]{:S(2)}, u32[]{:S(2)}) collective-permute-start(bf16[256,1024]{1,0:T(8,128)(2,1)} %get-tuple-element.80), channel_id=1, source_target_pairs={{0,1},{1,2},{2,3},{3,0},{4,5},{5,6},{6,7},{7,4},{8,9},{9,10},{10,1... | collective-permute-start | bytes 1572872 | tf_op jit(solution)/shard_map/ppermute | solution.py:619
  932.6 43.7 %collective-permute-start.27 = (f32[2048]{0:T(1024)S(1)}, f32[2048]{0:T(1024)S(1)}, u32[]{:S(2)}, u32[]{:S(2)}) collective-permute-start(f32[2048]{0:T(1024)S(1)} %add.153), channel_id=1, source_target_pairs={{0,2},{1,3},{2,0},{3,1},{4,6},{5,7},{6,4},{7,5},{8,10},{9,11},{10,... | collective-permute-start | bytes 24584 | tf_op jit(solution)/shard_map/ppermute | solution.py:69
  933.6 43.0 %collective-permute-start.22 = (f32[2048]{0:T(1024)S(1)}, f32[2048]{0:T(1024)S(1)}, u32[]{:S(2)}, u32[]{:S(2)}) collective-permute-start(f32[2048]{0:T(1024)S(1)} %add.148), channel_id=1, source_target_pairs={{0,2},{1,3},{2,0},{3,1},{4,6},{5,7},{6,4},{7,5},{8,10},{9,11},{10,... | collective-permute-start | bytes 24584 | tf_op jit(solution)/shard_map/ppermute | solution.py:69
  935.6 46.7 %collective-permute-start.15 = (bf16[256,2048]{1,0:T(8,128)(2,1)}, bf16[256,2048]{1,0:T(8,128)(2,1)S(1)}, u32[]{:S(2)}, u32[]{:S(2)}) collective-permute-start(bf16[256,2048]{1,0:T(8,128)(2,1)} %get-tuple-element.57), channel_id=1, source_target_pairs={{0,1},{1,2},{2,3},{3,0},{4,5},{5,6},{6,7},{7,4},{8,9},{9,10},{10,1... | collective-permute-start | bytes 3145736 | tf_op jit(solution)/shard_map/ppermute | solution.py:619
  976.2 29.9 %collective-permute-start.16 = (bf16[256,2048]{1,0:T(8,128)(2,1)}, bf16[256,2048]{1,0:T(8,128)(2,1)}, u32[]{:S(2)}, u32[]{:S(2)}) collective-permute-start(bf16[256,2048]{1,0:T(8,128)(2,1)} %get-tuple-element.58), channel_id=1, source_target_pairs={{0,2},{1,3},{2,0},{3,1},{4,6},{5,7},{6,4},{7,5},{8,10},{9,11},{10,... | collective-permute-start | bytes 3145736 | tf_op jit(solution)/shard_map/ppermute | solution.py:619
  976.6 35.5 %collective-permute-start.17 = (bf16[256,2048]{1,0:T(8,128)(2,1)}, bf16[256,2048]{1,0:T(8,128)(2,1)}, u32[]{:S(2)}, u32[]{:S(2)}) collective-permute-start(bf16[256,2048]{1,0:T(8,128)(2,1)} %get-tuple-element.59), channel_id=1, source_target_pairs={{0,3},{1,0},{2,1},{3,2},{4,7},{5,4},{6,5},{7,6},{8,11},{9,8},{10,9... | collective-permute-start | bytes 3145736 | tf_op jit(solution)/shard_map/ppermute | solution.py:619
  (32 other events, 330.5 us)
Sparse Core Ops, SparseCore 0:
  10.4 83.4 all-gather.18
  96.0 26.4 all-gather.22
  124.7 80.1 all-gather.20
  206.3 79.2 all-gather.10
  389.9 101.2 all-gather.12
Sparse Core Ops, SparseCore 1:
  14.4 36.2 reduce-scatter.4
  531.7 54.8 reduce-scatter.6
  590.6 116.0 reduce-scatter.8
  710.7 71.3 reduce-scatter.10
  784.0 59.1 all-gather.14
  845.1 89.9 all-gather.16

commit v10 on v9

--- a/solution.py
+++ b/solution.py
@@ -316,8 +316,11 @@
                 (0, first_ref, first_offsets),
                 (half, second_ref, second_offsets),
             ):
-                for part in range(parts):
-                    for g in range(groups):
+
+
+                @pl.loop(0, groups)
+                def _(g, side=side, part_ref=part_ref, offsets=offsets):
+                    for part in range(parts):
                         start = g * group_columns + (at_ref[1] ^ offsets[part]) * depth
                         at = pl.ds(pl.multiple_of(start, depth), depth)
                         weight_ref[at, side : side + half] = part_ref[part, g]
@@ -414,12 +417,12 @@
     columns = w_down.shape[0]
     tile = 512
 
-    def kernel(cot_ref, weight_ref, smooth_ref, slope_ref, d_gate_ref, d_up_ref):
+    def kernel(cot_ref, weight_ref, smooth_ref, slope_ref, out_ref):
         for start in range(0, tile, 256):
             here = slice(start, start + 256)
             d_active = dot_lanes(cot_ref[...], weight_ref[here, :])
-            d_up_ref[:, here] = (d_active * smooth_ref[:, here].astype(jnp.float32)).astype(LOW)
-            d_gate_ref[:, here] = (d_active * slope_ref[:, here].astype(jnp.float32)).astype(LOW)
+            out_ref[0, :, here] = (d_active * slope_ref[:, here].astype(jnp.float32)).astype(LOW)
+            out_ref[1, :, here] = (d_active * smooth_ref[:, here].astype(jnp.float32)).astype(LOW)
 
     column_block = pl.BlockSpec((rows, tile), lambda j: (0, j))
     return pl.pallas_call(
@@ -431,8 +434,8 @@
             column_block,
             column_block,
         ],
-        out_specs=[column_block] * 2,
-        out_shape=[jax.ShapeDtypeStruct((rows, columns), LOW)] * 2,
+        out_specs=pl.BlockSpec((2, rows, tile), lambda j: (0, 0, j)),
+        out_shape=jax.ShapeDtypeStruct((2, rows, columns), LOW),
         cost_estimate=pl.CostEstimate(
             flops=2 * rows * width * columns, transcendentals=0, bytes_accessed=28 << 20
         ),
@@ -440,38 +443,26 @@
     )(all_cot, w_down, smooth, slope)
 
 
-def product(left, rights, folds):
+def product(left, right, folds):
     rows, depth = left.shape
-    each = rights[0].shape[1]
+    right = right.reshape(-1, depth, right.shape[-1])
+    count, _, each = right.shape
     tile = 512
-    column_steps = each // tile
-    count = len(rights)
-    per = count * column_steps // folds
-
-    def kernel(left_ref, *refs):
-        out_ref = refs[count]
-        for k in range(count):
-
-            def _(k=k):
-                out_ref[...] = jnp.dot(
-                    left_ref[...], refs[k][...], preferred_element_type=jnp.float32
-                ).astype(LOW)
-
-            if count == 1:
-                _()
-            else:
-                pl.when(pl.program_id(0) // column_steps == k)(_)
-
-    def right_block(k):
-        return pl.BlockSpec(
-            (depth, tile), lambda j: (0, jnp.clip(j - k * column_steps, 0, column_steps - 1))
-        )
-
-    return pl.pallas_call(
-        kernel,
-        grid=(count * column_steps,),
-        in_specs=[pl.BlockSpec((rows, depth), lambda j: (0, 0))]
-        + [right_block(k) for k in range(count)],
+    steps = each // tile
+    per = count * steps // folds
+
+    def kernel(left_ref, right_ref, out_ref):
+        out_ref[...] = jnp.dot(
+            left_ref[...], right_ref[0], preferred_element_type=jnp.float32
+        ).astype(LOW)
+
+    return pl.pallas_call(
+        kernel,
+        grid=(count * steps,),
+        in_specs=[
+            pl.BlockSpec((rows, depth), lambda j: (0, 0)),
+            pl.BlockSpec((1, depth, tile), lambda j: (j // steps, 0, j % steps)),
+        ],
         out_specs=pl.BlockSpec((rows, tile), lambda j: (j // per, j % per)),
         out_shape=jax.ShapeDtypeStruct((rows * folds, count * each // folds), LOW),
         cost_estimate=pl.CostEstimate(
@@ -480,17 +471,17 @@
             bytes_accessed=2 * (rows * depth + (depth + rows) * count * each),
         ),
         name="product",
-    )(left, *rights)
-
-
-def pair_product(places, tile, first, first_weight, second, second_weight):
-    rows, depth = first.shape
+    )(left, right)
+
+
+def pair_product(places, tile, pair, first_weight, second_weight):
+    _, rows, depth = pair.shape
     columns = first_weight.shape[0]
     count = len(places)
     part = 512 if count == 1 else 256
     at = jnp.stack(places)
 
-    def kernel(at_ref, first_ref, second_ref, first_w_ref, second_w_ref, *out_refs):
+    def kernel(at_ref, pair_ref, first_w_ref, second_w_ref, *out_refs):
         for k, out_ref in enumerate(out_refs):
             here = (
                 slice(None)
@@ -498,14 +489,14 @@
                 else pl.ds(pl.multiple_of(at_ref[k] * tile, tile), tile)
             )
             out_ref[...] = (
-                dot_lanes(first_ref[here, :], first_w_ref[...])
-                + dot_lanes(second_ref[here, :], second_w_ref[...])
+                dot_lanes(pair_ref[0, here, :], first_w_ref[...])
+                + dot_lanes(pair_ref[1, here, :], second_w_ref[...])
             ).astype(LOW)
 
     held = (
-        pl.BlockSpec((tile, depth), lambda j, at_ref: (at_ref[0], 0))
+        pl.BlockSpec((2, tile, depth), lambda j, at_ref: (0, at_ref[0], 0))
         if count == 1
-        else pl.BlockSpec((rows, depth), lambda j, at_ref: (0, 0))
+        else pl.BlockSpec((2, rows, depth), lambda j, at_ref: (0, 0, 0))
     )
     weight_block = pl.BlockSpec((part, depth), lambda j, at_ref: (j, 0))
     return pl.pallas_call(
@@ -513,7 +504,7 @@
         grid_spec=pltpu.PrefetchScalarGridSpec(
             num_scalar_prefetch=1,
             grid=(columns // part,),
-            in_specs=[held, held, weight_block, weight_block],
+            in_specs=[held, weight_block, weight_block],
             out_specs=[pl.BlockSpec((tile, part), lambda j, at_ref: (0, j))] * count,
         ),
         out_shape=[jax.ShapeDtypeStruct((tile, columns), LOW)] * count,
@@ -521,7 +512,7 @@
             flops=4 * count * tile * depth * columns, transcendentals=0, bytes_accessed=20 << 20
         ),
         name="pair_product",
-    )(at, first, second, first_weight, second_weight)
+    )(at, pair, first_weight, second_weight)
 
 
 def projection_back(places, d_projected, weight_rows, gathered):
@@ -706,19 +697,8 @@
     )(shared)
 
 
-def add_all(blocks):
-    return sum(block.astype(jnp.float32) for block in blocks)
-
-
 def row_major(array):
     return with_layout_constraint(array, Layout(major_to_minor=tuple(range(array.ndim))))
-
-
-def split_columns(array, parts):
-    if parts == 1:
-        return array
-    rows, columns = array.shape[0], array.shape[1] // parts
-    return array.reshape(rows, parts, columns).swapaxes(0, 1).reshape(parts * rows, columns)
 
 
 def join_columns(array, parts):
@@ -773,32 +753,27 @@
         all_heads, all_output, gathered, norm2_gain.astype(jnp.float32) + nothing.astype(jnp.float32)
     )
     activated, active_rows, smooth, slope = gated_up(normed2, w_gate, w_up)
-    mlp_part = product(activated, [w_down], 1)
-    half_width = width // 2
-
-    def part_of(columns):
-        return lambda places: [
-            lax.dynamic_slice(mlp_part, (place * own_rows, columns), (own_rows, half_width))
-            for place in places
-        ]
-
-    first_half = exchange(part_of(0), TP)
-    second_half = exchange(part_of(half_width), TP)
-    output = (
-        hidden_state
-        + jnp.concatenate([add_all(first_half), add_all(second_half)], axis=1)
-    ).astype(LOW)
-    d_gate, d_up = gated_back(all_cot, w_down, smooth, slope)
-    grad_down = product(active_rows, [all_cot], ff_folds)
+    mlp_part = product(activated, w_down, 1)
+    n_tensor = lax.axis_size(TP)
+    me = lax.axis_index(TP)
+
+    def part_of(place):
+        return lax.dynamic_slice_in_dim(mlp_part, place * own_rows, own_rows, 0)
+
+    output = hidden_state + part_of(me).astype(jnp.float32)
+    for hop in list(range(1, n_tensor, 2)) + list(range(2, n_tensor, 2)):
+        pairs = [(i, (i + hop) % n_tensor) for i in range(n_tensor)]
+        moved = lax.ppermute(part_of((me + hop) % n_tensor), TP, pairs)
+        output = output + moved.astype(jnp.float32)
+    output = output.astype(LOW)
+    d_pair = gated_back(all_cot, w_down, smooth, slope)
+    grad_down = product(active_rows, all_cot, ff_folds)
     part_down = scatter_sum(grad_down, DP)
-    dn2_blocks = exchange(
-        lambda places: pair_product(places, own_rows, d_gate, w_gate, d_up, w_up), TP
-    )
-    gate_up_grads = product(normed2_rows, [d_gate, d_up], 1)
+    dn2_blocks = exchange(lambda places: pair_product(places, own_rows, d_pair, w_gate, w_up), TP)
+    gate_up_grads = product(normed2_rows, d_pair, 1)
     part_gate_up = scatter_sum(gate_up_grads, DP)
     d_state, state_low, gain_two = norm_back(hidden_state, norm2_gain, cotangent, dn2_blocks)
     d_state_low = gather_rows(state_low, TP)
-    gain_two_sum = cube_sum(gain_two[0], (DP, TP))
     d_heads_rows = contract_cols(w_output, d_state_low).astype(LOW)
     d_projected = attend_back(projected, d_heads_rows, totals, cos_rows, sin_rows)
     gains = []
@@ -809,16 +784,17 @@
         return made
 
     dn1_blocks = exchange(dn1_blocks_of, TP)
-    gain_one_sum = cube_sum(sum(gains)[0], (DP, TP))
+    gain_sums = cube_sum(jnp.concatenate([sum(gains), gain_two], axis=1)[0], (DP, TP))
+    gain_one_sum, gain_two_sum = gain_sums[:width], gain_sums[width:]
     grad_qkv = lax.dot_general(
         normed1,
         d_projected,
         (((0,), (1,)), ((), ())),
         preferred_element_type=jnp.float32,
     ).astype(LOW)
-    grad_output = jnp.dot(heads_rows, d_state_low, preferred_element_type=jnp.float32).astype(LOW)
+    output_grads = product(heads_rows, d_state_low, folds)
     low_attn = row_major(
-        jnp.concatenate([grad_qkv, split_columns(grad_output, folds)], axis=1)
+        jnp.concatenate([grad_qkv, output_grads], axis=1)
     )
     part_attn = scatter_sum(low_attn, DP)
     down_halves = cube_gather(part_down, DP, join=False)

time: 1080 us -> 1070 us (level)
  the two profiles are of different devices: /device:TPU:0 before, /device:TPU:9 now
where the time goes in v10:
time: 1070 us; the launch traced here: 1060 us
  waiting for transfers between devices  659 us (62%)
  Pallas kernels  235 us (22%)
  starting transfers between devices  55.5 us (5%)
  other arithmetic  50.7 us (5%)
  local copies, waits for them, and re-layouts  33.1 us (3%)
  between operations  16.4 us (2%)
  matrix products  11.9 us (1%)
    reduce_scatter x4, waiting for transfers between devices, scatter_sum(): return lax.psum_scatter(partial, axis, scatter_dimension=0, tiled=True)  206 us
    ppermute x6, waiting for transfers between devices, exchange(): moved.append(lax.ppermute(made[hop - 1], axis, pairs))  153 us
    all_gather x4, waiting for transfers between devices, gather_rows(): return lax.all_gather(block, axis, axis=0, tiled=True)  114 us
    pallas_call x4, Pallas kernels, product(): pl.pallas_call(kernel, grid=(count * steps,), in_specs=[pl.BlockSpec((row...  56.4 us
    all_gather x1, waiting for transfers between devices, block(): gathered = lax.all_gather(tokens, TP, axis=0)  55.1 us
    ppermute x5, waiting for transfers between devices, cube_sum(): lax.ppermute(vector, axis, [(i, i ^ bit) for i in range(n)])  55.1 us
    ppermute x12, waiting for transfers between devices, cube_gather(): moved = lax.ppermute(held, axis, [(i, i ^ bit) for i in range(n)])  42.6 us
    pallas_call x2, Pallas kernels, pair_product(): pl.pallas_call(kernel, grid_spec=pltpu.PrefetchScalarGridSpec(num_scalar_...  30.2 us
  transfers between devices with their start and end apart: 37, of which 23 were waited for; matrix products, arithmetic and copies ran while one was open for 6% of the time, Pallas kernels for 17%

profile of v10, /device:TPU:9, one launch (start us, length us, event | category | flops | bytes accessed | tf_op | source)
XLA Modules:
  0.0 1061.8 jit_solution(15984611558741139354)
XLA Ops:
  34.6 55.1 %all-gather.19.cloned.1.call-done = bf16[1024,2048]{1,0:T(8,128)(2,1)} async-done(((bf16[256,2048]{1,0:T(8,128)(2,1)}), bf16[1024,2048]{1,0:T(8,128)(2,1)}) %all-gather.19.cloned.1.call-update) | async-done | bytes 4194320 | tf_op jit(solution)/shard_map/all_gather | solution.py:734
  89.7 8.4 norm_project.1
  98.1 13.7 %attend.1 = (bf16[1024,512]{1,0:T(8,128)(2,1)}, bf16[512,1024]{1,0:T(8,128)(2,1)}, f32[2,4,1024]{2,1,0:T(4,128)}) custom-call(bf16[768,1024]{1,0:T(8,128)(2,1)} %get-tuple-element.40.packed_ref), custom_call_target="tpu_custom_call" | custom-call | flops 1073741824 | bytes 4194304 | tf_op jit(solution)/shard_map/attend/pallas_call | solution.py:185
  111.8 8.3 all-gather.23.cloned.1.call-done
  123.9 9.7 collective-permute-done
  139.6 18.6 %collective-permute-done.1 = bf16[2,4,64,1024]{3,2,1,0:T(8,128)(2,1)} collective-permute-done((bf16[2,4,64,1024]{3,2,1,0:T(8,128)(2,1)}, bf16[2,4,64,1024]{3,2,1,0:T(8,128)(2,1)}, u32[]{:S(2)}, u32[]{:S(2)}) %collective-permute-start.1) | collective-permute-done | bytes 1048608 | tf_op jit(solution)/shard_map/ppermute | solution.py:56
  178.7 22.0 %all-gather.21.cloned.1.call-done = bf16[4096,512]{1,0:T(8,128)(2,1)} async-done(((bf16[1024,512]{1,0:T(8,128)(2,1)}), bf16[4096,512]{1,0:T(8,128)(2,1)}) %all-gather.21.cloned.1.call-update) | async-done | bytes 4194320 | tf_op jit(solution)/shard_map/all_gather | solution.py:750
  200.6 18.8 %project_and_norm.1 = (f32[256,2048]{1,0:T(8,128)}, bf16[1024,2048]{1,0:T(8,128)(2,1)}, bf16[2048,1024]{1,0:T(8,128)(2,1)}) custom-call(s32[2]{0:T(128)} %pad_add_fusion.at_ref, bf16[4,1024,512]{2,1,0:T(8,128)(2,1)} %bitcast.51, bf16[8,4,64,1024]{3,2,1,0:T(8,128)(2,1)} %pad_maximum_fusion.1.first_ref, bf16[8,4,64,1024]{3,2,1,0:T(8,128)(2,1)} %pad_maximum_fusion.2.second_ref, ...), custom_call_target="tpu_custom_call" | custom-call | flops 8589934592 | bytes 25165824 | tf_op jit(solution)/shard_map/project_and_norm/pallas_call | solution.py:342
  219.4 25.1 %gated_up.1 = (bf16[1024,2048]{1,0:T(8,128)(2,1)}, bf16[2048,1024]{1,0:T(8,128)(2,1)}, bf16[1024,2048]{1,0:T(8,128)(2,1)}, bf16[1024,2048]{1,0:T(8,128)(2,1)}) custom-call(bf16[1024,2048]{1,0:T(8,128)(2,1)} %get-tuple-element.43.normed_ref, bf16[2048,2048]{1,0:T(8,128)(2,1)} %first_w_ref.3, bf16[2048,2048]{1,0:T(8,128)(2,1)} %second_w_ref.3), custom_call_target="tpu_custom_call" | custom-call | flops 17179869184 | bytes 37748736 | tf_op jit(solution)/shard_map/gated_up/pallas_call | solution.py:395
  244.5 36.8 %all-gather.11.cloned.1.call-done.cot_ref = bf16[1024,2048]{1,0:T(8,128)(2,1)} async-done(((bf16[256,2048]{1,0:T(8,128)(2,1)}), bf16[1024,2048]{1,0:T(8,128)(2,1)}) %all-gather.11.cloned.1.call-update) | async-done | bytes 4194320 | tf_op jit(solution)/shard_map/all_gather | solution.py:38
  281.3 16.2 %gated_back.1.pair_ref.right_ref = bf16[2,1024,2048]{2,1,0:T(8,128)(2,1)} custom-call(bf16[1024,2048]{1,0:T(8,128)(2,1)} %all-gather.11.cloned.1.call-done.cot_ref, bf16[2048,2048]{1,0:T(8,128)(2,1)} %weight_ref.1, bf16[1024,2048]{1,0:T(8,128)(2,1)} %get-tuple-element.45.smooth_ref, bf16[1024,2048]{1,0:T(8,128)(2,1)} %get-tuple-element.46.slope_ref), custom_call_target="tpu_custom_call" | custom-call | flops 8589934592 | bytes 29360128 | tf_op jit(solution)/shard_map/gated_back/pallas_call | solution.py:428
  297.5 10.0 pair_product.2
  309.7 20.2 %pair_product.3 = (bf16[256,2048]{1,0:T(8,128)(2,1)}, bf16[256,2048]{1,0:T(8,128)(2,1)}, bf16[256,2048]{1,0:T(8,128)(2,1)}) custom-call(s32[3]{0:T(128)} %pad_add_fusion.1.at_ref, bf16[2,1024,2048]{2,1,0:T(8,128)(2,1)} %gated_back.1.pair_ref.right_ref, bf16[2048,2048]{1,0:T(8,128)(2,1)} %first_w_ref.3, bf16[2048,2048]{1,0:T(8,128)(2,1)} %second_w_ref.3), custom_call_target="tpu_custom_call" | custom-call | flops 12884901888 | bytes 20971520 | tf_op jit(solution)/shard_map/pair_product/pallas_call | solution.py:502
  333.2 66.8 %collective-permute-done.10.refs_1_ = bf16[256,2048]{1,0:T(8,128)(2,1)} collective-permute-done((bf16[256,2048]{1,0:T(8,128)(2,1)}, bf16[256,2048]{1,0:T(8,128)(2,1)}, u32[]{:S(2)}, u32[]{:S(2)}) %collective-permute-start.10) | collective-permute-done | bytes 1048608 | tf_op jit(solution)/shard_map/ppermute | solution.py:610
  410.1 76.9 %all-gather.13.cloned.1.call-done = bf16[1024,2048]{1,0:T(8,128)(2,1)} async-done(((bf16[256,2048]{1,0:T(8,128)(2,1)}), bf16[1024,2048]{1,0:T(8,128)(2,1)}) %all-gather.13.cloned.1.call-update) | async-done | bytes 4194320 | tf_op jit(solution)/shard_map/all_gather | solution.py:38
  492.5 20.2 %attend_back.1.d_ref = bf16[768,1024]{1,0:T(8,128)(2,1)} custom-call(bf16[768,1024]{1,0:T(8,128)(2,1)} %get-tuple-element.40.packed_ref, bf16[512,1024]{1,0:T(8,128)(2,1)} %fusion.d_heads_ref, f32[2,4,1024]{2,1,0:T(4,128)} %get-tuple-element.52.total_ref, f32[32,512]{1,0:T(8,128)} %get-tuple-element.87.cos_ref, f32[32,512]{1,0:T(8,128)} %get-tuple-element.86.sin_ref), custom_call_target="tpu_custom_call" | custom-call | flops 2684354560 | bytes 6291456 | tf_op jit(solution)/shard_map/attend_back/pallas_call | solution.py:265
  527.9 23.0 %product.6 = bf16[2048,4096]{1,0:T(8,128)(2,1)} custom-call(bf16[2048,1024]{1,0:T(8,128)(2,1)} %get-tuple-element.67.left_ref, bf16[2,1024,2048]{2,1,0:T(8,128)(2,1)} %gated_back.1.pair_ref.right_ref), custom_call_target="tpu_custom_call" | custom-call | flops 17179869184 | bytes 29360128 | tf_op jit(solution)/shard_map/product/pallas_call | solution.py:459
  551.2 14.2 %product.7 = bf16[2048,2048]{1,0:T(8,128)(2,1)} custom-call(bf16[2048,1024]{1,0:T(8,128)(2,1)} %get-tuple-element.68.left_ref, bf16[1,1024,2048]{2,1,0:T(8,128)(2,1)} %bitcast.50), custom_call_target="tpu_custom_call" | custom-call | flops 8589934592 | bytes 16777216 | tf_op jit(solution)/shard_map/product/pallas_call | solution.py:459
  565.5 19.8 %reduce-scatter.7.cloned.1.call-done = bf16[256,1280]{1,0:T(8,128)(2,1)} async-done(((bf16[2048,1280]{1,0:T(8,128)(2,1)}), bf16[256,1280]{1,0:T(8,128)(2,1)}) %reduce-scatter.7.cloned.1.call-update) | async-done | bytes 655376 | tf_op jit(solution)/shard_map/reduce_scatter | solution.py:42
  585.3 120.0 %reduce-scatter.9.cloned.1.call-done = bf16[256,4096]{1,0:T(8,128)(2,1)} async-done(((bf16[2048,4096]{1,0:T(8,128)(2,1)}), bf16[256,4096]{1,0:T(8,128)(2,1)}) %reduce-scatter.9.cloned.1.call-update) | async-done | bytes 2097168 | tf_op jit(solution)/shard_map/reduce_scatter | solution.py:42
  705.3 8.8 projection_back.3
  714.1 66.7 %reduce-scatter.11.cloned.1.call-done = bf16[256,2048]{1,0:T(8,128)(2,1)} async-done(((bf16[2048,2048]{1,0:T(8,128)(2,1)}), bf16[256,2048]{1,0:T(8,128)(2,1)}) %reduce-scatter.11.cloned.1.call-update) | async-done | bytes 1048592 | tf_op jit(solution)/shard_map/reduce_scatter | solution.py:42
  797.4 10.6 collective-permute-done.23
  809.1 13.2 %product.4 = bf16[1024,2048]{1,0:T(8,128)(2,1)} custom-call(bf16[1024,2048]{1,0:T(8,128)(2,1)} %get-tuple-element.44.left_ref, bf16[1,2048,2048]{2,1,0:T(8,128)(2,1)} %bitcast.49), custom_call_target="tpu_custom_call" | custom-call | flops 8589934592 | bytes 16777216 | tf_op jit(solution)/shard_map/product/pallas_call | solution.py:459
  828.5 16.4 %collective-permute-done.17 = f32[4096]{0:T(1024)S(1)} collective-permute-done((f32[4096]{0:T(1024)S(1)}, f32[4096]{0:T(1024)S(1)}, u32[]{:S(2)}, u32[]{:S(2)}) %collective-permute-start.17) | collective-permute-done | bytes 16416 | tf_op jit(solution)/shard_map/ppermute | solution.py:69
  854.4 37.9 %collective-permute-done.18 = f32[4096]{0:T(1024)S(1)} collective-permute-done((f32[4096]{0:T(1024)S(1)}, f32[4096]{0:T(1024)S(1)}, u32[]{:S(2)}, u32[]{:S(2)}) %collective-permute-start.18) | collective-permute-done | bytes 16416 | tf_op jit(solution)/shard_map/ppermute | solution.py:69
  898.0 19.5 %collective-permute-start.19 = (f32[4096]{0:T(1024)S(1)}, f32[4096]{0:T(1024)S(1)}, u32[]{:S(2)}, u32[]{:S(2)}) collective-permute-start(f32[4096]{0:T(1024)S(1)} %add.111), channel_id=1, source_target_pairs={{0,2},{1,3},{2,0},{3,1},{4,6},{5,7},{6,4},{7,5},{8,10},{9,11},{10,... | collective-permute-start | bytes 49160 | tf_op jit(solution)/shard_map/ppermute | solution.py:69
  927.4 13.6 %collective-permute-done.12.refs_0_ = bf16[256,2048]{1,0:T(8,128)(2,1)S(1)} collective-permute-done((bf16[256,2048]{1,0:T(8,128)(2,1)}, bf16[256,2048]{1,0:T(8,128)(2,1)S(1)}, u32[]{:S(2)}, u32[]{:S(2)}) %collective-permute-start.12) | collective-permute-done | bytes 1048608 | tf_op jit(solution)/shard_map/ppermute | solution.py:610
  941.0 67.1 %collective-permute-done.13.refs_1_ = bf16[256,2048]{1,0:T(8,128)(2,1)} collective-permute-done((bf16[256,2048]{1,0:T(8,128)(2,1)}, bf16[256,2048]{1,0:T(8,128)(2,1)}, u32[]{:S(2)}, u32[]{:S(2)}) %collective-permute-start.13) | collective-permute-done | bytes 1048608 | tf_op jit(solution)/shard_map/ppermute | solution.py:610
  1016.4 13.9 %place_blocks.1 = f32[2048,2048]{1,0:T(8,128)} custom-call(s32[1]{0:T(128)} %bitcast.1.at_ref, bf16[4,256,1024]{2,1,0:T(8,128)(2,1)} %pad_maximum_fusion.5.refs_0_, bf16[4,256,1024]{2,1,0:T(8,128)(2,1)} %collective-permute-done.22.refs_1_, bf16[4,256,1024]{2,1,0:T(8,128)(2,1)} %pad_maximum_fusion.6.refs_2_, bf16[4,256,1024]{2,1,0:T(8,128)(2,1)} %collective-permute-done.25.refs_3_), custom_call_target="tpu_custom_call" | custom-call | bytes 25165824 | tf_op jit(solution)/shard_map/place_blocks/pallas_call | solution.py:642
  1030.3 7.0 unpack_attention.1
  1037.2 17.2 %slice_convert_fusion = (f32[2048,2048]{1,0:T(8,128)}, f32[2048,2048]{1,0:T(8,128)}) fusion(bf16[2048,4096]{1,0:T(8,128)(2,1)} %all-gather.17.cloned.1.call-done), kind=kLoop, calls=%fused_computation | loop fusion | flops 8388608 | bytes 50331648 | tf_op jit(solution)/shard_map/convert_element_type | solution.py:806
  (158 shorter events, 149.9 us)
Async XLA Ops:
  8.0 81.7 %all-gather.19.cloned.1.call-start = ((), (), s32[]{:S(2)}) async-start(), calls=%async_computation.12 | async-start | bytes 5242880 | tf_op jit(solution)/shard_map/all_gather | solution.py:734
  8.8 111.4 %all-gather.23.cloned.1.call-start = ((), (), s32[]{:S(2)}) async-start(), calls=%async_computation.14 | async-start | bytes 1310720 | tf_op jit(solution)/shard_map/all_gather | solution.py:736
  10.4 158.6 %reduce-scatter.5.cloned.1.call-start = ((), (), s32[]{:S(2)}) async-start(), calls=%async_computation.4 | async-start | bytes 73728 | tf_op jit(solution)/shard_map/reduce_scatter | solution.py:42
  11.9 188.7 %all-gather.21.cloned.1.call-start = ((), (), s32[]{:S(2)}) async-start(), calls=%async_computation.13 | async-start | bytes 5242880 | tf_op jit(solution)/shard_map/all_gather | solution.py:750
  111.8 169.5 %all-gather.11.cloned.1.call-start = ((), (), s32[]{:S(2)}) async-start(), calls=%async_computation.5 | async-start | bytes 5242880 | tf_op jit(solution)/shard_map/all_gather | solution.py:38
  122.7 14.5 %collective-permute-start.3 = (bf16[1,4,64,1024]{3,2,1,0:T(8,128)(2,1)S(1)}, bf16[1,4,64,1024]{3,2,1,0:T(8,128)(2,1)}, u32[]{:S(2)}, u32[]{:S(2)}) collective-permute-start(bf16[1,4,64,1024]{3,2,1,0:T(8,128)(2,1)S(1)} %get-tuple-element.78), channel_id=1, source_target_pairs={{0,16},{4,20},{8,24},{12,28},{16,0},{20,4},{24,8},{28,12},{1,17},{... | collective-permute-start | bytes 1572872 | tf_op jit(solution)/shard_map/ppermute | solution.py:56
  135.5 22.8 %collective-permute-start.1 = (bf16[2,4,64,1024]{3,2,1,0:T(8,128)(2,1)}, bf16[2,4,64,1024]{3,2,1,0:T(8,128)(2,1)}, u32[]{:S(2)}, u32[]{:S(2)}) collective-permute-start(bf16[2,4,64,1024]{3,2,1,0:T(8,128)(2,1)} %pad_maximum_fusion.7), channel_id=1, source_target_pairs={{0,16},{4,20},{8,24},{12,28},{16,0},{20,4},{24,8},{28,12},{1,17},{... | collective-permute-start | bytes 3145736 | tf_op jit(solution)/shard_map/ppermute | solution.py:56
  136.7 350.3 %all-gather.13.cloned.1.call-start = ((), (), s32[]{:S(2)}) async-start(), calls=%async_computation.6 | async-start | bytes 5242880 | tf_op jit(solution)/shard_map/all_gather | solution.py:38
  138.4 25.9 %collective-permute-start.4 = (bf16[2,4,64,1024]{3,2,1,0:T(8,128)(2,1)S(1)}, bf16[2,4,64,1024]{3,2,1,0:T(8,128)(2,1)S(1)}, u32[]{:S(2)}, u32[]{:S(2)}) collective-permute-start(bf16[2,4,64,1024]{3,2,1,0:T(8,128)(2,1)S(1)} %pad_maximum_fusion.8), channel_id=1, source_target_pairs={{0,8},{4,12},{8,0},{12,4},{16,24},{20,28},{24,16},{28,20},{1,9},{5... | collective-permute-start | bytes 3145736 | tf_op jit(solution)/shard_map/ppermute | solution.py:56
  307.5 25.7 %collective-permute-start.9 = (bf16[256,2048]{1,0:T(8,128)(2,1)}, bf16[256,2048]{1,0:T(8,128)(2,1)S(1)}, u32[]{:S(2)}, u32[]{:S(2)}) collective-permute-start(bf16[256,2048]{1,0:T(8,128)(2,1)} %pair_product.2), channel_id=1, source_target_pairs={{0,1},{1,2},{2,3},{3,0},{4,5},{5,6},{6,7},{7,4},{8,9},{9,10},{10,1... | collective-permute-start | bytes 3145736 | tf_op jit(solution)/shard_map/ppermute | solution.py:610
  329.9 70.1 %collective-permute-start.10 = (bf16[256,2048]{1,0:T(8,128)(2,1)}, bf16[256,2048]{1,0:T(8,128)(2,1)}, u32[]{:S(2)}, u32[]{:S(2)}) collective-permute-start(bf16[256,2048]{1,0:T(8,128)(2,1)} %get-tuple-element.47), channel_id=1, source_target_pairs={{0,2},{1,3},{2,0},{3,1},{4,6},{5,7},{6,4},{7,5},{8,10},{9,11},{10,... | collective-permute-start | bytes 3145736 | tf_op jit(solution)/shard_map/ppermute | solution.py:610
  332.5 71.2 %collective-permute-start.11 = (bf16[256,2048]{1,0:T(8,128)(2,1)}, bf16[256,2048]{1,0:T(8,128)(2,1)}, u32[]{:S(2)}, u32[]{:S(2)}) collective-permute-start(bf16[256,2048]{1,0:T(8,128)(2,1)} %get-tuple-element.48), channel_id=1, source_target_pairs={{0,3},{1,0},{2,1},{3,2},{4,7},{5,4},{6,5},{7,6},{8,11},{9,8},{10,9... | collective-permute-start | bytes 3145736 | tf_op jit(solution)/shard_map/ppermute | solution.py:610
  409.9 175.4 %reduce-scatter.7.cloned.1.call-start = ((), (), s32[]{:S(2)}) async-start(), calls=%async_computation.7 | async-start | bytes 5898240 | tf_op jit(solution)/shard_map/reduce_scatter | solution.py:42
  527.9 177.4 %reduce-scatter.9.cloned.1.call-start = ((), (), s32[]{:S(2)}) async-start(), calls=%async_computation.9 | async-start | bytes 18874368 | tf_op jit(solution)/shard_map/reduce_scatter | solution.py:42
  550.9 229.8 %reduce-scatter.11.cloned.1.call-start = ((), (), s32[]{:S(2)}) async-start(), calls=%async_computation.11 | async-start | bytes 9437184 | tf_op jit(solution)/shard_map/reduce_scatter | solution.py:42
  565.4 464.8 %all-gather.15.cloned.1.call-start = ((), (), s32[]{:S(2)}) async-start(), calls=%async_computation.8 | async-start | bytes 5898240 | tf_op jit(solution)/shard_map/all_gather | solution.py:38
  585.3 451.9 %all-gather.17.cloned.1.call-start = ((), (), s32[]{:S(2)}) async-start(), calls=%async_computation.10 | async-start | bytes 18874368 | tf_op jit(solution)/shard_map/all_gather | solution.py:38
  788.6 19.5 %collective-permute-start.23 = (bf16[1,256,1024]{2,1,0:T(8,128)(2,1)S(1)}, bf16[1,256,1024]{2,1,0:T(8,128)(2,1)S(1)}, u32[]{:S(2)}, u32[]{:S(2)}) collective-permute-start(bf16[1,256,1024]{2,1,0:T(8,128)(2,1)S(1)} %get-tuple-element.76), channel_id=1, source_target_pairs={{0,16},{4,20},{8,24},{12,28},{16,0},{20,4},{24,8},{28,12},{1,17},{... | collective-permute-start | bytes 1572872 | tf_op jit(solution)/shard_map/ppermute | solution.py:56
  791.3 31.0 %collective-permute-start.16 = (f32[4096]{0:T(1024)S(1)}, f32[4096]{0:T(1024)S(1)}, u32[]{:S(2)}, u32[]{:S(2)}) collective-permute-start(f32[4096]{0:T(1024)S(1)} %add.108), channel_id=1, source_target_pairs={{0,8},{4,12},{8,0},{12,4},{16,24},{20,28},{24,16},{28,20},{1,9},{5... | collective-permute-start | bytes 49160 | tf_op jit(solution)/shard_map/ppermute | solution.py:69
  796.2 49.9 %collective-permute-start.21 = (bf16[2,256,1024]{2,1,0:T(8,128)(2,1)S(1)}, bf16[2,256,1024]{2,1,0:T(8,128)(2,1)}, u32[]{:S(2)}, u32[]{:S(2)}) collective-permute-start(bf16[2,256,1024]{2,1,0:T(8,128)(2,1)S(1)} %pad_maximum_fusion.9), channel_id=1, source_target_pairs={{0,16},{4,20},{8,24},{12,28},{16,0},{20,4},{24,8},{28,12},{1,17},{... | collective-permute-start | bytes 3145736 | tf_op jit(solution)/shard_map/ppermute | solution.py:56
  809.1 40.1 %collective-permute-start.24 = (bf16[2,256,1024]{2,1,0:T(8,128)(2,1)}, bf16[2,256,1024]{2,1,0:T(8,128)(2,1)}, u32[]{:S(2)}, u32[]{:S(2)}) collective-permute-start(bf16[2,256,1024]{2,1,0:T(8,128)(2,1)} %pad_maximum_fusion.10), channel_id=1, source_target_pairs={{0,8},{4,12},{8,0},{12,4},{16,24},{20,28},{24,16},{28,20},{1,9},{5... | collective-permute-start | bytes 3145736 | tf_op jit(solution)/shard_map/ppermute | solution.py:56
  822.3 22.6 %collective-permute-start.17 = (f32[4096]{0:T(1024)S(1)}, f32[4096]{0:T(1024)S(1)}, u32[]{:S(2)}, u32[]{:S(2)}) collective-permute-start(f32[4096]{0:T(1024)S(1)} %add.109), channel_id=1, source_target_pairs={{0,16},{4,20},{8,24},{12,28},{16,0},{20,4},{24,8},{28,12},{1,17},{... | collective-permute-start | bytes 49160 | tf_op jit(solution)/shard_map/ppermute | solution.py:69
  826.1 71.9 %collective-permute-start.8 = (bf16[256,2048]{1,0:T(8,128)(2,1)S(1)}, bf16[256,2048]{1,0:T(8,128)(2,1)S(1)}, u32[]{:S(2)}, u32[]{:S(2)}) collective-permute-start(bf16[256,2048]{1,0:T(8,128)(2,1)S(1)} %get-tuple-element.72), channel_id=1, source_target_pairs={{0,2},{1,3},{2,0},{3,1},{4,6},{5,7},{6,4},{7,5},{8,10},{9,11},{10,... | collective-permute-start | bytes 3145736 | tf_op jit(solution)/shard_map/ppermute | solution.py:766
  828.3 89.6 %collective-permute-start.7 = (bf16[256,2048]{1,0:T(8,128)(2,1)S(1)}, bf16[256,2048]{1,0:T(8,128)(2,1)S(1)}, u32[]{:S(2)}, u32[]{:S(2)}) collective-permute-start(bf16[256,2048]{1,0:T(8,128)(2,1)S(1)} %get-tuple-element.73), channel_id=1, source_target_pairs={{0,3},{1,0},{2,1},{3,2},{4,7},{5,4},{6,5},{7,6},{8,11},{9,8},{10,9... | collective-permute-start | bytes 3145736 | tf_op jit(solution)/shard_map/ppermute | solution.py:766
  844.9 74.0 %collective-permute-start.6 = (bf16[256,2048]{1,0:T(8,128)(2,1)S(1)}, bf16[256,2048]{1,0:T(8,128)(2,1)S(1)}, u32[]{:S(2)}, u32[]{:S(2)}) collective-permute-start(bf16[256,2048]{1,0:T(8,128)(2,1)S(1)} %get-tuple-element.71), channel_id=1, source_target_pairs={{0,1},{1,2},{2,3},{3,0},{4,5},{5,6},{6,7},{7,4},{8,9},{9,10},{10,1... | collective-permute-start | bytes 3145736 | tf_op jit(solution)/shard_map/ppermute | solution.py:766
  846.1 46.2 %collective-permute-start.18 = (f32[4096]{0:T(1024)S(1)}, f32[4096]{0:T(1024)S(1)}, u32[]{:S(2)}, u32[]{:S(2)}) collective-permute-start(f32[4096]{0:T(1024)S(1)} %add.110), channel_id=1, source_target_pairs={{0,1},{1,0},{2,3},{3,2},{4,5},{5,4},{6,7},{7,6},{8,9},{9,8},{10,11... | collective-permute-start | bytes 49160 | tf_op jit(solution)/shard_map/ppermute | solution.py:69
  849.2 167.2 %collective-permute-start.22 = (bf16[4,256,1024]{2,1,0:T(8,128)(2,1)}, bf16[4,256,1024]{2,1,0:T(8,128)(2,1)}, u32[]{:S(2)}, u32[]{:S(2)}) collective-permute-start(bf16[4,256,1024]{2,1,0:T(8,128)(2,1)} %pad_maximum_fusion.5.refs_0_), channel_id=1, source_target_pairs={{0,4},{4,0},{8,12},{12,8},{16,20},{20,16},{24,28},{28,24},{1,5},{5... | collective-permute-start | bytes 6291464 | tf_op jit(solution)/shard_map/ppermute | solution.py:56
  892.3 124.1 %collective-permute-start.25 = (bf16[4,256,1024]{2,1,0:T(8,128)(2,1)}, bf16[4,256,1024]{2,1,0:T(8,128)(2,1)}, u32[]{:S(2)}, u32[]{:S(2)}) collective-permute-start(bf16[4,256,1024]{2,1,0:T(8,128)(2,1)} %pad_maximum_fusion.6.refs_2_), channel_id=1, source_target_pairs={{0,4},{4,0},{8,12},{12,8},{16,20},{20,16},{24,28},{28,24},{1,5},{5... | collective-permute-start | bytes 6291464 | tf_op jit(solution)/shard_map/ppermute | solution.py:56
  898.0 21.9 %collective-permute-start.19 = (f32[4096]{0:T(1024)S(1)}, f32[4096]{0:T(1024)S(1)}, u32[]{:S(2)}, u32[]{:S(2)}) collective-permute-start(f32[4096]{0:T(1024)S(1)} %add.111), channel_id=1, source_target_pairs={{0,2},{1,3},{2,0},{3,1},{4,6},{5,7},{6,4},{7,5},{8,10},{9,11},{10,... | collective-permute-start | bytes 49160 | tf_op jit(solution)/shard_map/ppermute | solution.py:69
  917.9 23.1 %collective-permute-start.12 = (bf16[256,2048]{1,0:T(8,128)(2,1)}, bf16[256,2048]{1,0:T(8,128)(2,1)S(1)}, u32[]{:S(2)}, u32[]{:S(2)}) collective-permute-start(bf16[256,2048]{1,0:T(8,128)(2,1)} %get-tuple-element.53), channel_id=1, source_target_pairs={{0,1},{1,2},{2,3},{3,0},{4,5},{5,6},{6,7},{7,4},{8,9},{9,10},{10,1... | collective-permute-start | bytes 3145736 | tf_op jit(solution)/shard_map/ppermute | solution.py:610
  918.9 89.2 %collective-permute-start.13 = (bf16[256,2048]{1,0:T(8,128)(2,1)}, bf16[256,2048]{1,0:T(8,128)(2,1)}, u32[]{:S(2)}, u32[]{:S(2)}) collective-permute-start(bf16[256,2048]{1,0:T(8,128)(2,1)} %get-tuple-element.54), channel_id=1, source_target_pairs={{0,2},{1,3},{2,0},{3,1},{4,6},{5,7},{6,4},{7,5},{8,10},{9,11},{10,... | collective-permute-start | bytes 3145736 | tf_op jit(solution)/shard_map/ppermute | solution.py:610
  919.9 90.3 %collective-permute-start.14 = (bf16[256,2048]{1,0:T(8,128)(2,1)}, bf16[256,2048]{1,0:T(8,128)(2,1)}, u32[]{:S(2)}, u32[]{:S(2)}) collective-permute-start(bf16[256,2048]{1,0:T(8,128)(2,1)} %get-tuple-element.55), channel_id=1, source_target_pairs={{0,3},{1,0},{2,1},{3,2},{4,7},{5,4},{6,5},{7,6},{8,11},{9,8},{10,9... | collective-permute-start | bytes 3145736 | tf_op jit(solution)/shard_map/ppermute | solution.py:610
  (23 other events, 347.4 us)
Sparse Core Ops, SparseCore 0:
  10.4 79.2 all-gather.18
  91.8 28.2 all-gather.22
  122.3 78.3 all-gather.20
  202.1 79.2 all-gather.10
  410.0 76.9 all-gather.12
Sparse Core Ops, SparseCore 1:
  14.4 34.4 reduce-scatter.4
  528.0 57.2 reduce-scatter.6
  589.3 116.0 reduce-scatter.8
  709.4 71.3 reduce-scatter.10
  782.7 62.9 all-gather.14
  847.5 89.6 all-gather.16

commit v11 on v9

--- a/solution.py
+++ b/solution.py
@@ -54,9 +54,9 @@
         held, offsets = part[None], [0]
         for bit in order:
             moved = lax.ppermute(held, axis, [(i, i ^ bit) for i in range(n)])
-            offsets = offsets + [o ^ bit for o in offsets]
             if join or bit != order[-1]:
                 held = jnp.concatenate([held, moved], axis=0)
+            offsets = offsets + [o ^ bit for o in offsets]
         halves.append((held if join else (held, moved), tuple(offsets)))
     return halves
 
@@ -798,7 +798,6 @@
     part_gate_up = scatter_sum(gate_up_grads, DP)
     d_state, state_low, gain_two = norm_back(hidden_state, norm2_gain, cotangent, dn2_blocks)
     d_state_low = gather_rows(state_low, TP)
-    gain_two_sum = cube_sum(gain_two[0], (DP, TP))
     d_heads_rows = contract_cols(w_output, d_state_low).astype(LOW)
     d_projected = attend_back(projected, d_heads_rows, totals, cos_rows, sin_rows)
     gains = []
@@ -809,7 +808,8 @@
         return made
 
     dn1_blocks = exchange(dn1_blocks_of, TP)
-    gain_one_sum = cube_sum(sum(gains)[0], (DP, TP))
+    gain_sums = cube_sum(jnp.concatenate([sum(gains), gain_two], axis=1)[0], (DP, TP))
+    gain_one_sum, gain_two_sum = gain_sums[:width], gain_sums[width:]
     grad_qkv = lax.dot_general(
         normed1,
         d_projected,
@@ -823,11 +823,12 @@
     part_attn = scatter_sum(low_attn, DP)
     down_halves = cube_gather(part_down, DP, join=False)
     full_down = join_columns(place_blocks(down_halves, DP), ff_folds)
-    shared_ff = row_major(gather_rows(part_gate_up, DP))
+    up_halves = cube_gather(part_gate_up[:, ff_columns:], DP, join=False)
+    full_up = place_blocks(up_halves, DP)
+    shared_gate = row_major(gather_rows(part_gate_up[:, :ff_columns], DP))
     shared_attn = row_major(gather_rows(part_attn, DP))
     _, input_grad, _ = norm_back(tokens, norm1_gain, d_state, dn1_blocks)
-    full_gate = shared_ff[:, :ff_columns].astype(jnp.float32)
-    full_up = shared_ff[:, ff_columns:].astype(jnp.float32)
+    full_gate = shared_gate.astype(jnp.float32)
     full_query, full_key, full_value, full_output = unpack_attention(
         shared_attn, q_columns, k_columns, folds
     )

time: 1080 us -> 1130 us (1.046)
  starting transfers between devices: 47.1 us -> 73.6 us
  Pallas kernels: 229 us -> 243 us
  waiting for transfers between devices: 669 us -> 681 us
    ppermute x10 -> x5, waiting for transfers between devices: 51.9 us -> 93.2 us  [cube_sum(): lax.ppermute(vector, axis, [(i, i ^ bit) for i in range(n)])]
    reduce_scatter x4, waiting for transfers between devices: 213 us -> 175 us  [scatter_sum(): return lax.psum_scatter(partial, axis, scatter_dimension=0, tiled=True)]
    ppermute x12, starting transfers between devices: 13.9 us -> 50.9 us  [exchange(): moved.append(lax.ppermute(made[hop - 1], axis, pairs))]
    ppermute x12, waiting for transfers between devices: 113 us -> 131 us  [exchange(): moved.append(lax.ppermute(made[hop - 1], axis, pairs))]
    ppermute x10 -> x5, starting transfers between devices: 20.7 us -> 4.04 us  [cube_sum(): lax.ppermute(vector, axis, [(i, i ^ bit) for i in range(n)])]
    pallas_call x1 -> x2, Pallas kernels: 13.9 us -> 27.7 us  [place_blocks(): pl.pallas_call(kernel, grid_spec=pltpu.PrefetchScalarGridSpec(num_scalar_...]
    ppermute x12 -> x18, waiting for transfers between devices: 61.8 us -> 56 us  [cube_gather(): moved = lax.ppermute(held, axis, [(i, i ^ bit) for i in range(n)])]
  transfers between devices with their start and end apart: 45 -> 46, of which waited for: 27 -> 23; matrix products, arithmetic and copies ran while one was open for 6% -> 6% of each run, Pallas kernels for 17% -> 17%
where the time goes in v11:
time: 1130 us; the launch traced here: 1120 us
  waiting for transfers between devices  681 us (60%)
  Pallas kernels  243 us (22%)
  starting transfers between devices  73.6 us (7%)
  other arithmetic  45.2 us (4%)
  local copies, waits for them, and re-layouts  44.7 us (4%)
  between operations  16.5 us (1%)
  matrix products  14.6 us (1%)
    reduce_scatter x4, waiting for transfers between devices, scatter_sum(): return lax.psum_scatter(partial, axis, scatter_dimension=0, tiled=True)  175 us
    all_gather x4, waiting for transfers between devices, gather_rows(): return lax.all_gather(block, axis, axis=0, tiled=True)  138 us
    ppermute x12, waiting for transfers between devices, exchange(): moved.append(lax.ppermute(made[hop - 1], axis, pairs))  131 us
    ppermute x5, waiting for transfers between devices, cube_sum(): lax.ppermute(vector, axis, [(i, i ^ bit) for i in range(n)])  93.2 us
    all_gather x1, waiting for transfers between devices, block(): gathered = lax.all_gather(tokens, TP, axis=0)  56.3 us
    ppermute x18, waiting for transfers between devices, cube_gather(): moved = lax.ppermute(held, axis, [(i, i ^ bit) for i in range(n)])  56 us
    ppermute x12, starting transfers between devices, exchange(): moved.append(lax.ppermute(made[hop - 1], axis, pairs))  50.9 us
    pallas_call x3, Pallas kernels, product(): pl.pallas_call(kernel, grid=(count * column_steps,), in_specs=[pl.BlockSp...  50.1 us
  transfers between devices with their start and end apart: 46, of which 23 were waited for; matrix products, arithmetic and copies ran while one was open for 6% of the time, Pallas kernels for 17%

profile of v11, /device:TPU:0, one launch (start us, length us, event | category | flops | bytes accessed | tf_op | source)
XLA Modules:
  0.0 1118.6 jit_solution(13686272285429596675)
XLA Ops:
  37.6 56.3 %all-gather.19.cloned.1.call-done = bf16[1024,2048]{1,0:T(8,128)(2,1)} async-done(((bf16[256,2048]{1,0:T(8,128)(2,1)}), bf16[1024,2048]{1,0:T(8,128)(2,1)}) %all-gather.19.cloned.1.call-update) | async-done | bytes 4194320 | tf_op jit(solution)/shard_map/all_gather | solution.py:754
  102.3 13.7 %attend.1 = (bf16[1024,512]{1,0:T(8,128)(2,1)}, bf16[512,1024]{1,0:T(8,128)(2,1)}, f32[2,4,1024]{2,1,0:T(4,128)}) custom-call(bf16[768,1024]{1,0:T(8,128)(2,1)} %get-tuple-element.42.packed_ref), custom_call_target="tpu_custom_call" | custom-call | flops 1073741824 | bytes 4194304 | tf_op jit(solution)/shard_map/attend/pallas_call | solution.py:185
  126.9 10.2 collective-permute-done.3
  143.4 19.6 %collective-permute-done.4 = bf16[2,4,64,1024]{3,2,1,0:T(8,128)(2,1)} collective-permute-done((bf16[2,4,64,1024]{3,2,1,0:T(8,128)(2,1)}, bf16[2,4,64,1024]{3,2,1,0:T(8,128)(2,1)}, u32[]{:S(2)}, u32[]{:S(2)}) %collective-permute-start.4) | collective-permute-done | bytes 1048608 | tf_op jit(solution)/shard_map/ppermute | solution.py:56
  180.8 24.0 %all-gather.21.cloned.1.call-done = bf16[4096,512]{1,0:T(8,128)(2,1)} async-done(((bf16[1024,512]{1,0:T(8,128)(2,1)}), bf16[4096,512]{1,0:T(8,128)(2,1)}) %all-gather.21.cloned.1.call-update) | async-done | bytes 4194320 | tf_op jit(solution)/shard_map/all_gather | solution.py:770
  204.9 18.8 %project_and_norm.1 = (f32[256,2048]{1,0:T(8,128)}, bf16[1024,2048]{1,0:T(8,128)(2,1)}, bf16[2048,1024]{1,0:T(8,128)(2,1)}) custom-call(s32[2]{0:T(128)} %pad_add_fusion.at_ref, bf16[4,1024,512]{2,1,0:T(8,128)(2,1)} %bitcast.61, bf16[8,4,64,1024]{3,2,1,0:T(8,128)(2,1)} %pad_maximum_fusion.1.first_ref, bf16[8,4,64,1024]{3,2,1,0:T(8,128)(2,1)} %pad_maximum_fusion.2.second_ref, ...), custom_call_target="tpu_custom_call" | custom-call | flops 8589934592 | bytes 25165824 | tf_op jit(solution)/shard_map/project_and_norm/pallas_call | solution.py:339
  223.6 25.1 %gated_up.1 = (bf16[1024,2048]{1,0:T(8,128)(2,1)}, bf16[2048,1024]{1,0:T(8,128)(2,1)}, bf16[1024,2048]{1,0:T(8,128)(2,1)}, bf16[1024,2048]{1,0:T(8,128)(2,1)}) custom-call(bf16[1024,2048]{1,0:T(8,128)(2,1)} %get-tuple-element.45.normed_ref, bf16[2048,2048]{1,0:T(8,128)(2,1)} %first_w_ref.3, bf16[2048,2048]{1,0:T(8,128)(2,1)} %second_w_ref.3), custom_call_target="tpu_custom_call" | custom-call | flops 17179869184 | bytes 37748736 | tf_op jit(solution)/shard_map/gated_up/pallas_call | solution.py:392
  248.7 36.8 %all-gather.11.cloned.1.call-done.cot_ref.refs_0_ = bf16[1024,2048]{1,0:T(8,128)(2,1)} async-done(((bf16[256,2048]{1,0:T(8,128)(2,1)}), bf16[1024,2048]{1,0:T(8,128)(2,1)}) %all-gather.11.cloned.1.call-update) | async-done | bytes 4194320 | tf_op jit(solution)/shard_map/all_gather | solution.py:38
  285.5 16.2 %gated_back.1 = (bf16[1024,2048]{1,0:T(8,128)(2,1)}, bf16[1024,2048]{1,0:T(8,128)(2,1)}) custom-call(bf16[1024,2048]{1,0:T(8,128)(2,1)} %all-gather.11.cloned.1.call-done.cot_ref.refs_0_, bf16[2048,2048]{1,0:T(8,128)(2,1)} %weight_ref.1, bf16[1024,2048]{1,0:T(8,128)(2,1)} %get-tuple-element.47.smooth_ref, bf16[1024,2048]{1,0:T(8,128)(2,1)} %get-tuple-element.48.slope_ref), custom_call_target="tpu_custom_call" | custom-call | flops 8589934592 | bytes 29360128 | tf_op jit(solution)/shard_map/gated_back/pallas_call | solution.py:425
  301.7 10.0 pair_product.2
  311.7 20.2 %pair_product.3 = (bf16[256,2048]{1,0:T(8,128)(2,1)}, bf16[256,2048]{1,0:T(8,128)(2,1)}, bf16[256,2048]{1,0:T(8,128)(2,1)}) custom-call(s32[3]{0:T(128)} %pad_add_fusion.1.at_ref, bf16[1024,2048]{1,0:T(8,128)(2,1)} %get-tuple-element.49.first_ref.refs_0_, bf16[1024,2048]{1,0:T(8,128)(2,1)} %get-tuple-element.50.second_ref.refs_1_, ...), custom_call_target="tpu_custom_call" | custom-call | flops 12884901888 | bytes 20971520 | tf_op jit(solution)/shard_map/pair_product/pallas_call | solution.py:511
  339.8 43.8 %collective-permute-done.13.refs_1_ = bf16[256,2048]{1,0:T(8,128)(2,1)} collective-permute-done((bf16[256,2048]{1,0:T(8,128)(2,1)}, bf16[256,2048]{1,0:T(8,128)(2,1)}, u32[]{:S(2)}, u32[]{:S(2)}) %collective-permute-start.13) | collective-permute-done | bytes 1048608 | tf_op jit(solution)/shard_map/ppermute | solution.py:619
  390.1 101.2 %all-gather.13.cloned.1.call-done = bf16[1024,2048]{1,0:T(8,128)(2,1)} async-done(((bf16[256,2048]{1,0:T(8,128)(2,1)}), bf16[1024,2048]{1,0:T(8,128)(2,1)}) %all-gather.13.cloned.1.call-update) | async-done | bytes 4194320 | tf_op jit(solution)/shard_map/all_gather | solution.py:38
  502.4 20.2 %attend_back.1.d_ref = bf16[768,1024]{1,0:T(8,128)(2,1)} custom-call(bf16[768,1024]{1,0:T(8,128)(2,1)} %get-tuple-element.42.packed_ref, bf16[512,1024]{1,0:T(8,128)(2,1)} %fusion.1.d_heads_ref, f32[2,4,1024]{2,1,0:T(4,128)} %get-tuple-element.56.total_ref, f32[32,512]{1,0:T(8,128)} %get-tuple-element.96.cos_ref, f32[32,512]{1,0:T(8,128)} %get-tuple-element.95.sin_ref), custom_call_target="tpu_custom_call" | custom-call | flops 2684354560 | bytes 6291456 | tf_op jit(solution)/shard_map/attend_back/pallas_call | solution.py:265
  532.2 23.5 %product.4 = bf16[2048,4096]{1,0:T(8,128)(2,1)} custom-call(bf16[2048,1024]{1,0:T(8,128)(2,1)} %get-tuple-element.71.left_ref, bf16[1024,2048]{1,0:T(8,128)(2,1)} %get-tuple-element.49.first_ref.refs_0_, bf16[1024,2048]{1,0:T(8,128)(2,1)} %get-tuple-element.50.second_ref.refs_1_), custom_call_target="tpu_custom_call" | custom-call | flops 17179869184 | bytes 29360128 | tf_op jit(solution)/shard_map/product/pallas_call | solution.py:470
  555.7 13.4 %product.5 = bf16[2048,2048]{1,0:T(8,128)(2,1)} custom-call(bf16[2048,1024]{1,0:T(8,128)(2,1)} %get-tuple-element.72.left_ref, bf16[1024,2048]{1,0:T(8,128)(2,1)} %all-gather.11.cloned.1.call-done.cot_ref.refs_0_), custom_call_target="tpu_custom_call" | custom-call | flops 8589934592 | bytes 16777216 | tf_op jit(solution)/shard_map/product/pallas_call | solution.py:470
  569.2 17.5 %reduce-scatter.7.cloned.1.call-done = bf16[256,1280]{1,0:T(8,128)(2,1)} async-done(((bf16[2048,1280]{1,0:T(8,128)(2,1)}), bf16[256,1280]{1,0:T(8,128)(2,1)}) %reduce-scatter.7.cloned.1.call-update) | async-done | bytes 655376 | tf_op jit(solution)/shard_map/reduce_scatter | solution.py:42
  586.7 120.0 %reduce-scatter.9.cloned.1.call-done = bf16[256,4096]{1,0:T(8,128)(2,1)} async-done(((bf16[2048,4096]{1,0:T(8,128)(2,1)}), bf16[256,4096]{1,0:T(8,128)(2,1)}) %reduce-scatter.9.cloned.1.call-update) | async-done | bytes 2097168 | tf_op jit(solution)/shard_map/reduce_scatter | solution.py:42
  709.1 13.3 %product.3 = bf16[1024,2048]{1,0:T(8,128)(2,1)} custom-call(bf16[1024,2048]{1,0:T(8,128)(2,1)} %get-tuple-element.46.left_ref, bf16[2048,2048]{1,0:T(8,128)(2,1)} %weight_ref.1), custom_call_target="tpu_custom_call" | custom-call | flops 8589934592 | bytes 16777216 | tf_op jit(solution)/shard_map/product/pallas_call | solution.py:470
  744.9 37.3 %reduce-scatter.11.cloned.1.call-done = bf16[256,2048]{1,0:T(8,128)(2,1)} async-done(((bf16[2048,2048]{1,0:T(8,128)(2,1)}), bf16[256,2048]{1,0:T(8,128)(2,1)}) %reduce-scatter.11.cloned.1.call-update) | async-done | bytes 1048592 | tf_op jit(solution)/shard_map/reduce_scatter | solution.py:42
  788.4 13.7 %collective-permute-done.32 = bf16[1,256,1024]{2,1,0:T(8,128)(2,1)S(1)} collective-permute-done((bf16[1,256,1024]{2,1,0:T(8,128)(2,1)S(1)}, bf16[1,256,1024]{2,1,0:T(8,128)(2,1)S(1)}, u32[]{:S(2)}, u32[]{:S(2)}) %collective-permute-start.32) | collective-permute-done | bytes 524320 | tf_op jit(solution)/shard_map/ppermute | solution.py:56
  805.8 11.0 collective-permute-done.26
  820.4 66.8 %collective-permute-done.19 = f32[4096]{0:T(1024)S(1)} collective-permute-done((f32[4096]{0:T(1024)S(1)}, f32[4096]{0:T(1024)S(1)}, u32[]{:S(2)}, u32[]{:S(2)}) %collective-permute-start.19) | collective-permute-done | bytes 16416 | tf_op jit(solution)/shard_map/ppermute | solution.py:69
  896.1 15.4 %collective-permute-done.10 = bf16[256,1024]{1,0:T(8,128)(2,1)S(1)} collective-permute-done((bf16[256,1024]{1,0:T(8,128)(2,1)S(1)}, bf16[256,1024]{1,0:T(8,128)(2,1)S(1)}, u32[]{:S(2)}, u32[]{:S(2)}) %collective-permute-start.10) | collective-permute-done | bytes 524320 | tf_op jit(solution)/shard_map/ppermute | solution.py:619
  925.8 28.7 %collective-permute-done.9 = bf16[256,1024]{1,0:T(8,128)(2,1)S(1)} collective-permute-done((bf16[256,1024]{1,0:T(8,128)(2,1)S(1)}, bf16[256,1024]{1,0:T(8,128)(2,1)S(1)}, u32[]{:S(2)}, u32[]{:S(2)}) %collective-permute-start.9) | collective-permute-done | bytes 524320 | tf_op jit(solution)/shard_map/ppermute | solution.py:619
  954.5 33.6 %collective-permute-start.16 = (bf16[256,2048]{1,0:T(8,128)(2,1)}, bf16[256,2048]{1,0:T(8,128)(2,1)S(1)}, u32[]{:S(2)}, u32[]{:S(2)}) collective-permute-start(bf16[256,2048]{1,0:T(8,128)(2,1)} %get-tuple-element.58), channel_id=1, source_target_pairs={{0,2},{1,3},{2,0},{3,1},{4,6},{5,7},{6,4},{7,5},{8,10},{9,11},{10,... | collective-permute-start | bytes 3145736 | tf_op jit(solution)/shard_map/ppermute | solution.py:619
  988.2 20.7 %collective-permute-done.7 = bf16[256,1024]{1,0:T(8,128)(2,1)S(1)} collective-permute-done((bf16[256,1024]{1,0:T(8,128)(2,1)S(1)}, bf16[256,1024]{1,0:T(8,128)(2,1)S(1)}, u32[]{:S(2)}, u32[]{:S(2)}) %collective-permute-start.7) | collective-permute-done | bytes 524320 | tf_op jit(solution)/shard_map/ppermute | solution.py:619
  1010.9 20.7 %collective-permute-done.22 = f32[4096]{0:T(1024)S(1)} collective-permute-done((f32[4096]{0:T(1024)S(1)}, f32[4096]{0:T(1024)S(1)}, u32[]{:S(2)}, u32[]{:S(2)}) %collective-permute-start.22) | collective-permute-done | bytes 16416 | tf_op jit(solution)/shard_map/ppermute | solution.py:69
  1039.5 19.1 %collective-permute-done.17.refs_2_ = bf16[256,2048]{1,0:T(8,128)(2,1)} collective-permute-done((bf16[256,2048]{1,0:T(8,128)(2,1)}, bf16[256,2048]{1,0:T(8,128)(2,1)}, u32[]{:S(2)}, u32[]{:S(2)}) %collective-permute-start.17) | collective-permute-done | bytes 1048608 | tf_op jit(solution)/shard_map/ppermute | solution.py:619
  1064.8 13.9 %place_blocks.3 = f32[2048,2048]{1,0:T(8,128)} custom-call(s32[1]{0:T(128)} %bitcast.1.at_ref, bf16[4,256,1024]{2,1,0:T(8,128)(2,1)} %pad_maximum_fusion.7.refs_0_, bf16[4,256,1024]{2,1,0:T(8,128)(2,1)} %collective-permute-done.31.refs_1_, bf16[4,256,1024]{2,1,0:T(8,128)(2,1)} %pad_maximum_fusion.8.refs_2_, bf16[4,256,1024]{2,1,0:T(8,128)(2,1)} %collective-permute-done.34.refs_3_), custom_call_target="tpu_custom_call" | custom-call | bytes 25165824 | tf_op jit(solution)/shard_map/place_blocks/pallas_call | solution.py:651
  1085.6 13.9 %place_blocks.2 = f32[2048,2048]{1,0:T(8,128)} custom-call(s32[1]{0:T(128)} %bitcast.1.at_ref, bf16[4,256,1024]{2,1,0:T(8,128)(2,1)} %pad_maximum_fusion.5.refs_0_, bf16[4,256,1024]{2,1,0:T(8,128)(2,1)} %collective-permute-done.25.refs_1_, bf16[4,256,1024]{2,1,0:T(8,128)(2,1)} %pad_maximum_fusion.6.refs_2_, bf16[4,256,1024]{2,1,0:T(8,128)(2,1)} %collective-permute-done.28.refs_3_), custom_call_target="tpu_custom_call" | custom-call | bytes 25165824 | tf_op jit(solution)/shard_map/place_blocks/pallas_call | solution.py:651
  1099.5 11.8 %convert_element_type.66 = f32[2048,2048]{1,0:T(8,128)} convert(bf16[2048,2048]{1,0:T(8,128)(2,1)} %all-gather.17.cloned.1.call-done) | non-fusion elementwise | flops 4194304 | bytes 25165824 | tf_op jit(solution)/shard_map/convert_element_type | solution.py:831
  (203 shorter events, 191.9 us)
Async XLA Ops:
  8.0 85.9 %all-gather.19.cloned.1.call-start = ((), (), s32[]{:S(2)}) async-start(), calls=%async_computation.12 | async-start | bytes 5242880 | tf_op jit(solution)/shard_map/all_gather | solution.py:754
  8.8 113.8 %all-gather.23.cloned.1.call-start = ((), (), s32[]{:S(2)}) async-start(), calls=%async_computation.14 | async-start | bytes 1310720 | tf_op jit(solution)/shard_map/all_gather | solution.py:756
  10.4 160.8 %reduce-scatter.5.cloned.1.call-start = ((), (), s32[]{:S(2)}) async-start(), calls=%async_computation.4 | async-start | bytes 73728 | tf_op jit(solution)/shard_map/reduce_scatter | solution.py:42
  11.9 192.9 %all-gather.21.cloned.1.call-start = ((), (), s32[]{:S(2)}) async-start(), calls=%async_computation.13 | async-start | bytes 5242880 | tf_op jit(solution)/shard_map/all_gather | solution.py:770
  116.0 169.5 %all-gather.11.cloned.1.call-start = ((), (), s32[]{:S(2)}) async-start(), calls=%async_computation.5 | async-start | bytes 5242880 | tf_op jit(solution)/shard_map/all_gather | solution.py:38
  140.5 350.8 %all-gather.13.cloned.1.call-start = ((), (), s32[]{:S(2)}) async-start(), calls=%async_computation.6 | async-start | bytes 5242880 | tf_op jit(solution)/shard_map/all_gather | solution.py:38
  331.9 51.7 %collective-permute-start.13 = (bf16[256,2048]{1,0:T(8,128)(2,1)}, bf16[256,2048]{1,0:T(8,128)(2,1)}, u32[]{:S(2)}, u32[]{:S(2)}) collective-permute-start(bf16[256,2048]{1,0:T(8,128)(2,1)} %get-tuple-element.51), channel_id=1, source_target_pairs={{0,2},{1,3},{2,0},{3,1},{4,6},{5,7},{6,4},{7,5},{8,10},{9,11},{10,... | collective-permute-start | bytes 3145736 | tf_op jit(solution)/shard_map/ppermute | solution.py:619
  333.1 50.5 %collective-permute-start.14 = (bf16[256,2048]{1,0:T(8,128)(2,1)}, bf16[256,2048]{1,0:T(8,128)(2,1)}, u32[]{:S(2)}, u32[]{:S(2)}) collective-permute-start(bf16[256,2048]{1,0:T(8,128)(2,1)} %get-tuple-element.52), channel_id=1, source_target_pairs={{0,3},{1,0},{2,1},{3,2},{4,7},{5,4},{6,5},{7,6},{8,11},{9,8},{10,9... | collective-permute-start | bytes 3145736 | tf_op jit(solution)/shard_map/ppermute | solution.py:619
  389.8 196.8 %reduce-scatter.7.cloned.1.call-start = ((), (), s32[]{:S(2)}) async-start(), calls=%async_computation.7 | async-start | bytes 5898240 | tf_op jit(solution)/shard_map/reduce_scatter | solution.py:42
  531.7 175.0 %reduce-scatter.9.cloned.1.call-start = ((), (), s32[]{:S(2)}) async-start(), calls=%async_computation.9 | async-start | bytes 18874368 | tf_op jit(solution)/shard_map/reduce_scatter | solution.py:42
  555.7 226.5 %reduce-scatter.11.cloned.1.call-start = ((), (), s32[]{:S(2)}) async-start(), calls=%async_computation.11 | async-start | bytes 9437184 | tf_op jit(solution)/shard_map/reduce_scatter | solution.py:42
  569.1 509.5 %all-gather.15.cloned.1.call-start = ((), (), s32[]{:S(2)}) async-start(), calls=%async_computation.8 | async-start | bytes 5898240 | tf_op jit(solution)/shard_map/all_gather | solution.py:38
  586.7 512.8 %all-gather.17.cloned.1.call-start = ((), (), s32[]{:S(2)}) async-start(), calls=%async_computation.10 | async-start | bytes 9437184 | tf_op jit(solution)/shard_map/all_gather | solution.py:38
  726.5 78.0 %collective-permute-start.6 = (bf16[256,1024]{1,0:T(8,128)(2,1)}, bf16[256,1024]{1,0:T(8,128)(2,1)S(1)}, u32[]{:S(2)}, u32[]{:S(2)}) collective-permute-start(bf16[256,1024]{1,0:T(8,128)(2,1)} %get-tuple-element.75), channel_id=1, source_target_pairs={{0,1},{1,2},{2,3},{3,0},{4,5},{5,6},{6,7},{7,4},{8,9},{9,10},{10,1... | collective-permute-start | bytes 1572872 | tf_op jit(solution)/shard_map/ppermute | solution.py:619
  728.0 91.1 %collective-permute-start.11 = (bf16[256,1024]{1,0:T(8,128)(2,1)}, bf16[256,1024]{1,0:T(8,128)(2,1)S(1)}, u32[]{:S(2)}, u32[]{:S(2)}) collective-permute-start(bf16[256,1024]{1,0:T(8,128)(2,1)} %get-tuple-element.76), channel_id=1, source_target_pairs={{0,3},{1,0},{2,1},{3,2},{4,7},{5,4},{6,5},{7,6},{8,11},{9,8},{10,9... | collective-permute-start | bytes 1572872 | tf_op jit(solution)/shard_map/ppermute | solution.py:619
  786.8 30.0 %collective-permute-start.26 = (bf16[1,256,1024]{2,1,0:T(8,128)(2,1)S(1)}, bf16[1,256,1024]{2,1,0:T(8,128)(2,1)S(1)}, u32[]{:S(2)}, u32[]{:S(2)}) collective-permute-start(bf16[1,256,1024]{2,1,0:T(8,128)(2,1)S(1)} %get-tuple-element.81), channel_id=1, source_target_pairs={{0,16},{4,20},{8,24},{12,28},{16,0},{20,4},{24,8},{28,12},{1,17},{... | collective-permute-start | bytes 1572872 | tf_op jit(solution)/shard_map/ppermute | solution.py:56
  803.6 112.0 %collective-permute-start.33 = (bf16[2,256,1024]{2,1,0:T(8,128)(2,1)S(1)}, bf16[2,256,1024]{2,1,0:T(8,128)(2,1)S(1)}, u32[]{:S(2)}, u32[]{:S(2)}) collective-permute-start(bf16[2,256,1024]{2,1,0:T(8,128)(2,1)S(1)} %pad_maximum_fusion.14), channel_id=1, source_target_pairs={{0,8},{4,12},{8,0},{12,4},{16,24},{20,28},{24,16},{28,20},{1,9},{5... | collective-permute-start | bytes 3145736 | tf_op jit(solution)/shard_map/ppermute | solution.py:56
  804.5 113.2 %collective-permute-start.30 = (bf16[2,256,1024]{2,1,0:T(8,128)(2,1)S(1)}, bf16[2,256,1024]{2,1,0:T(8,128)(2,1)S(1)}, u32[]{:S(2)}, u32[]{:S(2)}) collective-permute-start(bf16[2,256,1024]{2,1,0:T(8,128)(2,1)S(1)} %pad_maximum_fusion.13), channel_id=1, source_target_pairs={{0,16},{4,20},{8,24},{12,28},{16,0},{20,4},{24,8},{28,12},{1,17},{... | collective-permute-start | bytes 3145736 | tf_op jit(solution)/shard_map/ppermute | solution.py:56
  816.8 72.7 %collective-permute-start.23 = (bf16[1,256,1024]{2,1,0:T(8,128)(2,1)S(1)}, bf16[1,256,1024]{2,1,0:T(8,128)(2,1)S(1)}, u32[]{:S(2)}, u32[]{:S(2)}) collective-permute-start(bf16[1,256,1024]{2,1,0:T(8,128)(2,1)S(1)} %get-tuple-element.82), channel_id=1, source_target_pairs={{0,8},{4,12},{8,0},{12,4},{16,24},{20,28},{24,16},{28,20},{1,9},{5... | collective-permute-start | bytes 1572872 | tf_op jit(solution)/shard_map/ppermute | solution.py:56
  818.2 101.4 %collective-permute-start.27 = (bf16[2,256,1024]{2,1,0:T(8,128)(2,1)S(1)}, bf16[2,256,1024]{2,1,0:T(8,128)(2,1)S(1)}, u32[]{:S(2)}, u32[]{:S(2)}) collective-permute-start(bf16[2,256,1024]{2,1,0:T(8,128)(2,1)S(1)} %pad_maximum_fusion.12), channel_id=1, source_target_pairs={{0,8},{4,12},{8,0},{12,4},{16,24},{20,28},{24,16},{28,20},{1,9},{5... | collective-permute-start | bytes 3145736 | tf_op jit(solution)/shard_map/ppermute | solution.py:56
  819.0 68.2 %collective-permute-start.19 = (f32[4096]{0:T(1024)S(1)}, f32[4096]{0:T(1024)S(1)}, u32[]{:S(2)}, u32[]{:S(2)}) collective-permute-start(f32[4096]{0:T(1024)S(1)} %add.130), channel_id=1, source_target_pairs={{0,8},{4,12},{8,0},{12,4},{16,24},{20,28},{24,16},{28,20},{1,9},{5... | collective-permute-start | bytes 49160 | tf_op jit(solution)/shard_map/ppermute | solution.py:69
  894.1 114.7 %collective-permute-start.24 = (bf16[2,256,1024]{2,1,0:T(8,128)(2,1)S(1)}, bf16[2,256,1024]{2,1,0:T(8,128)(2,1)S(1)}, u32[]{:S(2)}, u32[]{:S(2)}) collective-permute-start(bf16[2,256,1024]{2,1,0:T(8,128)(2,1)S(1)} %pad_maximum_fusion.11), channel_id=1, source_target_pairs={{0,16},{4,20},{8,24},{12,28},{16,0},{20,4},{24,8},{28,12},{1,17},{... | collective-permute-start | bytes 3145736 | tf_op jit(solution)/shard_map/ppermute | solution.py:56
  915.3 116.3 %collective-permute-start.15 = (bf16[256,2048]{1,0:T(8,128)(2,1)S(1)}, bf16[256,2048]{1,0:T(8,128)(2,1)S(1)}, u32[]{:S(2)}, u32[]{:S(2)}) collective-permute-start(bf16[256,2048]{1,0:T(8,128)(2,1)S(1)} %copy-done.26), channel_id=1, source_target_pairs={{0,1},{1,2},{2,3},{3,0},{4,5},{5,6},{6,7},{7,4},{8,9},{9,10},{10,1... | collective-permute-start | bytes 3145736 | tf_op jit(solution)/shard_map/ppermute | solution.py:619
  915.6 38.9 %collective-permute-start.9 = (bf16[256,1024]{1,0:T(8,128)(2,1)S(1)}, bf16[256,1024]{1,0:T(8,128)(2,1)S(1)}, u32[]{:S(2)}, u32[]{:S(2)}) collective-permute-start(bf16[256,1024]{1,0:T(8,128)(2,1)S(1)} %copy-done.20), channel_id=1, source_target_pairs={{0,1},{1,2},{2,3},{3,0},{4,5},{5,6},{6,7},{7,4},{8,9},{9,10},{10,1... | collective-permute-start | bytes 1572872 | tf_op jit(solution)/shard_map/ppermute | solution.py:619
  917.7 70.4 %collective-permute-start.8 = (bf16[256,1024]{1,0:T(8,128)(2,1)S(1)}, bf16[256,1024]{1,0:T(8,128)(2,1)S(1)}, u32[]{:S(2)}, u32[]{:S(2)}) collective-permute-start(bf16[256,1024]{1,0:T(8,128)(2,1)S(1)} %copy-done.19), channel_id=1, source_target_pairs={{0,3},{1,0},{2,1},{3,2},{4,7},{5,4},{6,5},{7,6},{8,11},{9,8},{10,9... | collective-permute-start | bytes 1572872 | tf_op jit(solution)/shard_map/ppermute | solution.py:619
  919.6 89.3 %collective-permute-start.7 = (bf16[256,1024]{1,0:T(8,128)(2,1)S(1)}, bf16[256,1024]{1,0:T(8,128)(2,1)S(1)}, u32[]{:S(2)}, u32[]{:S(2)}) collective-permute-start(bf16[256,1024]{1,0:T(8,128)(2,1)S(1)} %copy-done.18), channel_id=1, source_target_pairs={{0,2},{1,3},{2,0},{3,1},{4,6},{5,7},{6,4},{7,5},{8,10},{9,11},{10,... | collective-permute-start | bytes 1572872 | tf_op jit(solution)/shard_map/ppermute | solution.py:619
  954.5 77.7 %collective-permute-start.16 = (bf16[256,2048]{1,0:T(8,128)(2,1)}, bf16[256,2048]{1,0:T(8,128)(2,1)S(1)}, u32[]{:S(2)}, u32[]{:S(2)}) collective-permute-start(bf16[256,2048]{1,0:T(8,128)(2,1)} %get-tuple-element.58), channel_id=1, source_target_pairs={{0,2},{1,3},{2,0},{3,1},{4,6},{5,7},{6,4},{7,5},{8,10},{9,11},{10,... | collective-permute-start | bytes 3145736 | tf_op jit(solution)/shard_map/ppermute | solution.py:619
  988.1 43.5 %collective-permute-start.22 = (f32[4096]{0:T(1024)S(1)}, f32[4096]{0:T(1024)S(1)}, u32[]{:S(2)}, u32[]{:S(2)}) collective-permute-start(f32[4096]{0:T(1024)S(1)} %add.133), channel_id=1, source_target_pairs={{0,2},{1,3},{2,0},{3,1},{4,6},{5,7},{6,4},{7,5},{8,10},{9,11},{10,... | collective-permute-start | bytes 49160 | tf_op jit(solution)/shard_map/ppermute | solution.py:69
  1008.9 55.9 %collective-permute-start.31 = (bf16[4,256,1024]{2,1,0:T(8,128)(2,1)}, bf16[4,256,1024]{2,1,0:T(8,128)(2,1)}, u32[]{:S(2)}, u32[]{:S(2)}) collective-permute-start(bf16[4,256,1024]{2,1,0:T(8,128)(2,1)} %pad_maximum_fusion.7.refs_0_), channel_id=1, source_target_pairs={{0,4},{4,0},{8,12},{12,8},{16,20},{20,16},{24,28},{28,24},{1,5},{5... | collective-permute-start | bytes 6291464 | tf_op jit(solution)/shard_map/ppermute | solution.py:56
  1008.9 55.9 %collective-permute-start.34 = (bf16[4,256,1024]{2,1,0:T(8,128)(2,1)}, bf16[4,256,1024]{2,1,0:T(8,128)(2,1)}, u32[]{:S(2)}, u32[]{:S(2)}) collective-permute-start(bf16[4,256,1024]{2,1,0:T(8,128)(2,1)} %pad_maximum_fusion.8.refs_2_), channel_id=1, source_target_pairs={{0,4},{4,0},{8,12},{12,8},{16,20},{20,16},{24,28},{28,24},{1,5},{5... | collective-permute-start | bytes 6291464 | tf_op jit(solution)/shard_map/ppermute | solution.py:56
  1031.6 54.0 %collective-permute-start.25 = (bf16[4,256,1024]{2,1,0:T(8,128)(2,1)}, bf16[4,256,1024]{2,1,0:T(8,128)(2,1)}, u32[]{:S(2)}, u32[]{:S(2)}) collective-permute-start(bf16[4,256,1024]{2,1,0:T(8,128)(2,1)} %pad_maximum_fusion.5.refs_0_), channel_id=1, source_target_pairs={{0,4},{4,0},{8,12},{12,8},{16,20},{20,16},{24,28},{28,24},{1,5},{5... | collective-permute-start | bytes 6291464 | tf_op jit(solution)/shard_map/ppermute | solution.py:56
  1031.6 54.0 %collective-permute-start.28 = (bf16[4,256,1024]{2,1,0:T(8,128)(2,1)}, bf16[4,256,1024]{2,1,0:T(8,128)(2,1)}, u32[]{:S(2)}, u32[]{:S(2)}) collective-permute-start(bf16[4,256,1024]{2,1,0:T(8,128)(2,1)} %pad_maximum_fusion.6.refs_2_), channel_id=1, source_target_pairs={{0,4},{4,0},{8,12},{12,8},{16,20},{20,16},{24,28},{28,24},{1,5},{5... | collective-permute-start | bytes 6291464 | tf_op jit(solution)/shard_map/ppermute | solution.py:56
  (41 other events, 1297.0 us)
Sparse Core Ops, SparseCore 0:
  10.4 83.4 all-gather.18
  96.0 26.4 all-gather.22
  124.7 80.1 all-gather.20
  206.3 79.2 all-gather.10
  389.9 101.2 all-gather.12
Sparse Core Ops, SparseCore 1:
  14.4 36.2 reduce-scatter.4
  531.8 54.8 reduce-scatter.6
  590.7 116.0 reduce-scatter.8
  710.8 71.3 reduce-scatter.10
  784.1 62.2 all-gather.14
  848.2 81.2 all-gather.16
